TPU v7x, 32 devices: a whole 2x2x4 slice. The times are simulated.
32 devices in a mesh: tm: 8 (over z, x), height: 2 (over y), width: 2 (over core).
Axes of the slice: x: 2, y: 2, z: 4, core: 2. Of those that a mesh axis runs over, the one named last changes fastest.
Arguments:
- features: bfloat16 [32, 32, 64, 128], P('tm', 'height', 'width'), may hold values from -6 to 6
- grad_out: bfloat16 [32, 32, 64, 128], P('tm', 'height', 'width'), may hold values from -60 to 60
- mean_saved: float32 [32, 32], P('tm'), may hold values from -3 to 3
- rstd_saved: float32 [32, 32], P('tm'), may hold values from 0.5 to 2
- gain: float32 [128], replicated, may hold values from 0.5 to 1.5
- bias: float32 [128], replicated, may hold values from -3 to 3
- weight: bfloat16 [3, 3, 3, 128, 128], replicated, may hold values from -0.109375 to 0.109375
- future_cot: bfloat16 [2, 32, 64, 128], P(None, 'height', 'width'), may hold values from -6 to 6
Outputs:
- input_cot: bfloat16 [32, 32, 64, 128], P('tm', 'height', 'width')
- weight_grad: float32 [3456, 128], P('tm')
All inputs are finite; a program needn't handle non-finite values.
Results may differ from a plain program's by a relative error of at most 0.003.
Values may be sent and summed in bfloat16 or wider, within the bound.
No kernel may reach another device: no remote copies, remote signals or barrier semaphores. Data moves between devices by JAX's collectives and lax.ppermute only.
A program may use at most 64 MiB of HBM per device.

v0:
```python
import math

import jax
import jax.numpy as jnp
from jax import lax
from jax.sharding import PartitionSpec as P


def extended_2(cells, sides, width):
    for axis, dim in sides:
        count = lax.axis_size(axis)
        ends = count - 1
        head = lax.slice_in_dim(cells, 0, width, axis=dim)
        tail = lax.slice_in_dim(cells, cells.shape[dim] - width, cells.shape[dim], axis=dim)
        cells = jnp.concatenate(
            [
                lax.ppermute(tail, axis, [(i, (i + 1) % count) for i in range(ends)]),
                cells,
                lax.ppermute(head, axis, [((i + 1) % count, i) for i in range(ends)]),
            ],
            axis=dim,
        )
    return cells


def shifted(value, axis, steps):
    count = lax.axis_size(axis)
    initial, last = (max(0, -steps), min(count, count - steps))
    return lax.ppermute(value, axis, [(source, source + steps) for source in range(initial, last)])


def on_device(features, grad_out, mean_saved, rstd_saved, gain, bias, weight, future_cot):
    frame_count, row_count, col_count, channels = features.shape
    groups = mean_saved.shape[1]
    group_width = channels // groups
    grouped_in = features.astype(jnp.float32).reshape(
        frame_count, row_count, col_count, groups, group_width
    )
    centred = (grouped_in - mean_saved[:, None, None, :, None]) * rstd_saved[:, None, None, :, None]
    normed = centred.reshape(frame_count, row_count, col_count, channels)
    pre_act = normed * gain + bias
    sigmoid_val = jax.nn.sigmoid(pre_act)
    activation = (pre_act * sigmoid_val).astype(jnp.bfloat16)
    flat_act = activation.reshape(-1, channels)
    padded = extended_2(grad_out, (("height", 1), ("width", 2)), 1)
    following = shifted(padded[:2], "tm", -1)
    extended = jnp.concatenate([padded, following], axis=0)
    act_cot = jnp.zeros((flat_act.shape[0], channels), jnp.float32)
    blocks = []
    for lag_t in range(3):
        for lag_h in range(3):
            for lag_w in range(3):
                window = extended[
                    2 - lag_t : 2 - lag_t + frame_count,
                    2 - lag_h : 2 - lag_h + row_count,
                    2 - lag_w : 2 - lag_w + col_count,
                ].reshape(-1, channels)
                act_cot = act_cot + lax.dot_general(
                    window,
                    weight[lag_t, lag_h, lag_w],
                    (((1,), (1,)), ((), ())),
                    preferred_element_type=jnp.float32,
                )
                blocks.append(
                    lax.dot_general(
                        flat_act,
                        window,
                        (((0,), (0,)), ((), ())),
                        preferred_element_type=jnp.float32,
                    )
                )
    act_cot = act_cot.reshape(frame_count, row_count, col_count, channels)
    is_last = lax.axis_index("tm") == lax.axis_size("tm") - 1
    tail_cot = jnp.where(
        is_last, future_cot.astype(jnp.float32), jnp.zeros(future_cot.shape, jnp.float32)
    )
    act_cot = jnp.concatenate(
        [act_cot[: frame_count - 2], act_cot[frame_count - 2 :] + tail_cot], axis=0
    )
    scaled = act_cot * sigmoid_val * (1.0 + pre_act * (1.0 - sigmoid_val)) * gain
    scaled_groups = scaled.reshape(frame_count, row_count, col_count, groups, group_width)
    sum_first = jnp.sum(scaled_groups, axis=(1, 2, 4))
    sum_second = jnp.sum(scaled_groups * centred, axis=(1, 2, 4))
    total_first, total_second = lax.psum((sum_first, sum_second), ("height", "width"))
    count = row_count * lax.axis_size("height") * col_count * lax.axis_size("width") * group_width
    first = total_first / count
    second = total_second / count
    corrected = rstd_saved[:, None, None, :, None] * (
        scaled_groups - first[:, None, None, :, None] - centred * second[:, None, None, :, None]
    )
    input_cot = (
        grad_out.astype(jnp.float32)
        + corrected.reshape(frame_count, row_count, col_count, channels)
    ).astype(jnp.bfloat16)
    all_cells = (
        frame_count
        * lax.axis_size("tm")
        * row_count
        * lax.axis_size("height")
        * col_count
        * lax.axis_size("width")
    )
    grad_scale = 1.0 / math.sqrt(all_cells)
    local_weight = jnp.stack(blocks).reshape(27 * channels, channels) * grad_scale
    weight_total = lax.psum(local_weight, ("tm", "height", "width"))
    share_rows = weight_total.shape[0] // lax.axis_size("tm")
    weight_grad = lax.dynamic_slice_in_dim(
        weight_total, lax.axis_index("tm") * share_rows, share_rows, 0
    )
    return (input_cot, weight_grad)


def solution(mesh):
    placed = (
        P("tm", "height", "width", None),
        P("tm", "height", "width", None),
        P("tm", None),
        P("tm", None),
        P(),
        P(),
        P(),
        P(None, "height", "width", None),
    )
    return jax.shard_map(
        on_device,
        mesh=mesh,
        in_specs=placed,
        out_specs=(P("tm", "height", "width", None), P("tm", None)),
        check_vma=False,
    )
```

profile of v0, /device:TPU:0, one launch (start us, length us, event | category | flops | bytes accessed | tf_op | source)
XLA Modules:
  0.0 202.9 jit_solution(10719018335675998459)
XLA Ops:
  7.2 0.8 fusion.117
  8.0 4.9 %collective-permute-start = (bf16[4,1,32,128]{3,2,1,0:T(8,128)(2,1)S(1)}, bf16[4,1,32,128]{3,2,1,0:T(8,128)(2,1)S(1)}, u32[]{:S(2)}, u32[]{:S(2)}) collective-permute-start(bf16[4,1,32,128]{3,2,1,0:T(8,128)(2,1)S(1)} %get-tuple-element.42), channel_id=1, source_target_pairs={{0,2},{1,3},{4,6},{5,7},{8,10},{9,11},{12,14},{13,15},{16,18},{17,... | collective-permute-start | bytes 98312 | tf_op jit(solution)/shard_map/ppermute | solution.py:17
  12.9 1.3 collective-permute-start.1
  14.2 0.8 mul.77
  15.1 0.8 sub.35
  16.0 2.7 %collective-permute-done.1 = bf16[4,1,32,128]{3,2,1,0:T(8,128)(2,1)S(1)} collective-permute-done((bf16[4,1,32,128]{3,2,1,0:T(8,128)(2,1)S(1)}, bf16[4,1,32,128]{3,2,1,0:T(8,128)(2,1)S(1)}, u32[]{:S(2)}, u32[]{:S(2)}) %collective-permute-start.1) | collective-permute-done | bytes 32800 | tf_op jit(solution)/shard_map/ppermute | solution.py:19
  18.7 1.8 pad_maximum_fusion.4
  20.6 1.3 collective-permute-start.2
  21.9 1.3 collective-permute-start.3
  23.2 1.1 fusion.38
  24.3 0.7 collective-permute-done.3
  25.2 1.3 collective-permute-start.4
  26.5 0.9 pad_maximum_fusion.3
  27.4 1.1 fusion.44
  28.5 2.0 %fusion.36 = f32[2048,128]{1,0:T(8,128)} fusion(bf16[2048,128]{1,0:T(8,128)(2,1)S(1)} %bitcast.388, bf16[3,3,3,128,128]{4,3,2,1,0:T(8,128)(2,1)} %param.14), kind=kOutput, calls=%fused_computation.113 | convolution fusion | flops 67108864 | bytes 1605632 | tf_op jit(solution)/shard_map/dot_general | solution.py:58
  30.6 7.4 %collective-permute-done.4 = bf16[2,18,34,128]{3,2,1,0:T(8,128)(2,1)S(1)} collective-permute-done((bf16[2,18,34,128]{3,2,1,0:T(8,128)(2,1)S(1)}, bf16[2,18,34,128]{3,2,1,0:T(8,128)(2,1)S(1)}, u32[]{:S(2)}, u32[]{:S(2)}) %collective-permute-start.4) | collective-permute-done | bytes 313376 | tf_op jit(solution)/shard_map/ppermute | solution.py:29
  38.4 4.2 %fusion.114 = (bf16[4,16,32,128]{3,2,1,0:T(8,128)(2,1)}, bf16[4,16,32,128]{3,2,1,0:T(8,128)(2,1)}, bf16[4,16,32,128]{3,2,1,0:T(8,128)(2,1)}, bf16[4,16,32,128]{3...) fusion(bf16[6,18,34,128]{3,2,1,0:T(8,128)(2,1)S(1)} %pad_maximu, ...), kind=kLoop, calls=%fused_computation.193 | loop fusion | bytes 18874368 | tf_op jit(solution)/shard_map/slice | solution.py:53
  42.6 0.7 fusion.29
  43.3 0.7 fusion.28
  44.0 0.6 fusion.27
  44.5 0.7 fusion.26
  45.2 0.7 fusion.25
  45.9 0.6 fusion.24
  46.4 0.7 fusion.23
  47.1 0.7 fusion.22
  47.8 0.6 fusion.21
  48.3 0.7 fusion.20
  49.0 0.7 fusion.19
  49.7 0.6 fusion.18
  50.2 0.7 fusion.17
  50.9 0.7 fusion.16
  51.6 0.6 fusion.15
  52.2 0.7 fusion.14
  52.8 0.7 fusion.13
  53.5 0.6 fusion.12
  54.1 0.6 fusion.11
  54.7 0.6 fusion.10
  55.2 0.8 fusion.9
  56.0 0.6 fusion.8
  57.1 0.6 fusion.7
  57.6 0.6 fusion.6
  58.2 0.6 fusion.5
  58.8 0.6 fusion.4
  59.3 0.6 fusion.3
  59.9 1.4 broadcast_multiply_fusion
  61.4 1.5 fusion.64
  62.8 1.1 convolution_add_fusion.22
  64.3 0.7 copy-done.19
  65.6 0.7 copy-done.17
  67.0 0.7 copy-done.15
  68.4 0.7 copy-done.13
  69.8 0.6 copy-done.11
  71.2 0.7 copy-done.9
  72.6 0.6 copy-done.7
  74.0 0.6 copy-done.5
  75.3 0.6 copy-done.4
  76.3 0.7 copy-done.27
  77.6 0.7 copy-done.25
  79.4 0.9 copy-done.31
  80.4 0.6 fusion.112
  81.4 5.9 %all-reduce = (f32[4,32]{1,0:T(4,128)S(1)}, f32[4,32]{1,0:T(4,128)S(1)}) all-reduce(f32[4,32]{1,0:T(4,128)S(1)} %reduce_sum.37, f32[4,32]{1,0:T(4,128)S(1)} %reduce_sum.25), channel_id=1, replica_groups=mesh['tm'=8,'height'=2,'width'=2] {'height','width'}, use_global_device_ids=true, to_apply=%region_5.6 | all-reduce | flops 256 | bytes 2048 | tf_op jit(solution)/shard_map/psum | solution.py:84
  87.8 1.2 add_convert_fusion
  88.9 105.5 %all-reduce.3.cloned.1.call-done = f32[3456,128]{1,0:T(8,128)} async-done(((f32[3456,128]{1,0:T(8,128)}), f32[3456,128]{1,0:T(8,128)}) %all-reduce.3.cloned.1.call-update) | async-done | bytes 1769488 | tf_op jit(solution)/shard_map/psum | solution.py:105
  194.4 1.6 constant_dynamic-slice_fusion
  (100 shorter events, 10.1 us)
Async XLA Ops:
  7.2 187.3 %all-reduce.3.cloned.1.call-start = ((), (), s32[]{:S(2)}) async-start(), calls=%async_computation | async-start | bytes 3538944 | tf_op jit(solution)/shard_map/psum | solution.py:105
  8.0 8.0 %collective-permute-start = (bf16[4,1,32,128]{3,2,1,0:T(8,128)(2,1)S(1)}, bf16[4,1,32,128]{3,2,1,0:T(8,128)(2,1)S(1)}, u32[]{:S(2)}, u32[]{:S(2)}) collective-permute-start(bf16[4,1,32,128]{3,2,1,0:T(8,128)(2,1)S(1)} %get-tuple-element.42), channel_id=1, source_target_pairs={{0,2},{1,3},{4,6},{5,7},{8,10},{9,11},{12,14},{13,15},{16,18},{17,... | collective-permute-start | bytes 98312 | tf_op jit(solution)/shard_map/ppermute | solution.py:17
  12.9 5.8 %collective-permute-start.1 = (bf16[4,1,32,128]{3,2,1,0:T(8,128)(2,1)S(1)}, bf16[4,1,32,128]{3,2,1,0:T(8,128)(2,1)S(1)}, u32[]{:S(2)}, u32[]{:S(2)}) collective-permute-start(bf16[4,1,32,128]{3,2,1,0:T(8,128)(2,1)S(1)} %get-tuple-element.41), channel_id=1, source_target_pairs={{2,0},{3,1},{6,4},{7,5},{10,8},{11,9},{14,12},{15,13},{18,16},{19,... | collective-permute-start | bytes 98312 | tf_op jit(solution)/shard_map/ppermute | solution.py:19
  20.5 34.1 %copy-start.3 = (bf16[4,16,32,128]{3,2,1,0:T(8,128)(2,1)}, bf16[4,16,32,128]{3,2,1,0:T(8,128)(2,1)S(1)}, u32[]{:S(2)}) copy-start(bf16[4,16,32,128]{3,2,1,0:T(8,128)(2,1)S(1)} %get-tuple-element.38) | copy-start | bytes 1572868
  20.6 3.7 %collective-permute-start.2 = (bf16[4,18,1,128]{3,2,1,0:T(2,128)(2,1)S(1)}, bf16[4,18,1,128]{3,2,1,0:T(2,128)(2,1)S(1)}, u32[]{:S(2)}, u32[]{:S(2)}) collective-permute-start(bf16[4,18,1,128]{3,2,1,0:T(2,128)(2,1)S(1)} %get-tuple-element.37), channel_id=1, source_target_pairs={{0,1},{2,3},{4,5},{6,7},{8,9},{10,11},{12,13},{14,15},{16,17},{18,... | collective-permute-start | bytes 55304 | tf_op jit(solution)/shard_map/ppermute | solution.py:17
  21.9 3.1 %collective-permute-start.3 = (bf16[4,18,1,128]{3,2,1,0:T(2,128)(2,1)S(1)}, bf16[4,18,1,128]{3,2,1,0:T(2,128)(2,1)S(1)}, u32[]{:S(2)}, u32[]{:S(2)}) collective-permute-start(bf16[4,18,1,128]{3,2,1,0:T(2,128)(2,1)S(1)} %get-tuple-element.36), channel_id=1, source_target_pairs={{1,0},{3,2},{5,4},{7,6},{9,8},{11,10},{13,12},{15,14},{17,16},{19,... | collective-permute-start | bytes 55304 | tf_op jit(solution)/shard_map/ppermute | solution.py:19
  25.2 12.8 %collective-permute-start.4 = (bf16[2,18,34,128]{3,2,1,0:T(8,128)(2,1)S(1)}, bf16[2,18,34,128]{3,2,1,0:T(8,128)(2,1)S(1)}, u32[]{:S(2)}, u32[]{:S(2)}) collective-permute-start(bf16[2,18,34,128]{3,2,1,0:T(8,128)(2,1)S(1)} %pad_maximum_fusion.5), channel_id=1, source_target_pairs={{4,0},{8,4},{12,8},{16,12},{20,16},{24,20},{28,24},{5,1},{9,5},{13... | collective-permute-start | bytes 940040 | tf_op jit(solution)/shard_map/ppermute | solution.py:29
  27.4 26.7 %copy-start.28 = (bf16[4,16,32,128]{3,2,1,0:T(8,128)(2,1)}, bf16[4,16,32,128]{3,2,1,0:T(8,128)(2,1)S(1)}, u32[]{:S(2)}) copy-start(bf16[4,16,32,128]{3,2,1,0:T(8,128)(2,1)S(1)} %get-tuple-element.28) | copy-start | bytes 1572868
  27.4 28.6 %copy-start.26 = (bf16[4,16,32,128]{3,2,1,0:T(8,128)(2,1)}, bf16[4,16,32,128]{3,2,1,0:T(8,128)(2,1)S(1)}, u32[]{:S(2)}) copy-start(bf16[4,16,32,128]{3,2,1,0:T(8,128)(2,1)S(1)} %get-tuple-element.29) | copy-start | bytes 1572868
  27.4 30.2 %copy-start.24 = (bf16[4,16,32,128]{3,2,1,0:T(8,128)(2,1)}, bf16[4,16,32,128]{3,2,1,0:T(8,128)(2,1)S(1)}, u32[]{:S(2)}) copy-start(bf16[4,16,32,128]{3,2,1,0:T(8,128)(2,1)S(1)} %get-tuple-element.35) | copy-start | bytes 1572868
  27.4 30.8 %copy-start.22 = (bf16[4,16,32,128]{3,2,1,0:T(8,128)(2,1)}, bf16[4,16,32,128]{3,2,1,0:T(8,128)(2,1)S(1)}, u32[]{:S(2)}) copy-start(bf16[4,16,32,128]{3,2,1,0:T(8,128)(2,1)S(1)} %get-tuple-element.27) | copy-start | bytes 1572868
  38.4 4.2 %copy-start.2 = (bf16[4,16,32,128]{3,2,1,0:T(8,128)(2,1)S(1)}, bf16[4,16,32,128]{3,2,1,0:T(8,128)(2,1)}, u32[]{:S(2)}) copy-start(bf16[4,16,32,128]{3,2,1,0:T(8,128)(2,1)} %param.8) | copy-start | bytes 1572868
  38.4 4.2 %copy-start.32 = (f32[128]{0:T(128)S(1)}, f32[128]{0:T(128)}, u32[]{:S(2)}) copy-start(f32[128]{0:T(128)} %param.13) | copy-start | bytes 1540
  38.4 4.2 %copy-start.33 = (f32[128]{0:T(128)S(1)}, f32[128]{0:T(128)}, u32[]{:S(2)}) copy-start(f32[128]{0:T(128)} %param.12) | copy-start | bytes 1540
  56.0 1.0 copy-start
  61.3 1.5 copy-start.21
  61.3 2.6 %copy-start.20 = (bf16[4,16,32,128]{3,2,1,0:T(8,128)(2,1)S(1)}, bf16[4,16,32,128]{3,2,1,0:T(8,128)(2,1)}, u32[]{:S(2)}) copy-start(bf16[4,16,32,128]{3,2,1,0:T(8,128)(2,1)} %get-tuple-element.22) | copy-start | bytes 1572868
  61.3 2.6 %copy-start.30 = (bf16[3,3,3,128,128]{4,3,2,1,0:T(8,128)(2,1)S(1)}, bf16[3,3,3,128,128]{4,3,2,1,0:T(8,128)(2,1)}, u32[]{:S(2)}) copy-start(bf16[3,3,3,128,128]{4,3,2,1,0:T(8,128)(2,1)} %param.14) | copy-start | bytes 2654212
  63.9 1.0 copy-start.19
  64.2 1.1 copy-start.18
  65.3 1.1 copy-start.17
  65.6 1.1 copy-start.16
  66.6 1.1 copy-start.15
  67.0 1.1 copy-start.14
  68.0 1.1 copy-start.13
  68.4 1.1 copy-start.12
  69.4 1.1 copy-start.11
  69.8 1.1 copy-start.10
  70.7 1.1 copy-start.9
  71.2 1.1 copy-start.8
  72.1 1.1 copy-start.7
  72.6 1.1 copy-start.6
  73.5 1.1 copy-start.5
  73.9 1.1 copy-start.29
  74.9 1.1 copy-start.4
  76.0 1.0 copy-start.27
  77.3 1.0 copy-start.25
  77.6 1.3 copy-start.1
  77.6 1.4 copy-start.23
  79.3 1.0 copy-start.31
Sparse Core Ops, SparseCore 0:
  61.4 132.9 all-reduce.2
where the time goes:
time: 204 us; the launch traced here: 203 us
  waiting for transfers between devices  116 us (57%)
  matrix products  29.8 us (15%)
  local copies, waits for them, and re-layouts  19.1 us (9%)
  between operations  14.9 us (7%)
  starting transfers between devices  10.1 us (5%)
  other arithmetic  6.71 us (3%)
  blocking collectives  5.91 us (3%)
    psum x1, waiting for transfers between devices, on_device(): weight_total = lax.psum(local_weight, ('tm', 'height', 'width'))  106 us
    dot_general x27, matrix products, on_device(): lax.dot_general(flat_act, window, (((0,), (0,)), ((), ())), preferred_ele...  16.6 us
    dot_general x27, matrix products, on_device(): lax.dot_general(window, weight[lag_t, lag_h, lag_w], (((1,), (1,)), ((),...  13.2 us
    unnamed x69, local copies, waits for them, and re-layouts  10 us
    ppermute x1, waiting for transfers between devices, shifted(): lax.ppermute(value, axis, [(source, source + steps) for source in range(i...  7.41 us
    ppermute x2, starting transfers between devices, extended_2(): lax.ppermute(tail, axis, [(i, (i + 1) % count) for i in range(ends)])  6.18 us
    psum x1, blocking collectives, on_device(): lax.psum((sum_first, sum_second), ('height', 'width'))  5.91 us
    slice x1, local copies, waits for them, and re-layouts, on_device(): extended[2 - lag_t:2 - lag_t + frame_count, 2 - lag_h:2 - lag_h + row_cou...  4.19 us
  transfers between devices with their start and end apart: 6, of which 4 were waited for; matrix products, arithmetic and copies ran while one was open for 9% of the time, Pallas kernels for 0%

commit v1 on v0

--- a/solution.py
+++ b/solution.py
@@ -27,6 +27,74 @@
     count = lax.axis_size(axis)
     initial, last = (max(0, -steps), min(count, count - steps))
     return lax.ppermute(value, axis, [(source, source + steps) for source in range(initial, last)])
+
+
+def exchanged(value, axis, distance):
+    count = lax.axis_size(axis)
+    return lax.ppermute(value, axis, [(i, i ^ distance) for i in range(count)])
+
+
+def kept_rows(rows):
+    return -(-rows // 16) * 8
+
+
+def halved(value, axis, wire):
+    rows = value.shape[1]
+    kept = kept_rows(rows)
+    index = lax.axis_index(axis)
+    mine = lax.dynamic_slice_in_dim(value, index * (rows - kept), kept, 1)
+    theirs = lax.dynamic_slice_in_dim(value, (1 - index) * (rows - kept), kept, 1)
+    return mine + exchanged(theirs.astype(wire), axis, 1).astype(jnp.float32)
+
+
+def joined(low, high, rows):
+    kept = low.shape[0]
+    return jnp.concatenate([low, high[2 * kept - rows :]], axis=0)
+
+
+def power_of_two(count):
+    return count & (count - 1) == 0
+
+
+def reduced_share(partial):
+    rows_all, channels = partial.shape
+    blocks = lax.axis_size("tm")
+    rows = rows_all // blocks
+    pairs = lax.axis_size("height") == 2 and lax.axis_size("width") == 2
+    if not (pairs and power_of_two(blocks) and rows % 8 == 0):
+        share = lax.psum_scatter(partial, "tm", scatter_dimension=0, tiled=True)
+        return lax.psum(share, ("height", "width"))
+    value = partial.reshape(blocks, rows, channels)
+    value = halved(value, "width", jnp.float32)
+    half = value.shape[1]
+    value = halved(value, "height", jnp.bfloat16)
+    place = lax.axis_index("tm")
+    distance = 1
+    while distance < blocks:
+        side = (place // distance) % 2
+        split = value.reshape(value.shape[0] // 2, 2, *value.shape[1:])
+        mine = lax.dynamic_index_in_dim(split, side, 1, keepdims=False)
+        theirs = lax.dynamic_index_in_dim(split, 1 - side, 1, keepdims=False)
+        wire = jnp.float32 if split.shape[0] == 1 else jnp.bfloat16
+        value = mine + exchanged(theirs.astype(wire), "tm", distance).astype(jnp.float32)
+        distance *= 2
+    own = value[0]
+    beside = exchanged(own, "width", 1)
+    below = exchanged(own, "height", 1)
+    across = lax.ppermute(own, ("height", "width"), [(i, 3 - i) for i in range(4)])
+    row_side = lax.axis_index("height")
+    col_side = lax.axis_index("width")
+    mine_half = joined(
+        jnp.where(row_side == 0, own, below), jnp.where(row_side == 0, below, own), half
+    )
+    other_half = joined(
+        jnp.where(row_side == 0, beside, across), jnp.where(row_side == 0, across, beside), half
+    )
+    return joined(
+        jnp.where(col_side == 0, mine_half, other_half),
+        jnp.where(col_side == 0, other_half, mine_half),
+        rows,
+    )
 
 
 def on_device(features, grad_out, mean_saved, rstd_saved, gain, bias, weight, future_cot):
@@ -102,11 +170,7 @@
     )
     grad_scale = 1.0 / math.sqrt(all_cells)
     local_weight = jnp.stack(blocks).reshape(27 * channels, channels) * grad_scale
-    weight_total = lax.psum(local_weight, ("tm", "height", "width"))
-    share_rows = weight_total.shape[0] // lax.axis_size("tm")
-    weight_grad = lax.dynamic_slice_in_dim(
-        weight_total, lax.axis_index("tm") * share_rows, share_rows, 0
-    )
+    weight_grad = reduced_share(local_weight)
     return (input_cot, weight_grad)
 
 

time: 204 us -> 93.5 us (0.46)
  waiting for transfers between devices: 116 us -> 29.6 us
  between operations: 14.9 us -> 1.44 us
  local copies, waits for them, and re-layouts: 19.1 us -> 6.59 us
  starting transfers between devices: 10.1 us -> 18.6 us
  matrix products: 29.8 us -> 24.7 us
    psum x1 -> x0, waiting for transfers between devices: 106 us -> none  [on_device(): weight_total = lax.psum(local_weight, ('tm', 'height', 'width'))]
    ppermute x0 -> x8, waiting for transfers between devices: none -> 15.8 us  [the longest x7 14.8 us: exchanged(): return lax.ppermute(value, axis, [(i, i ^ distance) for i in range(count)])]
    unnamed x69 -> x13, local copies, waits for them, and re-layouts: 10 us -> 0.5 us
    ppermute x0 -> x8, starting transfers between devices: none -> 8.51 us  [the longest x7 6.79 us: exchanged(): return lax.ppermute(value, axis, [(i, i ^ distance) for i in range(count)])]
    dot_general x27, matrix products: 13.2 us -> 8.06 us  [on_device(): lax.dot_general(window, weight[lag_t, lag_h, lag_w], (((1,), (1,)), ((),...]
    ppermute x1, waiting for transfers between devices: 7.41 us -> 9.75 us  [shifted(): lax.ppermute(value, axis, [(source, source + steps) for source in range(i...]
  transfers between devices with their start and end apart: 6 -> 13, of which waited for: 4 -> 8; matrix products, arithmetic and copies ran while one was open for 9% -> 14% of each run, Pallas kernels for 0% -> 0%
where the time goes in v1:
time: 93.5 us; the launch traced here: 93.1 us
  waiting for transfers between devices  29.6 us (32%)
  matrix products  24.7 us (26%)
  starting transfers between devices  18.6 us (20%)
  local copies, waits for them, and re-layouts  6.59 us (7%)
  other arithmetic  6.35 us (7%)
  blocking collectives  5.89 us (6%)
  between operations  1.44 us (2%)
    dot_general x27, matrix products, on_device(): lax.dot_general(flat_act, window, (((0,), (0,)), ((), ())), preferred_ele...  16.6 us
    ppermute x7, waiting for transfers between devices, exchanged(): return lax.ppermute(value, axis, [(i, i ^ distance) for i in range(count)])  14.8 us
    ppermute x1, waiting for transfers between devices, shifted(): lax.ppermute(value, axis, [(source, source + steps) for source in range(i...  9.75 us
    dot_general x27, matrix products, on_device(): lax.dot_general(window, weight[lag_t, lag_h, lag_w], (((1,), (1,)), ((),...  8.06 us
    ppermute x7, starting transfers between devices, exchanged(): return lax.ppermute(value, axis, [(i, i ^ distance) for i in range(count)])  6.79 us
    ppermute x2, starting transfers between devices, extended_2(): lax.ppermute(tail, axis, [(i, (i + 1) % count) for i in range(ends)])  6.18 us
    psum x1, blocking collectives, on_device(): lax.psum((sum_first, sum_second), ('height', 'width'))  5.89 us
    ppermute x2, waiting for transfers between devices, extended_2(): lax.ppermute(head, axis, [((i + 1) % count, i) for i in range(ends)])  4.09 us
  transfers between devices with their start and end apart: 13, of which 8 were waited for; matrix products, arithmetic and copies ran while one was open for 14% of the time, Pallas kernels for 0%

profile of v1, /device:TPU:0, one launch (start us, length us, event | category | flops | bytes accessed | tf_op | source)
XLA Modules:
  0.0 93.1 jit_solution(10049379913267681392)
XLA Ops:
  0.6 0.9 fusion.121
  1.5 4.9 %collective-permute-start = (bf16[4,1,32,128]{3,2,1,0:T(8,128)(2,1)S(1)}, bf16[4,1,32,128]{3,2,1,0:T(8,128)(2,1)S(1)}, u32[]{:S(2)}, u32[]{:S(2)}) collective-permute-start(bf16[4,1,32,128]{3,2,1,0:T(8,128)(2,1)S(1)} %get-tuple-element.42), channel_id=1, source_target_pairs={{0,2},{1,3},{4,6},{5,7},{8,10},{9,11},{12,14},{13,15},{16,18},{17,... | collective-permute-start | bytes 98312 | tf_op jit(solution)/shard_map/ppermute | solution.py:17
  6.4 1.3 %collective-permute-start.1 = (bf16[4,1,32,128]{3,2,1,0:T(8,128)(2,1)S(1)}, bf16[4,1,32,128]{3,2,1,0:T(8,128)(2,1)S(1)}, u32[]{:S(2)}, u32[]{:S(2)}) collective-permute-start(bf16[4,1,32,128]{3,2,1,0:T(8,128)(2,1)S(1)} %get-tuple-element.41), channel_id=1, source_target_pairs={{2,0},{3,1},{6,4},{7,5},{10,8},{11,9},{14,12},{15,13},{18,16},{19,... | collective-permute-start | bytes 98312 | tf_op jit(solution)/shard_map/ppermute | solution.py:19
  7.8 0.8 mul.87
  8.7 0.8 sub.58
  9.6 2.6 %collective-permute-done.1 = bf16[4,1,32,128]{3,2,1,0:T(8,128)(2,1)S(1)} collective-permute-done((bf16[4,1,32,128]{3,2,1,0:T(8,128)(2,1)S(1)}, bf16[4,1,32,128]{3,2,1,0:T(8,128)(2,1)S(1)}, u32[]{:S(2)}, u32[]{:S(2)}) %collective-permute-start.1) | collective-permute-done | bytes 32800 | tf_op jit(solution)/shard_map/ppermute | solution.py:19
  12.2 1.7 %pad_maximum_fusion.4 = (bf16[4,16,32,128]{3,2,1,0:T(8,128)(2,1)S(1)}, bf16[4,16,32,128]{3,2,1,0:T(8,128)(2,1)S(1)}, bf16[4,18,32,128]{3,2,1,0:T(8,128)(2,1)S(1)}) fusion(bf16[4,1,32,128]{3,2,1,0:T(8,128)(2,1)S(1)} %collective-permute-done.1, bf16[4,16,32,128]{3,2,1,0:T(8,128)(2,1)} %param.9, bf16[4,1,32,128]{3,2,1,0:T(8,128)(2,1)S(1)} %collective-permute-done, ...), kind=kLoop, calls=%fused_computation.107 | loop fusion | flops 2097152 | bytes 2162688 | tf_op jit(solution)/shard_map/concatenate | solution.py:15
  14.0 1.3 %collective-permute-start.2 = (bf16[4,18,1,128]{3,2,1,0:T(2,128)(2,1)S(1)}, bf16[4,18,1,128]{3,2,1,0:T(2,128)(2,1)S(1)}, u32[]{:S(2)}, u32[]{:S(2)}) collective-permute-start(bf16[4,18,1,128]{3,2,1,0:T(2,128)(2,1)S(1)} %get-tuple-element.37), channel_id=1, source_target_pairs={{0,1},{2,3},{4,5},{6,7},{8,9},{10,11},{12,13},{14,15},{16,17},{18,... | collective-permute-start | bytes 55304 | tf_op jit(solution)/shard_map/ppermute | solution.py:17
  15.3 1.3 %collective-permute-start.3 = (bf16[4,18,1,128]{3,2,1,0:T(2,128)(2,1)S(1)}, bf16[4,18,1,128]{3,2,1,0:T(2,128)(2,1)S(1)}, u32[]{:S(2)}, u32[]{:S(2)}) collective-permute-start(bf16[4,18,1,128]{3,2,1,0:T(2,128)(2,1)S(1)} %get-tuple-element.36), channel_id=1, source_target_pairs={{1,0},{3,2},{5,4},{7,6},{9,8},{11,10},{13,12},{15,14},{17,16},{19,... | collective-permute-start | bytes 55304 | tf_op jit(solution)/shard_map/ppermute | solution.py:19
  16.6 0.3 fusion.42
  16.9 1.5 %collective-permute-done.3 = bf16[4,18,1,128]{3,2,1,0:T(2,128)(2,1)S(1)} collective-permute-done((bf16[4,18,1,128]{3,2,1,0:T(2,128)(2,1)S(1)}, bf16[4,18,1,128]{3,2,1,0:T(2,128)(2,1)S(1)}, u32[]{:S(2)}, u32[]{:S(2)}) %collective-permute-start.3) | collective-permute-done | bytes 18464 | tf_op jit(solution)/shard_map/ppermute | solution.py:19
  18.6 1.3 %collective-permute-start.4 = (bf16[2,18,34,128]{3,2,1,0:T(8,128)(2,1)S(1)}, bf16[2,18,34,128]{3,2,1,0:T(8,128)(2,1)S(1)}, u32[]{:S(2)}, u32[]{:S(2)}) collective-permute-start(bf16[2,18,34,128]{3,2,1,0:T(8,128)(2,1)S(1)} %pad_maximum_fusion.5), channel_id=1, source_target_pairs={{4,0},{8,4},{12,8},{16,12},{20,16},{24,20},{28,24},{5,1},{9,5},{13... | collective-permute-start | bytes 940040 | tf_op jit(solution)/shard_map/ppermute | solution.py:29
  19.9 0.9 pad_maximum_fusion.3
  21.1 0.3 fusion.40
  21.4 9.8 %collective-permute-done.4 = bf16[2,18,34,128]{3,2,1,0:T(8,128)(2,1)S(1)} collective-permute-done((bf16[2,18,34,128]{3,2,1,0:T(8,128)(2,1)S(1)}, bf16[2,18,34,128]{3,2,1,0:T(8,128)(2,1)S(1)}, u32[]{:S(2)}, u32[]{:S(2)}) %collective-permute-start.4) | collective-permute-done | bytes 313376 | tf_op jit(solution)/shard_map/ppermute | solution.py:29
  31.1 0.4 pad_maximum_fusion
  31.5 2.6 %fusion.118 = (bf16[4,16,32,128]{3,2,1,0:T(8,128)(2,1)S(1)}, bf16[4,16,32,128]{3,2,1,0:T(8,128)(2,1)S(1)}, bf16[4,16,32,128]{3,2,1,0:T(8,128)(2,1)S(1)}, bf16[4,...) fusion(bf16[6,18,34,128]{3,2,1,0:T(8,128)(2,1)S(1)} %pad_maximu, ...), kind=kLoop, calls=%fused_computation.213 | loop fusion | bytes 18874368 | tf_op jit(solution)/shard_map/slice | solution.py:121
  34.2 0.7 fusion.29
  34.8 0.7 fusion.28
  35.5 0.6 fusion.27
  36.1 0.7 fusion.26
  36.7 0.7 fusion.25
  37.4 0.6 fusion.24
  38.0 0.7 fusion.23
  38.7 0.7 fusion.22
  39.3 0.6 fusion.21
  39.9 0.7 fusion.20
  40.6 0.7 fusion.19
  41.2 0.6 fusion.18
  41.8 0.7 fusion.17
  42.5 0.7 fusion.16
  43.1 0.6 fusion.15
  43.7 0.7 fusion.14
  44.4 0.7 fusion.13
  45.1 0.6 fusion.12
  45.6 0.6 fusion.11
  46.2 0.6 fusion.10
  46.8 0.8 fusion.9
  47.5 0.6 fusion.8
  48.1 0.5 copy-done
  48.6 0.6 fusion.7
  49.1 0.6 fusion.6
  49.7 0.6 fusion.5
  50.3 0.6 fusion.4
  50.8 0.6 fusion.3
  52.9 0.3 convolution_add_fusion.19
  54.5 0.3 convolution_add_fusion.14
  57.2 0.3 convolution_add_fusion.5
  57.5 0.3 fusion.2
  58.7 0.3 fusion.1
  59.5 7.9 %collective-permute-done.6 = bf16[8,112,128]{2,1,0:T(8,128)(2,1)S(1)} collective-permute-done((bf16[8,112,128]{2,1,0:T(8,128)(2,1)S(1)}, bf16[8,112,128]{2,1,0:T(8,128)(2,1)S(1)}, u32[]{:S(2)}, u32[]{:S(2)}) %collective-permute-start.6) | collective-permute-done | bytes 229408 | tf_op jit(solution)/shard_map/ppermute | solution.py:34
  67.4 2.5 %collective-permute-start.7 = (bf16[4,112,128]{2,1,0:T(8,128)(2,1)S(1)}, bf16[4,112,128]{2,1,0:T(8,128)(2,1)S(1)}, u32[]{:S(2)}, u32[]{:S(2)}) collective-permute-start(bf16[4,112,128]{2,1,0:T(8,128)(2,1)S(1)} %fusion.36), channel_id=1, source_target_pairs={{0,4},{4,0},{8,12},{12,8},{16,20},{20,16},{24,28},{28,24},{1,5},{5... | collective-permute-start | bytes 344072 | tf_op jit(solution)/shard_map/ppermute | solution.py:34
  70.0 2.8 %collective-permute-done.7 = bf16[4,112,128]{2,1,0:T(8,128)(2,1)S(1)} collective-permute-done((bf16[4,112,128]{2,1,0:T(8,128)(2,1)S(1)}, bf16[4,112,128]{2,1,0:T(8,128)(2,1)S(1)}, u32[]{:S(2)}, u32[]{:S(2)}) %collective-permute-start.7) | collective-permute-done | bytes 114720 | tf_op jit(solution)/shard_map/ppermute | solution.py:34
  72.8 1.6 %collective-permute-start.8 = (bf16[2,112,128]{2,1,0:T(8,128)(2,1)S(1)}, bf16[2,112,128]{2,1,0:T(8,128)(2,1)S(1)}, u32[]{:S(2)}, u32[]{:S(2)}) collective-permute-start(bf16[2,112,128]{2,1,0:T(8,128)(2,1)S(1)} %fusion.39), channel_id=1, source_target_pairs={{0,8},{4,12},{8,0},{12,4},{16,24},{20,28},{24,16},{28,20},{1,9},{5... | collective-permute-start | bytes 172040 | tf_op jit(solution)/shard_map/ppermute | solution.py:34
  74.5 0.6 fusion.116
  75.6 5.9 %all-reduce = (f32[4,32]{1,0:T(4,128)S(1)}, f32[4,32]{1,0:T(4,128)S(1)}) all-reduce(f32[4,32]{1,0:T(4,128)S(1)} %reduce_sum.37, f32[4,32]{1,0:T(4,128)S(1)} %reduce_sum.25), channel_id=1, replica_groups=mesh['tm'=8,'height'=2,'width'=2] {'height','width'}, use_global_device_ids=true, to_apply=%region_5.6 | all-reduce | flops 256 | bytes 2048 | tf_op jit(solution)/shard_map/psum | solution.py:152
  81.5 2.0 %collective-permute-start.9 = (f32[1,112,128]{2,1,0:T(8,128)S(1)}, f32[1,112,128]{2,1,0:T(8,128)S(1)}, u32[]{:S(2)}, u32[]{:S(2)}) collective-permute-start(f32[1,112,128]{2,1,0:T(8,128)S(1)} %constant_dynamic-slice_fusion), channel_id=1, source_target_pairs={{0,16},{4,20},{8,24},{12,28},{16,0},{20,4},{24,8},{28,12},{1,17},{... | collective-permute-start | bytes 172040 | tf_op jit(solution)/shard_map/ppermute | solution.py:34
  83.9 3.2 %collective-permute-done.9 = f32[1,112,128]{2,1,0:T(8,128)S(1)} collective-permute-done((f32[1,112,128]{2,1,0:T(8,128)S(1)}, f32[1,112,128]{2,1,0:T(8,128)S(1)}, u32[]{:S(2)}, u32[]{:S(2)}) %collective-permute-start.9) | collective-permute-done | bytes 57376 | tf_op jit(solution)/shard_map/ppermute | solution.py:34
  87.1 0.5 collective-permute-start.10
  87.6 1.1 %add_convert_fusion = bf16[4,16,32,128]{3,2,1,0:T(8,128)(2,1)} fusion(f32[4,16,32,128]{3,2,1,0:T(8,128)S(1)} %get-tuple-element.6, bf16[4,16,32,128]{3,2,1,0:T(8,128)(2,1)S(1)} %copy-done.1, bf16[4,16,32,128]{3,2,1,0:T(8,128)(2,1)S(1)} %copy-done, f32[4,128]{1,0:T(4,128)S(1)} %mul.99, f32[4,128]{1,0:T(4,128)S(1)} %sub.64, f32[4,128]{1,0:T(4,128)S(1)} %sub.59, ...), kind=kLoop, calls=%fused_computation.85 | loop fusion | flops 2621440 | bytes 2629632 | tf_op jit(solution)/shard_map/convert_element_type | solution.py:162
  88.8 1.7 %collective-permute-start.12 = (f32[112,128]{1,0:T(8,128)S(1)}, f32[112,128]{1,0:T(8,128)S(1)}, u32[]{:S(2)}, u32[]{:S(2)}) collective-permute-start(f32[112,128]{1,0:T(8,128)S(1)} %add_bitcast_fusion), channel_id=1, source_target_pairs={{0,3},{1,2},{2,1},{3,0},{4,7},{5,6},{6,5},{7,4},{8,11},{9,10},{10,... | collective-permute-start | bytes 172040 | tf_op jit(solution)/shard_map/ppermute | solution.py:84
  90.5 0.9 collective-permute-done.10
  91.4 1.0 %collective-permute-done.12 = f32[112,128]{1,0:T(8,128)S(1)} collective-permute-done((f32[112,128]{1,0:T(8,128)S(1)}, f32[112,128]{1,0:T(8,128)S(1)}, u32[]{:S(2)}, u32[]{:S(2)}) %collective-permute-start.12) | collective-permute-done | bytes 57376 | tf_op jit(solution)/shard_map/ppermute | solution.py:84
  92.4 0.7 pad_maximum_fusion.7
  (72 shorter events, 8.2 us)
Async XLA Ops:
  0.6 15.9 %copy-start.2 = (bf16[3,3,3,128,128]{4,3,2,1,0:T(8,128)(2,1)S(1)}, bf16[3,3,3,128,128]{4,3,2,1,0:T(8,128)(2,1)}, u32[]{:S(2)}) copy-start(bf16[3,3,3,128,128]{4,3,2,1,0:T(8,128)(2,1)} %param.14) | copy-start | bytes 2654212
  1.5 8.1 %collective-permute-start = (bf16[4,1,32,128]{3,2,1,0:T(8,128)(2,1)S(1)}, bf16[4,1,32,128]{3,2,1,0:T(8,128)(2,1)S(1)}, u32[]{:S(2)}, u32[]{:S(2)}) collective-permute-start(bf16[4,1,32,128]{3,2,1,0:T(8,128)(2,1)S(1)} %get-tuple-element.42), channel_id=1, source_target_pairs={{0,2},{1,3},{4,6},{5,7},{8,10},{9,11},{12,14},{13,15},{16,18},{17,... | collective-permute-start | bytes 98312 | tf_op jit(solution)/shard_map/ppermute | solution.py:17
  6.4 5.8 %collective-permute-start.1 = (bf16[4,1,32,128]{3,2,1,0:T(8,128)(2,1)S(1)}, bf16[4,1,32,128]{3,2,1,0:T(8,128)(2,1)S(1)}, u32[]{:S(2)}, u32[]{:S(2)}) collective-permute-start(bf16[4,1,32,128]{3,2,1,0:T(8,128)(2,1)S(1)} %get-tuple-element.41), channel_id=1, source_target_pairs={{2,0},{3,1},{6,4},{7,5},{10,8},{11,9},{14,12},{15,13},{18,16},{19,... | collective-permute-start | bytes 98312 | tf_op jit(solution)/shard_map/ppermute | solution.py:19
  14.0 2.9 %collective-permute-start.2 = (bf16[4,18,1,128]{3,2,1,0:T(2,128)(2,1)S(1)}, bf16[4,18,1,128]{3,2,1,0:T(2,128)(2,1)S(1)}, u32[]{:S(2)}, u32[]{:S(2)}) collective-permute-start(bf16[4,18,1,128]{3,2,1,0:T(2,128)(2,1)S(1)} %get-tuple-element.37), channel_id=1, source_target_pairs={{0,1},{2,3},{4,5},{6,7},{8,9},{10,11},{12,13},{14,15},{16,17},{18,... | collective-permute-start | bytes 55304 | tf_op jit(solution)/shard_map/ppermute | solution.py:17
  15.3 3.1 %collective-permute-start.3 = (bf16[4,18,1,128]{3,2,1,0:T(2,128)(2,1)S(1)}, bf16[4,18,1,128]{3,2,1,0:T(2,128)(2,1)S(1)}, u32[]{:S(2)}, u32[]{:S(2)}) collective-permute-start(bf16[4,18,1,128]{3,2,1,0:T(2,128)(2,1)S(1)} %get-tuple-element.36), channel_id=1, source_target_pairs={{1,0},{3,2},{5,4},{7,6},{9,8},{11,10},{13,12},{15,14},{17,16},{19,... | collective-permute-start | bytes 55304 | tf_op jit(solution)/shard_map/ppermute | solution.py:19
  18.6 12.5 %collective-permute-start.4 = (bf16[2,18,34,128]{3,2,1,0:T(8,128)(2,1)S(1)}, bf16[2,18,34,128]{3,2,1,0:T(8,128)(2,1)S(1)}, u32[]{:S(2)}, u32[]{:S(2)}) collective-permute-start(bf16[2,18,34,128]{3,2,1,0:T(8,128)(2,1)S(1)} %pad_maximum_fusion.5), channel_id=1, source_target_pairs={{4,0},{8,4},{12,8},{16,12},{20,16},{24,20},{28,24},{5,1},{9,5},{13... | collective-permute-start | bytes 940040 | tf_op jit(solution)/shard_map/ppermute | solution.py:29
  31.5 2.6 %copy-start.1 = (bf16[4,16,32,128]{3,2,1,0:T(8,128)(2,1)S(1)}, bf16[4,16,32,128]{3,2,1,0:T(8,128)(2,1)}, u32[]{:S(2)}) copy-start(bf16[4,16,32,128]{3,2,1,0:T(8,128)(2,1)} %param.8) | copy-start | bytes 1572868
  31.5 2.6 %copy-start.4 = (f32[128]{0:T(128)S(1)}, f32[128]{0:T(128)}, u32[]{:S(2)}) copy-start(f32[128]{0:T(128)} %param.13) | copy-start | bytes 1540
  31.5 2.6 %copy-start.5 = (f32[128]{0:T(128)S(1)}, f32[128]{0:T(128)}, u32[]{:S(2)}) copy-start(f32[128]{0:T(128)} %param.12) | copy-start | bytes 1540
  47.5 1.0 %copy-start = (bf16[4,16,32,128]{3,2,1,0:T(8,128)(2,1)S(1)}, bf16[4,16,32,128]{3,2,1,0:T(8,128)(2,1)}, u32[]{:S(2)}) copy-start(bf16[4,16,32,128]{3,2,1,0:T(8,128)(2,1)} %param.9) | copy-start | bytes 1572868
  51.7 7.4 %collective-permute-start.5 = (f32[8,216,128]{2,1,0:T(8,128)S(1)}, f32[8,216,128]{2,1,0:T(8,128)S(1)}, u32[]{:S(2)}, u32[]{:S(2)}) collective-permute-start(f32[8,216,128]{2,1,0:T(8,128)S(1)} %constant_dynamic-slice_fusion.1), channel_id=1, source_target_pairs={{0,1},{1,0},{2,3},{3,2},{4,5},{5,4},{6,7},{7,6},{8,9},{9,8},{10,11... | collective-permute-start | bytes 2654216 | tf_op jit(solution)/shard_map/ppermute | solution.py:34
  59.3 10.6 %copy-start.3 = (bf16[2,16,32,128]{3,2,1,0:T(8,128)(2,1)S(1)}, bf16[2,16,32,128]{3,2,1,0:T(8,128)(2,1)}, u32[]{:S(2)}) copy-start(bf16[2,16,32,128]{3,2,1,0:T(8,128)(2,1)} %param.15) | copy-start | bytes 786436
  59.3 8.0 %collective-permute-start.6 = (bf16[8,112,128]{2,1,0:T(8,128)(2,1)S(1)}, bf16[8,112,128]{2,1,0:T(8,128)(2,1)S(1)}, u32[]{:S(2)}, u32[]{:S(2)}) collective-permute-start(bf16[8,112,128]{2,1,0:T(8,128)(2,1)S(1)} %dynamic-slice_convert_fusion), channel_id=1, source_target_pairs={{0,2},{2,0},{1,3},{3,1},{4,6},{6,4},{5,7},{7,5},{8,10},{10,8},{9,1... | collective-permute-start | bytes 688136 | tf_op jit(solution)/shard_map/ppermute | solution.py:34
  67.4 5.4 %collective-permute-start.7 = (bf16[4,112,128]{2,1,0:T(8,128)(2,1)S(1)}, bf16[4,112,128]{2,1,0:T(8,128)(2,1)S(1)}, u32[]{:S(2)}, u32[]{:S(2)}) collective-permute-start(bf16[4,112,128]{2,1,0:T(8,128)(2,1)S(1)} %fusion.36), channel_id=1, source_target_pairs={{0,4},{4,0},{8,12},{12,8},{16,20},{20,16},{24,28},{28,24},{1,5},{5... | collective-permute-start | bytes 344072 | tf_op jit(solution)/shard_map/ppermute | solution.py:34
  72.8 8.6 %collective-permute-start.8 = (bf16[2,112,128]{2,1,0:T(8,128)(2,1)S(1)}, bf16[2,112,128]{2,1,0:T(8,128)(2,1)S(1)}, u32[]{:S(2)}, u32[]{:S(2)}) collective-permute-start(bf16[2,112,128]{2,1,0:T(8,128)(2,1)S(1)} %fusion.39), channel_id=1, source_target_pairs={{0,8},{4,12},{8,0},{12,4},{16,24},{20,28},{24,16},{28,20},{1,9},{5... | collective-permute-start | bytes 172040 | tf_op jit(solution)/shard_map/ppermute | solution.py:34
  81.5 5.6 %collective-permute-start.9 = (f32[1,112,128]{2,1,0:T(8,128)S(1)}, f32[1,112,128]{2,1,0:T(8,128)S(1)}, u32[]{:S(2)}, u32[]{:S(2)}) collective-permute-start(f32[1,112,128]{2,1,0:T(8,128)S(1)} %constant_dynamic-slice_fusion), channel_id=1, source_target_pairs={{0,16},{4,20},{8,24},{12,28},{16,0},{20,4},{24,8},{28,12},{1,17},{... | collective-permute-start | bytes 172040 | tf_op jit(solution)/shard_map/ppermute | solution.py:34
  87.1 4.2 %collective-permute-start.10 = (f32[112,128]{1,0:T(8,128)S(1)}, f32[112,128]{1,0:T(8,128)S(1)}, u32[]{:S(2)}, u32[]{:S(2)}) collective-permute-start(f32[112,128]{1,0:T(8,128)S(1)} %add_bitcast_fusion), channel_id=1, source_target_pairs={{0,2},{2,0},{1,3},{3,1},{4,6},{6,4},{5,7},{7,5},{8,10},{10,8},{9,1... | collective-permute-start | bytes 172040 | tf_op jit(solution)/shard_map/ppermute | solution.py:34
  88.8 2.6 %collective-permute-start.11 = (f32[112,128]{1,0:T(8,128)S(1)}, f32[112,128]{1,0:T(8,128)S(1)}, u32[]{:S(2)}, u32[]{:S(2)}) collective-permute-start(f32[112,128]{1,0:T(8,128)S(1)} %add_bitcast_fusion), channel_id=1, source_target_pairs={{0,1},{1,0},{2,3},{3,2},{4,5},{5,4},{6,7},{7,6},{8,9},{9,8},{10,11... | collective-permute-start | bytes 172040 | tf_op jit(solution)/shard_map/ppermute | solution.py:34
  88.8 3.6 %collective-permute-start.12 = (f32[112,128]{1,0:T(8,128)S(1)}, f32[112,128]{1,0:T(8,128)S(1)}, u32[]{:S(2)}, u32[]{:S(2)}) collective-permute-start(f32[112,128]{1,0:T(8,128)S(1)} %add_bitcast_fusion), channel_id=1, source_target_pairs={{0,3},{1,2},{2,1},{3,0},{4,7},{5,6},{6,5},{7,4},{8,11},{9,10},{10,... | collective-permute-start | bytes 172040 | tf_op jit(solution)/shard_map/ppermute | solution.py:84

commit v2 on v1

v2 whole, which is shorter than its diff:
```python
import functools
import math

import jax
import jax.numpy as jnp
from jax import lax
from jax.experimental import pallas as pl
from jax.experimental.pallas import tpu as pltpu
from jax.sharding import PartitionSpec as P

LEAD = 8
VMEM_BYTES = 56 * 1024 * 1024


def exchanged(value, axis, distance):
    count = lax.axis_size(axis)
    return lax.ppermute(value, axis, [(i, i ^ distance) for i in range(count)])


def shifted(value, axis, steps):
    count = lax.axis_size(axis)
    initial, last = (max(0, -steps), min(count, count - steps))
    return lax.ppermute(value, axis, [(source, source + steps) for source in range(initial, last)])


def power_of_two(count):
    return count & (count - 1) == 0


def paired():
    return lax.axis_size("height") == 2 and lax.axis_size("width") == 2


def kept_rows(rows):
    return -(-rows // 16) * 8


def joined(low, high, rows):
    kept = low.shape[0]
    return jnp.concatenate([low, high[2 * kept - rows :]], axis=0)


def in_halves(blocks, rows):
    return paired() and power_of_two(blocks) and rows % 16 == 0


def reduced_share(mine, theirs, rows):
    blocks = mine.shape[0]
    value = mine + exchanged(theirs, "width", 1)
    half = value.shape[1]
    kept = kept_rows(half)
    row_side = lax.axis_index("height")
    col_side = lax.axis_index("width")
    near = lax.dynamic_slice_in_dim(value, row_side * (half - kept), kept, 1)
    far = lax.dynamic_slice_in_dim(value, (1 - row_side) * (half - kept), kept, 1)
    value = near + exchanged(far.astype(jnp.bfloat16), "height", 1).astype(jnp.float32)
    place = lax.axis_index("tm")
    distance = 1
    while distance < blocks:
        side = (place // distance) % 2
        split = value.reshape(value.shape[0] // 2, 2, *value.shape[1:])
        near = lax.dynamic_index_in_dim(split, side, 1, keepdims=False)
        far = lax.dynamic_index_in_dim(split, 1 - side, 1, keepdims=False)
        wire = jnp.float32 if split.shape[0] == 1 else jnp.bfloat16
        value = near + exchanged(far.astype(wire), "tm", distance).astype(jnp.float32)
        distance *= 2
    own = value[0]
    beside = exchanged(own, "width", 1)
    below = exchanged(own, "height", 1)
    across = lax.ppermute(own, ("height", "width"), [(i, 3 - i) for i in range(4)])
    mine_half = joined(
        jnp.where(row_side == 0, own, below), jnp.where(row_side == 0, below, own), half
    )
    other_half = joined(
        jnp.where(row_side == 0, beside, across), jnp.where(row_side == 0, across, beside), half
    )
    return joined(
        jnp.where(col_side == 0, mine_half, other_half),
        jnp.where(col_side == 0, other_half, mine_half),
        rows,
    )


def group_matrix(rows, cols, row_width, col_width):
    row = lax.broadcasted_iota(jnp.int32, (rows, cols), 0) // row_width
    col = lax.broadcasted_iota(jnp.int32, (rows, cols), 1) // col_width
    return (row == col).astype(jnp.float32)


def exact_dot(left, right):
    return lax.dot_general(
        left,
        right,
        (((1,), (0,)), ((), ())),
        precision=lax.Precision.HIGHEST,
        preferred_element_type=jnp.float32,
    )


def per_channel(value, channels):
    groups = value.shape[1]
    return exact_dot(value, group_matrix(groups, channels, 1, channels // groups))


def act_kernel(features_ref, mean_ref, rstd_ref, gain_ref, bias_ref, act_ref):
    frames, rows, cols, channels = features_ref.shape
    cells = rows * cols
    mean = per_channel(mean_ref[...], channels)
    rstd = per_channel(rstd_ref[...], channels)
    for t in range(frames):
        value = features_ref[t].astype(jnp.float32).reshape(cells, channels)
        centred = (value - mean[t : t + 1]) * rstd[t : t + 1]
        pre_act = centred * gain_ref[...] + bias_ref[...]
        act = (pre_act * jax.nn.sigmoid(pre_act)).astype(jnp.bfloat16)
        act_ref[:, t * cells : (t + 1) * cells] = act.T


def fill_pair(grad_ref, halo_ref, row_ref, col_ref, corner_ref, tail_ref, stage_ref):
    frames, rows, cols, channels = grad_ref.shape
    extra = halo_ref.shape[0]
    row_side = lax.axis_index("height")
    col_side = lax.axis_index("width")
    rim_row = (1 - row_side) * (rows + 1)
    total = frames + extra
    for f in range(total):
        zeros = jnp.zeros((rows + 2, LEAD, channels), jnp.float32)
        stage_ref[f, :, 0:LEAD, :] = zeros
        stage_ref[f, :, LEAD + cols :, :] = zeros
        empty = jnp.zeros((cols, channels), jnp.float32)
        stage_ref[f, 0, LEAD : LEAD + cols, :] = empty
        stage_ref[f, rows + 1, LEAD : LEAD + cols, :] = empty
        inner = grad_ref[f] if f < frames else halo_ref[f - frames]
        stage_ref[f, 1 : rows + 1, LEAD : LEAD + cols, :] = inner.astype(jnp.float32)
        rim = row_ref[f] if f < frames else tail_ref[f - frames, 0:cols]
        stage_ref[f, rim_row, LEAD : LEAD + cols, :] = rim.astype(jnp.float32)

    def fill_columns(at):
        for f in range(total):
            if f < frames:
                column, corner = col_ref[f], corner_ref[f : f + 1]
            else:
                column = tail_ref[f - frames, cols : cols + rows]
                corner = tail_ref[f - frames, cols + rows : cols + rows + 1]
            column = column.astype(jnp.float32)
            for r in range(rows):
                stage_ref[f, r + 1, at : at + 1, :] = column[r : r + 1]
            stage_ref[f, rim_row, at : at + 1, :] = corner.astype(jnp.float32)

    @pl.when(col_side == 1)
    def _():
        fill_columns(LEAD - 1)

    @pl.when(col_side == 0)
    def _():
        fill_columns(LEAD + cols)


def weight_kernel(rows_out, scale, pair, halves, *refs):
    if pair:
        act_ref, grad_ref, halo_ref, row_ref, col_ref, corner_ref, tail_ref = refs[:7]
        refs = refs[7:]
    else:
        act_ref, stage_in_ref = refs[:2]
        refs = refs[2:]
    window_ref, outs, (stage_ref, sum_ref) = refs[0], refs[1:-2], refs[-2:]
    total, rows_ext, cols, wide = window_ref.shape
    rows = rows_ext - 2
    channels = wide // 3
    cells = rows * cols
    frames = act_ref.shape[1] // cells
    if pair:
        fill_pair(grad_ref, halo_ref, row_ref, col_ref, corner_ref, tail_ref, stage_ref)
    else:
        stage_ref[...] = stage_in_ref[...].astype(jnp.float32)

    def widen(f, carry):
        for e in range(3):
            at = LEAD - 1 + e
            window_ref[f, :, :, e * channels : (e + 1) * channels] = stage_ref[
                f, :, at : at + cols, :
            ].astype(jnp.bfloat16)
        return carry

    lax.fori_loop(0, total, widen, 0)

    for lag_t in range(3):
        for lag_h in range(3):
            acc = None
            for t in range(frames):
                window = window_ref[t + 2 - lag_t, 2 - lag_h : 2 - lag_h + rows]
                term = lax.dot_general(
                    act_ref[:, t * cells : (t + 1) * cells],
                    window.reshape(cells, wide),
                    (((1,), (0,)), ((), ())),
                    preferred_element_type=jnp.float32,
                )
                acc = term if acc is None else acc + term
            acc = acc * scale
            for lag_w in range(3):
                e = 2 - lag_w
                at = ((lag_t * 3 + lag_h) * 3 + lag_w) * channels
                sum_ref[at : at + channels, :] = acc[:, e * channels : (e + 1) * channels]
    if not halves:
        outs[0][...] = sum_ref[...]
        return
    mine_ref, theirs_ref = outs
    col_side = lax.axis_index("width")
    half = rows_out // 2

    def place(low_ref, high_ref):
        for block in range(mine_ref.shape[0]):
            at = block * rows_out
            low_ref[block] = sum_ref[at : at + half, :]
            high_ref[block] = sum_ref[at + half : at + rows_out, :]

    @pl.when(col_side == 0)
    def _():
        place(mine_ref, theirs_ref)

    @pl.when(col_side == 1)
    def _():
        place(theirs_ref, mine_ref)


def conv_kernel(
    window_ref,
    weight_ref,
    future_ref,
    features_ref,
    mean_ref,
    rstd_ref,
    gain_ref,
    bias_ref,
    scaled_ref,
    sums_ref,
):
    frames, rows, cols, channels = features_ref.shape
    cells = rows * cols
    wide = 3 * channels
    mean = per_channel(mean_ref[...], channels)
    rstd = per_channel(rstd_ref[...], channels)
    is_last = lax.axis_index("tm") == lax.axis_size("tm") - 1
    for t in range(frames):
        acc = None
        for lag_t in range(3):
            for lag_h in range(3):
                window = window_ref[t + 2 - lag_t, 2 - lag_h : 2 - lag_h + rows]
                taps = jnp.concatenate(
                    [weight_ref[lag_t, lag_h, 2 - e] for e in range(3)], axis=1
                )
                term = lax.dot_general(
                    window.reshape(cells, wide),
                    taps,
                    (((1,), (1,)), ((), ())),
                    preferred_element_type=jnp.float32,
                )
                acc = term if acc is None else acc + term
        later = t - (frames - future_ref.shape[0])
        if later >= 0:
            tail = future_ref[later].astype(jnp.float32).reshape(cells, channels)
            acc = acc + jnp.where(is_last, tail, jnp.zeros_like(tail))
        value = features_ref[t].astype(jnp.float32).reshape(cells, channels)
        centred = (value - mean[t : t + 1]) * rstd[t : t + 1]
        pre_act = centred * gain_ref[...] + bias_ref[...]
        sig = jax.nn.sigmoid(pre_act)
        scaled = acc * sig * (1.0 + pre_act * (1.0 - sig)) * gain_ref[...]
        scaled_ref[t] = scaled.reshape(rows, cols, channels)
        sums_ref[t : t + 1, :] = jnp.sum(scaled, axis=0, keepdims=True)
        sums_ref[frames + t : frames + t + 1, :] = jnp.sum(
            scaled * centred, axis=0, keepdims=True
        )


def final_kernel(count, terms, *refs):
    parts, (scaled_ref, features_ref, grad_ref, mean_ref, rstd_ref, out_ref) = (
        refs[:terms],
        refs[terms:],
    )
    frames, rows, cols, channels = features_ref.shape
    groups = mean_ref.shape[1]
    mean = per_channel(mean_ref[...], channels)
    rstd = per_channel(rstd_ref[...], channels)
    total = parts[0][...]
    for part in parts[1:]:
        total = total + part[...]
    width = channels // groups
    means = exact_dot(total, group_matrix(channels, channels, width, width)) / count
    for t in range(frames):
        value = features_ref[t].astype(jnp.float32)
        centred = (value - mean[t : t + 1]) * rstd[t : t + 1]
        first = means[t : t + 1]
        second = means[frames + t : frames + t + 1]
        corrected = rstd[t : t + 1] * (scaled_ref[t] - first - centred * second)
        out_ref[t] = (grad_ref[t].astype(jnp.float32) + corrected).astype(jnp.bfloat16)


def call(kernel, out_shape, scratch=(), flops=0, moved=0):
    return pl.pallas_call(
        kernel,
        out_shape=out_shape,
        scratch_shapes=list(scratch),
        compiler_params=pltpu.CompilerParams(vmem_limit_bytes=VMEM_BYTES),
        cost_estimate=pl.CostEstimate(flops=flops, bytes_accessed=moved, transcendentals=0),
    )


def extended(cells, sides, width):
    for axis, dim in sides:
        head = lax.slice_in_dim(cells, 0, width, axis=dim)
        tail = lax.slice_in_dim(cells, cells.shape[dim] - width, cells.shape[dim], axis=dim)
        cells = jnp.concatenate(
            [shifted(tail, axis, 1), cells, shifted(head, axis, -1)], axis=dim
        )
    return cells


def rims(grad_out, extra):
    frames, rows, cols, channels = grad_out.shape
    row_side = lax.axis_index("height")
    col_side = lax.axis_index("width")
    row_at = (1 - row_side) * (rows - 1)
    col_at = (1 - col_side) * (cols - 1)
    row = lax.dynamic_slice_in_dim(grad_out, row_at, 1, 1)[:, 0]
    col = lax.dynamic_slice_in_dim(grad_out, col_at, 1, 2)[:, :, 0]
    corner = lax.dynamic_slice_in_dim(row, col_at, 1, 1)[:, 0]
    halo = shifted(grad_out[:extra], "tm", -1)
    row = exchanged(row, "height", 1)
    col = exchanged(col, "width", 1)
    corner = lax.ppermute(corner, ("height", "width"), [(i, 3 - i) for i in range(4)])
    packed = jnp.concatenate([row[:extra], col[:extra], corner[:extra, None]], axis=1)
    return halo, row, col, corner, shifted(packed, "tm", -1)


def on_device(features, grad_out, mean_saved, rstd_saved, gain, bias, weight, future_cot):
    frames, rows, cols, channels = features.shape
    extra = weight.shape[0] - 1
    cells = rows * cols
    groups = mean_saved.shape[1]
    blocks = lax.axis_size("tm")
    taps = math.prod(weight.shape[:3])
    rows_out = taps * channels // blocks
    positions = cells * lax.axis_size("height") * lax.axis_size("width")
    grad_scale = 1.0 / math.sqrt(positions * frames * blocks)
    gain = gain.reshape(1, channels)
    bias = bias.reshape(1, channels)
    pair = paired()
    halves = in_halves(blocks, rows_out)
    f32 = jnp.float32

    if pair:
        sources = (grad_out, *rims(grad_out, extra))
    else:
        padded = extended(grad_out, (("height", 1), ("width", 2)), 1)
        whole = jnp.concatenate([padded, shifted(padded[:extra], "tm", -1)], axis=0)
        sources = (jnp.pad(whole, ((0, 0), (0, 0), (LEAD - 1, LEAD - 1), (0, 0))),)

    act = call(
        act_kernel,
        jax.ShapeDtypeStruct((channels, frames * cells), jnp.bfloat16),
        flops=20 * frames * cells * channels,
        moved=4 * frames * cells * channels,
    )(features, mean_saved, rstd_saved, gain, bias)

    total = frames + extra
    window_shape = (total, rows + 2, cols, 3 * channels)
    work = 2 * taps * channels * channels * frames * cells
    if halves:
        half_shape = jax.ShapeDtypeStruct((blocks, rows_out // 2, channels), f32)
        sum_shapes = (half_shape, half_shape)
    else:
        sum_shapes = (jax.ShapeDtypeStruct((taps * channels, channels), f32),)
    window, *sums = call(
        functools.partial(weight_kernel, rows_out, grad_scale, pair, halves),
        (jax.ShapeDtypeStruct(window_shape, jnp.bfloat16), *sum_shapes),
        scratch=(
            pltpu.VMEM((total, rows + 2, cols + 2 * LEAD, channels), f32),
            pltpu.VMEM((taps * channels, channels), f32),
        ),
        flops=work,
        moved=8 * 1024 * 1024,
    )(act, *sources)

    if halves:
        weight_grad = reduced_share(*sums, rows_out)
    else:
        share = lax.psum_scatter(sums[0], "tm", scatter_dimension=0, tiled=True)
        weight_grad = lax.psum(share, ("height", "width"))

    scaled, local = call(
        conv_kernel,
        (
            jax.ShapeDtypeStruct((frames, rows, cols, channels), f32),
            jax.ShapeDtypeStruct((2 * frames, channels), f32),
        ),
        flops=work,
        moved=8 * 1024 * 1024,
    )(window, weight, future_cot, features, mean_saved, rstd_saved, gain, bias)

    if pair:
        parts = [
            local,
            exchanged(local, "width", 1),
            exchanged(local, "height", 1),
            lax.ppermute(local, ("height", "width"), [(i, 3 - i) for i in range(4)]),
        ]
    else:
        parts = [lax.psum(local, ("height", "width"))]
    input_cot = call(
        functools.partial(final_kernel, positions * (channels // groups), len(parts)),
        jax.ShapeDtypeStruct(features.shape, jnp.bfloat16),
        flops=20 * frames * cells * channels,
        moved=10 * frames * cells * channels,
    )(*parts, scaled, features, grad_out, mean_saved, rstd_saved)
    return (input_cot, weight_grad)


def solution(mesh):
    placed = (
        P("tm", "height", "width", None),
        P("tm", "height", "width", None),
        P("tm", None),
        P("tm", None),
        P(),
        P(),
        P(),
        P(None, "height", "width", None),
    )
    return jax.shard_map(
        on_device,
        mesh=mesh,
        in_specs=placed,
        out_specs=(P("tm", "height", "width", None), P("tm", None)),
        check_vma=False,
    )
```

time: 93.5 us -> 74.1 us (0.79)
  matrix products: 24.7 us -> 0 us
  Pallas kernels: 0 us -> 19.2 us
  blocking collectives: 5.89 us -> 0 us
  other arithmetic: 6.35 us -> 2.11 us
  waiting for transfers between devices: 29.6 us -> 26.9 us
  local copies, waits for them, and re-layouts: 6.59 us -> 5.42 us
    dot_general x54 -> x0, matrix products: 24.7 us -> none  [the longest x27 16.6 us: on_device(): lax.dot_general(flat_act, window, (((0,), (0,)), ((), ())), preferred_ele...]
    pallas_call x0 -> x4, Pallas kernels: none -> 19.2 us  [the longest x1 7.14 us: on_device(): call(conv_kernel, (jax.ShapeDtypeStruct((frames, rows, cols, channels), f...]
    psum x1 -> x0, blocking collectives: 5.89 us -> none  [on_device(): lax.psum((sum_first, sum_second), ('height', 'width'))]
    ppermute x4 -> x2, starting transfers between devices: 8.77 us -> 3.72 us  [the longest x1 2.43 us: rims(): lax.ppermute(corner, ('height', 'width'), [(i, 3 - i) for i in range(4)])]
    ppermute x7 -> x11, starting transfers between devices: 6.79 us -> 11.4 us  [exchanged(): return lax.ppermute(value, axis, [(i, i ^ distance) for i in range(count)])]
    ppermute x4 -> x2, waiting for transfers between devices: 4.1 us -> 0.01 us  [the longest x1 0.01 us: rims(): lax.ppermute(corner, ('height', 'width'), [(i, 3 - i) for i in range(4)])]
    ppermute x1 -> x2, waiting for transfers between devices: 9.75 us -> 6.02 us  [shifted(): lax.ppermute(value, axis, [(source, source + steps) for source in range(i...]
    ppermute x7 -> x11, waiting for transfers between devices: 14.8 us -> 18.6 us  [exchanged(): return lax.ppermute(value, axis, [(i, i ^ distance) for i in range(count)])]
  transfers between devices with their start and end apart: 13 -> 16, of which waited for: 8 -> 8; matrix products, arithmetic and copies ran while one was open for 14% -> 4% of each run, Pallas kernels for 0% -> 17%
where the time goes in v2:
time: 74.1 us; the launch traced here: 73.6 us
  waiting for transfers between devices  26.9 us (36%)
  Pallas kernels  19.2 us (26%)
  starting transfers between devices  19.1 us (26%)
  local copies, waits for them, and re-layouts  5.42 us (7%)
  other arithmetic  2.11 us (3%)
  between operations  0.89 us (1%)
    ppermute x11, waiting for transfers between devices, exchanged(): return lax.ppermute(value, axis, [(i, i ^ distance) for i in range(count)])  18.6 us
    ppermute x11, starting transfers between devices, exchanged(): return lax.ppermute(value, axis, [(i, i ^ distance) for i in range(count)])  11.4 us
    pallas_call x1, Pallas kernels, on_device(): call(conv_kernel, (jax.ShapeDtypeStruct((frames, rows, cols, channels), f...  7.14 us
    pallas_call x1, Pallas kernels, on_device(): call(functools.partial(weight_kernel, rows_out, grad_scale, pair, halves)...  6.69 us
    ppermute x2, waiting for transfers between devices, shifted(): lax.ppermute(value, axis, [(source, source + steps) for source in range(i...  6.02 us
    pallas_call x1, Pallas kernels, on_device(): call(functools.partial(final_kernel, positions * (channels // groups), le...  3 us
    ppermute x2, starting transfers between devices, shifted(): lax.ppermute(value, axis, [(source, source + steps) for source in range(i...  2.58 us
    ppermute x1, starting transfers between devices, rims(): lax.ppermute(corner, ('height', 'width'), [(i, 3 - i) for i in range(4)])  2.43 us
  transfers between devices with their start and end apart: 16, of which 8 were waited for; matrix products, arithmetic and copies ran while one was open for 4% of the time, Pallas kernels for 17%

profile of v2, /device:TPU:0, one launch (start us, length us, event | category | flops | bytes accessed | tf_op | source)
XLA Modules:
  0.0 73.6 jit_solution(1121427690647213227)
XLA Ops:
  0.6 0.7 constant_dynamic-slice_fusion.1
  1.4 2.4 %collective-permute-start.3 = (bf16[4,128]{1,0:T(4,128)(2,1)S(1)}, bf16[4,128]{1,0:T(4,128)(2,1)S(1)}, u32[]{:S(2)}, u32[]{:S(2)}) collective-permute-start(bf16[4,128]{1,0:T(4,128)(2,1)S(1)} %bitcast.33), channel_id=1, source_target_pairs={{0,3},{1,2},{2,1},{3,0},{4,7},{5,6},{6,5},{7,4},{8,11},{9,10},{10,... | collective-permute-start | bytes 3080 | tf_op jit(solution)/shard_map/ppermute | solution.py:329
  3.8 0.8 %dynamic-slice_bitcast_fusion = bf16[4,32,128]{2,1,0:T(8,128)(2,1)S(1)} fusion(bf16[4,16,32,128]{3,2,1,0:T(8,128)(2,1)} %refs_6_.1, s32[]{:T(128)S(6)} %select_n.93), kind=kLoop, calls=%fused_computation.16 | loop fusion | bytes 65540 | tf_op jit(solution)/shard_map/squeeze | solution.py:323
  4.6 0.6 collective-permute-start.1
  5.1 0.9 %constant_dynamic-slice_fusion.2 = bf16[4,16,1,128]{3,2,1,0:T(2,128)(2,1)S(1)} fusion(bf16[4,16,32,128]{3,2,1,0:T(8,128)(2,1)} %refs_6_.1, s32[]{:T(128)S(6)} %select_n.94), kind=kLoop, calls=%fused_computation.23 | loop fusion | bytes 32772 | tf_op jit(solution)/shard_map/dynamic_slice | solution.py:324
  6.1 0.2 collective-permute-start.2
  6.3 1.0 %slice.18 = bf16[2,16,32,128]{3,2,1,0:T(8,128)(2,1)S(1)} slice(bf16[4,16,32,128]{3,2,1,0:T(8,128)(2,1)} %refs_6_.1), slice={[0:2], [0:16], [0:32], [0:128]} | slice | bytes 524288 | tf_op jit(solution)/shard_map/slice | solution.py:326
  7.2 1.3 %collective-permute-start = (bf16[2,16,32,128]{3,2,1,0:T(8,128)(2,1)S(1)}, bf16[2,16,32,128]{3,2,1,0:T(8,128)(2,1)S(1)}, u32[]{:S(2)}, u32[]{:S(2)}) collective-permute-start(bf16[2,16,32,128]{3,2,1,0:T(8,128)(2,1)S(1)} %slice.18), channel_id=1, source_target_pairs={{4,0},{8,4},{12,8},{16,12},{20,16},{24,20},{28,24},{5,1},{9,5},{13... | collective-permute-start | bytes 786440 | tf_op jit(solution)/shard_map/ppermute | solution.py:23
  8.5 0.0 collective-permute-done.3.refs_5_
  8.5 0.0 copy-start.7
  8.6 0.0 collective-permute-done.2.refs_4_
  8.6 0.0 copy-start.4
  8.6 0.0 collective-permute-done.1.refs_3_
  8.6 0.0 copy-start
  8.7 1.3 %collective-permute-start.4 = (bf16[2,49,128]{2,1,0:T(8,128)(2,1)S(1)}, bf16[2,49,128]{2,1,0:T(8,128)(2,1)S(1)}, u32[]{:S(2)}, u32[]{:S(2)}) collective-permute-start(bf16[2,49,128]{2,1,0:T(8,128)(2,1)S(1)} %pad_maximum_fusion.3), channel_id=1, source_target_pairs={{4,0},{8,4},{12,8},{16,12},{20,16},{24,20},{28,24},{5,1},{9,5},{13... | collective-permute-start | bytes 75272 | tf_op jit(solution)/shard_map/ppermute | solution.py:23
  10.0 2.4 %shard_map.95.refs_0_ = bf16[128,2048]{1,0:T(8,128)(2,1)} custom-call(bf16[4,16,32,128]{3,2,1,0:T(8,128)(2,1)} %refs_5_.1, f32[4,32]{1,0:T(4,128)} %refs_7_.1, f32[4,32]{1,0:T(4,128)} %refs_8_.1, f32[1,128]{1,0:T(1,128)} %bitcast.34, f32[1,128]{1,0:T(1,128)} %bitcast.36), custom_call_target="tpu_custom_call" | custom-call | flops 5242880 | bytes 1048576 | tf_op jit(solution)/shard_map/pallas_call | solution.py:357
  12.3 6.0 %collective-permute-done.4.refs_6_ = bf16[2,49,128]{2,1,0:T(8,128)(2,1)S(1)} collective-permute-done((bf16[2,49,128]{2,1,0:T(8,128)(2,1)S(1)}, bf16[2,49,128]{2,1,0:T(8,128)(2,1)S(1)}, u32[]{:S(2)}, u32[]{:S(2)}) %collective-permute-start.4) | collective-permute-done | bytes 25120 | tf_op jit(solution)/shard_map/ppermute | solution.py:23
  18.4 0.0 copy-start.6
  18.4 0.0 collective-permute-done.refs_2_
  18.4 0.0 copy-done.7
  18.4 0.0 copy-done.4
  18.4 0.0 copy-done
  18.4 0.6 copy-done.6
  19.0 0.0 copy-start.5
  19.0 0.7 copy-done.5
  19.7 6.7 %shard_map.96 = (bf16[6,18,32,384]{3,2,1,0:T(8,128)(2,1)}, f32[8,216,128]{2,1,0:T(8,128)}, f32[8,216,128]{2,1,0:T(8,128)}) custom-call(bf16[128,2048]{1,0:T(8,128)(2,1)} %shard_map.95.refs_0_, bf16[4,16,32,128]{3,2,1,0:T(8,128)(2,1)} %refs_6_.1, bf16[2,16,32,128]{3,2,1,0:T(8,128)(2,1)} %copy-done.5, bf16[4,32,128]{2,1,0:T(8,128)(2,1)} %copy-done, ...), custom_call_target="tpu_custom_call" | custom-call | flops 1811939328 | bytes 8388608 | tf_op jit(solution)/shard_map/pallas_call | solution.py:372
  26.4 0.0 collective-permute-start.8
  26.4 2.6 %collective-permute-done.8 = f32[8,216,128]{2,1,0:T(8,128)S(1)} collective-permute-done((f32[8,216,128]{2,1,0:T(8,128)}, f32[8,216,128]{2,1,0:T(8,128)S(1)}, u32[]{:S(2)}, u32[]{:S(2)}) %collective-permute-start.8) | collective-permute-done | bytes 884768 | tf_op jit(solution)/shard_map/ppermute | solution.py:17
  29.0 1.3 %add.71 = f32[8,216,128]{2,1,0:T(8,128)S(1)} add(f32[8,216,128]{2,1,0:T(8,128)} %get-tuple-element.10, f32[8,216,128]{2,1,0:T(8,128)S(1)} %collective-permute-done.8) | non-fusion elementwise | flops 221184 | bytes 2654208 | tf_op jit(solution)/shard_map/add | solution.py:49
  30.3 1.5 %collective-permute-start.9 = (bf16[8,112,128]{2,1,0:T(8,128)(2,1)S(1)}, bf16[8,112,128]{2,1,0:T(8,128)(2,1)S(1)}, u32[]{:S(2)}, u32[]{:S(2)}) collective-permute-start(bf16[8,112,128]{2,1,0:T(8,128)(2,1)S(1)} %dynamic-slice_convert_fusion), channel_id=1, source_target_pairs={{0,2},{2,0},{1,3},{3,1},{4,6},{6,4},{5,7},{7,5},{8,10},{10,8},{9,1... | collective-permute-start | bytes 688136 | tf_op jit(solution)/shard_map/ppermute | solution.py:17
  31.8 6.2 %collective-permute-done.9 = bf16[8,112,128]{2,1,0:T(8,128)(2,1)S(1)} collective-permute-done((bf16[8,112,128]{2,1,0:T(8,128)(2,1)S(1)}, bf16[8,112,128]{2,1,0:T(8,128)(2,1)S(1)}, u32[]{:S(2)}, u32[]{:S(2)}) %collective-permute-start.9) | collective-permute-done | bytes 229408 | tf_op jit(solution)/shard_map/ppermute | solution.py:17
  38.1 2.5 %collective-permute-start.10 = (bf16[4,112,128]{2,1,0:T(8,128)(2,1)S(1)}, bf16[4,112,128]{2,1,0:T(8,128)(2,1)S(1)}, u32[]{:S(2)}, u32[]{:S(2)}) collective-permute-start(bf16[4,112,128]{2,1,0:T(8,128)(2,1)S(1)} %fusion), channel_id=1, source_target_pairs={{0,4},{4,0},{8,12},{12,8},{16,20},{20,16},{24,28},{28,24},{1,5},{5... | collective-permute-start | bytes 344072 | tf_op jit(solution)/shard_map/ppermute | solution.py:17
  40.6 2.8 %collective-permute-done.10 = bf16[4,112,128]{2,1,0:T(8,128)(2,1)S(1)} collective-permute-done((bf16[4,112,128]{2,1,0:T(8,128)(2,1)S(1)}, bf16[4,112,128]{2,1,0:T(8,128)(2,1)S(1)}, u32[]{:S(2)}, u32[]{:S(2)}) %collective-permute-start.10) | collective-permute-done | bytes 114720 | tf_op jit(solution)/shard_map/ppermute | solution.py:17
  43.4 1.6 %collective-permute-start.11 = (bf16[2,112,128]{2,1,0:T(8,128)(2,1)S(1)}, bf16[2,112,128]{2,1,0:T(8,128)(2,1)S(1)}, u32[]{:S(2)}, u32[]{:S(2)}) collective-permute-start(bf16[2,112,128]{2,1,0:T(8,128)(2,1)S(1)} %fusion.3), channel_id=1, source_target_pairs={{0,8},{4,12},{8,0},{12,4},{16,24},{20,28},{24,16},{28,20},{1,9},{5... | collective-permute-start | bytes 172040 | tf_op jit(solution)/shard_map/ppermute | solution.py:17
  45.0 2.6 %collective-permute-done.11 = bf16[2,112,128]{2,1,0:T(8,128)(2,1)S(1)} collective-permute-done((bf16[2,112,128]{2,1,0:T(8,128)(2,1)S(1)}, bf16[2,112,128]{2,1,0:T(8,128)(2,1)S(1)}, u32[]{:S(2)}, u32[]{:S(2)}) %collective-permute-start.11) | collective-permute-done | bytes 57376 | tf_op jit(solution)/shard_map/ppermute | solution.py:17
  47.7 2.8 %collective-permute-start.12 = (f32[1,112,128]{2,1,0:T(8,128)S(1)}, f32[1,112,128]{2,1,0:T(8,128)S(1)}, u32[]{:S(2)}, u32[]{:S(2)}) collective-permute-start(f32[1,112,128]{2,1,0:T(8,128)S(1)} %constant_dynamic-slice_fusion), channel_id=1, source_target_pairs={{0,16},{4,20},{8,24},{12,28},{16,0},{20,4},{24,8},{28,12},{1,17},{... | collective-permute-start | bytes 172040 | tf_op jit(solution)/shard_map/ppermute | solution.py:17
  50.5 2.3 %collective-permute-done.12 = f32[1,112,128]{2,1,0:T(8,128)S(1)} collective-permute-done((f32[1,112,128]{2,1,0:T(8,128)S(1)}, f32[1,112,128]{2,1,0:T(8,128)S(1)}, u32[]{:S(2)}, u32[]{:S(2)}) %collective-permute-start.12) | collective-permute-done | bytes 57376 | tf_op jit(solution)/shard_map/ppermute | solution.py:17
  52.8 1.5 %collective-permute-start.13 = (f32[112,128]{1,0:T(8,128)S(1)}, f32[112,128]{1,0:T(8,128)S(1)}, u32[]{:S(2)}, u32[]{:S(2)}) collective-permute-start(f32[112,128]{1,0:T(8,128)S(1)} %add_bitcast_fusion), channel_id=1, source_target_pairs={{0,2},{2,0},{1,3},{3,1},{4,6},{6,4},{5,7},{7,5},{8,10},{10,8},{9,1... | collective-permute-start | bytes 172040 | tf_op jit(solution)/shard_map/ppermute | solution.py:17
  54.4 7.1 %shard_map.97 = (f32[4,16,32,128]{3,2,1,0:T(8,128)}, f32[8,128]{1,0:T(8,128)}) custom-call(bf16[6,18,32,384]{3,2,1,0:T(8,128)(2,1)} %get-tuple-element.7.window_ref, bf16[3,3,3,128,128]{4,3,2,1,0:T(8,128)(2,1)} %weight_ref.1, bf16[2,16,32,128]{3,2,1,0:T(8,128)(2,1)} %future_ref.1, bf16[4,16,32,128]{3,2,1,0:T(8,128)(2,1)} %refs_5_.1, f32[4,32]{1,0:T(4,128)} %refs_7_.1, ...), custom_call_target="tpu_custom_call" | custom-call | flops 1811939328 | bytes 8388608 | tf_op jit(solution)/shard_map/pallas_call | solution.py:389
  61.5 0.0 collective-permute-start.5
  61.5 0.6 collective-permute-start.6
  62.1 1.3 %collective-permute-start.7 = (f32[8,128]{1,0:T(8,128)}, f32[8,128]{1,0:T(8,128)S(1)}, u32[]{:S(2)}, u32[]{:S(2)}) collective-permute-start(f32[8,128]{1,0:T(8,128)} %get-tuple-element.8.refs_0_), channel_id=1, source_target_pairs={{0,3},{1,2},{2,1},{3,0},{4,7},{5,6},{6,5},{7,4},{8,11},{9,10},{10,... | collective-permute-start | bytes 12296 | tf_op jit(solution)/shard_map/ppermute | solution.py:404
  63.4 0.0 collective-permute-done.5.refs_1_
  63.4 0.0 copy-start.1
  63.4 2.0 %collective-permute-done.6.refs_2_ = f32[8,128]{1,0:T(8,128)S(1)} collective-permute-done((f32[8,128]{1,0:T(8,128)}, f32[8,128]{1,0:T(8,128)S(1)}, u32[]{:S(2)}, u32[]{:S(2)}) %collective-permute-start.6) | collective-permute-done | bytes 4128 | tf_op jit(solution)/shard_map/ppermute | solution.py:17
  65.4 0.0 copy-start.2
  65.4 0.0 collective-permute-done.7.refs_3_
  65.4 0.0 copy-start.3
  65.4 0.0 copy-done.1
  65.4 0.6 copy-done.2
  65.9 0.0 copy-done.3
  66.0 3.0 %shard_map.98 = bf16[4,16,32,128]{3,2,1,0:T(8,128)(2,1)} custom-call(f32[8,128]{1,0:T(8,128)} %get-tuple-element.8.refs_0_, f32[8,128]{1,0:T(8,128)} %copy-done.1, f32[8,128]{1,0:T(8,128)} %copy-done.2, f32[8,128]{1,0:T(8,128)} %copy-done.3, f32[4,16,32,128]{3,2,1,0:T(8,128)} %get-tuple-element.9.refs_4_, bf16[4,16,32,128]{3,2,1,0:T(8,128)(2,1)} %refs_5_.1, ...), custom_call_target="tpu_custom_call" | custom-call | flops 5242880 | bytes 2621440 | tf_op jit(solution)/shard_map/pallas_call | solution.py:408
  69.0 0.2 collective-permute-start.14
  69.1 1.3 %collective-permute-start.15 = (f32[112,128]{1,0:T(8,128)S(1)}, f32[112,128]{1,0:T(8,128)S(1)}, u32[]{:S(2)}, u32[]{:S(2)}) collective-permute-start(f32[112,128]{1,0:T(8,128)S(1)} %add_bitcast_fusion), channel_id=1, source_target_pairs={{0,3},{1,2},{2,1},{3,0},{4,7},{5,6},{6,5},{7,4},{8,11},{9,10},{10,... | collective-permute-start | bytes 172040 | tf_op jit(solution)/shard_map/ppermute | solution.py:70
  70.5 0.0 collective-permute-done.13
  70.5 0.0 collective-permute-done.14
  70.5 2.3 %collective-permute-done.15 = f32[112,128]{1,0:T(8,128)S(1)} collective-permute-done((f32[112,128]{1,0:T(8,128)S(1)}, f32[112,128]{1,0:T(8,128)S(1)}, u32[]{:S(2)}, u32[]{:S(2)}) %collective-permute-start.15) | collective-permute-done | bytes 57376 | tf_op jit(solution)/shard_map/ppermute | solution.py:70
  72.9 0.7 pad_maximum_fusion
  (20 shorter events, 0.3 us)
Async XLA Ops:
  1.4 7.2 %collective-permute-start.3 = (bf16[4,128]{1,0:T(4,128)(2,1)S(1)}, bf16[4,128]{1,0:T(4,128)(2,1)S(1)}, u32[]{:S(2)}, u32[]{:S(2)}) collective-permute-start(bf16[4,128]{1,0:T(4,128)(2,1)S(1)} %bitcast.33), channel_id=1, source_target_pairs={{0,3},{1,2},{2,1},{3,0},{4,7},{5,6},{6,5},{7,4},{8,11},{9,10},{10,... | collective-permute-start | bytes 3080 | tf_op jit(solution)/shard_map/ppermute | solution.py:329
  4.6 4.0 %collective-permute-start.1 = (bf16[4,32,128]{2,1,0:T(8,128)(2,1)S(1)}, bf16[4,32,128]{2,1,0:T(8,128)(2,1)S(1)}, u32[]{:S(2)}, u32[]{:S(2)}) collective-permute-start(bf16[4,32,128]{2,1,0:T(8,128)(2,1)S(1)} %dynamic-slice_bitcast_fusion), channel_id=1, source_target_pairs={{0,2},{2,0},{1,3},{3,1},{4,6},{6,4},{5,7},{7,5},{8,10},{10,8},{9,1... | collective-permute-start | bytes 98312 | tf_op jit(solution)/shard_map/ppermute | solution.py:17
  6.1 2.5 %collective-permute-start.2 = (bf16[4,16,128]{2,1,0:T(8,128)(2,1)S(1)}, bf16[4,16,128]{2,1,0:T(8,128)(2,1)S(1)}, u32[]{:S(2)}, u32[]{:S(2)}) collective-permute-start(bf16[4,16,128]{2,1,0:T(8,128)(2,1)S(1)} %bitcast.32), channel_id=1, source_target_pairs={{0,1},{1,0},{2,3},{3,2},{4,5},{5,4},{6,7},{7,6},{8,9},{9,8},{10,11... | collective-permute-start | bytes 49160 | tf_op jit(solution)/shard_map/ppermute | solution.py:17
  7.2 11.1 %collective-permute-start = (bf16[2,16,32,128]{3,2,1,0:T(8,128)(2,1)S(1)}, bf16[2,16,32,128]{3,2,1,0:T(8,128)(2,1)S(1)}, u32[]{:S(2)}, u32[]{:S(2)}) collective-permute-start(bf16[2,16,32,128]{3,2,1,0:T(8,128)(2,1)S(1)} %slice.18), channel_id=1, source_target_pairs={{4,0},{8,4},{12,8},{16,12},{20,16},{24,20},{28,24},{5,1},{9,5},{13... | collective-permute-start | bytes 786440 | tf_op jit(solution)/shard_map/ppermute | solution.py:23
  8.5 9.8 %copy-start.7 = (bf16[4,128]{1,0:T(4,128)(2,1)}, bf16[4,128]{1,0:T(4,128)(2,1)S(1)}, u32[]{:S(2)}) copy-start(bf16[4,128]{1,0:T(4,128)(2,1)S(1)} %collective-permute-done.3.refs_5_) | copy-start | bytes 3076
  8.6 9.8 %copy-start.4 = (bf16[4,16,128]{2,1,0:T(8,128)(2,1)}, bf16[4,16,128]{2,1,0:T(8,128)(2,1)S(1)}, u32[]{:S(2)}) copy-start(bf16[4,16,128]{2,1,0:T(8,128)(2,1)S(1)} %collective-permute-done.2.refs_4_) | copy-start | bytes 49156
  8.6 9.8 %copy-start = (bf16[4,32,128]{2,1,0:T(8,128)(2,1)}, bf16[4,32,128]{2,1,0:T(8,128)(2,1)S(1)}, u32[]{:S(2)}) copy-start(bf16[4,32,128]{2,1,0:T(8,128)(2,1)S(1)} %collective-permute-done.1.refs_3_) | copy-start | bytes 98308
  8.7 9.7 %collective-permute-start.4 = (bf16[2,49,128]{2,1,0:T(8,128)(2,1)S(1)}, bf16[2,49,128]{2,1,0:T(8,128)(2,1)S(1)}, u32[]{:S(2)}, u32[]{:S(2)}) collective-permute-start(bf16[2,49,128]{2,1,0:T(8,128)(2,1)S(1)} %pad_maximum_fusion.3), channel_id=1, source_target_pairs={{4,0},{8,4},{12,8},{16,12},{20,16},{24,20},{28,24},{5,1},{9,5},{13... | collective-permute-start | bytes 75272 | tf_op jit(solution)/shard_map/ppermute | solution.py:23
  18.4 0.6 copy-start.6
  19.0 0.7 copy-start.5
  26.4 2.6 %collective-permute-start.8 = (f32[8,216,128]{2,1,0:T(8,128)}, f32[8,216,128]{2,1,0:T(8,128)S(1)}, u32[]{:S(2)}, u32[]{:S(2)}) collective-permute-start(f32[8,216,128]{2,1,0:T(8,128)} %get-tuple-element.11), channel_id=1, source_target_pairs={{0,1},{1,0},{2,3},{3,2},{4,5},{5,4},{6,7},{7,6},{8,9},{9,8},{10,11... | collective-permute-start | bytes 2654216 | tf_op jit(solution)/shard_map/ppermute | solution.py:17
  30.3 7.7 %collective-permute-start.9 = (bf16[8,112,128]{2,1,0:T(8,128)(2,1)S(1)}, bf16[8,112,128]{2,1,0:T(8,128)(2,1)S(1)}, u32[]{:S(2)}, u32[]{:S(2)}) collective-permute-start(bf16[8,112,128]{2,1,0:T(8,128)(2,1)S(1)} %dynamic-slice_convert_fusion), channel_id=1, source_target_pairs={{0,2},{2,0},{1,3},{3,1},{4,6},{6,4},{5,7},{7,5},{8,10},{10,8},{9,1... | collective-permute-start | bytes 688136 | tf_op jit(solution)/shard_map/ppermute | solution.py:17
  38.1 5.2 %collective-permute-start.10 = (bf16[4,112,128]{2,1,0:T(8,128)(2,1)S(1)}, bf16[4,112,128]{2,1,0:T(8,128)(2,1)S(1)}, u32[]{:S(2)}, u32[]{:S(2)}) collective-permute-start(bf16[4,112,128]{2,1,0:T(8,128)(2,1)S(1)} %fusion), channel_id=1, source_target_pairs={{0,4},{4,0},{8,12},{12,8},{16,20},{20,16},{24,28},{28,24},{1,5},{5... | collective-permute-start | bytes 344072 | tf_op jit(solution)/shard_map/ppermute | solution.py:17
  43.4 4.2 %collective-permute-start.11 = (bf16[2,112,128]{2,1,0:T(8,128)(2,1)S(1)}, bf16[2,112,128]{2,1,0:T(8,128)(2,1)S(1)}, u32[]{:S(2)}, u32[]{:S(2)}) collective-permute-start(bf16[2,112,128]{2,1,0:T(8,128)(2,1)S(1)} %fusion.3), channel_id=1, source_target_pairs={{0,8},{4,12},{8,0},{12,4},{16,24},{20,28},{24,16},{28,20},{1,9},{5... | collective-permute-start | bytes 172040 | tf_op jit(solution)/shard_map/ppermute | solution.py:17
  47.7 5.1 %collective-permute-start.12 = (f32[1,112,128]{2,1,0:T(8,128)S(1)}, f32[1,112,128]{2,1,0:T(8,128)S(1)}, u32[]{:S(2)}, u32[]{:S(2)}) collective-permute-start(f32[1,112,128]{2,1,0:T(8,128)S(1)} %constant_dynamic-slice_fusion), channel_id=1, source_target_pairs={{0,16},{4,20},{8,24},{12,28},{16,0},{20,4},{24,8},{28,12},{1,17},{... | collective-permute-start | bytes 172040 | tf_op jit(solution)/shard_map/ppermute | solution.py:17
  52.8 17.6 %collective-permute-start.13 = (f32[112,128]{1,0:T(8,128)S(1)}, f32[112,128]{1,0:T(8,128)S(1)}, u32[]{:S(2)}, u32[]{:S(2)}) collective-permute-start(f32[112,128]{1,0:T(8,128)S(1)} %add_bitcast_fusion), channel_id=1, source_target_pairs={{0,2},{2,0},{1,3},{3,1},{4,6},{6,4},{5,7},{7,5},{8,10},{10,8},{9,1... | collective-permute-start | bytes 172040 | tf_op jit(solution)/shard_map/ppermute | solution.py:17
  61.5 1.9 %collective-permute-start.5 = (f32[8,128]{1,0:T(8,128)}, f32[8,128]{1,0:T(8,128)S(1)}, u32[]{:S(2)}, u32[]{:S(2)}) collective-permute-start(f32[8,128]{1,0:T(8,128)} %get-tuple-element.8.refs_0_), channel_id=1, source_target_pairs={{0,1},{1,0},{2,3},{3,2},{4,5},{5,4},{6,7},{7,6},{8,9},{9,8},{10,11... | collective-permute-start | bytes 12296 | tf_op jit(solution)/shard_map/ppermute | solution.py:17
  61.5 3.9 %collective-permute-start.6 = (f32[8,128]{1,0:T(8,128)}, f32[8,128]{1,0:T(8,128)S(1)}, u32[]{:S(2)}, u32[]{:S(2)}) collective-permute-start(f32[8,128]{1,0:T(8,128)} %get-tuple-element.8.refs_0_), channel_id=1, source_target_pairs={{0,2},{2,0},{1,3},{3,1},{4,6},{6,4},{5,7},{7,5},{8,10},{10,8},{9,1... | collective-permute-start | bytes 12296 | tf_op jit(solution)/shard_map/ppermute | solution.py:17
  62.1 3.3 %collective-permute-start.7 = (f32[8,128]{1,0:T(8,128)}, f32[8,128]{1,0:T(8,128)S(1)}, u32[]{:S(2)}, u32[]{:S(2)}) collective-permute-start(f32[8,128]{1,0:T(8,128)} %get-tuple-element.8.refs_0_), channel_id=1, source_target_pairs={{0,3},{1,2},{2,1},{3,0},{4,7},{5,6},{6,5},{7,4},{8,11},{9,10},{10,... | collective-permute-start | bytes 12296 | tf_op jit(solution)/shard_map/ppermute | solution.py:404
  63.4 2.0 %copy-start.1 = (f32[8,128]{1,0:T(8,128)}, f32[8,128]{1,0:T(8,128)S(1)}, u32[]{:S(2)}) copy-start(f32[8,128]{1,0:T(8,128)S(1)} %collective-permute-done.5.refs_1_) | copy-start | bytes 12292
  65.4 0.6 copy-start.2
  65.4 0.6 copy-start.3
  69.0 1.6 %collective-permute-start.14 = (f32[112,128]{1,0:T(8,128)S(1)}, f32[112,128]{1,0:T(8,128)S(1)}, u32[]{:S(2)}, u32[]{:S(2)}) collective-permute-start(f32[112,128]{1,0:T(8,128)S(1)} %add_bitcast_fusion), channel_id=1, source_target_pairs={{0,1},{1,0},{2,3},{3,2},{4,5},{5,4},{6,7},{7,6},{8,9},{9,8},{10,11... | collective-permute-start | bytes 172040 | tf_op jit(solution)/shard_map/ppermute | solution.py:17
  69.1 3.7 %collective-permute-start.15 = (f32[112,128]{1,0:T(8,128)S(1)}, f32[112,128]{1,0:T(8,128)S(1)}, u32[]{:S(2)}, u32[]{:S(2)}) collective-permute-start(f32[112,128]{1,0:T(8,128)S(1)} %add_bitcast_fusion), channel_id=1, source_target_pairs={{0,3},{1,2},{2,1},{3,0},{4,7},{5,6},{6,5},{7,4},{8,11},{9,10},{10,... | collective-permute-start | bytes 172040 | tf_op jit(solution)/shard_map/ppermute | solution.py:70

commit v3 on v2

--- a/solution.py
+++ b/solution.py
@@ -8,8 +8,9 @@
 from jax.experimental.pallas import tpu as pltpu
 from jax.sharding import PartitionSpec as P
 
+
 LEAD = 8
-VMEM_BYTES = 56 * 1024 * 1024
+VMEM_BYTES = 12 * 1024 * 1024
 
 
 def exchanged(value, axis, distance):
@@ -56,15 +57,19 @@
     value = near + exchanged(far.astype(jnp.bfloat16), "height", 1).astype(jnp.float32)
     place = lax.axis_index("tm")
     distance = 1
-    while distance < blocks:
+    while blocks // distance > 4:
         side = (place // distance) % 2
         split = value.reshape(value.shape[0] // 2, 2, *value.shape[1:])
         near = lax.dynamic_index_in_dim(split, side, 1, keepdims=False)
         far = lax.dynamic_index_in_dim(split, 1 - side, 1, keepdims=False)
-        wire = jnp.float32 if split.shape[0] == 1 else jnp.bfloat16
-        value = near + exchanged(far.astype(wire), "tm", distance).astype(jnp.float32)
+        value = near + exchanged(far.astype(jnp.bfloat16), "tm", distance).astype(jnp.float32)
         distance *= 2
-    own = value[0]
+    left = blocks // distance
+    spot = place // distance
+    own = lax.dynamic_index_in_dim(value, spot, 0, keepdims=False)
+    for step in range(1, left):
+        far = lax.dynamic_index_in_dim(value, spot ^ step, 0, keepdims=False)
+        own = own + exchanged(far.astype(jnp.bfloat16), "tm", step * distance).astype(jnp.float32)
     beside = exchanged(own, "width", 1)
     below = exchanged(own, "height", 1)
     across = lax.ppermute(own, ("height", "width"), [(i, 3 - i) for i in range(4)])
@@ -115,13 +120,11 @@
         act_ref[:, t * cells : (t + 1) * cells] = act.T
 
 
-def fill_pair(grad_ref, halo_ref, row_ref, col_ref, corner_ref, tail_ref, stage_ref):
-    frames, rows, cols, channels = grad_ref.shape
-    extra = halo_ref.shape[0]
+def fill_pair(stage_ref, inner_ref, row_of, col_of, corner_of):
+    total, rows, cols, channels = inner_ref.shape
     row_side = lax.axis_index("height")
     col_side = lax.axis_index("width")
     rim_row = (1 - row_side) * (rows + 1)
-    total = frames + extra
     for f in range(total):
         zeros = jnp.zeros((rows + 2, LEAD, channels), jnp.float32)
         stage_ref[f, :, 0:LEAD, :] = zeros
@@ -129,22 +132,15 @@
         empty = jnp.zeros((cols, channels), jnp.float32)
         stage_ref[f, 0, LEAD : LEAD + cols, :] = empty
         stage_ref[f, rows + 1, LEAD : LEAD + cols, :] = empty
-        inner = grad_ref[f] if f < frames else halo_ref[f - frames]
-        stage_ref[f, 1 : rows + 1, LEAD : LEAD + cols, :] = inner.astype(jnp.float32)
-        rim = row_ref[f] if f < frames else tail_ref[f - frames, 0:cols]
-        stage_ref[f, rim_row, LEAD : LEAD + cols, :] = rim.astype(jnp.float32)
+        stage_ref[f, 1 : rows + 1, LEAD : LEAD + cols, :] = inner_ref[f].astype(jnp.float32)
+        stage_ref[f, rim_row, LEAD : LEAD + cols, :] = row_of(f).astype(jnp.float32)
 
     def fill_columns(at):
         for f in range(total):
-            if f < frames:
-                column, corner = col_ref[f], corner_ref[f : f + 1]
-            else:
-                column = tail_ref[f - frames, cols : cols + rows]
-                corner = tail_ref[f - frames, cols + rows : cols + rows + 1]
-            column = column.astype(jnp.float32)
+            column = col_of(f).astype(jnp.float32)
             for r in range(rows):
                 stage_ref[f, r + 1, at : at + 1, :] = column[r : r + 1]
-            stage_ref[f, rim_row, at : at + 1, :] = corner.astype(jnp.float32)
+            stage_ref[f, rim_row, at : at + 1, :] = corner_of(f).astype(jnp.float32)
 
     @pl.when(col_side == 1)
     def _():
@@ -155,25 +151,11 @@
         fill_columns(LEAD + cols)
 
 
-def weight_kernel(rows_out, scale, pair, halves, *refs):
-    if pair:
-        act_ref, grad_ref, halo_ref, row_ref, col_ref, corner_ref, tail_ref = refs[:7]
-        refs = refs[7:]
-    else:
-        act_ref, stage_in_ref = refs[:2]
-        refs = refs[2:]
-    window_ref, outs, (stage_ref, sum_ref) = refs[0], refs[1:-2], refs[-2:]
-    total, rows_ext, cols, wide = window_ref.shape
-    rows = rows_ext - 2
+def widen(stage_ref, window_ref):
+    total, _, cols, wide = window_ref.shape
     channels = wide // 3
-    cells = rows * cols
-    frames = act_ref.shape[1] // cells
-    if pair:
-        fill_pair(grad_ref, halo_ref, row_ref, col_ref, corner_ref, tail_ref, stage_ref)
-    else:
-        stage_ref[...] = stage_in_ref[...].astype(jnp.float32)
-
-    def widen(f, carry):
+
+    def one(f, carry):
         for e in range(3):
             at = LEAD - 1 + e
             window_ref[f, :, :, e * channels : (e + 1) * channels] = stage_ref[
@@ -181,25 +163,88 @@
             ].astype(jnp.bfloat16)
         return carry
 
-    lax.fori_loop(0, total, widen, 0)
-
-    for lag_t in range(3):
+    lax.fori_loop(0, total, one, 0)
+
+
+def tap_sums(act_ref, window_of, frames, rows, cols, lag_h):
+    cells = rows * cols
+    acc = None
+    for t in range(frames):
+        window = window_of(t)[lag_h : lag_h + rows]
+        term = lax.dot_general(
+            act_ref[:, t * cells : (t + 1) * cells],
+            window.reshape(cells, window.shape[-1]),
+            (((1,), (0,)), ((), ())),
+            preferred_element_type=jnp.float32,
+        )
+        acc = term if acc is None else acc + term
+    return acc
+
+
+def near_kernel(scale, pair, act_ref, *refs):
+    sources, (window_ref, sum_ref, stage_ref) = refs[:-3], refs[-3:]
+    frames, rows_ext, cols, wide = window_ref.shape
+    rows = rows_ext - 2
+    channels = wide // 3
+    if pair:
+        grad_ref, row_ref, col_ref, corner_ref = sources
+        fill_pair(
+            stage_ref,
+            grad_ref,
+            lambda f: row_ref[f],
+            lambda f: col_ref[f],
+            lambda f: corner_ref[f : f + 1],
+        )
+    else:
+        stage_ref[...] = sources[0][...].astype(jnp.float32)
+    widen(stage_ref, window_ref)
+    for lag_h in range(3):
+        acc = scale * tap_sums(act_ref, lambda t: window_ref.at[t], frames, rows, cols, 2 - lag_h)
+        for lag_w in range(3):
+            e = 2 - lag_w
+            at = (lag_h * 3 + lag_w) * channels
+            sum_ref[at : at + channels, :] = acc[:, e * channels : (e + 1) * channels]
+
+
+def far_kernel(rows_out, scale, pair, halves, act_ref, near_ref, near_sum_ref, *refs):
+    count = 2 if pair else 1
+    sources, window_ref, outs, (stage_ref, sum_ref) = (
+        refs[:count],
+        refs[count],
+        refs[count + 1 : -2],
+        refs[-2:],
+    )
+    extra, rows_ext, cols, wide = window_ref.shape
+    frames = near_ref.shape[0]
+    rows = rows_ext - 2
+    channels = wide // 3
+    if pair:
+        halo_ref, tail_ref = sources
+        fill_pair(
+            stage_ref,
+            halo_ref,
+            lambda f: tail_ref[f, 0:cols],
+            lambda f: tail_ref[f, cols : cols + rows],
+            lambda f: tail_ref[f, cols + rows : cols + rows + 1],
+        )
+    else:
+        stage_ref[...] = sources[0][...].astype(jnp.float32)
+    widen(stage_ref, window_ref)
+
+    def window_of(f):
+        return near_ref.at[f] if f < frames else window_ref.at[f - frames]
+
+    for lag_t in range(extra):
         for lag_h in range(3):
-            acc = None
-            for t in range(frames):
-                window = window_ref[t + 2 - lag_t, 2 - lag_h : 2 - lag_h + rows]
-                term = lax.dot_general(
-                    act_ref[:, t * cells : (t + 1) * cells],
-                    window.reshape(cells, wide),
-                    (((1,), (0,)), ((), ())),
-                    preferred_element_type=jnp.float32,
-                )
-                acc = term if acc is None else acc + term
-            acc = acc * scale
+            acc = scale * tap_sums(
+                act_ref, lambda t: window_of(t + extra - lag_t), frames, rows, cols, 2 - lag_h
+            )
             for lag_w in range(3):
                 e = 2 - lag_w
                 at = ((lag_t * 3 + lag_h) * 3 + lag_w) * channels
                 sum_ref[at : at + channels, :] = acc[:, e * channels : (e + 1) * channels]
+    done = extra * 9 * channels
+    sum_ref[done:, :] = near_sum_ref[...]
     if not halves:
         outs[0][...] = sum_ref[...]
         return
@@ -223,7 +268,8 @@
 
 
 def conv_kernel(
-    window_ref,
+    near_ref,
+    far_ref,
     weight_ref,
     future_ref,
     features_ref,
@@ -244,7 +290,9 @@
         acc = None
         for lag_t in range(3):
             for lag_h in range(3):
-                window = window_ref[t + 2 - lag_t, 2 - lag_h : 2 - lag_h + rows]
+                f = t + far_ref.shape[0] - lag_t
+                source = near_ref.at[f] if f < frames else far_ref.at[f - frames]
+                window = source[2 - lag_h : 2 - lag_h + rows]
                 taps = jnp.concatenate(
                     [weight_ref[lag_t, lag_h, 2 - e] for e in range(3)], axis=1
                 )
@@ -276,7 +324,7 @@
         refs[:terms],
         refs[terms:],
     )
-    frames, rows, cols, channels = features_ref.shape
+    frames, _, _, channels = features_ref.shape
     groups = mean_ref.shape[1]
     mean = per_channel(mean_ref[...], channels)
     rstd = per_channel(rstd_ref[...], channels)
@@ -294,14 +342,21 @@
         out_ref[t] = (grad_ref[t].astype(jnp.float32) + corrected).astype(jnp.bfloat16)
 
 
-def call(kernel, out_shape, scratch=(), flops=0, moved=0):
-    return pl.pallas_call(
-        kernel,
-        out_shape=out_shape,
-        scratch_shapes=list(scratch),
-        compiler_params=pltpu.CompilerParams(vmem_limit_bytes=VMEM_BYTES),
-        cost_estimate=pl.CostEstimate(flops=flops, bytes_accessed=moved, transcendentals=0),
-    )
+def call(kernel, out_shape, scratch=(), flops=0, moved=0, out_specs=None):
+    here = pl.BlockSpec(memory_space=pltpu.VMEM)
+
+    def run(*args):
+        return pl.pallas_call(
+            kernel,
+            out_shape=out_shape,
+            in_specs=[here] * len(args),
+            out_specs=out_specs or jax.tree.map(lambda _: here, out_shape),
+            scratch_shapes=list(scratch),
+            compiler_params=pltpu.CompilerParams(vmem_limit_bytes=VMEM_BYTES),
+            cost_estimate=pl.CostEstimate(flops=flops, bytes_accessed=moved, transcendentals=0),
+        )(*args)
+
+    return run
 
 
 def extended(cells, sides, width):
@@ -315,20 +370,21 @@
 
 
 def rims(grad_out, extra):
-    frames, rows, cols, channels = grad_out.shape
+    _, rows, cols, _ = grad_out.shape
     row_side = lax.axis_index("height")
     col_side = lax.axis_index("width")
     row_at = (1 - row_side) * (rows - 1)
     col_at = (1 - col_side) * (cols - 1)
+    halo = shifted(grad_out[:extra], "tm", -1)
     row = lax.dynamic_slice_in_dim(grad_out, row_at, 1, 1)[:, 0]
     col = lax.dynamic_slice_in_dim(grad_out, col_at, 1, 2)[:, :, 0]
     corner = lax.dynamic_slice_in_dim(row, col_at, 1, 1)[:, 0]
-    halo = shifted(grad_out[:extra], "tm", -1)
     row = exchanged(row, "height", 1)
     col = exchanged(col, "width", 1)
     corner = lax.ppermute(corner, ("height", "width"), [(i, 3 - i) for i in range(4)])
     packed = jnp.concatenate([row[:extra], col[:extra], corner[:extra, None]], axis=1)
-    return halo, row, col, corner, shifted(packed, "tm", -1)
+    tail = shifted(packed, "tm", -1)
+    return (grad_out, row, col, corner), (halo, tail)
 
 
 def on_device(features, grad_out, mean_saved, rstd_saved, gain, bias, weight, future_cot):
@@ -348,11 +404,12 @@
     f32 = jnp.float32
 
     if pair:
-        sources = (grad_out, *rims(grad_out, extra))
+        near_sources, far_sources = rims(grad_out, extra)
     else:
         padded = extended(grad_out, (("height", 1), ("width", 2)), 1)
-        whole = jnp.concatenate([padded, shifted(padded[:extra], "tm", -1)], axis=0)
-        sources = (jnp.pad(whole, ((0, 0), (0, 0), (LEAD - 1, LEAD - 1), (0, 0))),)
+        sides = ((0, 0), (0, 0), (LEAD - 1, LEAD - 1), (0, 0))
+        near_sources = (jnp.pad(padded, sides),)
+        far_sources = (jnp.pad(shifted(padded[:extra], "tm", -1), sides),)
 
     act = call(
         act_kernel,
@@ -361,24 +418,34 @@
         moved=4 * frames * cells * channels,
     )(features, mean_saved, rstd_saved, gain, bias)
 
-    total = frames + extra
-    window_shape = (total, rows + 2, cols, 3 * channels)
+    def window_shape(count):
+        return jax.ShapeDtypeStruct((count, rows + 2, cols, 3 * channels), jnp.bfloat16)
+
+    def stage_shape(count):
+        return pltpu.VMEM((count, rows + 2, cols + 2 * LEAD, channels), f32)
+
     work = 2 * taps * channels * channels * frames * cells
+    part = taps // (extra + 1)
+    near_window, near_sum = call(
+        functools.partial(near_kernel, grad_scale, pair),
+        (window_shape(frames), jax.ShapeDtypeStruct((part * channels, channels), f32)),
+        scratch=(stage_shape(frames),),
+        flops=work // 3,
+        moved=4 * 1024 * 1024,
+    )(act, *near_sources)
+
     if halves:
         half_shape = jax.ShapeDtypeStruct((blocks, rows_out // 2, channels), f32)
         sum_shapes = (half_shape, half_shape)
     else:
         sum_shapes = (jax.ShapeDtypeStruct((taps * channels, channels), f32),)
-    window, *sums = call(
-        functools.partial(weight_kernel, rows_out, grad_scale, pair, halves),
-        (jax.ShapeDtypeStruct(window_shape, jnp.bfloat16), *sum_shapes),
-        scratch=(
-            pltpu.VMEM((total, rows + 2, cols + 2 * LEAD, channels), f32),
-            pltpu.VMEM((taps * channels, channels), f32),
-        ),
-        flops=work,
-        moved=8 * 1024 * 1024,
-    )(act, *sources)
+    far_window, *sums = call(
+        functools.partial(far_kernel, rows_out, grad_scale, pair, halves),
+        (window_shape(extra), *sum_shapes),
+        scratch=(stage_shape(extra), pltpu.VMEM((taps * channels, channels), f32)),
+        flops=2 * work // 3,
+        moved=4 * 1024 * 1024,
+    )(act, near_window, near_sum, *far_sources)
 
     if halves:
         weight_grad = reduced_share(*sums, rows_out)
@@ -394,15 +461,15 @@
         ),
         flops=work,
         moved=8 * 1024 * 1024,
-    )(window, weight, future_cot, features, mean_saved, rstd_saved, gain, bias)
+    )(near_window, far_window, weight, future_cot, features, mean_saved, rstd_saved, gain, bias)
 
     if pair:
-        parts = [
-            local,
-            exchanged(local, "width", 1),
-            exchanged(local, "height", 1),
-            lax.ppermute(local, ("height", "width"), [(i, 3 - i) for i in range(4)]),
-        ]
+        parts = [local]
+        parts.append(exchanged(local, "width", 1))
+        parts.append(exchanged(local, "height", 1))
+        parts.append(
+            lax.ppermute(local, ("height", "width"), [(i, 3 - i) for i in range(4)])
+        )
     else:
         parts = [lax.psum(local, ("height", "width"))]
     input_cot = call(
@@ -410,6 +477,7 @@
         jax.ShapeDtypeStruct(features.shape, jnp.bfloat16),
         flops=20 * frames * cells * channels,
         moved=10 * frames * cells * channels,
+        out_specs=pl.BlockSpec(features.shape, lambda: (0, 0, 0, 0)),
     )(*parts, scaled, features, grad_out, mean_saved, rstd_saved)
     return (input_cot, weight_grad)
 

time: 74.1 us -> 70.9 us (0.957)
  Pallas kernels: 19.2 us -> 9.45 us
  local copies, waits for them, and re-layouts: 5.42 us -> 11.8 us
  waiting for transfers between devices: 26.9 us -> 24.6 us
  starting transfers between devices: 19.1 us -> 20.5 us
  other arithmetic: 2.11 us -> 3.04 us
    pallas_call x4 -> x5, Pallas kernels: 19.2 us -> 9.45 us  [run(): pl.pallas_call(kernel, out_shape=out_shape, in_specs=[here] * len(args),...]
    unnamed x18 -> x38, local copies, waits for them, and re-layouts: 1.93 us -> 8.25 us
    ppermute x2, waiting for transfers between devices: 6.02 us -> 3.71 us  [shifted(): lax.ppermute(value, axis, [(source, source + steps) for source in range(i...]
    ppermute x11 -> x12, starting transfers between devices: 11.4 us -> 12.8 us  [exchanged(): return lax.ppermute(value, axis, [(i, i ^ distance) for i in range(count)])]
    add x1, other arithmetic: 0.04 us -> 0.98 us  [reduced_share(): near + exchanged(far.astype(jnp.bfloat16), 'height', 1).astype(jnp.float32)]
    ppermute x11 -> x12, waiting for transfers between devices: 18.6 us -> 18.7 us  [exchanged(): return lax.ppermute(value, axis, [(i, i ^ distance) for i in range(count)])]
  transfers between devices with their start and end apart: 16 -> 17, of which waited for: 8 -> 8; matrix products, arithmetic and copies ran while one was open for 4% -> 4% of each run, Pallas kernels for 17% -> 10%
where the time goes in v3:
time: 70.9 us; the launch traced here: 70.4 us
  waiting for transfers between devices  24.6 us (35%)
  starting transfers between devices  20.5 us (29%)
  local copies, waits for them, and re-layouts  11.8 us (17%)
  Pallas kernels  9.45 us (13%)
  other arithmetic  3.04 us (4%)
  between operations  1.01 us (1%)
    ppermute x12, waiting for transfers between devices, exchanged(): return lax.ppermute(value, axis, [(i, i ^ distance) for i in range(count)])  18.7 us
    ppermute x12, starting transfers between devices, exchanged(): return lax.ppermute(value, axis, [(i, i ^ distance) for i in range(count)])  12.8 us
    pallas_call x5, Pallas kernels, run(): pl.pallas_call(kernel, out_shape=out_shape, in_specs=[here] * len(args),...  9.45 us
    unnamed x38, local copies, waits for them, and re-layouts  8.25 us
    ppermute x2, waiting for transfers between devices, shifted(): lax.ppermute(value, axis, [(source, source + steps) for source in range(i...  3.71 us
    ppermute x2, starting transfers between devices, shifted(): lax.ppermute(value, axis, [(source, source + steps) for source in range(i...  2.58 us
    ppermute x1, starting transfers between devices, rims(): lax.ppermute(corner, ('height', 'width'), [(i, 3 - i) for i in range(4)])  2.43 us
    ppermute x1, waiting for transfers between devices, reduced_share(): lax.ppermute(own, ('height', 'width'), [(i, 3 - i) for i in range(4)])  2.14 us
  transfers between devices with their start and end apart: 17, of which 8 were waited for; matrix products, arithmetic and copies ran while one was open for 4% of the time, Pallas kernels for 10%

profile of v3, /device:TPU:0, one launch (start us, length us, event | category | flops | bytes accessed | tf_op | source)
XLA Modules:
  0.0 70.4 jit_solution(6561700941078513811)
XLA Ops:
  0.6 0.0 copy-start.2
  0.7 0.8 %constant_dynamic-slice_fusion = bf16[4,1,1,128]{3,2,1,0:T(2,128)(2,1)S(1)} fusion(bf16[4,16,32,128]{3,2,1,0:T(8,128)(2,1)} %refs_6_.1, s32[]{:T(128)S(6)} %select_n.83, s32[]{:T(128)S(6)} %select_n.84), kind=kLoop, calls=%fused_computation.26 | loop fusion | bytes 2056 | tf_op jit(solution)/shard_map/dynamic_slice | solution.py:381
  1.4 2.4 %collective-permute-start.2 = (bf16[4,128]{1,0:T(4,128)(2,1)S(1)}, bf16[4,128]{1,0:T(4,128)(2,1)S(1)}, u32[]{:S(2)}, u32[]{:S(2)}) collective-permute-start(bf16[4,128]{1,0:T(4,128)(2,1)S(1)} %bitcast.40), channel_id=1, source_target_pairs={{0,3},{1,2},{2,1},{3,0},{4,7},{5,6},{6,5},{7,4},{8,11},{9,10},{10,... | collective-permute-start | bytes 3080 | tf_op jit(solution)/shard_map/ppermute | solution.py:384
  3.9 0.8 %dynamic-slice_bitcast_fusion = bf16[4,32,128]{2,1,0:T(8,128)(2,1)S(1)} fusion(bf16[4,16,32,128]{3,2,1,0:T(8,128)(2,1)} %refs_6_.1, s32[]{:T(128)S(6)} %select_n.81), kind=kLoop, calls=%fused_computation.18 | loop fusion | bytes 65540 | tf_op jit(solution)/shard_map/squeeze | solution.py:379
  4.6 0.6 collective-permute-start
  5.2 0.9 %constant_dynamic-slice_fusion.1 = bf16[4,16,1,128]{3,2,1,0:T(2,128)(2,1)S(1)} fusion(bf16[4,16,32,128]{3,2,1,0:T(8,128)(2,1)} %refs_6_.1, s32[]{:T(128)S(6)} %select_n.82), kind=kLoop, calls=%fused_computation.27 | loop fusion | bytes 32772 | tf_op jit(solution)/shard_map/dynamic_slice | solution.py:380
  6.2 0.2 collective-permute-start.1
  6.3 1.0 %slice.18 = bf16[2,16,32,128]{3,2,1,0:T(8,128)(2,1)S(1)} slice(bf16[4,16,32,128]{3,2,1,0:T(8,128)(2,1)} %refs_6_.1), slice={[0:2], [0:16], [0:32], [0:128]} | slice | bytes 524288 | tf_op jit(solution)/shard_map/slice | solution.py:378
  7.3 1.3 %collective-permute-start.3 = (bf16[2,16,32,128]{3,2,1,0:T(8,128)(2,1)S(1)}, bf16[2,16,32,128]{3,2,1,0:T(8,128)(2,1)S(1)}, u32[]{:S(2)}, u32[]{:S(2)}) collective-permute-start(bf16[2,16,32,128]{3,2,1,0:T(8,128)(2,1)S(1)} %slice.18), channel_id=1, source_target_pairs={{4,0},{8,4},{12,8},{16,12},{20,16},{24,20},{28,24},{5,1},{9,5},{13... | collective-permute-start | bytes 786440 | tf_op jit(solution)/shard_map/ppermute | solution.py:24
  8.6 0.0 copy-start
  8.6 1.0 %copy-done = bf16[4,16,32,128]{3,2,1,0:T(8,128)(2,1)S(1)} copy-done((bf16[4,16,32,128]{3,2,1,0:T(8,128)(2,1)S(1)}, bf16[4,16,32,128]{3,2,1,0:T(8,128)(2,1)}, u32[]{:S(2)}) %copy-start) | copy-done | bytes 524312
  9.6 0.7 copy-done.3
  10.3 0.7 copy-done.5
  11.0 0.7 copy-done.7
  11.7 0.7 copy-done.9
  12.3 0.5 shard_map.95.act_ref
  12.8 0.0 collective-permute-done.2.refs_3_
  12.9 0.0 collective-permute-done.1.refs_2_
  12.9 0.0 collective-permute-done.refs_1_
  12.9 1.3 %collective-permute-start.4 = (bf16[2,49,128]{2,1,0:T(8,128)(2,1)S(1)}, bf16[2,49,128]{2,1,0:T(8,128)(2,1)S(1)}, u32[]{:S(2)}, u32[]{:S(2)}) collective-permute-start(bf16[2,49,128]{2,1,0:T(8,128)(2,1)S(1)} %pad_maximum_fusion.3), channel_id=1, source_target_pairs={{4,0},{8,4},{12,8},{16,12},{20,16},{24,20},{28,24},{5,1},{9,5},{13... | collective-permute-start | bytes 75272 | tf_op jit(solution)/shard_map/ppermute | solution.py:24
  14.2 1.4 %shard_map.96 = (bf16[4,18,32,384]{3,2,1,0:T(8,128)(2,1)S(1)}, f32[1152,128]{1,0:T(8,128)S(1)}) custom-call(bf16[128,2048]{1,0:T(8,128)(2,1)S(1)} %shard_map.95.act_ref, bf16[4,16,32,128]{3,2,1,0:T(8,128)(2,1)S(1)} %copy-done.2, bf16[4,32,128]{2,1,0:T(8,128)(2,1)S(1)} %collective-permute-done.refs_1_, ...), custom_call_target="tpu_custom_call" | custom-call | flops 603979776 | bytes 4194304 | tf_op jit(solution)/shard_map/pallas_call | solution.py:349
  15.6 3.7 %collective-permute-done.4.refs_1_ = bf16[2,49,128]{2,1,0:T(8,128)(2,1)S(1)} collective-permute-done((bf16[2,49,128]{2,1,0:T(8,128)(2,1)S(1)}, bf16[2,49,128]{2,1,0:T(8,128)(2,1)S(1)}, u32[]{:S(2)}, u32[]{:S(2)}) %collective-permute-start.4) | collective-permute-done | bytes 25120 | tf_op jit(solution)/shard_map/ppermute | solution.py:24
  19.3 0.0 collective-permute-done.3.refs_0_
  19.3 2.1 %shard_map.97 = (bf16[2,18,32,384]{3,2,1,0:T(8,128)(2,1)S(1)}, f32[8,216,128]{2,1,0:T(8,128)S(1)}, f32[8,216,128]{2,1,0:T(8,128)S(1)}) custom-call(bf16[128,2048]{1,0:T(8,128)(2,1)S(1)} %shard_map.95.act_ref, bf16[4,18,32,384]{3,2,1,0:T(8,128)(2,1)S(1)} %get-tuple-element.9.near_ref, f32[1152,128]{1,0:T(8,128)S(1)} %get-tuple-element.10.near_sum_ref, ...), custom_call_target="tpu_custom_call" | custom-call | flops 1207959552 | bytes 4194304 | tf_op jit(solution)/shard_map/pallas_call | solution.py:349
  21.5 0.9 %copy-done.15 = bf16[2,18,32,384]{3,2,1,0:T(8,128)(2,1)} copy-done((bf16[2,18,32,384]{3,2,1,0:T(8,128)(2,1)}, bf16[2,18,32,384]{3,2,1,0:T(8,128)(2,1)S(1)}, u32[]{:S(2)}) %copy-start.15) | copy-done | bytes 884760
  22.4 0.0 collective-permute-start.8
  22.4 2.4 %collective-permute-done.8 = f32[8,216,128]{2,1,0:T(8,128)S(1)} collective-permute-done((f32[8,216,128]{2,1,0:T(8,128)S(1)}, f32[8,216,128]{2,1,0:T(8,128)S(1)}, u32[]{:S(2)}, u32[]{:S(2)}) %collective-permute-start.8) | collective-permute-done | bytes 884768 | tf_op jit(solution)/shard_map/ppermute | solution.py:18
  24.8 0.9 %copy-done.17 = f32[8,216,128]{2,1,0:T(8,128)} copy-done((f32[8,216,128]{2,1,0:T(8,128)}, f32[8,216,128]{2,1,0:T(8,128)S(1)}, u32[]{:S(2)}) %copy-start.17) | copy-done | bytes 884760
  25.7 1.3 %add.64 = f32[8,216,128]{2,1,0:T(8,128)S(1)} add(f32[8,216,128]{2,1,0:T(8,128)S(1)} %get-tuple-element.14, f32[8,216,128]{2,1,0:T(8,128)} %copy-done.17) | non-fusion elementwise | flops 221184 | bytes 2654208 | tf_op jit(solution)/shard_map/add | solution.py:50
  27.0 0.0 copy-start.1
  27.0 0.0 copy-start.4
  27.0 0.0 copy-start.6
  27.0 0.0 copy-start.8
  27.0 0.0 copy-start.10
  27.0 0.0 copy-start.11
  27.1 0.0 copy-start.12
  27.1 1.8 %collective-permute-start.9 = (bf16[8,112,128]{2,1,0:T(8,128)(2,1)S(1)}, bf16[8,112,128]{2,1,0:T(8,128)(2,1)}, u32[]{:S(2)}, u32[]{:S(2)}) collective-permute-start(bf16[8,112,128]{2,1,0:T(8,128)(2,1)S(1)} %dynamic-slice_convert_fusion), channel_id=1, source_target_pairs={{0,2},{2,0},{1,3},{3,1},{4,6},{6,4},{5,7},{7,5},{8,10},{10,8},{9,1... | collective-permute-start | bytes 688136 | tf_op jit(solution)/shard_map/ppermute | solution.py:18
  28.9 6.0 %collective-permute-done.9 = bf16[8,112,128]{2,1,0:T(8,128)(2,1)} collective-permute-done((bf16[8,112,128]{2,1,0:T(8,128)(2,1)S(1)}, bf16[8,112,128]{2,1,0:T(8,128)(2,1)}, u32[]{:S(2)}, u32[]{:S(2)}) %collective-permute-start.9) | collective-permute-done | bytes 229408 | tf_op jit(solution)/shard_map/ppermute | solution.py:18
  34.9 1.0 %convert_add_fusion = f32[8,112,128]{2,1,0:T(8,128)S(1)} fusion(bf16[8,112,128]{2,1,0:T(8,128)(2,1)} %collective-permute-done.9, f32[8,216,128]{2,1,0:T(8,128)S(1)} %add.64, s32[]{:T(128)S(6)} %select_n.87), kind=kLoop, calls=%fused_computation | loop fusion | flops 229376 | bytes 1146884 | tf_op jit(solution)/shard_map/add | solution.py:57
  36.0 3.0 %collective-permute-start.10 = (bf16[4,112,128]{2,1,0:T(8,128)(2,1)S(1)}, bf16[4,112,128]{2,1,0:T(8,128)(2,1)S(1)}, u32[]{:S(2)}, u32[]{:S(2)}) collective-permute-start(bf16[4,112,128]{2,1,0:T(8,128)(2,1)S(1)} %fusion), channel_id=1, source_target_pairs={{0,4},{4,0},{8,12},{12,8},{16,20},{20,16},{24,28},{28,24},{1,5},{5... | collective-permute-start | bytes 344072 | tf_op jit(solution)/shard_map/ppermute | solution.py:18
  38.9 2.8 %collective-permute-done.10 = bf16[4,112,128]{2,1,0:T(8,128)(2,1)S(1)} collective-permute-done((bf16[4,112,128]{2,1,0:T(8,128)(2,1)S(1)}, bf16[4,112,128]{2,1,0:T(8,128)(2,1)S(1)}, u32[]{:S(2)}, u32[]{:S(2)}) %collective-permute-start.10) | collective-permute-done | bytes 114720 | tf_op jit(solution)/shard_map/ppermute | solution.py:18
  41.8 2.3 %collective-permute-start.11 = (bf16[112,128]{1,0:T(8,128)(2,1)S(1)}, bf16[112,128]{1,0:T(8,128)(2,1)S(1)}, u32[]{:S(2)}, u32[]{:S(2)}) collective-permute-start(bf16[112,128]{1,0:T(8,128)(2,1)S(1)} %get-tuple-element.16), channel_id=1, source_target_pairs={{0,8},{4,12},{8,0},{12,4},{16,24},{20,28},{24,16},{28,20},{1,9},{5... | collective-permute-start | bytes 86024 | tf_op jit(solution)/shard_map/ppermute | solution.py:18
  44.1 2.6 %collective-permute-start.12 = (bf16[112,128]{1,0:T(8,128)(2,1)S(1)}, bf16[112,128]{1,0:T(8,128)(2,1)S(1)}, u32[]{:S(2)}, u32[]{:S(2)}) collective-permute-start(bf16[112,128]{1,0:T(8,128)(2,1)S(1)} %get-tuple-element.18), channel_id=1, source_target_pairs={{0,16},{4,20},{8,24},{12,28},{16,0},{20,4},{24,8},{28,12},{1,17},{... | collective-permute-start | bytes 86024 | tf_op jit(solution)/shard_map/ppermute | solution.py:18
  46.7 0.0 collective-permute-start.13
  46.7 0.0 collective-permute-done.11
  46.7 2.6 %collective-permute-done.12 = bf16[112,128]{1,0:T(8,128)(2,1)S(1)} collective-permute-done((bf16[112,128]{1,0:T(8,128)(2,1)S(1)}, bf16[112,128]{1,0:T(8,128)(2,1)S(1)}, u32[]{:S(2)}, u32[]{:S(2)}) %collective-permute-start.12) | collective-permute-done | bytes 28704 | tf_op jit(solution)/shard_map/ppermute | solution.py:18
  49.3 3.0 %collective-permute-done.13 = bf16[112,128]{1,0:T(8,128)(2,1)S(1)} collective-permute-done((bf16[112,128]{1,0:T(8,128)(2,1)S(1)}, bf16[112,128]{1,0:T(8,128)(2,1)S(1)}, u32[]{:S(2)}, u32[]{:S(2)}) %collective-permute-start.13) | collective-permute-done | bytes 28704 | tf_op jit(solution)/shard_map/ppermute | solution.py:18
  52.4 1.6 %collective-permute-start.14 = (f32[112,128]{1,0:T(8,128)S(1)}, f32[112,128]{1,0:T(8,128)S(1)}, u32[]{:S(2)}, u32[]{:S(2)}) collective-permute-start(f32[112,128]{1,0:T(8,128)S(1)} %fusion.4), channel_id=1, source_target_pairs={{0,2},{2,0},{1,3},{3,1},{4,6},{6,4},{5,7},{7,5},{8,10},{10,8},{9,1... | collective-permute-start | bytes 172040 | tf_op jit(solution)/shard_map/ppermute | solution.py:18
  54.0 1.5 %copy-done.14 = bf16[4,18,32,384]{3,2,1,0:T(8,128)(2,1)S(1)} copy-done((bf16[4,18,32,384]{3,2,1,0:T(8,128)(2,1)S(1)}, bf16[4,18,32,384]{3,2,1,0:T(8,128)(2,1)}, u32[]{:S(2)}) %copy-start.14) | copy-done | bytes 1769496
  55.5 1.2 %copy-done.16 = bf16[2,18,32,384]{3,2,1,0:T(8,128)(2,1)S(1)} copy-done((bf16[2,18,32,384]{3,2,1,0:T(8,128)(2,1)S(1)}, bf16[2,18,32,384]{3,2,1,0:T(8,128)(2,1)}, u32[]{:S(2)}) %copy-start.16) | copy-done | bytes 884760
  56.7 4.0 %shard_map.98 = (f32[4,16,32,128]{3,2,1,0:T(8,128)S(1)}, f32[8,128]{1,0:T(8,128)S(1)}) custom-call(bf16[4,18,32,384]{3,2,1,0:T(8,128)(2,1)S(1)} %copy-done.14, bf16[2,18,32,384]{3,2,1,0:T(8,128)(2,1)S(1)} %copy-done.16, bf16[3,3,3,128,128]{4,3,2,1,0:T(8,128)(2,1)S(1)} %copy-done.11, bf16[2,16,32,128]{3,2,1,0:T(8,128)(2,1)S(1)} %copy-done.12, ...), custom_call_target="tpu_custom_call" | custom-call | flops 1811939328 | bytes 8388608 | tf_op jit(solution)/shard_map/pallas_call | solution.py:349
  60.7 0.1 collective-permute-start.5
  60.8 0.6 collective-permute-start.6
  61.3 1.3 %collective-permute-start.7 = (f32[8,128]{1,0:T(8,128)S(1)}, f32[8,128]{1,0:T(8,128)S(1)}, u32[]{:S(2)}, u32[]{:S(2)}) collective-permute-start(f32[8,128]{1,0:T(8,128)S(1)} %get-tuple-element.12.refs_0_), channel_id=1, source_target_pairs={{0,3},{1,2},{2,1},{3,0},{4,7},{5,6},{6,5},{7,4},{8,11},{9,10},{10,... | collective-permute-start | bytes 12296 | tf_op jit(solution)/shard_map/ppermute | solution.py:471
  62.6 0.0 collective-permute-done.5.refs_1_
  62.6 1.8 %collective-permute-done.6.refs_2_ = f32[8,128]{1,0:T(8,128)S(1)} collective-permute-done((f32[8,128]{1,0:T(8,128)S(1)}, f32[8,128]{1,0:T(8,128)S(1)}, u32[]{:S(2)}, u32[]{:S(2)}) %collective-permute-start.6) | collective-permute-done | bytes 4128 | tf_op jit(solution)/shard_map/ppermute | solution.py:18
  64.4 0.0 collective-permute-done.7.refs_3_
  64.4 1.4 %shard_map.99 = bf16[4,16,32,128]{3,2,1,0:T(8,128)(2,1)} custom-call(f32[8,128]{1,0:T(8,128)S(1)} %get-tuple-element.12.refs_0_, f32[8,128]{1,0:T(8,128)S(1)} %collective-permute-done.5.refs_1_, f32[8,128]{1,0:T(8,128)S(1)} %collective-permute-done.6.refs_2_, f32[8,128]{1,0:T(8,128)S(1)} %collective-permute-done.7.refs_3_, ...), custom_call_target="tpu_custom_call" | custom-call | flops 5242880 | bytes 2621440 | tf_op jit(solution)/shard_map/pallas_call | solution.py:349
  65.9 0.1 collective-permute-start.15
  66.0 1.5 %collective-permute-start.16 = (f32[112,128]{1,0:T(8,128)S(1)}, f32[112,128]{1,0:T(8,128)S(1)}, u32[]{:S(2)}, u32[]{:S(2)}) collective-permute-start(f32[112,128]{1,0:T(8,128)S(1)} %fusion.4), channel_id=1, source_target_pairs={{0,3},{1,2},{2,1},{3,0},{4,7},{5,6},{6,5},{7,4},{8,11},{9,10},{10,... | collective-permute-start | bytes 172040 | tf_op jit(solution)/shard_map/ppermute | solution.py:75
  67.4 0.0 collective-permute-done.14
  67.5 0.0 collective-permute-done.15
  67.5 2.1 %collective-permute-done.16 = f32[112,128]{1,0:T(8,128)S(1)} collective-permute-done((f32[112,128]{1,0:T(8,128)S(1)}, f32[112,128]{1,0:T(8,128)S(1)}, u32[]{:S(2)}, u32[]{:S(2)}) %collective-permute-start.16) | collective-permute-done | bytes 57376 | tf_op jit(solution)/shard_map/ppermute | solution.py:75
  69.7 0.7 pad_maximum_fusion
  (35 shorter events, 0.3 us)
Async XLA Ops:
  0.6 13.6 %copy-start.2 = (bf16[4,16,32,128]{3,2,1,0:T(8,128)(2,1)S(1)}, bf16[4,16,32,128]{3,2,1,0:T(8,128)(2,1)}, u32[]{:S(2)}) copy-start(bf16[4,16,32,128]{3,2,1,0:T(8,128)(2,1)} %refs_6_.1) | copy-start | bytes 1572868
  1.4 11.4 %collective-permute-start.2 = (bf16[4,128]{1,0:T(4,128)(2,1)S(1)}, bf16[4,128]{1,0:T(4,128)(2,1)S(1)}, u32[]{:S(2)}, u32[]{:S(2)}) collective-permute-start(bf16[4,128]{1,0:T(4,128)(2,1)S(1)} %bitcast.40), channel_id=1, source_target_pairs={{0,3},{1,2},{2,1},{3,0},{4,7},{5,6},{6,5},{7,4},{8,11},{9,10},{10,... | collective-permute-start | bytes 3080 | tf_op jit(solution)/shard_map/ppermute | solution.py:384
  4.6 8.3 %collective-permute-start = (bf16[4,32,128]{2,1,0:T(8,128)(2,1)S(1)}, bf16[4,32,128]{2,1,0:T(8,128)(2,1)S(1)}, u32[]{:S(2)}, u32[]{:S(2)}) collective-permute-start(bf16[4,32,128]{2,1,0:T(8,128)(2,1)S(1)} %dynamic-slice_bitcast_fusion), channel_id=1, source_target_pairs={{0,2},{2,0},{1,3},{3,1},{4,6},{6,4},{5,7},{7,5},{8,10},{10,8},{9,1... | collective-permute-start | bytes 98312 | tf_op jit(solution)/shard_map/ppermute | solution.py:18
  6.2 6.7 %collective-permute-start.1 = (bf16[4,16,128]{2,1,0:T(8,128)(2,1)S(1)}, bf16[4,16,128]{2,1,0:T(8,128)(2,1)S(1)}, u32[]{:S(2)}, u32[]{:S(2)}) collective-permute-start(bf16[4,16,128]{2,1,0:T(8,128)(2,1)S(1)} %bitcast.39), channel_id=1, source_target_pairs={{0,1},{1,0},{2,3},{3,2},{4,5},{5,4},{6,7},{7,6},{8,9},{9,8},{10,11... | collective-permute-start | bytes 49160 | tf_op jit(solution)/shard_map/ppermute | solution.py:18
  7.3 12.0 %collective-permute-start.3 = (bf16[2,16,32,128]{3,2,1,0:T(8,128)(2,1)S(1)}, bf16[2,16,32,128]{3,2,1,0:T(8,128)(2,1)S(1)}, u32[]{:S(2)}, u32[]{:S(2)}) collective-permute-start(bf16[2,16,32,128]{3,2,1,0:T(8,128)(2,1)S(1)} %slice.18), channel_id=1, source_target_pairs={{4,0},{8,4},{12,8},{16,12},{20,16},{24,20},{28,24},{5,1},{9,5},{13... | collective-permute-start | bytes 786440 | tf_op jit(solution)/shard_map/ppermute | solution.py:24
  8.6 1.0 %copy-start = (bf16[4,16,32,128]{3,2,1,0:T(8,128)(2,1)S(1)}, bf16[4,16,32,128]{3,2,1,0:T(8,128)(2,1)}, u32[]{:S(2)}) copy-start(bf16[4,16,32,128]{3,2,1,0:T(8,128)(2,1)} %refs_5_.1) | copy-start | bytes 1572868
  9.6 0.7 copy-start.3
  10.3 0.7 copy-start.5
  11.0 0.7 copy-start.7
  11.7 0.7 copy-start.9
  12.9 6.4 %collective-permute-start.4 = (bf16[2,49,128]{2,1,0:T(8,128)(2,1)S(1)}, bf16[2,49,128]{2,1,0:T(8,128)(2,1)S(1)}, u32[]{:S(2)}, u32[]{:S(2)}) collective-permute-start(bf16[2,49,128]{2,1,0:T(8,128)(2,1)S(1)} %pad_maximum_fusion.3), channel_id=1, source_target_pairs={{4,0},{8,4},{12,8},{16,12},{20,16},{24,20},{28,24},{5,1},{9,5},{13... | collective-permute-start | bytes 75272 | tf_op jit(solution)/shard_map/ppermute | solution.py:24
  15.6 5.9 %copy-start.13 = (bf16[4,18,32,384]{3,2,1,0:T(8,128)(2,1)}, bf16[4,18,32,384]{3,2,1,0:T(8,128)(2,1)S(1)}, u32[]{:S(2)}) copy-start(bf16[4,18,32,384]{3,2,1,0:T(8,128)(2,1)S(1)} %get-tuple-element.9.near_ref) | copy-start | bytes 5308420
  21.5 0.9 %copy-start.15 = (bf16[2,18,32,384]{3,2,1,0:T(8,128)(2,1)}, bf16[2,18,32,384]{3,2,1,0:T(8,128)(2,1)S(1)}, u32[]{:S(2)}) copy-start(bf16[2,18,32,384]{3,2,1,0:T(8,128)(2,1)S(1)} %get-tuple-element.11.far_ref) | copy-start | bytes 2654212
  22.4 2.4 %collective-permute-start.8 = (f32[8,216,128]{2,1,0:T(8,128)S(1)}, f32[8,216,128]{2,1,0:T(8,128)S(1)}, u32[]{:S(2)}, u32[]{:S(2)}) collective-permute-start(f32[8,216,128]{2,1,0:T(8,128)S(1)} %get-tuple-element.15), channel_id=1, source_target_pairs={{0,1},{1,0},{2,3},{3,2},{4,5},{5,4},{6,7},{7,6},{8,9},{9,8},{10,11... | collective-permute-start | bytes 2654216 | tf_op jit(solution)/shard_map/ppermute | solution.py:18
  24.8 0.9 %copy-start.17 = (f32[8,216,128]{2,1,0:T(8,128)}, f32[8,216,128]{2,1,0:T(8,128)S(1)}, u32[]{:S(2)}) copy-start(f32[8,216,128]{2,1,0:T(8,128)S(1)} %collective-permute-done.8) | copy-start | bytes 2654212
  27.0 27.0 %copy-start.1 = (bf16[4,16,32,128]{3,2,1,0:T(8,128)(2,1)S(1)}, bf16[4,16,32,128]{3,2,1,0:T(8,128)(2,1)}, u32[]{:S(2)}) copy-start(bf16[4,16,32,128]{3,2,1,0:T(8,128)(2,1)} %refs_5_.1) | copy-start | bytes 1572868
  27.0 27.0 %copy-start.4 = (f32[4,32]{1,0:T(4,128)S(1)}, f32[4,32]{1,0:T(4,128)}, u32[]{:S(2)}) copy-start(f32[4,32]{1,0:T(4,128)} %refs_7_.1) | copy-start | bytes 1540
  27.0 27.0 %copy-start.6 = (f32[4,32]{1,0:T(4,128)S(1)}, f32[4,32]{1,0:T(4,128)}, u32[]{:S(2)}) copy-start(f32[4,32]{1,0:T(4,128)} %refs_8_.1) | copy-start | bytes 1540
  27.0 27.0 %copy-start.8 = (f32[128]{0:T(128)S(1)}, f32[128]{0:T(128)}, u32[]{:S(2)}) copy-start(f32[128]{0:T(128)} %param.12) | copy-start | bytes 1540
  27.0 26.9 %copy-start.10 = (f32[128]{0:T(128)S(1)}, f32[128]{0:T(128)}, u32[]{:S(2)}) copy-start(f32[128]{0:T(128)} %param.13) | copy-start | bytes 1540
  27.0 26.9 %copy-start.11 = (bf16[3,3,3,128,128]{4,3,2,1,0:T(8,128)(2,1)S(1)}, bf16[3,3,3,128,128]{4,3,2,1,0:T(8,128)(2,1)}, u32[]{:S(2)}) copy-start(bf16[3,3,3,128,128]{4,3,2,1,0:T(8,128)(2,1)} %weight_ref.1) | copy-start | bytes 2654212
  27.1 26.9 %copy-start.12 = (bf16[2,16,32,128]{3,2,1,0:T(8,128)(2,1)S(1)}, bf16[2,16,32,128]{3,2,1,0:T(8,128)(2,1)}, u32[]{:S(2)}) copy-start(bf16[2,16,32,128]{3,2,1,0:T(8,128)(2,1)} %future_ref.1) | copy-start | bytes 786436
  27.1 7.8 %collective-permute-start.9 = (bf16[8,112,128]{2,1,0:T(8,128)(2,1)S(1)}, bf16[8,112,128]{2,1,0:T(8,128)(2,1)}, u32[]{:S(2)}, u32[]{:S(2)}) collective-permute-start(bf16[8,112,128]{2,1,0:T(8,128)(2,1)S(1)} %dynamic-slice_convert_fusion), channel_id=1, source_target_pairs={{0,2},{2,0},{1,3},{3,1},{4,6},{6,4},{5,7},{7,5},{8,10},{10,8},{9,1... | collective-permute-start | bytes 688136 | tf_op jit(solution)/shard_map/ppermute | solution.py:18
  36.0 5.8 %collective-permute-start.10 = (bf16[4,112,128]{2,1,0:T(8,128)(2,1)S(1)}, bf16[4,112,128]{2,1,0:T(8,128)(2,1)S(1)}, u32[]{:S(2)}, u32[]{:S(2)}) collective-permute-start(bf16[4,112,128]{2,1,0:T(8,128)(2,1)S(1)} %fusion), channel_id=1, source_target_pairs={{0,4},{4,0},{8,12},{12,8},{16,20},{20,16},{24,28},{28,24},{1,5},{5... | collective-permute-start | bytes 344072 | tf_op jit(solution)/shard_map/ppermute | solution.py:18
  41.8 4.9 %collective-permute-start.11 = (bf16[112,128]{1,0:T(8,128)(2,1)S(1)}, bf16[112,128]{1,0:T(8,128)(2,1)S(1)}, u32[]{:S(2)}, u32[]{:S(2)}) collective-permute-start(bf16[112,128]{1,0:T(8,128)(2,1)S(1)} %get-tuple-element.16), channel_id=1, source_target_pairs={{0,8},{4,12},{8,0},{12,4},{16,24},{20,28},{24,16},{28,20},{1,9},{5... | collective-permute-start | bytes 86024 | tf_op jit(solution)/shard_map/ppermute | solution.py:18
  44.1 5.2 %collective-permute-start.12 = (bf16[112,128]{1,0:T(8,128)(2,1)S(1)}, bf16[112,128]{1,0:T(8,128)(2,1)S(1)}, u32[]{:S(2)}, u32[]{:S(2)}) collective-permute-start(bf16[112,128]{1,0:T(8,128)(2,1)S(1)} %get-tuple-element.18), channel_id=1, source_target_pairs={{0,16},{4,20},{8,24},{12,28},{16,0},{20,4},{24,8},{28,12},{1,17},{... | collective-permute-start | bytes 86024 | tf_op jit(solution)/shard_map/ppermute | solution.py:18
  46.7 5.7 %collective-permute-start.13 = (bf16[112,128]{1,0:T(8,128)(2,1)S(1)}, bf16[112,128]{1,0:T(8,128)(2,1)S(1)}, u32[]{:S(2)}, u32[]{:S(2)}) collective-permute-start(bf16[112,128]{1,0:T(8,128)(2,1)S(1)} %get-tuple-element.17), channel_id=1, source_target_pairs={{0,24},{4,28},{8,16},{12,20},{16,8},{20,12},{24,0},{28,4},{1,25},{... | collective-permute-start | bytes 86024 | tf_op jit(solution)/shard_map/ppermute | solution.py:18
  52.4 15.1 %collective-permute-start.14 = (f32[112,128]{1,0:T(8,128)S(1)}, f32[112,128]{1,0:T(8,128)S(1)}, u32[]{:S(2)}, u32[]{:S(2)}) collective-permute-start(f32[112,128]{1,0:T(8,128)S(1)} %fusion.4), channel_id=1, source_target_pairs={{0,2},{2,0},{1,3},{3,1},{4,6},{6,4},{5,7},{7,5},{8,10},{10,8},{9,1... | collective-permute-start | bytes 172040 | tf_op jit(solution)/shard_map/ppermute | solution.py:18
  54.0 1.5 %copy-start.14 = (bf16[4,18,32,384]{3,2,1,0:T(8,128)(2,1)S(1)}, bf16[4,18,32,384]{3,2,1,0:T(8,128)(2,1)}, u32[]{:S(2)}) copy-start(bf16[4,18,32,384]{3,2,1,0:T(8,128)(2,1)} %copy-done.13) | copy-start | bytes 5308420
  55.5 1.2 %copy-start.16 = (bf16[2,18,32,384]{3,2,1,0:T(8,128)(2,1)S(1)}, bf16[2,18,32,384]{3,2,1,0:T(8,128)(2,1)}, u32[]{:S(2)}) copy-start(bf16[2,18,32,384]{3,2,1,0:T(8,128)(2,1)} %copy-done.15) | copy-start | bytes 2654212
  60.7 1.9 %collective-permute-start.5 = (f32[8,128]{1,0:T(8,128)S(1)}, f32[8,128]{1,0:T(8,128)S(1)}, u32[]{:S(2)}, u32[]{:S(2)}) collective-permute-start(f32[8,128]{1,0:T(8,128)S(1)} %get-tuple-element.12.refs_0_), channel_id=1, source_target_pairs={{0,1},{1,0},{2,3},{3,2},{4,5},{5,4},{6,7},{7,6},{8,9},{9,8},{10,11... | collective-permute-start | bytes 12296 | tf_op jit(solution)/shard_map/ppermute | solution.py:18
  60.8 3.7 %collective-permute-start.6 = (f32[8,128]{1,0:T(8,128)S(1)}, f32[8,128]{1,0:T(8,128)S(1)}, u32[]{:S(2)}, u32[]{:S(2)}) collective-permute-start(f32[8,128]{1,0:T(8,128)S(1)} %get-tuple-element.12.refs_0_), channel_id=1, source_target_pairs={{0,2},{2,0},{1,3},{3,1},{4,6},{6,4},{5,7},{7,5},{8,10},{10,8},{9,1... | collective-permute-start | bytes 12296 | tf_op jit(solution)/shard_map/ppermute | solution.py:18
  61.3 3.1 %collective-permute-start.7 = (f32[8,128]{1,0:T(8,128)S(1)}, f32[8,128]{1,0:T(8,128)S(1)}, u32[]{:S(2)}, u32[]{:S(2)}) collective-permute-start(f32[8,128]{1,0:T(8,128)S(1)} %get-tuple-element.12.refs_0_), channel_id=1, source_target_pairs={{0,3},{1,2},{2,1},{3,0},{4,7},{5,6},{6,5},{7,4},{8,11},{9,10},{10,... | collective-permute-start | bytes 12296 | tf_op jit(solution)/shard_map/ppermute | solution.py:471
  65.9 1.6 %collective-permute-start.15 = (f32[112,128]{1,0:T(8,128)S(1)}, f32[112,128]{1,0:T(8,128)S(1)}, u32[]{:S(2)}, u32[]{:S(2)}) collective-permute-start(f32[112,128]{1,0:T(8,128)S(1)} %fusion.4), channel_id=1, source_target_pairs={{0,1},{1,0},{2,3},{3,2},{4,5},{5,4},{6,7},{7,6},{8,9},{9,8},{10,11... | collective-permute-start | bytes 172040 | tf_op jit(solution)/shard_map/ppermute | solution.py:18
  66.0 3.6 %collective-permute-start.16 = (f32[112,128]{1,0:T(8,128)S(1)}, f32[112,128]{1,0:T(8,128)S(1)}, u32[]{:S(2)}, u32[]{:S(2)}) collective-permute-start(f32[112,128]{1,0:T(8,128)S(1)} %fusion.4), channel_id=1, source_target_pairs={{0,3},{1,2},{2,1},{3,0},{4,7},{5,6},{6,5},{7,4},{8,11},{9,10},{10,... | collective-permute-start | bytes 172040 | tf_op jit(solution)/shard_map/ppermute | solution.py:75

commit v4 on v3

--- a/solution.py
+++ b/solution.py
@@ -36,54 +36,114 @@
     return -(-rows // 16) * 8
 
 
-def joined(low, high, rows):
-    kept = low.shape[0]
-    return jnp.concatenate([low, high[2 * kept - rows :]], axis=0)
-
-
 def in_halves(blocks, rows):
-    return paired() and power_of_two(blocks) and rows % 16 == 0
+    return paired() and power_of_two(blocks) and blocks > 1 and rows % 16 == 0
+
+
+def split_rows_kernel(mine_ref, got_ref, near_ref, far_ref):
+    half, kept = mine_ref.shape[1], near_ref.shape[1]
+    side = lax.axis_index("height")
+
+    def place(low_ref, high_ref):
+        for block in range(mine_ref.shape[0]):
+            value = mine_ref[block] + got_ref[block]
+            low_ref[block] = value[:kept].astype(low_ref.dtype)
+            high_ref[block] = value[half - kept :].astype(high_ref.dtype)
+
+    @pl.when(side == 0)
+    def _():
+        place(near_ref, far_ref)
+
+    @pl.when(side == 1)
+    def _():
+        place(far_ref, near_ref)
+
+
+def split_blocks_kernel(distance, mine_ref, got_ref, near_ref, far_ref):
+    side = (lax.axis_index("tm") // distance) % 2
+    for pair in range(near_ref.shape[0]):
+        at = 2 * pair + side
+        near_ref[pair] = mine_ref[at] + got_ref[at].astype(jnp.float32)
+        at = 2 * pair + 1 - side
+        far_ref[pair] = (mine_ref[at] + got_ref[at].astype(jnp.float32)).astype(far_ref.dtype)
+
+
+def split_all_kernel(distance, mine_ref, got_ref, own_ref, *far_refs):
+    spot = lax.axis_index("tm") // distance
+    own_ref[...] = mine_ref[spot] + got_ref[spot].astype(jnp.float32)
+    for step, far_ref in enumerate(far_refs, 1):
+        at = lax.bitwise_xor(spot, step)
+        far_ref[...] = (mine_ref[at] + got_ref[at].astype(jnp.float32)).astype(far_ref.dtype)
+
+
+def add_kernel(own_ref, *refs):
+    total = own_ref[...]
+    for ref in refs[:-1]:
+        total = total + ref[...].astype(jnp.float32)
+    refs[-1][...] = total
+
+
+def assemble_kernel(own_ref, beside_ref, below_ref, across_ref, out_ref):
+    kept = own_ref.shape[0]
+    half = out_ref.shape[0] // 2
+    col_side = lax.axis_index("width")
+    mine = pl.multiple_of(col_side * half, 8)
+    other = pl.multiple_of((1 - col_side) * half, 8)
+
+    def place(lows, highs):
+        for at, low_ref, high_ref in zip((mine, other), lows, highs):
+            out_ref[pl.ds(at, kept), :] = low_ref[...]
+            out_ref[pl.ds(at + kept, half - kept), :] = high_ref[2 * kept - half :, :]
+
+    @pl.when(lax.axis_index("height") == 0)
+    def _():
+        place((own_ref, beside_ref), (below_ref, across_ref))
+
+    @pl.when(lax.axis_index("height") == 1)
+    def _():
+        place((below_ref, across_ref), (own_ref, beside_ref))
 
 
 def reduced_share(mine, theirs, rows):
-    blocks = mine.shape[0]
-    value = mine + exchanged(theirs, "width", 1)
-    half = value.shape[1]
+    blocks, half, channels = mine.shape
     kept = kept_rows(half)
-    row_side = lax.axis_index("height")
-    col_side = lax.axis_index("width")
-    near = lax.dynamic_slice_in_dim(value, row_side * (half - kept), kept, 1)
-    far = lax.dynamic_slice_in_dim(value, (1 - row_side) * (half - kept), kept, 1)
-    value = near + exchanged(far.astype(jnp.bfloat16), "height", 1).astype(jnp.float32)
-    place = lax.axis_index("tm")
+    f32, wire = jnp.float32, jnp.bfloat16
+
+    def pieces(count, dtype):
+        return jax.ShapeDtypeStruct((count, kept, channels), dtype)
+
+    def single(dtype):
+        return jax.ShapeDtypeStruct((kept, channels), dtype)
+
+    got = exchanged(theirs, "width", 1)
+    near, far = call(split_rows_kernel, (pieces(blocks, f32), pieces(blocks, wire)))(mine, got)
+    got = exchanged(far, "height", 1)
     distance = 1
     while blocks // distance > 4:
-        side = (place // distance) % 2
-        split = value.reshape(value.shape[0] // 2, 2, *value.shape[1:])
-        near = lax.dynamic_index_in_dim(split, side, 1, keepdims=False)
-        far = lax.dynamic_index_in_dim(split, 1 - side, 1, keepdims=False)
-        value = near + exchanged(far.astype(jnp.bfloat16), "tm", distance).astype(jnp.float32)
+        count = near.shape[0] // 2
+        near, far = call(
+            functools.partial(split_blocks_kernel, distance),
+            (pieces(count, f32), pieces(count, wire)),
+        )(near, got)
+        got = exchanged(far, "tm", distance)
         distance *= 2
     left = blocks // distance
-    spot = place // distance
-    own = lax.dynamic_index_in_dim(value, spot, 0, keepdims=False)
-    for step in range(1, left):
-        far = lax.dynamic_index_in_dim(value, spot ^ step, 0, keepdims=False)
-        own = own + exchanged(far.astype(jnp.bfloat16), "tm", step * distance).astype(jnp.float32)
-    beside = exchanged(own, "width", 1)
+    own, *fars = call(
+        functools.partial(split_all_kernel, distance),
+        (single(f32), *[single(wire)] * (left - 1)),
+    )(near, got)
+    arrived = []
+    for step, far in enumerate(fars, 1):
+        arrived.append(exchanged(far, "tm", step * distance))
+    own = call(add_kernel, single(f32))(own, *arrived)
     below = exchanged(own, "height", 1)
     across = lax.ppermute(own, ("height", "width"), [(i, 3 - i) for i in range(4)])
-    mine_half = joined(
-        jnp.where(row_side == 0, own, below), jnp.where(row_side == 0, below, own), half
-    )
-    other_half = joined(
-        jnp.where(row_side == 0, beside, across), jnp.where(row_side == 0, across, beside), half
-    )
-    return joined(
-        jnp.where(col_side == 0, mine_half, other_half),
-        jnp.where(col_side == 0, other_half, mine_half),
-        rows,
-    )
+    beside = exchanged(own, "width", 1)
+    return call(
+        assemble_kernel,
+        jax.ShapeDtypeStruct((rows, channels), f32),
+        out_specs=pl.BlockSpec((rows, channels), lambda: (0, 0)),
+    )(own, beside, below, across)
 
 
 def group_matrix(rows, cols, row_width, col_width):
@@ -107,15 +167,60 @@
     return exact_dot(value, group_matrix(groups, channels, 1, channels // groups))
 
 
-def act_kernel(features_ref, mean_ref, rstd_ref, gain_ref, bias_ref, act_ref):
+def cut_kernel(grad_ref, halo_ref, row_ref, col_ref, corner_ref):
+    frames, rows, cols, _ = grad_ref.shape
+    halo_ref[...] = grad_ref[: halo_ref.shape[0]]
+    row_at = (1 - lax.axis_index("height")) * (rows - 1)
+
+    def columns(at):
+        corners = []
+        for f in range(frames):
+            col_ref[f] = grad_ref[f].astype(jnp.float32)[:, at].astype(jnp.bfloat16)
+            corners.append(grad_ref[f, row_at].astype(jnp.float32)[at : at + 1])
+        corner_ref[...] = jnp.concatenate(corners, axis=0).astype(jnp.bfloat16)
+
+    for f in range(frames):
+        row_ref[f] = grad_ref[f, row_at]
+
+    @pl.when(lax.axis_index("width") == 0)
+    def _():
+        columns(cols - 1)
+
+    @pl.when(lax.axis_index("width") == 1)
+    def _():
+        columns(0)
+
+
+def pack_kernel(row_ref, col_ref, corner_ref, tail_ref):
+    cols, rows = row_ref.shape[1], col_ref.shape[1]
+    for f in range(tail_ref.shape[0]):
+        tail_ref[f, 0:cols] = row_ref[f]
+        tail_ref[f, cols : cols + rows] = col_ref[f]
+        tail_ref[f, cols + rows :] = corner_ref[f : f + 1]
+
+
+def act_kernel(features_hbm, mean_hbm, rstd_hbm, gain_hbm, bias_hbm, act_ref, params_ref, *scratch):
+    buffers, sems = scratch[:5], scratch[5]
+    sources = (features_hbm, mean_hbm, rstd_hbm, gain_hbm, bias_hbm)
+    copies = [
+        pltpu.make_async_copy(source, buffer, sems.at[i])
+        for i, (source, buffer) in enumerate(zip(sources, buffers))
+    ]
+    for copy in copies:
+        copy.start()
+    for copy in copies:
+        copy.wait()
+    features_ref, mean_ref, rstd_ref, gain_ref, bias_ref = buffers
     frames, rows, cols, channels = features_ref.shape
     cells = rows * cols
     mean = per_channel(mean_ref[...], channels)
     rstd = per_channel(rstd_ref[...], channels)
+    gain, bias = gain_ref[...], bias_ref[...]
+    params_ref[...] = jnp.concatenate([mean, rstd, gain, bias], axis=0)
     for t in range(frames):
         value = features_ref[t].astype(jnp.float32).reshape(cells, channels)
         centred = (value - mean[t : t + 1]) * rstd[t : t + 1]
-        pre_act = centred * gain_ref[...] + bias_ref[...]
+        pre_act = centred * gain + bias
         act = (pre_act * jax.nn.sigmoid(pre_act)).astype(jnp.bfloat16)
         act_ref[:, t * cells : (t + 1) * cells] = act.T
 
@@ -166,26 +271,34 @@
     lax.fori_loop(0, total, one, 0)
 
 
-def tap_sums(act_ref, window_of, frames, rows, cols, lag_h):
+def tap_sums(act_ref, scale, pairs, window_of, shape, lag_t, add):
+    rows, cols, channels = shape
     cells = rows * cols
-    acc = None
-    for t in range(frames):
-        window = window_of(t)[lag_h : lag_h + rows]
-        term = lax.dot_general(
-            act_ref[:, t * cells : (t + 1) * cells],
-            window.reshape(cells, window.shape[-1]),
-            (((1,), (0,)), ((), ())),
-            preferred_element_type=jnp.float32,
-        )
-        acc = term if acc is None else acc + term
-    return acc
-
-
-def near_kernel(scale, pair, act_ref, *refs):
+    for lag_h in range(3):
+        acc = None
+        for t, f in pairs:
+            window = window_of(f)[2 - lag_h : 2 - lag_h + rows]
+            term = lax.dot_general(
+                act_ref[:, t * cells : (t + 1) * cells],
+                window.reshape(cells, window.shape[-1]),
+                (((1,), (0,)), ((), ())),
+                preferred_element_type=jnp.float32,
+            )
+            acc = term if acc is None else acc + term
+        for lag_w in range(3):
+            e = 2 - lag_w
+            at = ((lag_t * 3 + lag_h) * 3 + lag_w) * channels
+            if acc is None:
+                value = jnp.zeros((channels, channels), jnp.float32)
+            else:
+                value = scale * acc[:, e * channels : (e + 1) * channels]
+            add(at, value)
+
+
+def near_kernel(scale, pair, extra, act_ref, *refs):
     sources, (window_ref, sum_ref, stage_ref) = refs[:-3], refs[-3:]
     frames, rows_ext, cols, wide = window_ref.shape
-    rows = rows_ext - 2
-    channels = wide // 3
+    shape = (rows_ext - 2, cols, wide // 3)
     if pair:
         grad_ref, row_ref, col_ref, corner_ref = sources
         fill_pair(
@@ -198,15 +311,17 @@
     else:
         stage_ref[...] = sources[0][...].astype(jnp.float32)
     widen(stage_ref, window_ref)
-    for lag_h in range(3):
-        acc = scale * tap_sums(act_ref, lambda t: window_ref.at[t], frames, rows, cols, 2 - lag_h)
-        for lag_w in range(3):
-            e = 2 - lag_w
-            at = (lag_h * 3 + lag_w) * channels
-            sum_ref[at : at + channels, :] = acc[:, e * channels : (e + 1) * channels]
-
-
-def far_kernel(rows_out, scale, pair, halves, act_ref, near_ref, near_sum_ref, *refs):
+
+    def put(at, value):
+        sum_ref[at : at + value.shape[0], :] = value
+
+    for lag_t in range(extra + 1):
+        ahead = extra - lag_t
+        pairs = [(t, t + ahead) for t in range(frames) if t + ahead < frames]
+        tap_sums(act_ref, scale, pairs, lambda f: window_ref.at[f], shape, lag_t, put)
+
+
+def far_kernel(rows_out, scale, pair, halves, frames, act_ref, near_sum_ref, *refs):
     count = 2 if pair else 1
     sources, window_ref, outs, (stage_ref, sum_ref) = (
         refs[:count],
@@ -215,7 +330,6 @@
         refs[-2:],
     )
     extra, rows_ext, cols, wide = window_ref.shape
-    frames = near_ref.shape[0]
     rows = rows_ext - 2
     channels = wide // 3
     if pair:
@@ -231,20 +345,18 @@
         stage_ref[...] = sources[0][...].astype(jnp.float32)
     widen(stage_ref, window_ref)
 
-    def window_of(f):
-        return near_ref.at[f] if f < frames else window_ref.at[f - frames]
+    def put(at, value):
+        rows_at = slice(at, at + value.shape[0])
+        sum_ref[rows_at, :] = near_sum_ref[rows_at, :] + value
 
     for lag_t in range(extra):
-        for lag_h in range(3):
-            acc = scale * tap_sums(
-                act_ref, lambda t: window_of(t + extra - lag_t), frames, rows, cols, 2 - lag_h
-            )
-            for lag_w in range(3):
-                e = 2 - lag_w
-                at = ((lag_t * 3 + lag_h) * 3 + lag_w) * channels
-                sum_ref[at : at + channels, :] = acc[:, e * channels : (e + 1) * channels]
+        ahead = extra - lag_t
+        pairs = [(t, t + ahead - frames) for t in range(frames) if t + ahead >= frames]
+        tap_sums(
+            act_ref, scale, pairs, lambda f: window_ref.at[f], (rows, cols, channels), lag_t, put
+        )
     done = extra * 9 * channels
-    sum_ref[done:, :] = near_sum_ref[...]
+    sum_ref[done:, :] = near_sum_ref[done:, :]
     if not halves:
         outs[0][...] = sum_ref[...]
         return
@@ -273,18 +385,17 @@
     weight_ref,
     future_ref,
     features_ref,
-    mean_ref,
-    rstd_ref,
-    gain_ref,
-    bias_ref,
+    params_ref,
     scaled_ref,
     sums_ref,
 ):
     frames, rows, cols, channels = features_ref.shape
     cells = rows * cols
     wide = 3 * channels
-    mean = per_channel(mean_ref[...], channels)
-    rstd = per_channel(rstd_ref[...], channels)
+    mean = params_ref[0:frames]
+    rstd = params_ref[frames : 2 * frames]
+    gain = params_ref[2 * frames : 2 * frames + 1]
+    bias = params_ref[2 * frames + 1 : 2 * frames + 2]
     is_last = lax.axis_index("tm") == lax.axis_size("tm") - 1
     for t in range(frames):
         acc = None
@@ -309,9 +420,9 @@
             acc = acc + jnp.where(is_last, tail, jnp.zeros_like(tail))
         value = features_ref[t].astype(jnp.float32).reshape(cells, channels)
         centred = (value - mean[t : t + 1]) * rstd[t : t + 1]
-        pre_act = centred * gain_ref[...] + bias_ref[...]
+        pre_act = centred * gain + bias
         sig = jax.nn.sigmoid(pre_act)
-        scaled = acc * sig * (1.0 + pre_act * (1.0 - sig)) * gain_ref[...]
+        scaled = acc * sig * (1.0 + pre_act * (1.0 - sig)) * gain
         scaled_ref[t] = scaled.reshape(rows, cols, channels)
         sums_ref[t : t + 1, :] = jnp.sum(scaled, axis=0, keepdims=True)
         sums_ref[frames + t : frames + t + 1, :] = jnp.sum(
@@ -319,15 +430,11 @@
         )
 
 
-def final_kernel(count, terms, *refs):
-    parts, (scaled_ref, features_ref, grad_ref, mean_ref, rstd_ref, out_ref) = (
-        refs[:terms],
-        refs[terms:],
-    )
+def final_kernel(groups, count, terms, *refs):
+    parts, (scaled_ref, features_ref, grad_ref, params_ref, out_ref) = refs[:terms], refs[terms:]
     frames, _, _, channels = features_ref.shape
-    groups = mean_ref.shape[1]
-    mean = per_channel(mean_ref[...], channels)
-    rstd = per_channel(rstd_ref[...], channels)
+    mean = params_ref[0:frames]
+    rstd = params_ref[frames : 2 * frames]
     total = parts[0][...]
     for part in parts[1:]:
         total = total + part[...]
@@ -342,14 +449,14 @@
         out_ref[t] = (grad_ref[t].astype(jnp.float32) + corrected).astype(jnp.bfloat16)
 
 
-def call(kernel, out_shape, scratch=(), flops=0, moved=0, out_specs=None):
+def call(kernel, out_shape, scratch=(), flops=0, moved=0, in_specs=None, out_specs=None):
     here = pl.BlockSpec(memory_space=pltpu.VMEM)
 
     def run(*args):
         return pl.pallas_call(
             kernel,
             out_shape=out_shape,
-            in_specs=[here] * len(args),
+            in_specs=in_specs or [here] * len(args),
             out_specs=out_specs or jax.tree.map(lambda _: here, out_shape),
             scratch_shapes=list(scratch),
             compiler_params=pltpu.CompilerParams(vmem_limit_bytes=VMEM_BYTES),
@@ -370,19 +477,20 @@
 
 
 def rims(grad_out, extra):
-    _, rows, cols, _ = grad_out.shape
-    row_side = lax.axis_index("height")
-    col_side = lax.axis_index("width")
-    row_at = (1 - row_side) * (rows - 1)
-    col_at = (1 - col_side) * (cols - 1)
-    halo = shifted(grad_out[:extra], "tm", -1)
-    row = lax.dynamic_slice_in_dim(grad_out, row_at, 1, 1)[:, 0]
-    col = lax.dynamic_slice_in_dim(grad_out, col_at, 1, 2)[:, :, 0]
-    corner = lax.dynamic_slice_in_dim(row, col_at, 1, 1)[:, 0]
+    frames, rows, cols, channels = grad_out.shape
+
+    def piece(*shape):
+        return jax.ShapeDtypeStruct((*shape, channels), grad_out.dtype)
+
+    halo, row, col, corner = call(
+        cut_kernel,
+        (piece(extra, rows, cols), piece(frames, cols), piece(frames, rows), piece(frames)),
+    )(grad_out)
+    halo = shifted(halo, "tm", -1)
     row = exchanged(row, "height", 1)
+    corner = lax.ppermute(corner, ("height", "width"), [(i, 3 - i) for i in range(4)])
     col = exchanged(col, "width", 1)
-    corner = lax.ppermute(corner, ("height", "width"), [(i, 3 - i) for i in range(4)])
-    packed = jnp.concatenate([row[:extra], col[:extra], corner[:extra, None]], axis=1)
+    packed = call(pack_kernel, piece(extra, cols + rows + 1))(row, col, corner)
     tail = shifted(packed, "tm", -1)
     return (grad_out, row, col, corner), (halo, tail)
 
@@ -411,12 +519,21 @@
         near_sources = (jnp.pad(padded, sides),)
         far_sources = (jnp.pad(shifted(padded[:extra], "tm", -1), sides),)
 
-    act = call(
+    inputs = (features, mean_saved, rstd_saved, gain, bias)
+    act, params = call(
         act_kernel,
-        jax.ShapeDtypeStruct((channels, frames * cells), jnp.bfloat16),
+        (
+            jax.ShapeDtypeStruct((channels, frames * cells), jnp.bfloat16),
+            jax.ShapeDtypeStruct((2 * frames + 2, channels), f32),
+        ),
+        scratch=(
+            *[pltpu.VMEM(value.shape, value.dtype) for value in inputs],
+            pltpu.SemaphoreType.DMA((len(inputs),)),
+        ),
+        in_specs=[pl.BlockSpec(memory_space=pltpu.HBM)] * len(inputs),
         flops=20 * frames * cells * channels,
         moved=4 * frames * cells * channels,
-    )(features, mean_saved, rstd_saved, gain, bias)
+    )(*inputs)
 
     def window_shape(count):
         return jax.ShapeDtypeStruct((count, rows + 2, cols, 3 * channels), jnp.bfloat16)
@@ -425,12 +542,12 @@
         return pltpu.VMEM((count, rows + 2, cols + 2 * LEAD, channels), f32)
 
     work = 2 * taps * channels * channels * frames * cells
-    part = taps // (extra + 1)
+    sum_shape = jax.ShapeDtypeStruct((taps * channels, channels), f32)
     near_window, near_sum = call(
-        functools.partial(near_kernel, grad_scale, pair),
-        (window_shape(frames), jax.ShapeDtypeStruct((part * channels, channels), f32)),
+        functools.partial(near_kernel, grad_scale, pair, extra),
+        (window_shape(frames), sum_shape),
         scratch=(stage_shape(frames),),
-        flops=work // 3,
+        flops=3 * work // 4,
         moved=4 * 1024 * 1024,
     )(act, *near_sources)
 
@@ -438,14 +555,14 @@
         half_shape = jax.ShapeDtypeStruct((blocks, rows_out // 2, channels), f32)
         sum_shapes = (half_shape, half_shape)
     else:
-        sum_shapes = (jax.ShapeDtypeStruct((taps * channels, channels), f32),)
+        sum_shapes = (sum_shape,)
     far_window, *sums = call(
-        functools.partial(far_kernel, rows_out, grad_scale, pair, halves),
+        functools.partial(far_kernel, rows_out, grad_scale, pair, halves, frames),
         (window_shape(extra), *sum_shapes),
         scratch=(stage_shape(extra), pltpu.VMEM((taps * channels, channels), f32)),
-        flops=2 * work // 3,
+        flops=work // 4,
         moved=4 * 1024 * 1024,
-    )(act, near_window, near_sum, *far_sources)
+    )(act, near_sum, *far_sources)
 
     if halves:
         weight_grad = reduced_share(*sums, rows_out)
@@ -461,7 +578,7 @@
         ),
         flops=work,
         moved=8 * 1024 * 1024,
-    )(near_window, far_window, weight, future_cot, features, mean_saved, rstd_saved, gain, bias)
+    )(near_window, far_window, weight, future_cot, features, params)
 
     if pair:
         parts = [local]
@@ -473,12 +590,12 @@
     else:
         parts = [lax.psum(local, ("height", "width"))]
     input_cot = call(
-        functools.partial(final_kernel, positions * (channels // groups), len(parts)),
+        functools.partial(final_kernel, groups, positions * (channels // groups), len(parts)),
         jax.ShapeDtypeStruct(features.shape, jnp.bfloat16),
         flops=20 * frames * cells * channels,
         moved=10 * frames * cells * channels,
         out_specs=pl.BlockSpec(features.shape, lambda: (0, 0, 0, 0)),
-    )(*parts, scaled, features, grad_out, mean_saved, rstd_saved)
+    )(*parts, scaled, features, grad_out, params)
     return (input_cot, weight_grad)
 
 

time: 70.9 us -> 58.9 us (0.83)
  local copies, waits for them, and re-layouts: 11.8 us -> 5.81 us
  waiting for transfers between devices: 24.6 us -> 21 us
  other arithmetic: 3.04 us -> 0 us
  Pallas kernels: 9.45 us -> 10.7 us
    ppermute x12, starting transfers between devices: 12.8 us -> 16.1 us  [exchanged(): return lax.ppermute(value, axis, [(i, i ^ distance) for i in range(count)])]
    unnamed x38 -> x22, local copies, waits for them, and re-layouts: 8.25 us -> 5.81 us
    add x4 -> x0, other arithmetic: 2.27 us -> none  [the longest x1 1.25 us: reduced_share(): value = mine + exchanged(theirs, 'width', 1)]
    ppermute x1, starting transfers between devices: 2.43 us -> 0.19 us  [rims(): lax.ppermute(corner, ('height', 'width'), [(i, 3 - i) for i in range(4)])]
    ppermute x1, waiting for transfers between devices: 2.14 us -> 0.01 us  [reduced_share(): lax.ppermute(own, ('height', 'width'), [(i, 3 - i) for i in range(4)])]
    ppermute x2, waiting for transfers between devices: 3.71 us -> 1.59 us  [shifted(): lax.ppermute(value, axis, [(source, source + steps) for source in range(i...]
    dynamic_slice x2 -> x0, local copies, waits for them, and re-layouts: 1.7 us -> none  [the longest x1 0.94 us: rims(): col = lax.dynamic_slice_in_dim(grad_out, col_at, 1, 2)[:, :, 0]]
    ppermute x1, starting transfers between devices: 1.45 us -> 0.07 us  [reduced_share(): lax.ppermute(own, ('height', 'width'), [(i, 3 - i) for i in range(4)])]
  transfers between devices with their start and end apart: 17 -> 17, of which waited for: 8 -> 8; matrix products, arithmetic and copies ran while one was open for 4% -> 0% of each run, Pallas kernels for 10% -> 15%
where the time goes in v4:
time: 58.9 us; the launch traced here: 58.5 us
  waiting for transfers between devices  21 us (36%)
  starting transfers between devices  20.1 us (34%)
  Pallas kernels  10.7 us (18%)
  local copies, waits for them, and re-layouts  5.81 us (10%)
  between operations  0.8 us (1%)
    ppermute x12, waiting for transfers between devices, exchanged(): return lax.ppermute(value, axis, [(i, i ^ distance) for i in range(count)])  18.3 us
    ppermute x12, starting transfers between devices, exchanged(): return lax.ppermute(value, axis, [(i, i ^ distance) for i in range(count)])  16.1 us
    pallas_call x12, Pallas kernels, run(): pl.pallas_call(kernel, out_shape=out_shape, in_specs=in_specs or [here] *...  10.7 us
    unnamed x22, local copies, waits for them, and re-layouts  5.81 us
    ppermute x2, starting transfers between devices, shifted(): lax.ppermute(value, axis, [(source, source + steps) for source in range(i...  2.58 us
    ppermute x2, waiting for transfers between devices, shifted(): lax.ppermute(value, axis, [(source, source + steps) for source in range(i...  1.59 us
    ppermute x1, starting transfers between devices, on_device(): lax.ppermute(local, ('height', 'width'), [(i, 3 - i) for i in range(4)])  1.22 us
  transfers between devices with their start and end apart: 17, of which 8 were waited for; matrix products, arithmetic and copies ran while one was open for 0% of the time, Pallas kernels for 15%

profile of v4, /device:TPU:0, one launch (start us, length us, event | category | flops | bytes accessed | tf_op | source)
XLA Modules:
  0.0 58.5 jit_solution(8591329399138403939)
XLA Ops:
  0.6 0.0 copy-start.2
  0.6 1.0 %copy-done.2 = bf16[4,16,32,128]{3,2,1,0:T(8,128)(2,1)S(1)} copy-done((bf16[4,16,32,128]{3,2,1,0:T(8,128)(2,1)S(1)}, bf16[4,16,32,128]{3,2,1,0:T(8,128)(2,1)}, u32[]{:S(2)}) %copy-start.2) | copy-done | bytes 524312
  1.7 1.3 %collective-permute-start.3 = (bf16[2,16,32,128]{3,2,1,0:T(8,128)(2,1)S(1)}, bf16[2,16,32,128]{3,2,1,0:T(8,128)(2,1)S(1)}, u32[]{:S(2)}, u32[]{:S(2)}) collective-permute-start(bf16[2,16,32,128]{3,2,1,0:T(8,128)(2,1)S(1)} %get-tuple-element.29), channel_id=1, source_target_pairs={{4,0},{8,4},{12,8},{16,12},{20,16},{24,20},{28,24},{5,1},{9,5},{13... | collective-permute-start | bytes 786440 | tf_op jit(solution)/shard_map/ppermute | solution.py:24
  3.0 3.1 %collective-permute-start = (bf16[4,32,128]{2,1,0:T(8,128)(2,1)S(1)}, bf16[4,32,128]{2,1,0:T(8,128)(2,1)S(1)}, u32[]{:S(2)}, u32[]{:S(2)}) collective-permute-start(bf16[4,32,128]{2,1,0:T(8,128)(2,1)S(1)} %get-tuple-element.24), channel_id=1, source_target_pairs={{0,2},{2,0},{1,3},{3,1},{4,6},{6,4},{5,7},{7,5},{8,10},{10,8},{9,1... | collective-permute-start | bytes 98312 | tf_op jit(solution)/shard_map/ppermute | solution.py:18
  6.1 0.0 collective-permute-start.1
  6.1 0.2 collective-permute-start.2
  6.3 0.0 copy-start
  6.3 1.0 %copy-done = bf16[4,16,32,128]{3,2,1,0:T(8,128)(2,1)S(1)} copy-done((bf16[4,16,32,128]{3,2,1,0:T(8,128)(2,1)S(1)}, bf16[4,16,32,128]{3,2,1,0:T(8,128)(2,1)}, u32[]{:S(2)}) %copy-start) | copy-done | bytes 524312
  7.3 0.0 copy-start.5
  7.3 0.7 %copy-done.5 = f32[4,32]{1,0:T(4,128)S(1)} copy-done((f32[4,32]{1,0:T(4,128)S(1)}, f32[4,32]{1,0:T(4,128)}, u32[]{:S(2)}) %copy-start.5) | copy-done | bytes 536
  8.0 0.0 copy-start.6
  8.0 0.7 %copy-done.6 = f32[4,32]{1,0:T(4,128)S(1)} copy-done((f32[4,32]{1,0:T(4,128)S(1)}, f32[4,32]{1,0:T(4,128)}, u32[]{:S(2)}) %copy-start.6) | copy-done | bytes 536
  8.7 0.0 copy-start.7
  8.7 0.7 %copy-done.7 = f32[128]{0:T(128)S(1)} copy-done((f32[128]{0:T(128)S(1)}, f32[128]{0:T(128)}, u32[]{:S(2)}) %copy-start.7) | copy-done | bytes 536
  9.3 0.0 copy-start.8
  9.3 0.7 %copy-done.8 = f32[128]{0:T(128)S(1)} copy-done((f32[128]{0:T(128)S(1)}, f32[128]{0:T(128)}, u32[]{:S(2)}) %copy-start.8) | copy-done | bytes 536
  10.0 0.6 %shard_map.95 = (bf16[128,2048]{1,0:T(8,128)(2,1)S(1)}, f32[10,128]{1,0:T(8,128)S(1)}) custom-call(bf16[4,16,32,128]{3,2,1,0:T(8,128)(2,1)S(1)} %copy-done, f32[4,32]{1,0:T(4,128)S(1)} %copy-done.5, f32[4,32]{1,0:T(4,128)S(1)} %copy-done.6, f32[1,128]{1,0:T(1,128)S(1)} %bitcast.2, f32[1,128]{1,0:T(1,128)S(1)} %bitcast.3), custom_call_target="tpu_custom_call" | custom-call | flops 5242880 | bytes 1048576 | tf_op jit(solution)/shard_map/pallas_call | solution.py:456
  10.6 0.0 collective-permute-done.2.refs_3_.corner_ref
  10.6 0.0 collective-permute-done.1.refs_2_.col_ref
  10.6 0.0 collective-permute-done.refs_1_.row_ref
  10.7 1.3 %collective-permute-start.4 = (bf16[2,49,128]{2,1,0:T(8,128)(2,1)S(1)}, bf16[2,49,128]{2,1,0:T(8,128)(2,1)S(1)}, u32[]{:S(2)}, u32[]{:S(2)}) collective-permute-start(bf16[2,49,128]{2,1,0:T(8,128)(2,1)S(1)} %shard_map.98), channel_id=1, source_target_pairs={{4,0},{8,4},{12,8},{16,12},{20,16},{24,20},{28,24},{5,1},{9,5},{13... | collective-permute-start | bytes 75272 | tf_op jit(solution)/shard_map/ppermute | solution.py:24
  12.0 0.0 copy-start.3
  12.0 1.0 %copy-done.3 = bf16[4,16,32,128]{3,2,1,0:T(8,128)(2,1)S(1)} copy-done((bf16[4,16,32,128]{3,2,1,0:T(8,128)(2,1)S(1)}, bf16[4,16,32,128]{3,2,1,0:T(8,128)(2,1)}, u32[]{:S(2)}) %copy-start.3) | copy-done | bytes 524312
  13.0 2.5 %shard_map.97 = (bf16[4,18,32,384]{3,2,1,0:T(8,128)(2,1)S(1)}, f32[3456,128]{1,0:T(8,128)S(1)}) custom-call(bf16[128,2048]{1,0:T(8,128)(2,1)S(1)} %get-tuple-element.23.act_ref, bf16[4,16,32,128]{3,2,1,0:T(8,128)(2,1)S(1)} %copy-done.3, bf16[4,32,128]{2,1,0:T(8,128)(2,1)S(1)} %collective-permute-done.refs_1_.row_ref, ...), custom_call_target="tpu_custom_call" | custom-call | flops 1358954496 | bytes 4194304 | tf_op jit(solution)/shard_map/pallas_call | solution.py:456
  15.5 1.6 %collective-permute-done.4.refs_1_ = bf16[2,49,128]{2,1,0:T(8,128)(2,1)S(1)} collective-permute-done((bf16[2,49,128]{2,1,0:T(8,128)(2,1)S(1)}, bf16[2,49,128]{2,1,0:T(8,128)(2,1)S(1)}, u32[]{:S(2)}, u32[]{:S(2)}) %collective-permute-start.4) | collective-permute-done | bytes 25120 | tf_op jit(solution)/shard_map/ppermute | solution.py:24
  17.0 0.0 collective-permute-done.3.refs_0_
  17.0 1.1 %shard_map.99 = (bf16[2,18,32,384]{3,2,1,0:T(8,128)(2,1)S(1)}, f32[8,216,128]{2,1,0:T(8,128)S(1)}, f32[8,216,128]{2,1,0:T(8,128)S(1)}) custom-call(bf16[128,2048]{1,0:T(8,128)(2,1)S(1)} %get-tuple-element.23.act_ref, f32[3456,128]{1,0:T(8,128)S(1)} %get-tuple-element.28.near_sum_ref, bf16[2,16,32,128]{3,2,1,0:T(8,128)(2,1)S(1)} %collective-permute-done.3.refs_0_, ...), custom_call_target="tpu_custom_call" | custom-call | flops 452984832 | bytes 4194304 | tf_op jit(solution)/shard_map/pallas_call | solution.py:456
  18.2 0.0 copy-start.1
  18.2 0.0 copy-start.9
  18.2 0.0 copy-start.10
  18.2 0.1 collective-permute-start.8
  18.3 2.4 %collective-permute-done.8.got_ref = f32[8,216,128]{2,1,0:T(8,128)S(1)} collective-permute-done((f32[8,216,128]{2,1,0:T(8,128)S(1)}, f32[8,216,128]{2,1,0:T(8,128)S(1)}, u32[]{:S(2)}, u32[]{:S(2)}) %collective-permute-start.8) | collective-permute-done | bytes 884768 | tf_op jit(solution)/shard_map/ppermute | solution.py:18
  20.7 0.1 shard_map.102
  20.8 2.0 %collective-permute-start.9 = (bf16[8,112,128]{2,1,0:T(8,128)(2,1)S(1)}, bf16[8,112,128]{2,1,0:T(8,128)(2,1)S(1)}, u32[]{:S(2)}, u32[]{:S(2)}) collective-permute-start(bf16[8,112,128]{2,1,0:T(8,128)(2,1)S(1)} %get-tuple-element.37), channel_id=1, source_target_pairs={{0,2},{2,0},{1,3},{3,1},{4,6},{6,4},{5,7},{7,5},{8,10},{10,8},{9,1... | collective-permute-start | bytes 688136 | tf_op jit(solution)/shard_map/ppermute | solution.py:18
  22.9 5.9 %collective-permute-done.9.got_ref = bf16[8,112,128]{2,1,0:T(8,128)(2,1)S(1)} collective-permute-done((bf16[8,112,128]{2,1,0:T(8,128)(2,1)S(1)}, bf16[8,112,128]{2,1,0:T(8,128)(2,1)S(1)}, u32[]{:S(2)}, u32[]{:S(2)}) %collective-permute-start.9) | collective-permute-done | bytes 229408 | tf_op jit(solution)/shard_map/ppermute | solution.py:18
  28.8 3.0 %collective-permute-start.10 = (bf16[4,112,128]{2,1,0:T(8,128)(2,1)S(1)}, bf16[4,112,128]{2,1,0:T(8,128)(2,1)S(1)}, u32[]{:S(2)}, u32[]{:S(2)}) collective-permute-start(bf16[4,112,128]{2,1,0:T(8,128)(2,1)S(1)} %get-tuple-element.39), channel_id=1, source_target_pairs={{0,4},{4,0},{8,12},{12,8},{16,20},{20,16},{24,28},{28,24},{1,5},{5... | collective-permute-start | bytes 344072 | tf_op jit(solution)/shard_map/ppermute | solution.py:18
  31.8 2.8 %collective-permute-done.10.got_ref = bf16[4,112,128]{2,1,0:T(8,128)(2,1)S(1)} collective-permute-done((bf16[4,112,128]{2,1,0:T(8,128)(2,1)S(1)}, bf16[4,112,128]{2,1,0:T(8,128)(2,1)S(1)}, u32[]{:S(2)}, u32[]{:S(2)}) %collective-permute-start.10) | collective-permute-done | bytes 114720 | tf_op jit(solution)/shard_map/ppermute | solution.py:18
  34.6 2.3 %collective-permute-start.11 = (bf16[112,128]{1,0:T(8,128)(2,1)S(1)}, bf16[112,128]{1,0:T(8,128)(2,1)S(1)}, u32[]{:S(2)}, u32[]{:S(2)}) collective-permute-start(bf16[112,128]{1,0:T(8,128)(2,1)S(1)} %get-tuple-element.41), channel_id=1, source_target_pairs={{0,8},{4,12},{8,0},{12,4},{16,24},{20,28},{24,16},{28,20},{1,9},{5... | collective-permute-start | bytes 86024 | tf_op jit(solution)/shard_map/ppermute | solution.py:18
  36.9 2.8 %collective-permute-start.12 = (bf16[112,128]{1,0:T(8,128)(2,1)S(1)}, bf16[112,128]{1,0:T(8,128)(2,1)S(1)}, u32[]{:S(2)}, u32[]{:S(2)}) collective-permute-start(bf16[112,128]{1,0:T(8,128)(2,1)S(1)} %get-tuple-element.42), channel_id=1, source_target_pairs={{0,16},{4,20},{8,24},{12,28},{16,0},{20,4},{24,8},{28,12},{1,17},{... | collective-permute-start | bytes 86024 | tf_op jit(solution)/shard_map/ppermute | solution.py:18
  39.7 0.0 collective-permute-start.13
  39.7 0.0 collective-permute-done.11.refs_0_
  39.7 2.6 %collective-permute-done.12.refs_1_ = bf16[112,128]{1,0:T(8,128)(2,1)S(1)} collective-permute-done((bf16[112,128]{1,0:T(8,128)(2,1)S(1)}, bf16[112,128]{1,0:T(8,128)(2,1)S(1)}, u32[]{:S(2)}, u32[]{:S(2)}) %collective-permute-start.12) | collective-permute-done | bytes 28704 | tf_op jit(solution)/shard_map/ppermute | solution.py:18
  42.3 3.1 %collective-permute-done.13.refs_2_ = bf16[112,128]{1,0:T(8,128)(2,1)S(1)} collective-permute-done((bf16[112,128]{1,0:T(8,128)(2,1)S(1)}, bf16[112,128]{1,0:T(8,128)(2,1)S(1)}, u32[]{:S(2)}, u32[]{:S(2)}) %collective-permute-start.13) | collective-permute-done | bytes 28704 | tf_op jit(solution)/shard_map/ppermute | solution.py:18
  45.4 0.1 collective-permute-start.16
  45.5 1.6 %collective-permute-start.15 = (f32[112,128]{1,0:T(8,128)S(1)}, f32[112,128]{1,0:T(8,128)S(1)}, u32[]{:S(2)}, u32[]{:S(2)}) collective-permute-start(f32[112,128]{1,0:T(8,128)S(1)} %shard_map.105.own_ref), channel_id=1, source_target_pairs={{0,2},{2,0},{1,3},{3,1},{4,6},{6,4},{5,7},{7,5},{8,10},{10,8},{9,1... | collective-permute-start | bytes 172040 | tf_op jit(solution)/shard_map/ppermute | solution.py:18
  47.1 0.3 collective-permute-start.14
  47.3 0.0 copy-done.1
  47.3 0.0 copy-done.9
  47.3 0.0 copy-done.10
  47.3 0.0 copy-start.4
  47.4 4.2 %shard_map.100 = (f32[4,16,32,128]{3,2,1,0:T(8,128)S(1)}, f32[8,128]{1,0:T(8,128)S(1)}) custom-call(bf16[4,18,32,384]{3,2,1,0:T(8,128)(2,1)S(1)} %get-tuple-element.27.near_ref, bf16[2,18,32,384]{3,2,1,0:T(8,128)(2,1)S(1)} %get-tuple-element.30.far_ref, bf16[3,3,3,128,128]{4,3,2,1,0:T(8,128)(2,1)S(1)} %copy-done.9, bf16[2,16,32,128]{3,2,1,0:T(8,128)(2,1)S(1)} %copy-done.10, ...), custom_call_target="tpu_custom_call" | custom-call | flops 1811939328 | bytes 8388608 | tf_op jit(solution)/shard_map/pallas_call | solution.py:456
  51.6 1.2 %collective-permute-start.7 = (f32[8,128]{1,0:T(8,128)S(1)}, f32[8,128]{1,0:T(8,128)S(1)}, u32[]{:S(2)}, u32[]{:S(2)}) collective-permute-start(f32[8,128]{1,0:T(8,128)S(1)} %get-tuple-element.32.refs_0_), channel_id=1, source_target_pairs={{0,3},{1,2},{2,1},{3,0},{4,7},{5,6},{6,5},{7,4},{8,11},{9,10},{10,... | collective-permute-start | bytes 12296 | tf_op jit(solution)/shard_map/ppermute | solution.py:588
  52.8 0.7 %collective-permute-start.6 = (f32[8,128]{1,0:T(8,128)S(1)}, f32[8,128]{1,0:T(8,128)S(1)}, u32[]{:S(2)}, u32[]{:S(2)}) collective-permute-start(f32[8,128]{1,0:T(8,128)S(1)} %get-tuple-element.32.refs_0_), channel_id=1, source_target_pairs={{0,2},{2,0},{1,3},{3,1},{4,6},{6,4},{5,7},{7,5},{8,10},{10,8},{9,1... | collective-permute-start | bytes 12296 | tf_op jit(solution)/shard_map/ppermute | solution.py:18
  53.5 1.1 %collective-permute-done.7.refs_3_ = f32[8,128]{1,0:T(8,128)S(1)} collective-permute-done((f32[8,128]{1,0:T(8,128)S(1)}, f32[8,128]{1,0:T(8,128)S(1)}, u32[]{:S(2)}, u32[]{:S(2)}) %collective-permute-start.7) | collective-permute-done | bytes 4128 | tf_op jit(solution)/shard_map/ppermute | solution.py:588
  54.7 0.3 collective-permute-start.5
  54.9 1.5 %collective-permute-done.6.refs_2_ = f32[8,128]{1,0:T(8,128)S(1)} collective-permute-done((f32[8,128]{1,0:T(8,128)S(1)}, f32[8,128]{1,0:T(8,128)S(1)}, u32[]{:S(2)}, u32[]{:S(2)}) %collective-permute-start.6) | collective-permute-done | bytes 4128 | tf_op jit(solution)/shard_map/ppermute | solution.py:18
  56.4 0.0 collective-permute-done.5.refs_1_
  56.4 0.0 copy-done.4
  56.4 1.4 %shard_map.101 = bf16[4,16,32,128]{3,2,1,0:T(8,128)(2,1)} custom-call(f32[8,128]{1,0:T(8,128)S(1)} %get-tuple-element.32.refs_0_, f32[8,128]{1,0:T(8,128)S(1)} %collective-permute-done.5.refs_1_, f32[8,128]{1,0:T(8,128)S(1)} %collective-permute-done.6.refs_2_, f32[8,128]{1,0:T(8,128)S(1)} %collective-permute-done.7.refs_3_, ...), custom_call_target="tpu_custom_call" | custom-call | flops 5242880 | bytes 2621440 | tf_op jit(solution)/shard_map/pallas_call | solution.py:456
  57.8 0.0 collective-permute-done.16.across_ref
  57.8 0.0 collective-permute-done.15.below_ref
  57.8 0.0 collective-permute-done.14.beside_ref
  57.8 0.7 %shard_map.106 = f32[432,128]{1,0:T(8,128)} custom-call(f32[112,128]{1,0:T(8,128)S(1)} %shard_map.105.own_ref, f32[112,128]{1,0:T(8,128)S(1)} %collective-permute-done.14.beside_ref, f32[112,128]{1,0:T(8,128)S(1)} %collective-permute-done.15.below_ref, f32[112,128]{1,0:T(8,128)S(1)} %collective-permute-done.16.across_ref), custom_call_target="tpu_custom_call" | custom-call | tf_op jit(solution)/shard_map/pallas_call | solution.py:456
  (5 shorter events, 0.1 us)
Async XLA Ops:
  0.6 1.0 %copy-start.2 = (bf16[4,16,32,128]{3,2,1,0:T(8,128)(2,1)S(1)}, bf16[4,16,32,128]{3,2,1,0:T(8,128)(2,1)}, u32[]{:S(2)}) copy-start(bf16[4,16,32,128]{3,2,1,0:T(8,128)(2,1)} %refs_6_.1) | copy-start | bytes 1572868
  1.7 15.3 %collective-permute-start.3 = (bf16[2,16,32,128]{3,2,1,0:T(8,128)(2,1)S(1)}, bf16[2,16,32,128]{3,2,1,0:T(8,128)(2,1)S(1)}, u32[]{:S(2)}, u32[]{:S(2)}) collective-permute-start(bf16[2,16,32,128]{3,2,1,0:T(8,128)(2,1)S(1)} %get-tuple-element.29), channel_id=1, source_target_pairs={{4,0},{8,4},{12,8},{16,12},{20,16},{24,20},{28,24},{5,1},{9,5},{13... | collective-permute-start | bytes 786440 | tf_op jit(solution)/shard_map/ppermute | solution.py:24
  3.0 7.6 %collective-permute-start = (bf16[4,32,128]{2,1,0:T(8,128)(2,1)S(1)}, bf16[4,32,128]{2,1,0:T(8,128)(2,1)S(1)}, u32[]{:S(2)}, u32[]{:S(2)}) collective-permute-start(bf16[4,32,128]{2,1,0:T(8,128)(2,1)S(1)} %get-tuple-element.24), channel_id=1, source_target_pairs={{0,2},{2,0},{1,3},{3,1},{4,6},{6,4},{5,7},{7,5},{8,10},{10,8},{9,1... | collective-permute-start | bytes 98312 | tf_op jit(solution)/shard_map/ppermute | solution.py:18
  6.1 4.5 %collective-permute-start.1 = (bf16[4,16,128]{2,1,0:T(8,128)(2,1)S(1)}, bf16[4,16,128]{2,1,0:T(8,128)(2,1)S(1)}, u32[]{:S(2)}, u32[]{:S(2)}) collective-permute-start(bf16[4,16,128]{2,1,0:T(8,128)(2,1)S(1)} %get-tuple-element.25), channel_id=1, source_target_pairs={{0,1},{1,0},{2,3},{3,2},{4,5},{5,4},{6,7},{7,6},{8,9},{9,8},{10,11... | collective-permute-start | bytes 49160 | tf_op jit(solution)/shard_map/ppermute | solution.py:18
  6.1 4.5 %collective-permute-start.2 = (bf16[4,128]{1,0:T(4,128)(2,1)S(1)}, bf16[4,128]{1,0:T(4,128)(2,1)S(1)}, u32[]{:S(2)}, u32[]{:S(2)}) collective-permute-start(bf16[4,128]{1,0:T(4,128)(2,1)S(1)} %get-tuple-element.26), channel_id=1, source_target_pairs={{0,3},{1,2},{2,1},{3,0},{4,7},{5,6},{6,5},{7,4},{8,11},{9,10},{10,... | collective-permute-start | bytes 3080 | tf_op jit(solution)/shard_map/ppermute | solution.py:491
  6.3 1.0 %copy-start = (bf16[4,16,32,128]{3,2,1,0:T(8,128)(2,1)S(1)}, bf16[4,16,32,128]{3,2,1,0:T(8,128)(2,1)}, u32[]{:S(2)}) copy-start(bf16[4,16,32,128]{3,2,1,0:T(8,128)(2,1)} %refs_5_.1) | copy-start | bytes 1572868
  7.3 0.7 %copy-start.5 = (f32[4,32]{1,0:T(4,128)S(1)}, f32[4,32]{1,0:T(4,128)}, u32[]{:S(2)}) copy-start(f32[4,32]{1,0:T(4,128)} %mean_hbm.1) | copy-start | bytes 1540
  8.0 0.7 %copy-start.6 = (f32[4,32]{1,0:T(4,128)S(1)}, f32[4,32]{1,0:T(4,128)}, u32[]{:S(2)}) copy-start(f32[4,32]{1,0:T(4,128)} %rstd_hbm.1) | copy-start | bytes 1540
  8.7 0.7 %copy-start.7 = (f32[128]{0:T(128)S(1)}, f32[128]{0:T(128)}, u32[]{:S(2)}) copy-start(f32[128]{0:T(128)} %param.12) | copy-start | bytes 1540
  9.3 0.7 %copy-start.8 = (f32[128]{0:T(128)S(1)}, f32[128]{0:T(128)}, u32[]{:S(2)}) copy-start(f32[128]{0:T(128)} %param.13) | copy-start | bytes 1540
  10.7 6.4 %collective-permute-start.4 = (bf16[2,49,128]{2,1,0:T(8,128)(2,1)S(1)}, bf16[2,49,128]{2,1,0:T(8,128)(2,1)S(1)}, u32[]{:S(2)}, u32[]{:S(2)}) collective-permute-start(bf16[2,49,128]{2,1,0:T(8,128)(2,1)S(1)} %shard_map.98), channel_id=1, source_target_pairs={{4,0},{8,4},{12,8},{16,12},{20,16},{24,20},{28,24},{5,1},{9,5},{13... | collective-permute-start | bytes 75272 | tf_op jit(solution)/shard_map/ppermute | solution.py:24
  12.0 1.0 %copy-start.3 = (bf16[4,16,32,128]{3,2,1,0:T(8,128)(2,1)S(1)}, bf16[4,16,32,128]{3,2,1,0:T(8,128)(2,1)}, u32[]{:S(2)}) copy-start(bf16[4,16,32,128]{3,2,1,0:T(8,128)(2,1)} %refs_6_.1) | copy-start | bytes 1572868
  18.2 29.2 %copy-start.1 = (bf16[4,16,32,128]{3,2,1,0:T(8,128)(2,1)S(1)}, bf16[4,16,32,128]{3,2,1,0:T(8,128)(2,1)}, u32[]{:S(2)}) copy-start(bf16[4,16,32,128]{3,2,1,0:T(8,128)(2,1)} %refs_5_.1) | copy-start | bytes 1572868
  18.2 29.2 %copy-start.9 = (bf16[3,3,3,128,128]{4,3,2,1,0:T(8,128)(2,1)S(1)}, bf16[3,3,3,128,128]{4,3,2,1,0:T(8,128)(2,1)}, u32[]{:S(2)}) copy-start(bf16[3,3,3,128,128]{4,3,2,1,0:T(8,128)(2,1)} %weight_ref.1) | copy-start | bytes 2654212
  18.2 29.2 %copy-start.10 = (bf16[2,16,32,128]{3,2,1,0:T(8,128)(2,1)S(1)}, bf16[2,16,32,128]{3,2,1,0:T(8,128)(2,1)}, u32[]{:S(2)}) copy-start(bf16[2,16,32,128]{3,2,1,0:T(8,128)(2,1)} %future_ref.1) | copy-start | bytes 786436
  18.2 2.5 %collective-permute-start.8 = (f32[8,216,128]{2,1,0:T(8,128)S(1)}, f32[8,216,128]{2,1,0:T(8,128)S(1)}, u32[]{:S(2)}, u32[]{:S(2)}) collective-permute-start(f32[8,216,128]{2,1,0:T(8,128)S(1)} %get-tuple-element.35), channel_id=1, source_target_pairs={{0,1},{1,0},{2,3},{3,2},{4,5},{5,4},{6,7},{7,6},{8,9},{9,8},{10,11... | collective-permute-start | bytes 2654216 | tf_op jit(solution)/shard_map/ppermute | solution.py:18
  20.8 7.9 %collective-permute-start.9 = (bf16[8,112,128]{2,1,0:T(8,128)(2,1)S(1)}, bf16[8,112,128]{2,1,0:T(8,128)(2,1)S(1)}, u32[]{:S(2)}, u32[]{:S(2)}) collective-permute-start(bf16[8,112,128]{2,1,0:T(8,128)(2,1)S(1)} %get-tuple-element.37), channel_id=1, source_target_pairs={{0,2},{2,0},{1,3},{3,1},{4,6},{6,4},{5,7},{7,5},{8,10},{10,8},{9,1... | collective-permute-start | bytes 688136 | tf_op jit(solution)/shard_map/ppermute | solution.py:18
  28.8 5.8 %collective-permute-start.10 = (bf16[4,112,128]{2,1,0:T(8,128)(2,1)S(1)}, bf16[4,112,128]{2,1,0:T(8,128)(2,1)S(1)}, u32[]{:S(2)}, u32[]{:S(2)}) collective-permute-start(bf16[4,112,128]{2,1,0:T(8,128)(2,1)S(1)} %get-tuple-element.39), channel_id=1, source_target_pairs={{0,4},{4,0},{8,12},{12,8},{16,20},{20,16},{24,28},{28,24},{1,5},{5... | collective-permute-start | bytes 344072 | tf_op jit(solution)/shard_map/ppermute | solution.py:18
  34.6 5.1 %collective-permute-start.11 = (bf16[112,128]{1,0:T(8,128)(2,1)S(1)}, bf16[112,128]{1,0:T(8,128)(2,1)S(1)}, u32[]{:S(2)}, u32[]{:S(2)}) collective-permute-start(bf16[112,128]{1,0:T(8,128)(2,1)S(1)} %get-tuple-element.41), channel_id=1, source_target_pairs={{0,8},{4,12},{8,0},{12,4},{16,24},{20,28},{24,16},{28,20},{1,9},{5... | collective-permute-start | bytes 86024 | tf_op jit(solution)/shard_map/ppermute | solution.py:18
  36.9 5.4 %collective-permute-start.12 = (bf16[112,128]{1,0:T(8,128)(2,1)S(1)}, bf16[112,128]{1,0:T(8,128)(2,1)S(1)}, u32[]{:S(2)}, u32[]{:S(2)}) collective-permute-start(bf16[112,128]{1,0:T(8,128)(2,1)S(1)} %get-tuple-element.42), channel_id=1, source_target_pairs={{0,16},{4,20},{8,24},{12,28},{16,0},{20,4},{24,8},{28,12},{1,17},{... | collective-permute-start | bytes 86024 | tf_op jit(solution)/shard_map/ppermute | solution.py:18
  39.7 5.7 %collective-permute-start.13 = (bf16[112,128]{1,0:T(8,128)(2,1)S(1)}, bf16[112,128]{1,0:T(8,128)(2,1)S(1)}, u32[]{:S(2)}, u32[]{:S(2)}) collective-permute-start(bf16[112,128]{1,0:T(8,128)(2,1)S(1)} %get-tuple-element.43), channel_id=1, source_target_pairs={{0,24},{4,28},{8,16},{12,20},{16,8},{20,12},{24,0},{28,4},{1,25},{... | collective-permute-start | bytes 86024 | tf_op jit(solution)/shard_map/ppermute | solution.py:18
  45.4 12.4 %collective-permute-start.16 = (f32[112,128]{1,0:T(8,128)S(1)}, f32[112,128]{1,0:T(8,128)S(1)}, u32[]{:S(2)}, u32[]{:S(2)}) collective-permute-start(f32[112,128]{1,0:T(8,128)S(1)} %shard_map.105.own_ref), channel_id=1, source_target_pairs={{0,3},{1,2},{2,1},{3,0},{4,7},{5,6},{6,5},{7,4},{8,11},{9,10},{10,... | collective-permute-start | bytes 172040 | tf_op jit(solution)/shard_map/ppermute | solution.py:140
  45.5 12.3 %collective-permute-start.15 = (f32[112,128]{1,0:T(8,128)S(1)}, f32[112,128]{1,0:T(8,128)S(1)}, u32[]{:S(2)}, u32[]{:S(2)}) collective-permute-start(f32[112,128]{1,0:T(8,128)S(1)} %shard_map.105.own_ref), channel_id=1, source_target_pairs={{0,2},{2,0},{1,3},{3,1},{4,6},{6,4},{5,7},{7,5},{8,10},{10,8},{9,1... | collective-permute-start | bytes 172040 | tf_op jit(solution)/shard_map/ppermute | solution.py:18
  47.1 10.7 %collective-permute-start.14 = (f32[112,128]{1,0:T(8,128)S(1)}, f32[112,128]{1,0:T(8,128)S(1)}, u32[]{:S(2)}, u32[]{:S(2)}) collective-permute-start(f32[112,128]{1,0:T(8,128)S(1)} %shard_map.105.own_ref), channel_id=1, source_target_pairs={{0,1},{1,0},{2,3},{3,2},{4,5},{5,4},{6,7},{7,6},{8,9},{9,8},{10,11... | collective-permute-start | bytes 172040 | tf_op jit(solution)/shard_map/ppermute | solution.py:18
  47.3 9.0 %copy-start.4 = (bf16[4,16,32,128]{3,2,1,0:T(8,128)(2,1)S(1)}, bf16[4,16,32,128]{3,2,1,0:T(8,128)(2,1)}, u32[]{:S(2)}) copy-start(bf16[4,16,32,128]{3,2,1,0:T(8,128)(2,1)} %refs_6_.1) | copy-start | bytes 1572868
  51.6 3.1 %collective-permute-start.7 = (f32[8,128]{1,0:T(8,128)S(1)}, f32[8,128]{1,0:T(8,128)S(1)}, u32[]{:S(2)}, u32[]{:S(2)}) collective-permute-start(f32[8,128]{1,0:T(8,128)S(1)} %get-tuple-element.32.refs_0_), channel_id=1, source_target_pairs={{0,3},{1,2},{2,1},{3,0},{4,7},{5,6},{6,5},{7,4},{8,11},{9,10},{10,... | collective-permute-start | bytes 12296 | tf_op jit(solution)/shard_map/ppermute | solution.py:588
  52.8 3.6 %collective-permute-start.6 = (f32[8,128]{1,0:T(8,128)S(1)}, f32[8,128]{1,0:T(8,128)S(1)}, u32[]{:S(2)}, u32[]{:S(2)}) collective-permute-start(f32[8,128]{1,0:T(8,128)S(1)} %get-tuple-element.32.refs_0_), channel_id=1, source_target_pairs={{0,2},{2,0},{1,3},{3,1},{4,6},{6,4},{5,7},{7,5},{8,10},{10,8},{9,1... | collective-permute-start | bytes 12296 | tf_op jit(solution)/shard_map/ppermute | solution.py:18
  54.7 1.7 %collective-permute-start.5 = (f32[8,128]{1,0:T(8,128)S(1)}, f32[8,128]{1,0:T(8,128)S(1)}, u32[]{:S(2)}, u32[]{:S(2)}) collective-permute-start(f32[8,128]{1,0:T(8,128)S(1)} %get-tuple-element.32.refs_0_), channel_id=1, source_target_pairs={{0,1},{1,0},{2,3},{3,2},{4,5},{5,4},{6,7},{7,6},{8,9},{9,8},{10,11... | collective-permute-start | bytes 12296 | tf_op jit(solution)/shard_map/ppermute | solution.py:18

commit v5 on v4

--- a/solution.py
+++ b/solution.py
@@ -37,71 +37,94 @@
 
 
 def in_halves(blocks, rows):
-    return paired() and power_of_two(blocks) and blocks > 1 and rows % 16 == 0
-
-
-def split_rows_kernel(mine_ref, got_ref, near_ref, far_ref):
-    half, kept = mine_ref.shape[1], near_ref.shape[1]
-    side = lax.axis_index("height")
+    return paired() and power_of_two(blocks) and blocks >= 8 and rows % 16 == 0
+
+
+def store_rows(value, near_ref, far_ref, at, side):
+    rows, kept = value.shape[0], near_ref.shape[1]
+
+    @pl.when(side == 0)
+    def _():
+        near_ref[at] = value[:kept]
+        far_ref[at] = value[rows - kept :].astype(far_ref.dtype)
+
+    @pl.when(side == 1)
+    def _():
+        near_ref[at] = value[rows - kept :]
+        far_ref[at] = value[:kept].astype(far_ref.dtype)
+
+
+def first_kernel(mine_ref, got_ref, rows_near_ref, rows_far_ref, pair_near_ref, pair_far_ref):
+    low = rows_near_ref.shape[0]
+    row_side = lax.axis_index("height")
+    side = lax.axis_index("tm") % 2
+    for block in range(low):
+        value = mine_ref[block] + got_ref[block]
+        store_rows(value, rows_near_ref, rows_far_ref, block, row_side)
+    for pair in range(pair_near_ref.shape[0]):
+        at = low + 2 * pair + side
+        pair_near_ref[pair] = mine_ref[at] + got_ref[at]
+        at = low + 2 * pair + 1 - side
+        pair_far_ref[pair] = (mine_ref[at] + got_ref[at]).astype(pair_far_ref.dtype)
+
+
+def second_kernel(
+    rows_ref, rows_got_ref, pair_ref, pair_got_ref, low_near, low_far, high_near, high_far
+):
+    row_side = lax.axis_index("height")
+    side = lax.axis_index("tm") % 2
+    for pair in range(low_near.shape[0]):
+        at = 2 * pair + side
+        low_near[pair] = rows_ref[at] + rows_got_ref[at].astype(jnp.float32)
+        at = 2 * pair + 1 - side
+        low_far[pair] = (rows_ref[at] + rows_got_ref[at].astype(jnp.float32)).astype(low_far.dtype)
+        value = pair_ref[pair] + pair_got_ref[pair].astype(jnp.float32)
+        store_rows(value, high_near, high_far, pair, row_side)
+
+
+def split_kernel(distance, low, *refs):
+    *parts, near_ref, far_ref = refs
+    side = (lax.axis_index("tm") // distance) % 2
+
+    def block(pair, which):
+        at = 2 * pair + which
+        if 2 * pair < low:
+            value_ref, got_ref = parts[:2]
+        else:
+            value_ref, got_ref = parts[-2:]
+            at = at - low
+        return value_ref[at] + got_ref[at].astype(jnp.float32)
+
+    for pair in range(near_ref.shape[0]):
+        near_ref[pair] = block(pair, side)
+        far_ref[pair] = block(pair, 1 - side).astype(far_ref.dtype)
+
+
+def add_kernel(near_ref, got_ref, out_ref):
+    out_ref[...] = near_ref[0] + got_ref[0].astype(jnp.float32)
+
+
+def half_kernel(own_ref, below_ref, out_ref):
+    kept, half = own_ref.shape[0], out_ref.shape[0]
 
     def place(low_ref, high_ref):
-        for block in range(mine_ref.shape[0]):
-            value = mine_ref[block] + got_ref[block]
-            low_ref[block] = value[:kept].astype(low_ref.dtype)
-            high_ref[block] = value[half - kept :].astype(high_ref.dtype)
-
-    @pl.when(side == 0)
-    def _():
-        place(near_ref, far_ref)
-
-    @pl.when(side == 1)
-    def _():
-        place(far_ref, near_ref)
-
-
-def split_blocks_kernel(distance, mine_ref, got_ref, near_ref, far_ref):
-    side = (lax.axis_index("tm") // distance) % 2
-    for pair in range(near_ref.shape[0]):
-        at = 2 * pair + side
-        near_ref[pair] = mine_ref[at] + got_ref[at].astype(jnp.float32)
-        at = 2 * pair + 1 - side
-        far_ref[pair] = (mine_ref[at] + got_ref[at].astype(jnp.float32)).astype(far_ref.dtype)
-
-
-def split_all_kernel(distance, mine_ref, got_ref, own_ref, *far_refs):
-    spot = lax.axis_index("tm") // distance
-    own_ref[...] = mine_ref[spot] + got_ref[spot].astype(jnp.float32)
-    for step, far_ref in enumerate(far_refs, 1):
-        at = lax.bitwise_xor(spot, step)
-        far_ref[...] = (mine_ref[at] + got_ref[at].astype(jnp.float32)).astype(far_ref.dtype)
-
-
-def add_kernel(own_ref, *refs):
-    total = own_ref[...]
-    for ref in refs[:-1]:
-        total = total + ref[...].astype(jnp.float32)
-    refs[-1][...] = total
-
-
-def assemble_kernel(own_ref, beside_ref, below_ref, across_ref, out_ref):
-    kept = own_ref.shape[0]
-    half = out_ref.shape[0] // 2
-    col_side = lax.axis_index("width")
-    mine = pl.multiple_of(col_side * half, 8)
-    other = pl.multiple_of((1 - col_side) * half, 8)
-
-    def place(lows, highs):
-        for at, low_ref, high_ref in zip((mine, other), lows, highs):
-            out_ref[pl.ds(at, kept), :] = low_ref[...]
-            out_ref[pl.ds(at + kept, half - kept), :] = high_ref[2 * kept - half :, :]
+        out_ref[:kept, :] = low_ref[...]
+        out_ref[kept:, :] = high_ref[2 * kept - half :, :]
 
     @pl.when(lax.axis_index("height") == 0)
     def _():
-        place((own_ref, beside_ref), (below_ref, across_ref))
+        place(own_ref, below_ref)
 
     @pl.when(lax.axis_index("height") == 1)
     def _():
-        place((below_ref, across_ref), (own_ref, beside_ref))
+        place(below_ref, own_ref)
+
+
+def whole_kernel(own_ref, beside_ref, out_ref):
+    half = own_ref.shape[0]
+    side = lax.axis_index("width")
+    out_ref[pl.ds(pl.multiple_of(side * half, 8), half), :] = own_ref[...]
+    out_ref[pl.ds(pl.multiple_of((1 - side) * half, 8), half), :] = beside_ref[...]
 
 
 def reduced_share(mine, theirs, rows):
@@ -109,41 +132,38 @@
     kept = kept_rows(half)
     f32, wire = jnp.float32, jnp.bfloat16
 
-    def pieces(count, dtype):
-        return jax.ShapeDtypeStruct((count, kept, channels), dtype)
-
-    def single(dtype):
-        return jax.ShapeDtypeStruct((kept, channels), dtype)
+    def both(count, high):
+        return tuple(jax.ShapeDtypeStruct((count, high, channels), kind) for kind in (f32, wire))
 
     got = exchanged(theirs, "width", 1)
-    near, far = call(split_rows_kernel, (pieces(blocks, f32), pieces(blocks, wire)))(mine, got)
-    got = exchanged(far, "height", 1)
-    distance = 1
-    while blocks // distance > 4:
-        count = near.shape[0] // 2
-        near, far = call(
-            functools.partial(split_blocks_kernel, distance),
-            (pieces(count, f32), pieces(count, wire)),
-        )(near, got)
-        got = exchanged(far, "tm", distance)
+    low, pairs = blocks // 2, blocks // 4
+    near_rows, far_rows, near_pair, far_pair = call(
+        first_kernel, (*both(low, kept), *both(pairs, half))
+    )(mine, got)
+    got_rows = exchanged(far_rows, "height", 1)
+    got_pair = exchanged(far_pair, "tm", 1)
+    near_low, far_low, near_high, far_high = call(
+        second_kernel, (*both(pairs, kept), *both(pairs, kept))
+    )(near_rows, got_rows, near_pair, got_pair)
+    got_low = exchanged(far_low, "tm", 1)
+    got_high = exchanged(far_high, "height", 1)
+    parts = (near_low, got_low, near_high, got_high)
+    low, distance = pairs, 2
+    while distance < blocks:
+        count = blocks // distance // 2
+        near, far = call(functools.partial(split_kernel, distance, low), both(count, kept))(*parts)
+        parts = (near, exchanged(far, "tm", distance))
+        low = count
         distance *= 2
-    left = blocks // distance
-    own, *fars = call(
-        functools.partial(split_all_kernel, distance),
-        (single(f32), *[single(wire)] * (left - 1)),
-    )(near, got)
-    arrived = []
-    for step, far in enumerate(fars, 1):
-        arrived.append(exchanged(far, "tm", step * distance))
-    own = call(add_kernel, single(f32))(own, *arrived)
+    own = call(add_kernel, jax.ShapeDtypeStruct((kept, channels), f32))(*parts)
     below = exchanged(own, "height", 1)
-    across = lax.ppermute(own, ("height", "width"), [(i, 3 - i) for i in range(4)])
+    own = call(half_kernel, jax.ShapeDtypeStruct((half, channels), f32))(own, below)
     beside = exchanged(own, "width", 1)
     return call(
-        assemble_kernel,
+        whole_kernel,
         jax.ShapeDtypeStruct((rows, channels), f32),
         out_specs=pl.BlockSpec((rows, channels), lambda: (0, 0)),
-    )(own, beside, below, across)
+    )(own, beside)
 
 
 def group_matrix(rows, cols, row_width, col_width):
@@ -167,8 +187,9 @@
     return exact_dot(value, group_matrix(groups, channels, 1, channels // groups))
 
 
-def cut_kernel(grad_ref, halo_ref, row_ref, col_ref, corner_ref):
+def cut_kernel(grad_ref, halo_ref, row_ref, col_ref, corner_ref, copy_ref):
     frames, rows, cols, _ = grad_ref.shape
+    copy_ref[...] = grad_ref[...]
     halo_ref[...] = grad_ref[: halo_ref.shape[0]]
     row_at = (1 - lax.axis_index("height")) * (rows - 1)
 
@@ -482,9 +503,15 @@
     def piece(*shape):
         return jax.ShapeDtypeStruct((*shape, channels), grad_out.dtype)
 
-    halo, row, col, corner = call(
+    halo, row, col, corner, held = call(
         cut_kernel,
-        (piece(extra, rows, cols), piece(frames, cols), piece(frames, rows), piece(frames)),
+        (
+            piece(extra, rows, cols),
+            piece(frames, cols),
+            piece(frames, rows),
+            piece(frames),
+            piece(frames, rows, cols),
+        ),
     )(grad_out)
     halo = shifted(halo, "tm", -1)
     row = exchanged(row, "height", 1)
@@ -492,7 +519,7 @@
     col = exchanged(col, "width", 1)
     packed = call(pack_kernel, piece(extra, cols + rows + 1))(row, col, corner)
     tail = shifted(packed, "tm", -1)
-    return (grad_out, row, col, corner), (halo, tail)
+    return (held, row, col, corner), (halo, tail)
 
 
 def on_device(features, grad_out, mean_saved, rstd_saved, gain, bias, weight, future_cot):
@@ -519,7 +546,10 @@
         near_sources = (jnp.pad(padded, sides),)
         far_sources = (jnp.pad(shifted(padded[:extra], "tm", -1), sides),)
 
-    inputs = (features, mean_saved, rstd_saved, gain, bias)
+    inputs = tuple(
+        pltpu.with_memory_space_constraint(value, pltpu.HBM)
+        for value in (features, mean_saved, rstd_saved, gain, bias)
+    )
     act, params = call(
         act_kernel,
         (

time: 58.9 us -> 57.3 us (0.973)
  local copies, waits for them, and re-layouts: 5.81 us -> 1.06 us
  waiting for transfers between devices: 21 us -> 22.9 us
  Pallas kernels: 10.7 us -> 11.7 us
  starting transfers between devices: 20.1 us -> 20.7 us
    unnamed x22 -> x10, local copies, waits for them, and re-layouts: 5.81 us -> 1.06 us
    ppermute x2, waiting for transfers between devices: 1.59 us -> 2.83 us  [shifted(): lax.ppermute(value, axis, [(source, source + steps) for source in range(i...]
    ppermute x1, waiting for transfers between devices: 0.01 us -> 1.21 us  [rims(): lax.ppermute(corner, ('height', 'width'), [(i, 3 - i) for i in range(4)])]
    pallas_call x12 -> x14, Pallas kernels: 10.7 us -> 11.7 us  [run(): pl.pallas_call(kernel, out_shape=out_shape, in_specs=in_specs or [here] *...]
    ppermute x12 -> x13, starting transfers between devices: 16.1 us -> 16.5 us  [exchanged(): return lax.ppermute(value, axis, [(i, i ^ distance) for i in range(count)])]
    ppermute x12 -> x13, waiting for transfers between devices: 18.3 us -> 17.9 us  [exchanged(): return lax.ppermute(value, axis, [(i, i ^ distance) for i in range(count)])]
  transfers between devices with their start and end apart: 17 -> 17, of which waited for: 8 -> 11; matrix products, arithmetic and copies ran while one was open for 0% -> 0% of each run, Pallas kernels for 15% -> 17%
where the time goes in v5:
time: 57.3 us; the launch traced here: 57.1 us
  waiting for transfers between devices  22.9 us (40%)
  starting transfers between devices  20.7 us (36%)
  Pallas kernels  11.7 us (20%)
  local copies, waits for them, and re-layouts  1.06 us (2%)
  between operations  0.79 us (1%)
    ppermute x13, waiting for transfers between devices, exchanged(): return lax.ppermute(value, axis, [(i, i ^ distance) for i in range(count)])  17.9 us
    ppermute x13, starting transfers between devices, exchanged(): return lax.ppermute(value, axis, [(i, i ^ distance) for i in range(count)])  16.5 us
    pallas_call x14, Pallas kernels, run(): pl.pallas_call(kernel, out_shape=out_shape, in_specs=in_specs or [here] *...  11.7 us
    ppermute x2, waiting for transfers between devices, shifted(): lax.ppermute(value, axis, [(source, source + steps) for source in range(i...  2.83 us
    ppermute x2, starting transfers between devices, shifted(): lax.ppermute(value, axis, [(source, source + steps) for source in range(i...  2.58 us
    ppermute x1, starting transfers between devices, on_device(): lax.ppermute(local, ('height', 'width'), [(i, 3 - i) for i in range(4)])  1.42 us
    ppermute x1, waiting for transfers between devices, rims(): lax.ppermute(corner, ('height', 'width'), [(i, 3 - i) for i in range(4)])  1.21 us
  transfers between devices with their start and end apart: 17, of which 11 were waited for; matrix products, arithmetic and copies ran while one was open for 0% of the time, Pallas kernels for 17%

profile of v5, /device:TPU:0, one launch (start us, length us, event | category | flops | bytes accessed | tf_op | source)
XLA Modules:
  0.0 57.1 jit_solution(18322635522076996627)
XLA Ops:
  0.6 0.0 copy-start.1
  0.6 1.0 %copy-done.1 = bf16[4,16,32,128]{3,2,1,0:T(8,128)(2,1)S(1)} copy-done((bf16[4,16,32,128]{3,2,1,0:T(8,128)(2,1)S(1)}, bf16[4,16,32,128]{3,2,1,0:T(8,128)(2,1)}, u32[]{:S(2)}) %copy-start.1) | copy-done | bytes 524312
  1.7 0.1 shard_map.96
  1.8 1.3 %collective-permute-start.3 = (bf16[2,16,32,128]{3,2,1,0:T(8,128)(2,1)S(1)}, bf16[2,16,32,128]{3,2,1,0:T(8,128)(2,1)S(1)}, u32[]{:S(2)}, u32[]{:S(2)}) collective-permute-start(bf16[2,16,32,128]{3,2,1,0:T(8,128)(2,1)S(1)} %get-tuple-element.35), channel_id=1, source_target_pairs={{4,0},{8,4},{12,8},{16,12},{20,16},{24,20},{28,24},{5,1},{9,5},{13... | collective-permute-start | bytes 786440 | tf_op jit(solution)/shard_map/ppermute | solution.py:24
  3.1 3.1 %collective-permute-start = (bf16[4,32,128]{2,1,0:T(8,128)(2,1)S(1)}, bf16[4,32,128]{2,1,0:T(8,128)(2,1)S(1)}, u32[]{:S(2)}, u32[]{:S(2)}) collective-permute-start(bf16[4,32,128]{2,1,0:T(8,128)(2,1)S(1)} %get-tuple-element.30), channel_id=1, source_target_pairs={{0,2},{2,0},{1,3},{3,1},{4,6},{6,4},{5,7},{7,5},{8,10},{10,8},{9,1... | collective-permute-start | bytes 98312 | tf_op jit(solution)/shard_map/ppermute | solution.py:18
  6.1 0.0 collective-permute-start.1
  6.1 0.2 collective-permute-start.2
  6.3 1.6 %shard_map.95 = (bf16[128,2048]{1,0:T(8,128)(2,1)S(1)}, f32[10,128]{1,0:T(8,128)S(1)}) custom-call(bf16[4,16,32,128]{3,2,1,0:T(8,128)(2,1)} %refs_5_.1, f32[4,32]{1,0:T(4,128)} %mean_hbm.1, f32[4,32]{1,0:T(4,128)} %rstd_hbm.1, f32[1,128]{1,0:T(1,128)} %bitcast.2, f32[1,128]{1,0:T(1,128)} %bitcast.3), custom_call_target="tpu_custom_call" | custom-call | flops 5242880 | bytes 1048576 | tf_op jit(solution)/shard_map/pallas_call | solution.py:477
  7.9 1.2 %collective-permute-done.2.refs_3_.corner_ref = bf16[4,128]{1,0:T(4,128)(2,1)S(1)} collective-permute-done((bf16[4,128]{1,0:T(4,128)(2,1)S(1)}, bf16[4,128]{1,0:T(4,128)(2,1)S(1)}, u32[]{:S(2)}, u32[]{:S(2)}) %collective-permute-start.2) | collective-permute-done | bytes 1056 | tf_op jit(solution)/shard_map/ppermute | solution.py:518
  9.1 0.0 collective-permute-done.1.refs_2_.col_ref
  9.1 0.0 collective-permute-done.refs_1_.row_ref
  9.1 1.3 %collective-permute-start.4 = (bf16[2,49,128]{2,1,0:T(8,128)(2,1)S(1)}, bf16[2,49,128]{2,1,0:T(8,128)(2,1)S(1)}, u32[]{:S(2)}, u32[]{:S(2)}) collective-permute-start(bf16[2,49,128]{2,1,0:T(8,128)(2,1)S(1)} %shard_map.98), channel_id=1, source_target_pairs={{4,0},{8,4},{12,8},{16,12},{20,16},{24,20},{28,24},{5,1},{9,5},{13... | collective-permute-start | bytes 75272 | tf_op jit(solution)/shard_map/ppermute | solution.py:24
  10.4 2.5 %shard_map.97 = (bf16[4,18,32,384]{3,2,1,0:T(8,128)(2,1)S(1)}, f32[3456,128]{1,0:T(8,128)S(1)}) custom-call(bf16[128,2048]{1,0:T(8,128)(2,1)S(1)} %get-tuple-element.28.act_ref, bf16[4,16,32,128]{3,2,1,0:T(8,128)(2,1)S(1)} %get-tuple-element.29.refs_0_, bf16[4,32,128]{2,1,0:T(8,128)(2,1)S(1)} %collective-permute-done.refs_1_.row_ref, ...), custom_call_target="tpu_custom_call" | custom-call | flops 1358954496 | bytes 4194304 | tf_op jit(solution)/shard_map/pallas_call | solution.py:477
  12.9 2.8 %collective-permute-done.4.refs_1_ = bf16[2,49,128]{2,1,0:T(8,128)(2,1)S(1)} collective-permute-done((bf16[2,49,128]{2,1,0:T(8,128)(2,1)S(1)}, bf16[2,49,128]{2,1,0:T(8,128)(2,1)S(1)}, u32[]{:S(2)}, u32[]{:S(2)}) %collective-permute-start.4) | collective-permute-done | bytes 25120 | tf_op jit(solution)/shard_map/ppermute | solution.py:24
  15.7 0.0 collective-permute-done.3.refs_0_
  15.7 1.1 %shard_map.99 = (bf16[2,18,32,384]{3,2,1,0:T(8,128)(2,1)S(1)}, f32[8,216,128]{2,1,0:T(8,128)S(1)}, f32[8,216,128]{2,1,0:T(8,128)S(1)}) custom-call(bf16[128,2048]{1,0:T(8,128)(2,1)S(1)} %get-tuple-element.28.act_ref, f32[3456,128]{1,0:T(8,128)S(1)} %get-tuple-element.34.near_sum_ref, bf16[2,16,32,128]{3,2,1,0:T(8,128)(2,1)S(1)} %collective-permute-done.3.refs_0_, ...), custom_call_target="tpu_custom_call" | custom-call | flops 452984832 | bytes 4194304 | tf_op jit(solution)/shard_map/pallas_call | solution.py:477
  16.9 0.0 copy-start
  16.9 0.0 copy-start.3
  16.9 0.0 copy-start.4
  16.9 0.2 collective-permute-start.8
  17.1 2.3 %collective-permute-done.8.got_ref = f32[8,216,128]{2,1,0:T(8,128)S(1)} collective-permute-done((f32[8,216,128]{2,1,0:T(8,128)S(1)}, f32[8,216,128]{2,1,0:T(8,128)S(1)}, u32[]{:S(2)}, u32[]{:S(2)}) %collective-permute-start.8) | collective-permute-done | bytes 884768 | tf_op jit(solution)/shard_map/ppermute | solution.py:18
  19.4 0.1 shard_map.102
  19.5 0.8 %collective-permute-start.9 = (bf16[4,112,128]{2,1,0:T(8,128)(2,1)S(1)}, bf16[4,112,128]{2,1,0:T(8,128)(2,1)S(1)}, u32[]{:S(2)}, u32[]{:S(2)}) collective-permute-start(bf16[4,112,128]{2,1,0:T(8,128)(2,1)S(1)} %get-tuple-element.43), channel_id=1, source_target_pairs={{0,2},{2,0},{1,3},{3,1},{4,6},{6,4},{5,7},{7,5},{8,10},{10,8},{9,1... | collective-permute-start | bytes 344072 | tf_op jit(solution)/shard_map/ppermute | solution.py:18
  20.3 2.9 %collective-permute-start.10 = (bf16[2,216,128]{2,1,0:T(8,128)(2,1)S(1)}, bf16[2,216,128]{2,1,0:T(8,128)(2,1)S(1)}, u32[]{:S(2)}, u32[]{:S(2)}) collective-permute-start(bf16[2,216,128]{2,1,0:T(8,128)(2,1)S(1)} %get-tuple-element.45), channel_id=1, source_target_pairs={{0,4},{4,0},{8,12},{12,8},{16,20},{20,16},{24,28},{28,24},{1,5},{5... | collective-permute-start | bytes 331784 | tf_op jit(solution)/shard_map/ppermute | solution.py:18
  23.2 3.1 %collective-permute-done.10.pair_got_ref = bf16[2,216,128]{2,1,0:T(8,128)(2,1)S(1)} collective-permute-done((bf16[2,216,128]{2,1,0:T(8,128)(2,1)S(1)}, bf16[2,216,128]{2,1,0:T(8,128)(2,1)S(1)}, u32[]{:S(2)}, u32[]{:S(2)}) %collective-permute-start.10) | collective-permute-done | bytes 110624 | tf_op jit(solution)/shard_map/ppermute | solution.py:18
  26.3 0.0 collective-permute-done.9.rows_got_ref
  26.3 0.1 shard_map.103
  26.3 1.8 %collective-permute-start.11 = (bf16[2,112,128]{2,1,0:T(8,128)(2,1)S(1)}, bf16[2,112,128]{2,1,0:T(8,128)(2,1)S(1)}, u32[]{:S(2)}, u32[]{:S(2)}) collective-permute-start(bf16[2,112,128]{2,1,0:T(8,128)(2,1)S(1)} %get-tuple-element.47), channel_id=1, source_target_pairs={{0,4},{4,0},{8,12},{12,8},{16,20},{20,16},{24,28},{28,24},{1,5},{5... | collective-permute-start | bytes 172040 | tf_op jit(solution)/shard_map/ppermute | solution.py:18
  28.1 1.3 %collective-permute-start.12 = (bf16[2,112,128]{2,1,0:T(8,128)(2,1)S(1)}, bf16[2,112,128]{2,1,0:T(8,128)(2,1)S(1)}, u32[]{:S(2)}, u32[]{:S(2)}) collective-permute-start(bf16[2,112,128]{2,1,0:T(8,128)(2,1)S(1)} %get-tuple-element.49), channel_id=1, source_target_pairs={{0,2},{2,0},{1,3},{3,1},{4,6},{6,4},{5,7},{7,5},{8,10},{10,8},{9,1... | collective-permute-start | bytes 172040 | tf_op jit(solution)/shard_map/ppermute | solution.py:18
  29.4 1.2 %collective-permute-done.11.refs_1_ = bf16[2,112,128]{2,1,0:T(8,128)(2,1)S(1)} collective-permute-done((bf16[2,112,128]{2,1,0:T(8,128)(2,1)S(1)}, bf16[2,112,128]{2,1,0:T(8,128)(2,1)S(1)}, u32[]{:S(2)}, u32[]{:S(2)}) %collective-permute-start.11) | collective-permute-done | bytes 57376 | tf_op jit(solution)/shard_map/ppermute | solution.py:18
  30.6 1.7 %collective-permute-done.12.refs_3_ = bf16[2,112,128]{2,1,0:T(8,128)(2,1)S(1)} collective-permute-done((bf16[2,112,128]{2,1,0:T(8,128)(2,1)S(1)}, bf16[2,112,128]{2,1,0:T(8,128)(2,1)S(1)}, u32[]{:S(2)}, u32[]{:S(2)}) %collective-permute-start.12) | collective-permute-done | bytes 57376 | tf_op jit(solution)/shard_map/ppermute | solution.py:18
  32.4 1.6 %collective-permute-start.13 = (bf16[2,112,128]{2,1,0:T(8,128)(2,1)S(1)}, bf16[2,112,128]{2,1,0:T(8,128)(2,1)S(1)}, u32[]{:S(2)}, u32[]{:S(2)}) collective-permute-start(bf16[2,112,128]{2,1,0:T(8,128)(2,1)S(1)} %get-tuple-element.51), channel_id=1, source_target_pairs={{0,8},{4,12},{8,0},{12,4},{16,24},{20,28},{24,16},{28,20},{1,9},{5... | collective-permute-start | bytes 172040 | tf_op jit(solution)/shard_map/ppermute | solution.py:18
  34.0 2.6 %collective-permute-done.13.refs_1_ = bf16[2,112,128]{2,1,0:T(8,128)(2,1)S(1)} collective-permute-done((bf16[2,112,128]{2,1,0:T(8,128)(2,1)S(1)}, bf16[2,112,128]{2,1,0:T(8,128)(2,1)S(1)}, u32[]{:S(2)}, u32[]{:S(2)}) %collective-permute-start.13) | collective-permute-done | bytes 57376 | tf_op jit(solution)/shard_map/ppermute | solution.py:18
  36.6 2.7 %collective-permute-start.14 = (bf16[1,112,128]{2,1,0:T(8,128)(2,1)S(1)}, bf16[1,112,128]{2,1,0:T(8,128)(2,1)S(1)}, u32[]{:S(2)}, u32[]{:S(2)}) collective-permute-start(bf16[1,112,128]{2,1,0:T(8,128)(2,1)S(1)} %get-tuple-element.53), channel_id=1, source_target_pairs={{0,16},{4,20},{8,24},{12,28},{16,0},{20,4},{24,8},{28,12},{1,17},{... | collective-permute-start | bytes 86024 | tf_op jit(solution)/shard_map/ppermute | solution.py:18
  39.3 2.2 %collective-permute-done.14.got_ref = bf16[1,112,128]{2,1,0:T(8,128)(2,1)S(1)} collective-permute-done((bf16[1,112,128]{2,1,0:T(8,128)(2,1)S(1)}, bf16[1,112,128]{2,1,0:T(8,128)(2,1)S(1)}, u32[]{:S(2)}, u32[]{:S(2)}) %collective-permute-start.14) | collective-permute-done | bytes 28704 | tf_op jit(solution)/shard_map/ppermute | solution.py:18
  41.5 1.3 %collective-permute-start.15 = (f32[112,128]{1,0:T(8,128)S(1)}, f32[112,128]{1,0:T(8,128)S(1)}, u32[]{:S(2)}, u32[]{:S(2)}) collective-permute-start(f32[112,128]{1,0:T(8,128)S(1)} %shard_map.106.own_ref), channel_id=1, source_target_pairs={{0,2},{2,0},{1,3},{3,1},{4,6},{6,4},{5,7},{7,5},{8,10},{10,8},{9,1... | collective-permute-start | bytes 172040 | tf_op jit(solution)/shard_map/ppermute | solution.py:18
  42.8 2.9 %collective-permute-done.15.below_ref = f32[112,128]{1,0:T(8,128)S(1)} collective-permute-done((f32[112,128]{1,0:T(8,128)S(1)}, f32[112,128]{1,0:T(8,128)S(1)}, u32[]{:S(2)}, u32[]{:S(2)}) %collective-permute-start.15) | collective-permute-done | bytes 57376 | tf_op jit(solution)/shard_map/ppermute | solution.py:18
  45.7 0.1 collective-permute-start.16
  45.8 0.0 copy-done
  45.8 0.0 copy-done.3
  45.8 0.0 copy-done.4
  45.8 0.0 copy-start.2
  45.8 4.2 %shard_map.100 = (f32[4,16,32,128]{3,2,1,0:T(8,128)S(1)}, f32[8,128]{1,0:T(8,128)S(1)}) custom-call(bf16[4,18,32,384]{3,2,1,0:T(8,128)(2,1)S(1)} %get-tuple-element.33.near_ref, bf16[2,18,32,384]{3,2,1,0:T(8,128)(2,1)S(1)} %get-tuple-element.36.far_ref, bf16[3,3,3,128,128]{4,3,2,1,0:T(8,128)(2,1)S(1)} %copy-done.3, bf16[2,16,32,128]{3,2,1,0:T(8,128)(2,1)S(1)} %copy-done.4, ...), custom_call_target="tpu_custom_call" | custom-call | flops 1811939328 | bytes 8388608 | tf_op jit(solution)/shard_map/pallas_call | solution.py:477
  50.0 1.4 %collective-permute-start.7 = (f32[8,128]{1,0:T(8,128)S(1)}, f32[8,128]{1,0:T(8,128)S(1)}, u32[]{:S(2)}, u32[]{:S(2)}) collective-permute-start(f32[8,128]{1,0:T(8,128)S(1)} %get-tuple-element.38.refs_0_), channel_id=1, source_target_pairs={{0,3},{1,2},{2,1},{3,0},{4,7},{5,6},{6,5},{7,4},{8,11},{9,10},{10,... | collective-permute-start | bytes 12296 | tf_op jit(solution)/shard_map/ppermute | solution.py:618
  51.4 0.8 %collective-permute-start.6 = (f32[8,128]{1,0:T(8,128)S(1)}, f32[8,128]{1,0:T(8,128)S(1)}, u32[]{:S(2)}, u32[]{:S(2)}) collective-permute-start(f32[8,128]{1,0:T(8,128)S(1)} %get-tuple-element.38.refs_0_), channel_id=1, source_target_pairs={{0,2},{2,0},{1,3},{3,1},{4,6},{6,4},{5,7},{7,5},{8,10},{10,8},{9,1... | collective-permute-start | bytes 12296 | tf_op jit(solution)/shard_map/ppermute | solution.py:18
  52.2 0.0 collective-permute-start.5
  52.2 0.9 %collective-permute-done.7.refs_3_ = f32[8,128]{1,0:T(8,128)S(1)} collective-permute-done((f32[8,128]{1,0:T(8,128)S(1)}, f32[8,128]{1,0:T(8,128)S(1)}, u32[]{:S(2)}, u32[]{:S(2)}) %collective-permute-start.7) | collective-permute-done | bytes 4128 | tf_op jit(solution)/shard_map/ppermute | solution.py:618
  53.1 1.9 %collective-permute-done.6.refs_2_ = f32[8,128]{1,0:T(8,128)S(1)} collective-permute-done((f32[8,128]{1,0:T(8,128)S(1)}, f32[8,128]{1,0:T(8,128)S(1)}, u32[]{:S(2)}, u32[]{:S(2)}) %collective-permute-start.6) | collective-permute-done | bytes 4128 | tf_op jit(solution)/shard_map/ppermute | solution.py:18
  55.0 0.0 collective-permute-done.5.refs_1_
  55.0 0.0 copy-done.2
  55.0 1.4 %shard_map.101 = bf16[4,16,32,128]{3,2,1,0:T(8,128)(2,1)} custom-call(f32[8,128]{1,0:T(8,128)S(1)} %get-tuple-element.38.refs_0_, f32[8,128]{1,0:T(8,128)S(1)} %collective-permute-done.5.refs_1_, f32[8,128]{1,0:T(8,128)S(1)} %collective-permute-done.6.refs_2_, f32[8,128]{1,0:T(8,128)S(1)} %collective-permute-done.7.refs_3_, ...), custom_call_target="tpu_custom_call" | custom-call | flops 5242880 | bytes 2621440 | tf_op jit(solution)/shard_map/pallas_call | solution.py:477
  56.4 0.0 collective-permute-done.16.beside_ref
  56.4 0.7 %shard_map.108 = f32[432,128]{1,0:T(8,128)} custom-call(f32[216,128]{1,0:T(8,128)S(1)} %shard_map.107.own_ref, f32[216,128]{1,0:T(8,128)S(1)} %collective-permute-done.16.beside_ref), custom_call_target="tpu_custom_call" | custom-call | tf_op jit(solution)/shard_map/pallas_call | solution.py:477
  (5 shorter events, 0.1 us)
Async XLA Ops:
  0.6 1.0 %copy-start.1 = (bf16[4,16,32,128]{3,2,1,0:T(8,128)(2,1)S(1)}, bf16[4,16,32,128]{3,2,1,0:T(8,128)(2,1)}, u32[]{:S(2)}) copy-start(bf16[4,16,32,128]{3,2,1,0:T(8,128)(2,1)} %refs_6_.1) | copy-start | bytes 1572868
  1.8 14.0 %collective-permute-start.3 = (bf16[2,16,32,128]{3,2,1,0:T(8,128)(2,1)S(1)}, bf16[2,16,32,128]{3,2,1,0:T(8,128)(2,1)S(1)}, u32[]{:S(2)}, u32[]{:S(2)}) collective-permute-start(bf16[2,16,32,128]{3,2,1,0:T(8,128)(2,1)S(1)} %get-tuple-element.35), channel_id=1, source_target_pairs={{4,0},{8,4},{12,8},{16,12},{20,16},{24,20},{28,24},{5,1},{9,5},{13... | collective-permute-start | bytes 786440 | tf_op jit(solution)/shard_map/ppermute | solution.py:24
  3.1 6.1 %collective-permute-start = (bf16[4,32,128]{2,1,0:T(8,128)(2,1)S(1)}, bf16[4,32,128]{2,1,0:T(8,128)(2,1)S(1)}, u32[]{:S(2)}, u32[]{:S(2)}) collective-permute-start(bf16[4,32,128]{2,1,0:T(8,128)(2,1)S(1)} %get-tuple-element.30), channel_id=1, source_target_pairs={{0,2},{2,0},{1,3},{3,1},{4,6},{6,4},{5,7},{7,5},{8,10},{10,8},{9,1... | collective-permute-start | bytes 98312 | tf_op jit(solution)/shard_map/ppermute | solution.py:18
  6.1 3.0 %collective-permute-start.1 = (bf16[4,16,128]{2,1,0:T(8,128)(2,1)S(1)}, bf16[4,16,128]{2,1,0:T(8,128)(2,1)S(1)}, u32[]{:S(2)}, u32[]{:S(2)}) collective-permute-start(bf16[4,16,128]{2,1,0:T(8,128)(2,1)S(1)} %get-tuple-element.31), channel_id=1, source_target_pairs={{0,1},{1,0},{2,3},{3,2},{4,5},{5,4},{6,7},{7,6},{8,9},{9,8},{10,11... | collective-permute-start | bytes 49160 | tf_op jit(solution)/shard_map/ppermute | solution.py:18
  6.1 3.0 %collective-permute-start.2 = (bf16[4,128]{1,0:T(4,128)(2,1)S(1)}, bf16[4,128]{1,0:T(4,128)(2,1)S(1)}, u32[]{:S(2)}, u32[]{:S(2)}) collective-permute-start(bf16[4,128]{1,0:T(4,128)(2,1)S(1)} %get-tuple-element.32), channel_id=1, source_target_pairs={{0,3},{1,2},{2,1},{3,0},{4,7},{5,6},{6,5},{7,4},{8,11},{9,10},{10,... | collective-permute-start | bytes 3080 | tf_op jit(solution)/shard_map/ppermute | solution.py:518
  9.1 6.6 %collective-permute-start.4 = (bf16[2,49,128]{2,1,0:T(8,128)(2,1)S(1)}, bf16[2,49,128]{2,1,0:T(8,128)(2,1)S(1)}, u32[]{:S(2)}, u32[]{:S(2)}) collective-permute-start(bf16[2,49,128]{2,1,0:T(8,128)(2,1)S(1)} %shard_map.98), channel_id=1, source_target_pairs={{4,0},{8,4},{12,8},{16,12},{20,16},{24,20},{28,24},{5,1},{9,5},{13... | collective-permute-start | bytes 75272 | tf_op jit(solution)/shard_map/ppermute | solution.py:24
  16.9 29.0 %copy-start = (bf16[4,16,32,128]{3,2,1,0:T(8,128)(2,1)S(1)}, bf16[4,16,32,128]{3,2,1,0:T(8,128)(2,1)}, u32[]{:S(2)}) copy-start(bf16[4,16,32,128]{3,2,1,0:T(8,128)(2,1)} %refs_5_.1) | copy-start | bytes 1572868
  16.9 29.0 %copy-start.3 = (bf16[3,3,3,128,128]{4,3,2,1,0:T(8,128)(2,1)S(1)}, bf16[3,3,3,128,128]{4,3,2,1,0:T(8,128)(2,1)}, u32[]{:S(2)}) copy-start(bf16[3,3,3,128,128]{4,3,2,1,0:T(8,128)(2,1)} %weight_ref.1) | copy-start | bytes 2654212
  16.9 28.9 %copy-start.4 = (bf16[2,16,32,128]{3,2,1,0:T(8,128)(2,1)S(1)}, bf16[2,16,32,128]{3,2,1,0:T(8,128)(2,1)}, u32[]{:S(2)}) copy-start(bf16[2,16,32,128]{3,2,1,0:T(8,128)(2,1)} %future_ref.1) | copy-start | bytes 786436
  16.9 2.5 %collective-permute-start.8 = (f32[8,216,128]{2,1,0:T(8,128)S(1)}, f32[8,216,128]{2,1,0:T(8,128)S(1)}, u32[]{:S(2)}, u32[]{:S(2)}) collective-permute-start(f32[8,216,128]{2,1,0:T(8,128)S(1)} %get-tuple-element.41), channel_id=1, source_target_pairs={{0,1},{1,0},{2,3},{3,2},{4,5},{5,4},{6,7},{7,6},{8,9},{9,8},{10,11... | collective-permute-start | bytes 2654216 | tf_op jit(solution)/shard_map/ppermute | solution.py:18
  19.5 6.8 %collective-permute-start.9 = (bf16[4,112,128]{2,1,0:T(8,128)(2,1)S(1)}, bf16[4,112,128]{2,1,0:T(8,128)(2,1)S(1)}, u32[]{:S(2)}, u32[]{:S(2)}) collective-permute-start(bf16[4,112,128]{2,1,0:T(8,128)(2,1)S(1)} %get-tuple-element.43), channel_id=1, source_target_pairs={{0,2},{2,0},{1,3},{3,1},{4,6},{6,4},{5,7},{7,5},{8,10},{10,8},{9,1... | collective-permute-start | bytes 344072 | tf_op jit(solution)/shard_map/ppermute | solution.py:18
  20.3 6.0 %collective-permute-start.10 = (bf16[2,216,128]{2,1,0:T(8,128)(2,1)S(1)}, bf16[2,216,128]{2,1,0:T(8,128)(2,1)S(1)}, u32[]{:S(2)}, u32[]{:S(2)}) collective-permute-start(bf16[2,216,128]{2,1,0:T(8,128)(2,1)S(1)} %get-tuple-element.45), channel_id=1, source_target_pairs={{0,4},{4,0},{8,12},{12,8},{16,20},{20,16},{24,28},{28,24},{1,5},{5... | collective-permute-start | bytes 331784 | tf_op jit(solution)/shard_map/ppermute | solution.py:18
  26.3 4.2 %collective-permute-start.11 = (bf16[2,112,128]{2,1,0:T(8,128)(2,1)S(1)}, bf16[2,112,128]{2,1,0:T(8,128)(2,1)S(1)}, u32[]{:S(2)}, u32[]{:S(2)}) collective-permute-start(bf16[2,112,128]{2,1,0:T(8,128)(2,1)S(1)} %get-tuple-element.47), channel_id=1, source_target_pairs={{0,4},{4,0},{8,12},{12,8},{16,20},{20,16},{24,28},{28,24},{1,5},{5... | collective-permute-start | bytes 172040 | tf_op jit(solution)/shard_map/ppermute | solution.py:18
  28.1 4.2 %collective-permute-start.12 = (bf16[2,112,128]{2,1,0:T(8,128)(2,1)S(1)}, bf16[2,112,128]{2,1,0:T(8,128)(2,1)S(1)}, u32[]{:S(2)}, u32[]{:S(2)}) collective-permute-start(bf16[2,112,128]{2,1,0:T(8,128)(2,1)S(1)} %get-tuple-element.49), channel_id=1, source_target_pairs={{0,2},{2,0},{1,3},{3,1},{4,6},{6,4},{5,7},{7,5},{8,10},{10,8},{9,1... | collective-permute-start | bytes 172040 | tf_op jit(solution)/shard_map/ppermute | solution.py:18
  32.4 4.2 %collective-permute-start.13 = (bf16[2,112,128]{2,1,0:T(8,128)(2,1)S(1)}, bf16[2,112,128]{2,1,0:T(8,128)(2,1)S(1)}, u32[]{:S(2)}, u32[]{:S(2)}) collective-permute-start(bf16[2,112,128]{2,1,0:T(8,128)(2,1)S(1)} %get-tuple-element.51), channel_id=1, source_target_pairs={{0,8},{4,12},{8,0},{12,4},{16,24},{20,28},{24,16},{28,20},{1,9},{5... | collective-permute-start | bytes 172040 | tf_op jit(solution)/shard_map/ppermute | solution.py:18
  36.6 4.8 %collective-permute-start.14 = (bf16[1,112,128]{2,1,0:T(8,128)(2,1)S(1)}, bf16[1,112,128]{2,1,0:T(8,128)(2,1)S(1)}, u32[]{:S(2)}, u32[]{:S(2)}) collective-permute-start(bf16[1,112,128]{2,1,0:T(8,128)(2,1)S(1)} %get-tuple-element.53), channel_id=1, source_target_pairs={{0,16},{4,20},{8,24},{12,28},{16,0},{20,4},{24,8},{28,12},{1,17},{... | collective-permute-start | bytes 86024 | tf_op jit(solution)/shard_map/ppermute | solution.py:18
  41.5 4.2 %collective-permute-start.15 = (f32[112,128]{1,0:T(8,128)S(1)}, f32[112,128]{1,0:T(8,128)S(1)}, u32[]{:S(2)}, u32[]{:S(2)}) collective-permute-start(f32[112,128]{1,0:T(8,128)S(1)} %shard_map.106.own_ref), channel_id=1, source_target_pairs={{0,2},{2,0},{1,3},{3,1},{4,6},{6,4},{5,7},{7,5},{8,10},{10,8},{9,1... | collective-permute-start | bytes 172040 | tf_op jit(solution)/shard_map/ppermute | solution.py:18
  45.7 10.7 %collective-permute-start.16 = (f32[216,128]{1,0:T(8,128)S(1)}, f32[216,128]{1,0:T(8,128)S(1)}, u32[]{:S(2)}, u32[]{:S(2)}) collective-permute-start(f32[216,128]{1,0:T(8,128)S(1)} %shard_map.107.own_ref), channel_id=1, source_target_pairs={{0,1},{1,0},{2,3},{3,2},{4,5},{5,4},{6,7},{7,6},{8,9},{9,8},{10,11... | collective-permute-start | bytes 331784 | tf_op jit(solution)/shard_map/ppermute | solution.py:18
  45.8 9.2 %copy-start.2 = (bf16[4,16,32,128]{3,2,1,0:T(8,128)(2,1)S(1)}, bf16[4,16,32,128]{3,2,1,0:T(8,128)(2,1)}, u32[]{:S(2)}) copy-start(bf16[4,16,32,128]{3,2,1,0:T(8,128)(2,1)} %refs_6_.1) | copy-start | bytes 1572868
  50.0 3.1 %collective-permute-start.7 = (f32[8,128]{1,0:T(8,128)S(1)}, f32[8,128]{1,0:T(8,128)S(1)}, u32[]{:S(2)}, u32[]{:S(2)}) collective-permute-start(f32[8,128]{1,0:T(8,128)S(1)} %get-tuple-element.38.refs_0_), channel_id=1, source_target_pairs={{0,3},{1,2},{2,1},{3,0},{4,7},{5,6},{6,5},{7,4},{8,11},{9,10},{10,... | collective-permute-start | bytes 12296 | tf_op jit(solution)/shard_map/ppermute | solution.py:618
  51.4 3.6 %collective-permute-start.6 = (f32[8,128]{1,0:T(8,128)S(1)}, f32[8,128]{1,0:T(8,128)S(1)}, u32[]{:S(2)}, u32[]{:S(2)}) collective-permute-start(f32[8,128]{1,0:T(8,128)S(1)} %get-tuple-element.38.refs_0_), channel_id=1, source_target_pairs={{0,2},{2,0},{1,3},{3,1},{4,6},{6,4},{5,7},{7,5},{8,10},{10,8},{9,1... | collective-permute-start | bytes 12296 | tf_op jit(solution)/shard_map/ppermute | solution.py:18
  52.2 2.9 %collective-permute-start.5 = (f32[8,128]{1,0:T(8,128)S(1)}, f32[8,128]{1,0:T(8,128)S(1)}, u32[]{:S(2)}, u32[]{:S(2)}) collective-permute-start(f32[8,128]{1,0:T(8,128)S(1)} %get-tuple-element.38.refs_0_), channel_id=1, source_target_pairs={{0,1},{1,0},{2,3},{3,2},{4,5},{5,4},{6,7},{7,6},{8,9},{9,8},{10,11... | collective-permute-start | bytes 12296 | tf_op jit(solution)/shard_map/ppermute | solution.py:18

commit v6 on v5

--- a/solution.py
+++ b/solution.py
@@ -32,138 +32,115 @@
     return lax.axis_size("height") == 2 and lax.axis_size("width") == 2
 
 
-def kept_rows(rows):
-    return -(-rows // 16) * 8
-
-
 def in_halves(blocks, rows):
     return paired() and power_of_two(blocks) and blocks >= 8 and rows % 16 == 0
 
 
-def store_rows(value, near_ref, far_ref, at, side):
-    rows, kept = value.shape[0], near_ref.shape[1]
-
-    @pl.when(side == 0)
-    def _():
-        near_ref[at] = value[:kept]
-        far_ref[at] = value[rows - kept :].astype(far_ref.dtype)
-
-    @pl.when(side == 1)
-    def _():
-        near_ref[at] = value[rows - kept :]
-        far_ref[at] = value[:kept].astype(far_ref.dtype)
-
-
-def first_kernel(mine_ref, got_ref, rows_near_ref, rows_far_ref, pair_near_ref, pair_far_ref):
-    low = rows_near_ref.shape[0]
-    row_side = lax.axis_index("height")
-    side = lax.axis_index("tm") % 2
-    for block in range(low):
-        value = mine_ref[block] + got_ref[block]
-        store_rows(value, rows_near_ref, rows_far_ref, block, row_side)
-    for pair in range(pair_near_ref.shape[0]):
-        at = low + 2 * pair + side
-        pair_near_ref[pair] = mine_ref[at] + got_ref[at]
-        at = low + 2 * pair + 1 - side
-        pair_far_ref[pair] = (mine_ref[at] + got_ref[at]).astype(pair_far_ref.dtype)
-
-
-def second_kernel(
-    rows_ref, rows_got_ref, pair_ref, pair_got_ref, low_near, low_far, high_near, high_far
-):
-    row_side = lax.axis_index("height")
-    side = lax.axis_index("tm") % 2
-    for pair in range(low_near.shape[0]):
-        at = 2 * pair + side
-        low_near[pair] = rows_ref[at] + rows_got_ref[at].astype(jnp.float32)
-        at = 2 * pair + 1 - side
-        low_far[pair] = (rows_ref[at] + rows_got_ref[at].astype(jnp.float32)).astype(low_far.dtype)
-        value = pair_ref[pair] + pair_got_ref[pair].astype(jnp.float32)
-        store_rows(value, high_near, high_far, pair, row_side)
-
-
-def split_kernel(distance, low, *refs):
+def tm_side(distance):
+    return (lax.axis_index("tm") // distance) % 2
+
+
+def first_kernel(mine_ref, got_ref, low_near, low_far, high_near, high_far):
+    half = mine_ref.shape[0] // 2
+    near_side, next_side = tm_side(1), tm_side(2)
+
+    def block(at):
+        return mine_ref[at] + got_ref[at]
+
+    for i in range(low_near.shape[0]):
+        low_near[i] = block(2 * i + near_side)
+        low_far[i] = block(2 * i + 1 - near_side).astype(low_far.dtype)
+    for i in range(high_near.shape[0]):
+        at = half + 4 * (i // 2) + i % 2
+        high_near[i] = block(at + 2 * next_side)
+        high_far[i] = block(at + 2 * (1 - next_side)).astype(high_far.dtype)
+
+
+def second_kernel(low_ref, low_got_ref, high_ref, high_got_ref, *outs):
+    low_near, low_far, high_near, high_far = outs
+
+    def halve(value_ref, got_ref, near_ref, far_ref, side):
+        for i in range(near_ref.shape[0]):
+            at = 2 * i + side
+            near_ref[i] = value_ref[at] + got_ref[at].astype(jnp.float32)
+            at = 2 * i + 1 - side
+            value = value_ref[at] + got_ref[at].astype(jnp.float32)
+            far_ref[i] = value.astype(far_ref.dtype)
+
+    halve(low_ref, low_got_ref, low_near, low_far, tm_side(2))
+    halve(high_ref, high_got_ref, high_near, high_far, tm_side(1))
+
+
+def split_kernel(distance, *refs):
     *parts, near_ref, far_ref = refs
-    side = (lax.axis_index("tm") // distance) % 2
-
-    def block(pair, which):
-        at = 2 * pair + which
-        if 2 * pair < low:
-            value_ref, got_ref = parts[:2]
-        else:
-            value_ref, got_ref = parts[-2:]
-            at = at - low
+    blocks = [
+        (value_ref, got_ref, at)
+        for value_ref, got_ref in zip(parts[::2], parts[1::2])
+        for at in range(value_ref.shape[0])
+    ]
+
+    def block(i):
+        value_ref, got_ref, at = blocks[i]
         return value_ref[at] + got_ref[at].astype(jnp.float32)
 
-    for pair in range(near_ref.shape[0]):
-        near_ref[pair] = block(pair, side)
-        far_ref[pair] = block(pair, 1 - side).astype(far_ref.dtype)
-
-
-def add_kernel(near_ref, got_ref, out_ref):
-    out_ref[...] = near_ref[0] + got_ref[0].astype(jnp.float32)
-
-
-def half_kernel(own_ref, below_ref, out_ref):
-    kept, half = own_ref.shape[0], out_ref.shape[0]
-
-    def place(low_ref, high_ref):
-        out_ref[:kept, :] = low_ref[...]
-        out_ref[kept:, :] = high_ref[2 * kept - half :, :]
-
-    @pl.when(lax.axis_index("height") == 0)
-    def _():
-        place(own_ref, below_ref)
-
-    @pl.when(lax.axis_index("height") == 1)
-    def _():
-        place(below_ref, own_ref)
-
-
-def whole_kernel(own_ref, beside_ref, out_ref):
-    half = own_ref.shape[0]
+    for which in range(2):
+
+        @pl.when(tm_side(distance) == which)
+        def _():
+            for i in range(near_ref.shape[0]):
+                near_ref[i] = block(2 * i + which)
+                far_ref[i] = block(2 * i + 1 - which).astype(far_ref.dtype)
+
+
+def add_kernel(own_ref, got_ref, out_ref):
+    out_ref[...] = own_ref[...] + got_ref[...].astype(jnp.float32)
+
+
+def whole_kernel(own_ref, got_ref, beside_ref, out_ref):
+    half = own_ref.shape[1]
     side = lax.axis_index("width")
-    out_ref[pl.ds(pl.multiple_of(side * half, 8), half), :] = own_ref[...]
-    out_ref[pl.ds(pl.multiple_of((1 - side) * half, 8), half), :] = beside_ref[...]
+    mine = pl.multiple_of(side * half, 8)
+    other = pl.multiple_of((1 - side) * half, 8)
+    out_ref[pl.ds(mine, half), :] = own_ref[0] + got_ref[0]
+    out_ref[pl.ds(other, half), :] = beside_ref[0]
 
 
 def reduced_share(mine, theirs, rows):
     blocks, half, channels = mine.shape
-    kept = kept_rows(half)
     f32, wire = jnp.float32, jnp.bfloat16
 
-    def both(count, high):
-        return tuple(jax.ShapeDtypeStruct((count, high, channels), kind) for kind in (f32, wire))
+    def both(count):
+        return tuple(jax.ShapeDtypeStruct((count, half, channels), kind) for kind in (f32, wire))
 
     got = exchanged(theirs, "width", 1)
-    low, pairs = blocks // 2, blocks // 4
-    near_rows, far_rows, near_pair, far_pair = call(
-        first_kernel, (*both(low, kept), *both(pairs, half))
+    low, low_far, high, high_far = call(
+        first_kernel, (*both(blocks // 4), *both(blocks // 4))
     )(mine, got)
-    got_rows = exchanged(far_rows, "height", 1)
-    got_pair = exchanged(far_pair, "tm", 1)
-    near_low, far_low, near_high, far_high = call(
-        second_kernel, (*both(pairs, kept), *both(pairs, kept))
-    )(near_rows, got_rows, near_pair, got_pair)
-    got_low = exchanged(far_low, "tm", 1)
-    got_high = exchanged(far_high, "height", 1)
-    parts = (near_low, got_low, near_high, got_high)
-    low, distance = pairs, 2
+    low_got = exchanged(low_far, "tm", 1)
+    high_got = exchanged(high_far, "tm", 2)
+    low, low_far, high, high_far = call(
+        second_kernel, (*both(blocks // 8), *both(blocks // 8))
+    )(low, low_got, high, high_got)
+    low_got = exchanged(low_far, "tm", 2)
+    high_got = exchanged(high_far, "tm", 1)
+    parts = (low, low_got, high, high_got)
+    distance = 4
     while distance < blocks:
-        count = blocks // distance // 2
-        near, far = call(functools.partial(split_kernel, distance, low), both(count, kept))(*parts)
+        near, far = call(
+            functools.partial(split_kernel, distance), both(blocks // distance // 2)
+        )(*parts)
         parts = (near, exchanged(far, "tm", distance))
-        low = count
         distance *= 2
-    own = call(add_kernel, jax.ShapeDtypeStruct((kept, channels), f32))(*parts)
-    below = exchanged(own, "height", 1)
-    own = call(half_kernel, jax.ShapeDtypeStruct((half, channels), f32))(own, below)
-    beside = exchanged(own, "width", 1)
+    share = both(1)[0]
+    own = call(add_kernel, share)(*parts)
+    got = exchanged(own, "height", 1)
+    total = call(add_kernel, share)(own, got)
+    beside = exchanged(total, "width", 1)
     return call(
         whole_kernel,
         jax.ShapeDtypeStruct((rows, channels), f32),
         out_specs=pl.BlockSpec((rows, channels), lambda: (0, 0)),
-    )(own, beside)
+    )(own, got, beside)
 
 
 def group_matrix(rows, cols, row_width, col_width):

time: 57.3 us -> 54.8 us (0.956)
  starting transfers between devices: 20.7 us -> 17.7 us
    ppermute x13 -> x12, starting transfers between devices: 16.5 us -> 14 us  [exchanged(): return lax.ppermute(value, axis, [(i, i ^ distance) for i in range(count)])]
    ppermute x13 -> x12, waiting for transfers between devices: 17.9 us -> 18.2 us  [exchanged(): return lax.ppermute(value, axis, [(i, i ^ distance) for i in range(count)])]
    pallas_call x14 -> x13, Pallas kernels: 11.7 us -> 11.8 us  [run(): pl.pallas_call(kernel, out_shape=out_shape, in_specs=in_specs or [here] *...]
  transfers between devices with their start and end apart: 17 -> 16, of which waited for: 11 -> 11; matrix products, arithmetic and copies ran while one was open for 0% -> 0% of each run, Pallas kernels for 17% -> 18%
where the time goes in v6:
time: 54.8 us; the launch traced here: 54.5 us
  waiting for transfers between devices  23.2 us (42%)
  starting transfers between devices  17.7 us (32%)
  Pallas kernels  11.8 us (22%)
  local copies, waits for them, and re-layouts  1.06 us (2%)
  between operations  0.78 us (1%)
    ppermute x12, waiting for transfers between devices, exchanged(): return lax.ppermute(value, axis, [(i, i ^ distance) for i in range(count)])  18.2 us
    ppermute x12, starting transfers between devices, exchanged(): return lax.ppermute(value, axis, [(i, i ^ distance) for i in range(count)])  14 us
    pallas_call x13, Pallas kernels, run(): pl.pallas_call(kernel, out_shape=out_shape, in_specs=in_specs or [here] *...  11.8 us
    ppermute x2, waiting for transfers between devices, shifted(): lax.ppermute(value, axis, [(source, source + steps) for source in range(i...  2.83 us
    ppermute x2, starting transfers between devices, shifted(): lax.ppermute(value, axis, [(source, source + steps) for source in range(i...  2.58 us
    ppermute x1, waiting for transfers between devices, rims(): lax.ppermute(corner, ('height', 'width'), [(i, 3 - i) for i in range(4)])  1.21 us
  transfers between devices with their start and end apart: 16, of which 11 were waited for; matrix products, arithmetic and copies ran while one was open for 0% of the time, Pallas kernels for 18%

profile of v6, /device:TPU:0, one launch (start us, length us, event | category | flops | bytes accessed | tf_op | source)
XLA Modules:
  0.0 54.5 jit_solution(12210769715247762179)
XLA Ops:
  0.6 0.0 copy-start.1
  0.6 1.0 %copy-done.1 = bf16[4,16,32,128]{3,2,1,0:T(8,128)(2,1)S(1)} copy-done((bf16[4,16,32,128]{3,2,1,0:T(8,128)(2,1)S(1)}, bf16[4,16,32,128]{3,2,1,0:T(8,128)(2,1)}, u32[]{:S(2)}) %copy-start.1) | copy-done | bytes 524312
  1.7 0.1 shard_map.96
  1.8 1.3 %collective-permute-start.3 = (bf16[2,16,32,128]{3,2,1,0:T(8,128)(2,1)S(1)}, bf16[2,16,32,128]{3,2,1,0:T(8,128)(2,1)S(1)}, u32[]{:S(2)}, u32[]{:S(2)}) collective-permute-start(bf16[2,16,32,128]{3,2,1,0:T(8,128)(2,1)S(1)} %get-tuple-element.33), channel_id=1, source_target_pairs={{4,0},{8,4},{12,8},{16,12},{20,16},{24,20},{28,24},{5,1},{9,5},{13... | collective-permute-start | bytes 786440 | tf_op jit(solution)/shard_map/ppermute | solution.py:24
  3.1 3.1 %collective-permute-start = (bf16[4,32,128]{2,1,0:T(8,128)(2,1)S(1)}, bf16[4,32,128]{2,1,0:T(8,128)(2,1)S(1)}, u32[]{:S(2)}, u32[]{:S(2)}) collective-permute-start(bf16[4,32,128]{2,1,0:T(8,128)(2,1)S(1)} %get-tuple-element.28), channel_id=1, source_target_pairs={{0,2},{2,0},{1,3},{3,1},{4,6},{6,4},{5,7},{7,5},{8,10},{10,8},{9,1... | collective-permute-start | bytes 98312 | tf_op jit(solution)/shard_map/ppermute | solution.py:18
  6.1 0.0 collective-permute-start.1
  6.1 0.2 collective-permute-start.2
  6.3 1.6 %shard_map.95 = (bf16[128,2048]{1,0:T(8,128)(2,1)S(1)}, f32[10,128]{1,0:T(8,128)S(1)}) custom-call(bf16[4,16,32,128]{3,2,1,0:T(8,128)(2,1)} %refs_5_.1, f32[4,32]{1,0:T(4,128)} %mean_hbm.1, f32[4,32]{1,0:T(4,128)} %rstd_hbm.1, f32[1,128]{1,0:T(1,128)} %bitcast.2, f32[1,128]{1,0:T(1,128)} %bitcast.3), custom_call_target="tpu_custom_call" | custom-call | flops 5242880 | bytes 1048576 | tf_op jit(solution)/shard_map/pallas_call | solution.py:454
  7.9 1.2 %collective-permute-done.2.refs_3_.corner_ref = bf16[4,128]{1,0:T(4,128)(2,1)S(1)} collective-permute-done((bf16[4,128]{1,0:T(4,128)(2,1)S(1)}, bf16[4,128]{1,0:T(4,128)(2,1)S(1)}, u32[]{:S(2)}, u32[]{:S(2)}) %collective-permute-start.2) | collective-permute-done | bytes 1056 | tf_op jit(solution)/shard_map/ppermute | solution.py:495
  9.1 0.0 collective-permute-done.1.refs_2_.col_ref
  9.1 0.0 collective-permute-done.refs_1_.row_ref
  9.1 1.3 %collective-permute-start.4 = (bf16[2,49,128]{2,1,0:T(8,128)(2,1)S(1)}, bf16[2,49,128]{2,1,0:T(8,128)(2,1)S(1)}, u32[]{:S(2)}, u32[]{:S(2)}) collective-permute-start(bf16[2,49,128]{2,1,0:T(8,128)(2,1)S(1)} %shard_map.98), channel_id=1, source_target_pairs={{4,0},{8,4},{12,8},{16,12},{20,16},{24,20},{28,24},{5,1},{9,5},{13... | collective-permute-start | bytes 75272 | tf_op jit(solution)/shard_map/ppermute | solution.py:24
  10.4 2.5 %shard_map.97 = (bf16[4,18,32,384]{3,2,1,0:T(8,128)(2,1)S(1)}, f32[3456,128]{1,0:T(8,128)S(1)}) custom-call(bf16[128,2048]{1,0:T(8,128)(2,1)S(1)} %get-tuple-element.26.act_ref, bf16[4,16,32,128]{3,2,1,0:T(8,128)(2,1)S(1)} %get-tuple-element.27.refs_0_, bf16[4,32,128]{2,1,0:T(8,128)(2,1)S(1)} %collective-permute-done.refs_1_.row_ref, ...), custom_call_target="tpu_custom_call" | custom-call | flops 1358954496 | bytes 4194304 | tf_op jit(solution)/shard_map/pallas_call | solution.py:454
  12.9 2.8 %collective-permute-done.4.refs_1_ = bf16[2,49,128]{2,1,0:T(8,128)(2,1)S(1)} collective-permute-done((bf16[2,49,128]{2,1,0:T(8,128)(2,1)S(1)}, bf16[2,49,128]{2,1,0:T(8,128)(2,1)S(1)}, u32[]{:S(2)}, u32[]{:S(2)}) %collective-permute-start.4) | collective-permute-done | bytes 25120 | tf_op jit(solution)/shard_map/ppermute | solution.py:24
  15.7 0.0 collective-permute-done.3.refs_0_
  15.7 1.1 %shard_map.99 = (bf16[2,18,32,384]{3,2,1,0:T(8,128)(2,1)S(1)}, f32[8,216,128]{2,1,0:T(8,128)S(1)}, f32[8,216,128]{2,1,0:T(8,128)S(1)}) custom-call(bf16[128,2048]{1,0:T(8,128)(2,1)S(1)} %get-tuple-element.26.act_ref, f32[3456,128]{1,0:T(8,128)S(1)} %get-tuple-element.32.near_sum_ref, bf16[2,16,32,128]{3,2,1,0:T(8,128)(2,1)S(1)} %collective-permute-done.3.refs_0_, ...), custom_call_target="tpu_custom_call" | custom-call | flops 452984832 | bytes 4194304 | tf_op jit(solution)/shard_map/pallas_call | solution.py:454
  16.9 0.0 copy-start
  16.9 0.0 copy-start.3
  16.9 0.0 copy-start.4
  16.9 0.2 collective-permute-start.8
  17.1 2.3 %collective-permute-done.8.got_ref = f32[8,216,128]{2,1,0:T(8,128)S(1)} collective-permute-done((f32[8,216,128]{2,1,0:T(8,128)S(1)}, f32[8,216,128]{2,1,0:T(8,128)S(1)}, u32[]{:S(2)}, u32[]{:S(2)}) %collective-permute-start.8) | collective-permute-done | bytes 884768 | tf_op jit(solution)/shard_map/ppermute | solution.py:18
  19.4 0.1 shard_map.102
  19.5 2.9 %collective-permute-start.9 = (bf16[2,216,128]{2,1,0:T(8,128)(2,1)S(1)}, bf16[2,216,128]{2,1,0:T(8,128)(2,1)S(1)}, u32[]{:S(2)}, u32[]{:S(2)}) collective-permute-start(bf16[2,216,128]{2,1,0:T(8,128)(2,1)S(1)} %get-tuple-element.41), channel_id=1, source_target_pairs={{0,4},{4,0},{8,12},{12,8},{16,20},{20,16},{24,28},{28,24},{1,5},{5... | collective-permute-start | bytes 331784 | tf_op jit(solution)/shard_map/ppermute | solution.py:18
  22.5 1.6 %collective-permute-start.10 = (bf16[2,216,128]{2,1,0:T(8,128)(2,1)S(1)}, bf16[2,216,128]{2,1,0:T(8,128)(2,1)S(1)}, u32[]{:S(2)}, u32[]{:S(2)}) collective-permute-start(bf16[2,216,128]{2,1,0:T(8,128)(2,1)S(1)} %get-tuple-element.43), channel_id=1, source_target_pairs={{0,8},{4,12},{8,0},{12,4},{16,24},{20,28},{24,16},{28,20},{1,9},{5... | collective-permute-start | bytes 331784 | tf_op jit(solution)/shard_map/ppermute | solution.py:18
  24.0 1.8 %collective-permute-done.9.low_got_ref = bf16[2,216,128]{2,1,0:T(8,128)(2,1)S(1)} collective-permute-done((bf16[2,216,128]{2,1,0:T(8,128)(2,1)S(1)}, bf16[2,216,128]{2,1,0:T(8,128)(2,1)S(1)}, u32[]{:S(2)}, u32[]{:S(2)}) %collective-permute-start.9) | collective-permute-done | bytes 110624 | tf_op jit(solution)/shard_map/ppermute | solution.py:18
  25.8 1.5 %collective-permute-done.10.high_got_ref = bf16[2,216,128]{2,1,0:T(8,128)(2,1)S(1)} collective-permute-done((bf16[2,216,128]{2,1,0:T(8,128)(2,1)S(1)}, bf16[2,216,128]{2,1,0:T(8,128)(2,1)S(1)}, u32[]{:S(2)}, u32[]{:S(2)}) %collective-permute-start.10) | collective-permute-done | bytes 110624 | tf_op jit(solution)/shard_map/ppermute | solution.py:18
  27.3 0.1 shard_map.103
  27.3 1.6 %collective-permute-start.11 = (bf16[1,216,128]{2,1,0:T(8,128)(2,1)S(1)}, bf16[1,216,128]{2,1,0:T(8,128)(2,1)S(1)}, u32[]{:S(2)}, u32[]{:S(2)}) collective-permute-start(bf16[1,216,128]{2,1,0:T(8,128)(2,1)S(1)} %get-tuple-element.45), channel_id=1, source_target_pairs={{0,8},{4,12},{8,0},{12,4},{16,24},{20,28},{24,16},{28,20},{1,9},{5... | collective-permute-start | bytes 165896 | tf_op jit(solution)/shard_map/ppermute | solution.py:18
  29.0 0.5 collective-permute-start.12
  29.5 2.1 %collective-permute-done.11.refs_1_ = bf16[1,216,128]{2,1,0:T(8,128)(2,1)S(1)} collective-permute-done((bf16[1,216,128]{2,1,0:T(8,128)(2,1)S(1)}, bf16[1,216,128]{2,1,0:T(8,128)(2,1)S(1)}, u32[]{:S(2)}, u32[]{:S(2)}) %collective-permute-start.11) | collective-permute-done | bytes 55328 | tf_op jit(solution)/shard_map/ppermute | solution.py:18
  31.6 1.6 %collective-permute-done.12.refs_3_ = bf16[1,216,128]{2,1,0:T(8,128)(2,1)S(1)} collective-permute-done((bf16[1,216,128]{2,1,0:T(8,128)(2,1)S(1)}, bf16[1,216,128]{2,1,0:T(8,128)(2,1)S(1)}, u32[]{:S(2)}, u32[]{:S(2)}) %collective-permute-start.12) | collective-permute-done | bytes 55328 | tf_op jit(solution)/shard_map/ppermute | solution.py:18
  33.2 2.0 %collective-permute-start.13 = (bf16[1,216,128]{2,1,0:T(8,128)(2,1)S(1)}, bf16[1,216,128]{2,1,0:T(8,128)(2,1)S(1)}, u32[]{:S(2)}, u32[]{:S(2)}) collective-permute-start(bf16[1,216,128]{2,1,0:T(8,128)(2,1)S(1)} %get-tuple-element.49), channel_id=1, source_target_pairs={{0,16},{4,20},{8,24},{12,28},{16,0},{20,4},{24,8},{28,12},{1,17},{... | collective-permute-start | bytes 165896 | tf_op jit(solution)/shard_map/ppermute | solution.py:18
  35.2 3.6 %collective-permute-done.13.got_ref = bf16[1,216,128]{2,1,0:T(8,128)(2,1)S(1)} collective-permute-done((bf16[1,216,128]{2,1,0:T(8,128)(2,1)S(1)}, bf16[1,216,128]{2,1,0:T(8,128)(2,1)S(1)}, u32[]{:S(2)}, u32[]{:S(2)}) %collective-permute-start.13) | collective-permute-done | bytes 55328 | tf_op jit(solution)/shard_map/ppermute | solution.py:18
  38.8 0.8 %collective-permute-start.14 = (f32[1,216,128]{2,1,0:T(8,128)S(1)}, f32[1,216,128]{2,1,0:T(8,128)S(1)}, u32[]{:S(2)}, u32[]{:S(2)}) collective-permute-start(f32[1,216,128]{2,1,0:T(8,128)S(1)} %shard_map.105.own_ref), channel_id=1, source_target_pairs={{0,2},{2,0},{1,3},{3,1},{4,6},{6,4},{5,7},{7,5},{8,10},{10,8},{9,1... | collective-permute-start | bytes 331784 | tf_op jit(solution)/shard_map/ppermute | solution.py:18
  39.6 4.0 %collective-permute-done.14.got_ref = f32[1,216,128]{2,1,0:T(8,128)S(1)} collective-permute-done((f32[1,216,128]{2,1,0:T(8,128)S(1)}, f32[1,216,128]{2,1,0:T(8,128)S(1)}, u32[]{:S(2)}, u32[]{:S(2)}) %collective-permute-start.14) | collective-permute-done | bytes 110624 | tf_op jit(solution)/shard_map/ppermute | solution.py:18
  43.6 0.1 collective-permute-start.15
  43.7 0.0 copy-done
  43.7 0.0 copy-done.3
  43.7 0.0 copy-done.4
  43.7 0.0 copy-start.2
  43.7 4.2 %shard_map.100 = (f32[4,16,32,128]{3,2,1,0:T(8,128)S(1)}, f32[8,128]{1,0:T(8,128)S(1)}) custom-call(bf16[4,18,32,384]{3,2,1,0:T(8,128)(2,1)S(1)} %get-tuple-element.31.near_ref, bf16[2,18,32,384]{3,2,1,0:T(8,128)(2,1)S(1)} %get-tuple-element.34.far_ref, bf16[3,3,3,128,128]{4,3,2,1,0:T(8,128)(2,1)S(1)} %copy-done.3, bf16[2,16,32,128]{3,2,1,0:T(8,128)(2,1)S(1)} %copy-done.4, ...), custom_call_target="tpu_custom_call" | custom-call | flops 1811939328 | bytes 8388608 | tf_op jit(solution)/shard_map/pallas_call | solution.py:454
  47.9 0.9 %collective-permute-start.7 = (f32[8,128]{1,0:T(8,128)S(1)}, f32[8,128]{1,0:T(8,128)S(1)}, u32[]{:S(2)}, u32[]{:S(2)}) collective-permute-start(f32[8,128]{1,0:T(8,128)S(1)} %get-tuple-element.36.refs_0_), channel_id=1, source_target_pairs={{0,3},{1,2},{2,1},{3,0},{4,7},{5,6},{6,5},{7,4},{8,11},{9,10},{10,... | collective-permute-start | bytes 12296 | tf_op jit(solution)/shard_map/ppermute | solution.py:595
  48.8 1.3 %collective-permute-start.6 = (f32[8,128]{1,0:T(8,128)S(1)}, f32[8,128]{1,0:T(8,128)S(1)}, u32[]{:S(2)}, u32[]{:S(2)}) collective-permute-start(f32[8,128]{1,0:T(8,128)S(1)} %get-tuple-element.36.refs_0_), channel_id=1, source_target_pairs={{0,2},{2,0},{1,3},{3,1},{4,6},{6,4},{5,7},{7,5},{8,10},{10,8},{9,1... | collective-permute-start | bytes 12296 | tf_op jit(solution)/shard_map/ppermute | solution.py:18
  50.1 0.0 collective-permute-start.5
  50.1 0.9 %collective-permute-done.7.refs_3_ = f32[8,128]{1,0:T(8,128)S(1)} collective-permute-done((f32[8,128]{1,0:T(8,128)S(1)}, f32[8,128]{1,0:T(8,128)S(1)}, u32[]{:S(2)}, u32[]{:S(2)}) %collective-permute-start.7) | collective-permute-done | bytes 4128 | tf_op jit(solution)/shard_map/ppermute | solution.py:595
  51.0 1.4 %collective-permute-done.6.refs_2_ = f32[8,128]{1,0:T(8,128)S(1)} collective-permute-done((f32[8,128]{1,0:T(8,128)S(1)}, f32[8,128]{1,0:T(8,128)S(1)}, u32[]{:S(2)}, u32[]{:S(2)}) %collective-permute-start.6) | collective-permute-done | bytes 4128 | tf_op jit(solution)/shard_map/ppermute | solution.py:18
  52.4 0.0 collective-permute-done.5.refs_1_
  52.4 0.0 copy-done.2
  52.4 1.4 %shard_map.101 = bf16[4,16,32,128]{3,2,1,0:T(8,128)(2,1)} custom-call(f32[8,128]{1,0:T(8,128)S(1)} %get-tuple-element.36.refs_0_, f32[8,128]{1,0:T(8,128)S(1)} %collective-permute-done.5.refs_1_, f32[8,128]{1,0:T(8,128)S(1)} %collective-permute-done.6.refs_2_, f32[8,128]{1,0:T(8,128)S(1)} %collective-permute-done.7.refs_3_, ...), custom_call_target="tpu_custom_call" | custom-call | flops 5242880 | bytes 2621440 | tf_op jit(solution)/shard_map/pallas_call | solution.py:454
  53.8 0.0 collective-permute-done.15.beside_ref
  53.8 0.7 %shard_map.107 = f32[432,128]{1,0:T(8,128)} custom-call(f32[1,216,128]{2,1,0:T(8,128)S(1)} %shard_map.105.own_ref, f32[1,216,128]{2,1,0:T(8,128)S(1)} %collective-permute-done.14.got_ref, f32[1,216,128]{2,1,0:T(8,128)S(1)} %collective-permute-done.15.beside_ref), custom_call_target="tpu_custom_call" | custom-call | tf_op jit(solution)/shard_map/pallas_call | solution.py:454
  (4 shorter events, 0.1 us)
Async XLA Ops:
  0.6 1.0 %copy-start.1 = (bf16[4,16,32,128]{3,2,1,0:T(8,128)(2,1)S(1)}, bf16[4,16,32,128]{3,2,1,0:T(8,128)(2,1)}, u32[]{:S(2)}) copy-start(bf16[4,16,32,128]{3,2,1,0:T(8,128)(2,1)} %refs_6_.1) | copy-start | bytes 1572868
  1.8 14.0 %collective-permute-start.3 = (bf16[2,16,32,128]{3,2,1,0:T(8,128)(2,1)S(1)}, bf16[2,16,32,128]{3,2,1,0:T(8,128)(2,1)S(1)}, u32[]{:S(2)}, u32[]{:S(2)}) collective-permute-start(bf16[2,16,32,128]{3,2,1,0:T(8,128)(2,1)S(1)} %get-tuple-element.33), channel_id=1, source_target_pairs={{4,0},{8,4},{12,8},{16,12},{20,16},{24,20},{28,24},{5,1},{9,5},{13... | collective-permute-start | bytes 786440 | tf_op jit(solution)/shard_map/ppermute | solution.py:24
  3.1 6.1 %collective-permute-start = (bf16[4,32,128]{2,1,0:T(8,128)(2,1)S(1)}, bf16[4,32,128]{2,1,0:T(8,128)(2,1)S(1)}, u32[]{:S(2)}, u32[]{:S(2)}) collective-permute-start(bf16[4,32,128]{2,1,0:T(8,128)(2,1)S(1)} %get-tuple-element.28), channel_id=1, source_target_pairs={{0,2},{2,0},{1,3},{3,1},{4,6},{6,4},{5,7},{7,5},{8,10},{10,8},{9,1... | collective-permute-start | bytes 98312 | tf_op jit(solution)/shard_map/ppermute | solution.py:18
  6.1 3.0 %collective-permute-start.1 = (bf16[4,16,128]{2,1,0:T(8,128)(2,1)S(1)}, bf16[4,16,128]{2,1,0:T(8,128)(2,1)S(1)}, u32[]{:S(2)}, u32[]{:S(2)}) collective-permute-start(bf16[4,16,128]{2,1,0:T(8,128)(2,1)S(1)} %get-tuple-element.29), channel_id=1, source_target_pairs={{0,1},{1,0},{2,3},{3,2},{4,5},{5,4},{6,7},{7,6},{8,9},{9,8},{10,11... | collective-permute-start | bytes 49160 | tf_op jit(solution)/shard_map/ppermute | solution.py:18
  6.1 3.0 %collective-permute-start.2 = (bf16[4,128]{1,0:T(4,128)(2,1)S(1)}, bf16[4,128]{1,0:T(4,128)(2,1)S(1)}, u32[]{:S(2)}, u32[]{:S(2)}) collective-permute-start(bf16[4,128]{1,0:T(4,128)(2,1)S(1)} %get-tuple-element.30), channel_id=1, source_target_pairs={{0,3},{1,2},{2,1},{3,0},{4,7},{5,6},{6,5},{7,4},{8,11},{9,10},{10,... | collective-permute-start | bytes 3080 | tf_op jit(solution)/shard_map/ppermute | solution.py:495
  9.1 6.6 %collective-permute-start.4 = (bf16[2,49,128]{2,1,0:T(8,128)(2,1)S(1)}, bf16[2,49,128]{2,1,0:T(8,128)(2,1)S(1)}, u32[]{:S(2)}, u32[]{:S(2)}) collective-permute-start(bf16[2,49,128]{2,1,0:T(8,128)(2,1)S(1)} %shard_map.98), channel_id=1, source_target_pairs={{4,0},{8,4},{12,8},{16,12},{20,16},{24,20},{28,24},{5,1},{9,5},{13... | collective-permute-start | bytes 75272 | tf_op jit(solution)/shard_map/ppermute | solution.py:24
  16.9 26.8 %copy-start = (bf16[4,16,32,128]{3,2,1,0:T(8,128)(2,1)S(1)}, bf16[4,16,32,128]{3,2,1,0:T(8,128)(2,1)}, u32[]{:S(2)}) copy-start(bf16[4,16,32,128]{3,2,1,0:T(8,128)(2,1)} %refs_5_.1) | copy-start | bytes 1572868
  16.9 26.8 %copy-start.3 = (bf16[3,3,3,128,128]{4,3,2,1,0:T(8,128)(2,1)S(1)}, bf16[3,3,3,128,128]{4,3,2,1,0:T(8,128)(2,1)}, u32[]{:S(2)}) copy-start(bf16[3,3,3,128,128]{4,3,2,1,0:T(8,128)(2,1)} %weight_ref.1) | copy-start | bytes 2654212
  16.9 26.8 %copy-start.4 = (bf16[2,16,32,128]{3,2,1,0:T(8,128)(2,1)S(1)}, bf16[2,16,32,128]{3,2,1,0:T(8,128)(2,1)}, u32[]{:S(2)}) copy-start(bf16[2,16,32,128]{3,2,1,0:T(8,128)(2,1)} %future_ref.1) | copy-start | bytes 786436
  16.9 2.5 %collective-permute-start.8 = (f32[8,216,128]{2,1,0:T(8,128)S(1)}, f32[8,216,128]{2,1,0:T(8,128)S(1)}, u32[]{:S(2)}, u32[]{:S(2)}) collective-permute-start(f32[8,216,128]{2,1,0:T(8,128)S(1)} %get-tuple-element.39), channel_id=1, source_target_pairs={{0,1},{1,0},{2,3},{3,2},{4,5},{5,4},{6,7},{7,6},{8,9},{9,8},{10,11... | collective-permute-start | bytes 2654216 | tf_op jit(solution)/shard_map/ppermute | solution.py:18
  19.5 6.3 %collective-permute-start.9 = (bf16[2,216,128]{2,1,0:T(8,128)(2,1)S(1)}, bf16[2,216,128]{2,1,0:T(8,128)(2,1)S(1)}, u32[]{:S(2)}, u32[]{:S(2)}) collective-permute-start(bf16[2,216,128]{2,1,0:T(8,128)(2,1)S(1)} %get-tuple-element.41), channel_id=1, source_target_pairs={{0,4},{4,0},{8,12},{12,8},{16,20},{20,16},{24,28},{28,24},{1,5},{5... | collective-permute-start | bytes 331784 | tf_op jit(solution)/shard_map/ppermute | solution.py:18
  22.5 4.8 %collective-permute-start.10 = (bf16[2,216,128]{2,1,0:T(8,128)(2,1)S(1)}, bf16[2,216,128]{2,1,0:T(8,128)(2,1)S(1)}, u32[]{:S(2)}, u32[]{:S(2)}) collective-permute-start(bf16[2,216,128]{2,1,0:T(8,128)(2,1)S(1)} %get-tuple-element.43), channel_id=1, source_target_pairs={{0,8},{4,12},{8,0},{12,4},{16,24},{20,28},{24,16},{28,20},{1,9},{5... | collective-permute-start | bytes 331784 | tf_op jit(solution)/shard_map/ppermute | solution.py:18
  27.3 4.2 %collective-permute-start.11 = (bf16[1,216,128]{2,1,0:T(8,128)(2,1)S(1)}, bf16[1,216,128]{2,1,0:T(8,128)(2,1)S(1)}, u32[]{:S(2)}, u32[]{:S(2)}) collective-permute-start(bf16[1,216,128]{2,1,0:T(8,128)(2,1)S(1)} %get-tuple-element.45), channel_id=1, source_target_pairs={{0,8},{4,12},{8,0},{12,4},{16,24},{20,28},{24,16},{28,20},{1,9},{5... | collective-permute-start | bytes 165896 | tf_op jit(solution)/shard_map/ppermute | solution.py:18
  29.0 4.2 %collective-permute-start.12 = (bf16[1,216,128]{2,1,0:T(8,128)(2,1)S(1)}, bf16[1,216,128]{2,1,0:T(8,128)(2,1)S(1)}, u32[]{:S(2)}, u32[]{:S(2)}) collective-permute-start(bf16[1,216,128]{2,1,0:T(8,128)(2,1)S(1)} %get-tuple-element.47), channel_id=1, source_target_pairs={{0,4},{4,0},{8,12},{12,8},{16,20},{20,16},{24,28},{28,24},{1,5},{5... | collective-permute-start | bytes 165896 | tf_op jit(solution)/shard_map/ppermute | solution.py:18
  33.2 5.6 %collective-permute-start.13 = (bf16[1,216,128]{2,1,0:T(8,128)(2,1)S(1)}, bf16[1,216,128]{2,1,0:T(8,128)(2,1)S(1)}, u32[]{:S(2)}, u32[]{:S(2)}) collective-permute-start(bf16[1,216,128]{2,1,0:T(8,128)(2,1)S(1)} %get-tuple-element.49), channel_id=1, source_target_pairs={{0,16},{4,20},{8,24},{12,28},{16,0},{20,4},{24,8},{28,12},{1,17},{... | collective-permute-start | bytes 165896 | tf_op jit(solution)/shard_map/ppermute | solution.py:18
  38.8 4.8 %collective-permute-start.14 = (f32[1,216,128]{2,1,0:T(8,128)S(1)}, f32[1,216,128]{2,1,0:T(8,128)S(1)}, u32[]{:S(2)}, u32[]{:S(2)}) collective-permute-start(f32[1,216,128]{2,1,0:T(8,128)S(1)} %shard_map.105.own_ref), channel_id=1, source_target_pairs={{0,2},{2,0},{1,3},{3,1},{4,6},{6,4},{5,7},{7,5},{8,10},{10,8},{9,1... | collective-permute-start | bytes 331784 | tf_op jit(solution)/shard_map/ppermute | solution.py:18
  43.6 10.2 %collective-permute-start.15 = (f32[1,216,128]{2,1,0:T(8,128)S(1)}, f32[1,216,128]{2,1,0:T(8,128)S(1)}, u32[]{:S(2)}, u32[]{:S(2)}) collective-permute-start(f32[1,216,128]{2,1,0:T(8,128)S(1)} %shard_map.106), channel_id=1, source_target_pairs={{0,1},{1,0},{2,3},{3,2},{4,5},{5,4},{6,7},{7,6},{8,9},{9,8},{10,11... | collective-permute-start | bytes 331784 | tf_op jit(solution)/shard_map/ppermute | solution.py:18
  43.7 8.7 %copy-start.2 = (bf16[4,16,32,128]{3,2,1,0:T(8,128)(2,1)S(1)}, bf16[4,16,32,128]{3,2,1,0:T(8,128)(2,1)}, u32[]{:S(2)}) copy-start(bf16[4,16,32,128]{3,2,1,0:T(8,128)(2,1)} %refs_6_.1) | copy-start | bytes 1572868
  47.9 3.1 %collective-permute-start.7 = (f32[8,128]{1,0:T(8,128)S(1)}, f32[8,128]{1,0:T(8,128)S(1)}, u32[]{:S(2)}, u32[]{:S(2)}) collective-permute-start(f32[8,128]{1,0:T(8,128)S(1)} %get-tuple-element.36.refs_0_), channel_id=1, source_target_pairs={{0,3},{1,2},{2,1},{3,0},{4,7},{5,6},{6,5},{7,4},{8,11},{9,10},{10,... | collective-permute-start | bytes 12296 | tf_op jit(solution)/shard_map/ppermute | solution.py:595
  48.8 3.6 %collective-permute-start.6 = (f32[8,128]{1,0:T(8,128)S(1)}, f32[8,128]{1,0:T(8,128)S(1)}, u32[]{:S(2)}, u32[]{:S(2)}) collective-permute-start(f32[8,128]{1,0:T(8,128)S(1)} %get-tuple-element.36.refs_0_), channel_id=1, source_target_pairs={{0,2},{2,0},{1,3},{3,1},{4,6},{6,4},{5,7},{7,5},{8,10},{10,8},{9,1... | collective-permute-start | bytes 12296 | tf_op jit(solution)/shard_map/ppermute | solution.py:18
  50.1 2.3 %collective-permute-start.5 = (f32[8,128]{1,0:T(8,128)S(1)}, f32[8,128]{1,0:T(8,128)S(1)}, u32[]{:S(2)}, u32[]{:S(2)}) collective-permute-start(f32[8,128]{1,0:T(8,128)S(1)} %get-tuple-element.36.refs_0_), channel_id=1, source_target_pairs={{0,1},{1,0},{2,3},{3,2},{4,5},{5,4},{6,7},{7,6},{8,9},{9,8},{10,11... | collective-permute-start | bytes 12296 | tf_op jit(solution)/shard_map/ppermute | solution.py:18

commit v7 on v6

--- a/solution.py
+++ b/solution.py
@@ -164,21 +164,38 @@
     return exact_dot(value, group_matrix(groups, channels, 1, channels // groups))
 
 
-def cut_kernel(grad_ref, halo_ref, row_ref, col_ref, corner_ref, copy_ref):
+def cut_kernel(*refs):
+    sources, (halo_ref, row_ref, col_ref, corner_ref), held, sems = (
+        refs[:6],
+        refs[6:10],
+        refs[10:-1],
+        refs[-1],
+    )
+    extra = halo_ref.shape[0]
+    pairs = [(sources[0].at[0:extra], halo_ref), *zip(sources, held)]
+    copies = [
+        pltpu.make_async_copy(source, target, sems.at[i])
+        for i, (source, target) in enumerate(pairs)
+    ]
+    for copy in copies:
+        copy.start()
+    for copy in copies:
+        copy.wait()
+    grad_ref, features_ref = held[:2]
     frames, rows, cols, _ = grad_ref.shape
-    copy_ref[...] = grad_ref[...]
-    halo_ref[...] = grad_ref[: halo_ref.shape[0]]
     row_at = (1 - lax.axis_index("height")) * (rows - 1)
+    taken = [grad_ref.at[f] for f in range(frames)]
+    taken += [features_ref.at[f] for f in range(frames - extra, frames)]
 
     def columns(at):
         corners = []
-        for f in range(frames):
-            col_ref[f] = grad_ref[f].astype(jnp.float32)[:, at].astype(jnp.bfloat16)
-            corners.append(grad_ref[f, row_at].astype(jnp.float32)[at : at + 1])
+        for i, ref in enumerate(taken):
+            col_ref[i] = ref[...].astype(jnp.float32)[:, at].astype(jnp.bfloat16)
+            corners.append(ref[row_at].astype(jnp.float32)[at : at + 1])
         corner_ref[...] = jnp.concatenate(corners, axis=0).astype(jnp.bfloat16)
 
-    for f in range(frames):
-        row_ref[f] = grad_ref[f, row_at]
+    for i, ref in enumerate(taken):
+        row_ref[i] = ref[row_at]
 
     @pl.when(lax.axis_index("width") == 0)
     def _():
@@ -197,30 +214,31 @@
         tail_ref[f, cols + rows :] = corner_ref[f : f + 1]
 
 
-def act_kernel(features_hbm, mean_hbm, rstd_hbm, gain_hbm, bias_hbm, act_ref, params_ref, *scratch):
-    buffers, sems = scratch[:5], scratch[5]
-    sources = (features_hbm, mean_hbm, rstd_hbm, gain_hbm, bias_hbm)
-    copies = [
-        pltpu.make_async_copy(source, buffer, sems.at[i])
-        for i, (source, buffer) in enumerate(zip(sources, buffers))
-    ]
-    for copy in copies:
-        copy.start()
-    for copy in copies:
-        copy.wait()
-    features_ref, mean_ref, rstd_ref, gain_ref, bias_ref = buffers
+def activation(value, params, frames, t):
+    centred = (value - params[t : t + 1]) * params[frames + t : frames + t + 1]
+    pre_act = centred * params[2 * frames : 2 * frames + 1]
+    pre_act = pre_act + params[2 * frames + 1 : 2 * frames + 2]
+    sig = jax.nn.sigmoid(pre_act)
+    return centred, pre_act, sig
+
+
+def act_kernel(
+    features_ref, mean_ref, rstd_ref, gain_ref, bias_ref, act_ref, last_ref, params_ref
+):
     frames, rows, cols, channels = features_ref.shape
     cells = rows * cols
     mean = per_channel(mean_ref[...], channels)
     rstd = per_channel(rstd_ref[...], channels)
-    gain, bias = gain_ref[...], bias_ref[...]
-    params_ref[...] = jnp.concatenate([mean, rstd, gain, bias], axis=0)
+    params = jnp.concatenate([mean, rstd, gain_ref[...], bias_ref[...]], axis=0)
+    params_ref[...] = params
     for t in range(frames):
         value = features_ref[t].astype(jnp.float32).reshape(cells, channels)
-        centred = (value - mean[t : t + 1]) * rstd[t : t + 1]
-        pre_act = centred * gain + bias
-        act = (pre_act * jax.nn.sigmoid(pre_act)).astype(jnp.bfloat16)
+        _, pre_act, sig = activation(value, params, frames, t)
+        act = (pre_act * sig).astype(jnp.bfloat16)
         act_ref[:, t * cells : (t + 1) * cells] = act.T
+        later = t - (frames - last_ref.shape[0])
+        if later >= 0:
+            last_ref[later] = act.reshape(rows, cols, channels)
 
 
 def fill_pair(stage_ref, inner_ref, row_of, col_of, corner_of):
@@ -294,11 +312,18 @@
 
 
 def near_kernel(scale, pair, extra, act_ref, *refs):
-    sources, (window_ref, sum_ref, stage_ref) = refs[:-3], refs[-3:]
+    sources, (window_ref, sum_ref, act_window_ref, stage_ref) = refs[:-4], refs[-4:]
     frames, rows_ext, cols, wide = window_ref.shape
     shape = (rows_ext - 2, cols, wide // 3)
     if pair:
-        grad_ref, row_ref, col_ref, corner_ref = sources
+        grad_ref, row_ref, col_ref, corner_ref, last_ref, params_ref = sources
+        params = params_ref[...]
+
+        def rim_act(value, f):
+            value = value.astype(jnp.float32)
+            _, pre_act, sig = activation(value, params, frames, frames - extra + f)
+            return (pre_act * sig).astype(jnp.bfloat16)
+
         fill_pair(
             stage_ref,
             grad_ref,
@@ -306,9 +331,20 @@
             lambda f: col_ref[f],
             lambda f: corner_ref[f : f + 1],
         )
+        widen(stage_ref, window_ref)
+        fill_pair(
+            stage_ref,
+            last_ref,
+            lambda f: rim_act(row_ref[frames + f], f),
+            lambda f: rim_act(col_ref[frames + f], f),
+            lambda f: rim_act(corner_ref[frames + f : frames + f + 1], f),
+        )
+        widen(stage_ref, act_window_ref)
     else:
         stage_ref[...] = sources[0][...].astype(jnp.float32)
-    widen(stage_ref, window_ref)
+        widen(stage_ref, window_ref)
+        stage_ref[:extra] = sources[1][...].astype(jnp.float32)
+        widen(stage_ref, act_window_ref)
 
     def put(at, value):
         sum_ref[at : at + value.shape[0], :] = value
@@ -319,17 +355,110 @@
         tap_sums(act_ref, scale, pairs, lambda f: window_ref.at[f], shape, lag_t, put)
 
 
-def far_kernel(rows_out, scale, pair, halves, frames, act_ref, near_sum_ref, *refs):
+def far_kernel(rows_out, scale, halves, frames, act_window_ref, near_sum_ref, halo_ref, *refs):
+    outs, sum_ref = refs[:-1], refs[-1]
+    extra, rows, cols, channels = halo_ref.shape
+    cells = rows * cols
+    flipped = [halo_ref[f].reshape(cells, channels).T for f in range(extra)]
+    for lag_t in range(extra):
+        ahead = extra - lag_t
+        pairs = [(t, t + ahead - frames) for t in range(frames) if t + ahead >= frames]
+        for lag_h in range(3):
+            acc = None
+            for t, f in pairs:
+                window = act_window_ref[t - (frames - extra), lag_h : lag_h + rows]
+                term = lax.dot_general(
+                    flipped[f],
+                    window.reshape(cells, 3 * channels),
+                    (((1,), (0,)), ((), ())),
+                    preferred_element_type=jnp.float32,
+                )
+                acc = term if acc is None else acc + term
+            for lag_w in range(3):
+                at = ((lag_t * 3 + lag_h) * 3 + lag_w) * channels
+                value = scale * acc[:, lag_w * channels : (lag_w + 1) * channels].T
+                sum_ref[at : at + channels, :] = near_sum_ref[at : at + channels, :] + value
+    done = extra * 9 * channels
+    sum_ref[done:, :] = near_sum_ref[done:, :]
+    if not halves:
+        outs[0][...] = sum_ref[...]
+        return
+    mine_ref, theirs_ref = outs
+    col_side = lax.axis_index("width")
+    half = rows_out // 2
+
+    def place(low_ref, high_ref):
+        for block in range(mine_ref.shape[0]):
+            at = block * rows_out
+            low_ref[block] = sum_ref[at : at + half, :]
+            high_ref[block] = sum_ref[at + half : at + rows_out, :]
+
+    @pl.when(col_side == 0)
+    def _():
+        place(mine_ref, theirs_ref)
+
+    @pl.when(col_side == 1)
+    def _():
+        place(theirs_ref, mine_ref)
+
+
+def conv_frames(window_of, weight_ref, future_ref, features_ref, params, span, scaled_ref, put):
+    frames, rows, cols, channels = features_ref.shape
+    cells = rows * cols
+    extra = weight_ref.shape[0] - 1
+    gain = params[2 * frames : 2 * frames + 1]
+    is_last = lax.axis_index("tm") == lax.axis_size("tm") - 1
+    for t in span:
+        acc = None
+        for lag_t in range(extra + 1):
+            for lag_h in range(3):
+                window = window_of(t + extra - lag_t)[2 - lag_h : 2 - lag_h + rows]
+                taps = jnp.concatenate(
+                    [weight_ref[lag_t, lag_h, 2 - e] for e in range(3)], axis=1
+                )
+                term = lax.dot_general(
+                    window.reshape(cells, 3 * channels),
+                    taps,
+                    (((1,), (1,)), ((), ())),
+                    preferred_element_type=jnp.float32,
+                )
+                acc = term if acc is None else acc + term
+        later = t - (frames - extra)
+        if later >= 0:
+            tail = future_ref[later].astype(jnp.float32).reshape(cells, channels)
+            acc = acc + jnp.where(is_last, tail, jnp.zeros_like(tail))
+        value = features_ref[t].astype(jnp.float32).reshape(cells, channels)
+        centred, pre_act, sig = activation(value, params, frames, t)
+        scaled = acc * sig * (1.0 + pre_act * (1.0 - sig)) * gain
+        scaled_ref[t - span[0]] = scaled.reshape(rows, cols, channels)
+        put(t, jnp.sum(scaled, axis=0, keepdims=True))
+        put(frames + t, jnp.sum(scaled * centred, axis=0, keepdims=True))
+
+
+def early_kernel(near_ref, weight_ref, features_ref, params_ref, scaled_ref, sums_ref):
+    sums_ref[...] = jnp.zeros_like(sums_ref)
+
+    def put(at, value):
+        sums_ref[at : at + 1, :] = value
+
+    conv_frames(
+        lambda f: near_ref.at[f],
+        weight_ref,
+        None,
+        features_ref,
+        params_ref[...],
+        range(scaled_ref.shape[0]),
+        scaled_ref,
+        put,
+    )
+
+
+def late_kernel(pair, early, *refs):
     count = 2 if pair else 1
-    sources, window_ref, outs, (stage_ref, sum_ref) = (
-        refs[:count],
-        refs[count],
-        refs[count + 1 : -2],
-        refs[-2:],
-    )
-    extra, rows_ext, cols, wide = window_ref.shape
-    rows = rows_ext - 2
-    channels = wide // 3
+    sources = refs[:count]
+    near_ref, weight_ref, future_ref, features_ref, params_ref = refs[count : count + 5]
+    before, (scaled_ref, sums_ref, window_ref, stage_ref) = refs[count + 5 : -4], refs[-4:]
+    frames, rows, cols, _ = features_ref.shape
     if pair:
         halo_ref, tail_ref = sources
         fill_pair(
@@ -342,94 +471,31 @@
     else:
         stage_ref[...] = sources[0][...].astype(jnp.float32)
     widen(stage_ref, window_ref)
+    if before:
+        sums_ref[...] = before[0][...]
 
     def put(at, value):
-        rows_at = slice(at, at + value.shape[0])
-        sum_ref[rows_at, :] = near_sum_ref[rows_at, :] + value
-
-    for lag_t in range(extra):
-        ahead = extra - lag_t
-        pairs = [(t, t + ahead - frames) for t in range(frames) if t + ahead >= frames]
-        tap_sums(
-            act_ref, scale, pairs, lambda f: window_ref.at[f], (rows, cols, channels), lag_t, put
-        )
-    done = extra * 9 * channels
-    sum_ref[done:, :] = near_sum_ref[done:, :]
-    if not halves:
-        outs[0][...] = sum_ref[...]
-        return
-    mine_ref, theirs_ref = outs
-    col_side = lax.axis_index("width")
-    half = rows_out // 2
-
-    def place(low_ref, high_ref):
-        for block in range(mine_ref.shape[0]):
-            at = block * rows_out
-            low_ref[block] = sum_ref[at : at + half, :]
-            high_ref[block] = sum_ref[at + half : at + rows_out, :]
-
-    @pl.when(col_side == 0)
-    def _():
-        place(mine_ref, theirs_ref)
-
-    @pl.when(col_side == 1)
-    def _():
-        place(theirs_ref, mine_ref)
-
-
-def conv_kernel(
-    near_ref,
-    far_ref,
-    weight_ref,
-    future_ref,
-    features_ref,
-    params_ref,
-    scaled_ref,
-    sums_ref,
-):
-    frames, rows, cols, channels = features_ref.shape
-    cells = rows * cols
-    wide = 3 * channels
-    mean = params_ref[0:frames]
-    rstd = params_ref[frames : 2 * frames]
-    gain = params_ref[2 * frames : 2 * frames + 1]
-    bias = params_ref[2 * frames + 1 : 2 * frames + 2]
-    is_last = lax.axis_index("tm") == lax.axis_size("tm") - 1
-    for t in range(frames):
-        acc = None
-        for lag_t in range(3):
-            for lag_h in range(3):
-                f = t + far_ref.shape[0] - lag_t
-                source = near_ref.at[f] if f < frames else far_ref.at[f - frames]
-                window = source[2 - lag_h : 2 - lag_h + rows]
-                taps = jnp.concatenate(
-                    [weight_ref[lag_t, lag_h, 2 - e] for e in range(3)], axis=1
-                )
-                term = lax.dot_general(
-                    window.reshape(cells, wide),
-                    taps,
-                    (((1,), (1,)), ((), ())),
-                    preferred_element_type=jnp.float32,
-                )
-                acc = term if acc is None else acc + term
-        later = t - (frames - future_ref.shape[0])
-        if later >= 0:
-            tail = future_ref[later].astype(jnp.float32).reshape(cells, channels)
-            acc = acc + jnp.where(is_last, tail, jnp.zeros_like(tail))
-        value = features_ref[t].astype(jnp.float32).reshape(cells, channels)
-        centred = (value - mean[t : t + 1]) * rstd[t : t + 1]
-        pre_act = centred * gain + bias
-        sig = jax.nn.sigmoid(pre_act)
-        scaled = acc * sig * (1.0 + pre_act * (1.0 - sig)) * gain
-        scaled_ref[t] = scaled.reshape(rows, cols, channels)
-        sums_ref[t : t + 1, :] = jnp.sum(scaled, axis=0, keepdims=True)
-        sums_ref[frames + t : frames + t + 1, :] = jnp.sum(
-            scaled * centred, axis=0, keepdims=True
-        )
+        sums_ref[at : at + 1, :] = value
+
+    conv_frames(
+        lambda f: near_ref.at[f] if f < frames else window_ref.at[f - frames],
+        weight_ref,
+        future_ref,
+        features_ref,
+        params_ref[...],
+        range(early, frames),
+        scaled_ref,
+        put,
+    )
 
 
 def final_kernel(groups, count, terms, *refs):
-    parts, (scaled_ref, features_ref, grad_ref, params_ref, out_ref) = refs[:terms], refs[terms:]
+    parts, scaled_refs, (features_ref, grad_ref, params_ref, out_ref) = (
+        refs[:terms],
+        refs[terms:-4],
+        refs[-4:],
+    )
+    scaled = [ref.at[t] for ref in scaled_refs for t in range(ref.shape[0])]
     frames, _, _, channels = features_ref.shape
     mean = params_ref[0:frames]
     rstd = params_ref[frames : 2 * frames]
@@ -443,7 +509,7 @@
         centred = (value - mean[t : t + 1]) * rstd[t : t + 1]
         first = means[t : t + 1]
         second = means[frames + t : frames + t + 1]
-        corrected = rstd[t : t + 1] * (scaled_ref[t] - first - centred * second)
+        corrected = rstd[t : t + 1] * (scaled[t][...] - first - centred * second)
         out_ref[t] = (grad_ref[t].astype(jnp.float32) + corrected).astype(jnp.bfloat16)
 
 
@@ -474,29 +540,31 @@
     return cells
 
 
-def rims(grad_out, extra):
-    frames, rows, cols, channels = grad_out.shape
+def rims(inputs, extra):
+    frames, rows, cols, channels = inputs[0].shape
 
     def piece(*shape):
-        return jax.ShapeDtypeStruct((*shape, channels), grad_out.dtype)
-
-    halo, row, col, corner, held = call(
+        return jax.ShapeDtypeStruct((*shape, channels), inputs[0].dtype)
+
+    halo, row, col, corner, *held = call(
         cut_kernel,
         (
             piece(extra, rows, cols),
-            piece(frames, cols),
-            piece(frames, rows),
-            piece(frames),
-            piece(frames, rows, cols),
+            piece(frames + extra, cols),
+            piece(frames + extra, rows),
+            piece(frames + extra),
+            *[jax.ShapeDtypeStruct(value.shape, value.dtype) for value in inputs],
         ),
-    )(grad_out)
+        scratch=(pltpu.SemaphoreType.DMA((len(inputs) + 1,)),),
+        in_specs=[pl.BlockSpec(memory_space=pltpu.HBM)] * len(inputs),
+    )(*[pltpu.with_memory_space_constraint(value, pltpu.HBM) for value in inputs])
     halo = shifted(halo, "tm", -1)
     row = exchanged(row, "height", 1)
     corner = lax.ppermute(corner, ("height", "width"), [(i, 3 - i) for i in range(4)])
     col = exchanged(col, "width", 1)
     packed = call(pack_kernel, piece(extra, cols + rows + 1))(row, col, corner)
     tail = shifted(packed, "tm", -1)
-    return (held, row, col, corner), (halo, tail)
+    return held, (row, col, corner), (halo, tail)
 
 
 def on_device(features, grad_out, mean_saved, rstd_saved, gain, bias, weight, future_cot):
@@ -513,63 +581,66 @@
     bias = bias.reshape(1, channels)
     pair = paired()
     halves = in_halves(blocks, rows_out)
-    f32 = jnp.float32
+    f32, bf16 = jnp.float32, jnp.bfloat16
+    work = 2 * taps * channels * channels * frames * cells
+    early = frames - extra
+
+    def shape(*dims, kind=f32):
+        return jax.ShapeDtypeStruct((*dims, channels), kind)
+
+    def window_shape(count):
+        return jax.ShapeDtypeStruct((count, rows + 2, cols, 3 * channels), bf16)
+
+    def stage_shape(count):
+        return pltpu.VMEM((count, rows + 2, cols + 2 * LEAD, channels), f32)
 
     if pair:
-        near_sources, far_sources = rims(grad_out, extra)
-    else:
-        padded = extended(grad_out, (("height", 1), ("width", 2)), 1)
-        sides = ((0, 0), (0, 0), (LEAD - 1, LEAD - 1), (0, 0))
-        near_sources = (jnp.pad(padded, sides),)
-        far_sources = (jnp.pad(shifted(padded[:extra], "tm", -1), sides),)
-
-    inputs = tuple(
-        pltpu.with_memory_space_constraint(value, pltpu.HBM)
-        for value in (features, mean_saved, rstd_saved, gain, bias)
-    )
-    act, params = call(
+        held, near_rims, (halo, tail) = rims(
+            (grad_out, features, mean_saved, rstd_saved, gain, bias), extra
+        )
+        grad_out, features, mean_saved, rstd_saved, gain, bias = held
+        late_sources = (halo, tail)
+
+    act, last, params = call(
         act_kernel,
         (
-            jax.ShapeDtypeStruct((channels, frames * cells), jnp.bfloat16),
-            jax.ShapeDtypeStruct((2 * frames + 2, channels), f32),
+            jax.ShapeDtypeStruct((channels, frames * cells), bf16),
+            shape(extra, rows, cols, kind=bf16),
+            shape(2 * frames + 2),
         ),
-        scratch=(
-            *[pltpu.VMEM(value.shape, value.dtype) for value in inputs],
-            pltpu.SemaphoreType.DMA((len(inputs),)),
-        ),
-        in_specs=[pl.BlockSpec(memory_space=pltpu.HBM)] * len(inputs),
         flops=20 * frames * cells * channels,
         moved=4 * frames * cells * channels,
-    )(*inputs)
-
-    def window_shape(count):
-        return jax.ShapeDtypeStruct((count, rows + 2, cols, 3 * channels), jnp.bfloat16)
-
-    def stage_shape(count):
-        return pltpu.VMEM((count, rows + 2, cols + 2 * LEAD, channels), f32)
-
-    work = 2 * taps * channels * channels * frames * cells
-    sum_shape = jax.ShapeDtypeStruct((taps * channels, channels), f32)
-    near_window, near_sum = call(
+    )(features, mean_saved, rstd_saved, gain, bias)
+
+    if pair:
+        near_sources = (grad_out, *near_rims, last, params)
+    else:
+        axes = (("height", 1), ("width", 2))
+        sides = ((0, 0), (0, 0), (LEAD - 1, LEAD - 1), (0, 0))
+        padded = extended(grad_out, axes, 1)
+        near_sources = (jnp.pad(padded, sides), jnp.pad(extended(last, axes, 1), sides))
+        halo = shifted(grad_out[:extra], "tm", -1)
+        late_sources = (jnp.pad(shifted(padded[:extra], "tm", -1), sides),)
+
+    near_window, near_sum, act_window = call(
         functools.partial(near_kernel, grad_scale, pair, extra),
-        (window_shape(frames), sum_shape),
+        (window_shape(frames), shape(taps * channels), window_shape(extra)),
         scratch=(stage_shape(frames),),
         flops=3 * work // 4,
         moved=4 * 1024 * 1024,
     )(act, *near_sources)
 
     if halves:
-        half_shape = jax.ShapeDtypeStruct((blocks, rows_out // 2, channels), f32)
-        sum_shapes = (half_shape, half_shape)
+        sum_shapes = (shape(blocks, rows_out // 2), shape(blocks, rows_out // 2))
     else:
-        sum_shapes = (sum_shape,)
-    far_window, *sums = call(
-        functools.partial(far_kernel, rows_out, grad_scale, pair, halves, frames),
-        (window_shape(extra), *sum_shapes),
-        scratch=(stage_shape(extra), pltpu.VMEM((taps * channels, channels), f32)),
+        sum_shapes = (shape(taps * channels),)
+    sums = call(
+        functools.partial(far_kernel, rows_out, grad_scale, halves, frames),
+        sum_shapes,
+        scratch=(pltpu.VMEM((taps * channels, channels), f32),),
         flops=work // 4,
         moved=4 * 1024 * 1024,
-    )(act, near_sum, *far_sources)
+    )(act_window, near_sum, halo)
 
     if halves:
         weight_grad = reduced_share(*sums, rows_out)
@@ -577,15 +648,27 @@
         share = lax.psum_scatter(sums[0], "tm", scatter_dimension=0, tiled=True)
         weight_grad = lax.psum(share, ("height", "width"))
 
-    scaled, local = call(
-        conv_kernel,
-        (
-            jax.ShapeDtypeStruct((frames, rows, cols, channels), f32),
-            jax.ShapeDtypeStruct((2 * frames, channels), f32),
+    scaled, before = [], []
+    if early:
+        value, local = call(
+            early_kernel,
+            (shape(early, rows, cols), shape(2 * frames)),
+            flops=work * early // frames,
+            moved=4 * 1024 * 1024,
+        )(near_window, weight, features, params)
+        scaled.append(value)
+        before.append(local)
+    value, local = call(
+        functools.partial(late_kernel, pair, early),
+        (shape(extra, rows, cols), shape(2 * frames)),
+        scratch=(
+            pltpu.VMEM(window_shape(extra).shape, bf16),
+            stage_shape(extra),
         ),
-        flops=work,
-        moved=8 * 1024 * 1024,
-    )(near_window, far_window, weight, future_cot, features, params)
+        flops=work * extra // frames,
+        moved=4 * 1024 * 1024,
+    )(*late_sources, near_window, weight, future_cot, features, params, *before)
+    scaled.append(value)
 
     if pair:
         parts = [local]
@@ -598,11 +681,11 @@
         parts = [lax.psum(local, ("height", "width"))]
     input_cot = call(
         functools.partial(final_kernel, groups, positions * (channels // groups), len(parts)),
-        jax.ShapeDtypeStruct(features.shape, jnp.bfloat16),
+        shape(frames, rows, cols, kind=bf16),
         flops=20 * frames * cells * channels,
         moved=10 * frames * cells * channels,
         out_specs=pl.BlockSpec(features.shape, lambda: (0, 0, 0, 0)),
-    )(*parts, scaled, features, grad_out, params)
+    )(*parts, *scaled, features, grad_out, params)
     return (input_cot, weight_grad)
 
 

time: 54.8 us -> 52.8 us (0.964)
  waiting for transfers between devices: 23.2 us -> 21 us
  local copies, waits for them, and re-layouts: 1.06 us -> 0.01 us
  starting transfers between devices: 17.7 us -> 18.4 us
  Pallas kernels: 11.8 us -> 12.4 us
    ppermute x12, waiting for transfers between devices: 18.2 us -> 16.2 us  [exchanged(): return lax.ppermute(value, axis, [(i, i ^ distance) for i in range(count)])]
    ppermute x2, waiting for transfers between devices: 2.83 us -> 1.55 us  [shifted(): lax.ppermute(value, axis, [(source, source + steps) for source in range(i...]
    ppermute x12, starting transfers between devices: 14 us -> 15.3 us  [exchanged(): return lax.ppermute(value, axis, [(i, i ^ distance) for i in range(count)])]
    ppermute x1, waiting for transfers between devices: 1.21 us -> 2.3 us  [rims(): lax.ppermute(corner, ('height', 'width'), [(i, 3 - i) for i in range(4)])]
    unnamed x10 -> x4, local copies, waits for them, and re-layouts: 1.06 us -> 0.01 us
    ppermute x1, starting transfers between devices: 0.89 us -> 0.24 us  [on_device(): lax.ppermute(local, ('height', 'width'), [(i, 3 - i) for i in range(4)])]
    pallas_call x13 -> x14, Pallas kernels: 11.8 us -> 12.4 us  [run(): pl.pallas_call(kernel, out_shape=out_shape, in_specs=in_specs or [here] *...]
  transfers between devices with their start and end apart: 16 -> 16, of which waited for: 11 -> 12; matrix products, arithmetic and copies ran while one was open for 0% -> 0% of each run, Pallas kernels for 18% -> 17%
where the time goes in v7:
time: 52.8 us; the launch traced here: 52.6 us
  waiting for transfers between devices  21 us (40%)
  starting transfers between devices  18.4 us (35%)
  Pallas kernels  12.4 us (23%)
  between operations  0.74 us (1%)
    ppermute x12, waiting for transfers between devices, exchanged(): return lax.ppermute(value, axis, [(i, i ^ distance) for i in range(count)])  16.2 us
    ppermute x12, starting transfers between devices, exchanged(): return lax.ppermute(value, axis, [(i, i ^ distance) for i in range(count)])  15.3 us
    pallas_call x14, Pallas kernels, run(): pl.pallas_call(kernel, out_shape=out_shape, in_specs=in_specs or [here] *...  12.4 us
    ppermute x2, starting transfers between devices, shifted(): lax.ppermute(value, axis, [(source, source + steps) for source in range(i...  2.7 us
    ppermute x1, waiting for transfers between devices, rims(): lax.ppermute(corner, ('height', 'width'), [(i, 3 - i) for i in range(4)])  2.3 us
    ppermute x2, waiting for transfers between devices, shifted(): lax.ppermute(value, axis, [(source, source + steps) for source in range(i...  1.55 us
  transfers between devices with their start and end apart: 16, of which 12 were waited for; matrix products, arithmetic and copies ran while one was open for 0% of the time, Pallas kernels for 17%

profile of v7, /device:TPU:0, one launch (start us, length us, event | category | flops | bytes accessed | tf_op | source)
XLA Modules:
  0.0 52.6 jit_solution(10787049748183521414)
XLA Ops:
  0.6 1.4 %shard_map.95 = (bf16[2,16,32,128]{3,2,1,0:T(8,128)(2,1)S(1)}, bf16[6,32,128]{2,1,0:T(8,128)(2,1)S(1)}, bf16[6,16,128]{2,1,0:T(8,128)(2,1)S(1)}, bf16[6,128]{1,0...) custom-call(bf16[4,16,32,128]{3,2,1,0:T(8,128)(2,1)} %refs_0_.1, ...), custom_call_target="tpu_custom_call" | custom-call | tf_op jit(solution)/shard_map/pallas_call | solution.py:520
  2.0 1.3 %collective-permute-start = (bf16[2,16,32,128]{3,2,1,0:T(8,128)(2,1)S(1)}, bf16[2,16,32,128]{3,2,1,0:T(8,128)(2,1)S(1)}, u32[]{:S(2)}, u32[]{:S(2)}) collective-permute-start(bf16[2,16,32,128]{3,2,1,0:T(8,128)(2,1)S(1)} %get-tuple-element.34), channel_id=1, source_target_pairs={{4,0},{8,4},{12,8},{16,12},{20,16},{24,20},{28,24},{5,1},{9,5},{13... | collective-permute-start | bytes 786440 | tf_op jit(solution)/shard_map/ppermute | solution.py:24
  3.3 3.1 %collective-permute-start.1 = (bf16[6,32,128]{2,1,0:T(8,128)(2,1)S(1)}, bf16[6,32,128]{2,1,0:T(8,128)(2,1)S(1)}, u32[]{:S(2)}, u32[]{:S(2)}) collective-permute-start(bf16[6,32,128]{2,1,0:T(8,128)(2,1)S(1)} %get-tuple-element.35), channel_id=1, source_target_pairs={{0,2},{2,0},{1,3},{3,1},{4,6},{6,4},{5,7},{7,5},{8,10},{10,8},{9,1... | collective-permute-start | bytes 147464 | tf_op jit(solution)/shard_map/ppermute | solution.py:18
  6.4 0.0 collective-permute-start.2
  6.4 0.2 collective-permute-start.3
  6.6 0.5 shard_map.97
  7.1 2.3 %collective-permute-done.3.corner_ref.refs_3_ = bf16[6,128]{1,0:T(8,128)(2,1)S(1)} collective-permute-done((bf16[6,128]{1,0:T(8,128)(2,1)S(1)}, bf16[6,128]{1,0:T(8,128)(2,1)S(1)}, u32[]{:S(2)}, u32[]{:S(2)}) %collective-permute-start.3) | collective-permute-done | bytes 1568 | tf_op jit(solution)/shard_map/ppermute | solution.py:563
  9.4 0.0 collective-permute-done.2.col_ref.refs_2_
  9.4 0.0 collective-permute-done.1.row_ref.refs_1_
  9.4 2.7 %shard_map.98 = (bf16[4,18,32,384]{3,2,1,0:T(8,128)(2,1)S(1)}, f32[3456,128]{1,0:T(8,128)S(1)}, bf16[2,18,32,384]{3,2,1,0:T(8,128)(2,1)S(1)}) custom-call(bf16[128,2048]{1,0:T(8,128)(2,1)S(1)} %get-tuple-element.43.act_ref, bf16[4,16,32,128]{3,2,1,0:T(8,128)(2,1)S(1)} %get-tuple-element.44.refs_0_.refs_7_, ...), custom_call_target="tpu_custom_call" | custom-call | flops 1358954496 | bytes 4194304 | tf_op jit(solution)/shard_map/pallas_call | solution.py:520
  12.1 1.1 %collective-permute-done.refs_0_.halo_ref = bf16[2,16,32,128]{3,2,1,0:T(8,128)(2,1)S(1)} collective-permute-done((bf16[2,16,32,128]{3,2,1,0:T(8,128)(2,1)S(1)}, bf16[2,16,32,128]{3,2,1,0:T(8,128)(2,1)S(1)}, u32[]{:S(2)}, u32[]{:S(2)}) %collective-permute-start) | collective-permute-done | bytes 262176 | tf_op jit(solution)/shard_map/ppermute | solution.py:24
  13.2 1.0 %shard_map.102 = (f32[8,216,128]{2,1,0:T(8,128)S(1)}, f32[8,216,128]{2,1,0:T(8,128)S(1)}) custom-call(bf16[2,18,32,384]{3,2,1,0:T(8,128)(2,1)S(1)} %get-tuple-element.52.act_window_ref, f32[3456,128]{1,0:T(8,128)S(1)} %get-tuple-element.53.near_sum_ref, bf16[2,16,32,128]{3,2,1,0:T(8,128)(2,1)S(1)} %collective-permute-done.refs_0_.halo_ref), custom_call_target="tpu_custom_call" | custom-call | flops 452984832 | bytes 4194304 | tf_op jit(solution)/shard_map/pallas_call | solution.py:520
  14.2 0.0 copy-start
  14.3 0.1 collective-permute-start.8
  14.3 2.4 %collective-permute-done.8.got_ref = f32[8,216,128]{2,1,0:T(8,128)S(1)} collective-permute-done((f32[8,216,128]{2,1,0:T(8,128)S(1)}, f32[8,216,128]{2,1,0:T(8,128)S(1)}, u32[]{:S(2)}, u32[]{:S(2)}) %collective-permute-start.8) | collective-permute-done | bytes 884768 | tf_op jit(solution)/shard_map/ppermute | solution.py:18
  16.7 0.1 shard_map.103
  16.9 2.7 %collective-permute-start.9 = (bf16[2,216,128]{2,1,0:T(8,128)(2,1)S(1)}, bf16[2,216,128]{2,1,0:T(8,128)(2,1)S(1)}, u32[]{:S(2)}, u32[]{:S(2)}) collective-permute-start(bf16[2,216,128]{2,1,0:T(8,128)(2,1)S(1)} %get-tuple-element.57), channel_id=1, source_target_pairs={{0,4},{4,0},{8,12},{12,8},{16,20},{20,16},{24,28},{28,24},{1,5},{5... | collective-permute-start | bytes 331784 | tf_op jit(solution)/shard_map/ppermute | solution.py:18
  19.6 1.6 %collective-permute-start.10 = (bf16[2,216,128]{2,1,0:T(8,128)(2,1)S(1)}, bf16[2,216,128]{2,1,0:T(8,128)(2,1)S(1)}, u32[]{:S(2)}, u32[]{:S(2)}) collective-permute-start(bf16[2,216,128]{2,1,0:T(8,128)(2,1)S(1)} %get-tuple-element.59), channel_id=1, source_target_pairs={{0,8},{4,12},{8,0},{12,4},{16,24},{20,28},{24,16},{28,20},{1,9},{5... | collective-permute-start | bytes 331784 | tf_op jit(solution)/shard_map/ppermute | solution.py:18
  21.2 1.8 %collective-permute-done.9.low_got_ref = bf16[2,216,128]{2,1,0:T(8,128)(2,1)S(1)} collective-permute-done((bf16[2,216,128]{2,1,0:T(8,128)(2,1)S(1)}, bf16[2,216,128]{2,1,0:T(8,128)(2,1)S(1)}, u32[]{:S(2)}, u32[]{:S(2)}) %collective-permute-start.9) | collective-permute-done | bytes 110624 | tf_op jit(solution)/shard_map/ppermute | solution.py:18
  22.9 1.5 %collective-permute-done.10.high_got_ref = bf16[2,216,128]{2,1,0:T(8,128)(2,1)S(1)} collective-permute-done((bf16[2,216,128]{2,1,0:T(8,128)(2,1)S(1)}, bf16[2,216,128]{2,1,0:T(8,128)(2,1)S(1)}, u32[]{:S(2)}, u32[]{:S(2)}) %collective-permute-start.10) | collective-permute-done | bytes 110624 | tf_op jit(solution)/shard_map/ppermute | solution.py:18
  24.4 0.1 shard_map.104
  24.5 1.6 %collective-permute-start.11 = (bf16[1,216,128]{2,1,0:T(8,128)(2,1)S(1)}, bf16[1,216,128]{2,1,0:T(8,128)(2,1)S(1)}, u32[]{:S(2)}, u32[]{:S(2)}) collective-permute-start(bf16[1,216,128]{2,1,0:T(8,128)(2,1)S(1)} %get-tuple-element.61), channel_id=1, source_target_pairs={{0,8},{4,12},{8,0},{12,4},{16,24},{20,28},{24,16},{28,20},{1,9},{5... | collective-permute-start | bytes 165896 | tf_op jit(solution)/shard_map/ppermute | solution.py:18
  26.1 0.9 %collective-permute-start.12 = (bf16[1,216,128]{2,1,0:T(8,128)(2,1)S(1)}, bf16[1,216,128]{2,1,0:T(8,128)(2,1)S(1)}, u32[]{:S(2)}, u32[]{:S(2)}) collective-permute-start(bf16[1,216,128]{2,1,0:T(8,128)(2,1)S(1)} %get-tuple-element.63), channel_id=1, source_target_pairs={{0,4},{4,0},{8,12},{12,8},{16,20},{20,16},{24,28},{28,24},{1,5},{5... | collective-permute-start | bytes 165896 | tf_op jit(solution)/shard_map/ppermute | solution.py:18
  27.0 1.6 %collective-permute-done.11.refs_1_ = bf16[1,216,128]{2,1,0:T(8,128)(2,1)S(1)} collective-permute-done((bf16[1,216,128]{2,1,0:T(8,128)(2,1)S(1)}, bf16[1,216,128]{2,1,0:T(8,128)(2,1)S(1)}, u32[]{:S(2)}, u32[]{:S(2)}) %collective-permute-start.11) | collective-permute-done | bytes 55328 | tf_op jit(solution)/shard_map/ppermute | solution.py:18
  28.7 1.6 %collective-permute-done.12.refs_3_ = bf16[1,216,128]{2,1,0:T(8,128)(2,1)S(1)} collective-permute-done((bf16[1,216,128]{2,1,0:T(8,128)(2,1)S(1)}, bf16[1,216,128]{2,1,0:T(8,128)(2,1)S(1)}, u32[]{:S(2)}, u32[]{:S(2)}) %collective-permute-start.12) | collective-permute-done | bytes 55328 | tf_op jit(solution)/shard_map/ppermute | solution.py:18
  30.3 1.9 %collective-permute-start.13 = (bf16[1,216,128]{2,1,0:T(8,128)(2,1)S(1)}, bf16[1,216,128]{2,1,0:T(8,128)(2,1)S(1)}, u32[]{:S(2)}, u32[]{:S(2)}) collective-permute-start(bf16[1,216,128]{2,1,0:T(8,128)(2,1)S(1)} %get-tuple-element.65), channel_id=1, source_target_pairs={{0,16},{4,20},{8,24},{12,28},{16,0},{20,4},{24,8},{28,12},{1,17},{... | collective-permute-start | bytes 165896 | tf_op jit(solution)/shard_map/ppermute | solution.py:18
  32.2 3.7 %collective-permute-done.13.got_ref = bf16[1,216,128]{2,1,0:T(8,128)(2,1)S(1)} collective-permute-done((bf16[1,216,128]{2,1,0:T(8,128)(2,1)S(1)}, bf16[1,216,128]{2,1,0:T(8,128)(2,1)S(1)}, u32[]{:S(2)}, u32[]{:S(2)}) %collective-permute-start.13) | collective-permute-done | bytes 55328 | tf_op jit(solution)/shard_map/ppermute | solution.py:18
  35.9 1.6 %collective-permute-start.14 = (f32[1,216,128]{2,1,0:T(8,128)S(1)}, f32[1,216,128]{2,1,0:T(8,128)S(1)}, u32[]{:S(2)}, u32[]{:S(2)}) collective-permute-start(f32[1,216,128]{2,1,0:T(8,128)S(1)} %shard_map.106.own_ref), channel_id=1, source_target_pairs={{0,2},{2,0},{1,3},{3,1},{4,6},{6,4},{5,7},{7,5},{8,10},{10,8},{9,1... | collective-permute-start | bytes 331784 | tf_op jit(solution)/shard_map/ppermute | solution.py:18
  37.5 0.0 copy-start.1
  37.5 1.4 %collective-permute-start.4 = (bf16[2,49,128]{2,1,0:T(8,128)(2,1)S(1)}, bf16[2,49,128]{2,1,0:T(8,128)(2,1)S(1)}, u32[]{:S(2)}, u32[]{:S(2)}) collective-permute-start(bf16[2,49,128]{2,1,0:T(8,128)(2,1)S(1)} %shard_map.96), channel_id=1, source_target_pairs={{4,0},{8,4},{12,8},{16,12},{20,16},{24,20},{28,24},{5,1},{9,5},{13... | collective-permute-start | bytes 75272 | tf_op jit(solution)/shard_map/ppermute | solution.py:24
  38.9 1.8 %collective-permute-done.14.got_ref = f32[1,216,128]{2,1,0:T(8,128)S(1)} collective-permute-done((f32[1,216,128]{2,1,0:T(8,128)S(1)}, f32[1,216,128]{2,1,0:T(8,128)S(1)}, u32[]{:S(2)}, u32[]{:S(2)}) %collective-permute-start.14) | collective-permute-done | bytes 110624 | tf_op jit(solution)/shard_map/ppermute | solution.py:18
  40.7 0.1 collective-permute-start.15
  40.8 0.0 copy-done
  40.8 2.1 %shard_map.99 = (f32[2,16,32,128]{3,2,1,0:T(8,128)S(1)}, f32[8,128]{1,0:T(8,128)S(1)}) custom-call(bf16[4,18,32,384]{3,2,1,0:T(8,128)(2,1)S(1)} %get-tuple-element.47.near_ref.refs_2_, bf16[3,3,3,128,128]{4,3,2,1,0:T(8,128)(2,1)S(1)} %copy-done, bf16[4,16,32,128]{3,2,1,0:T(8,128)(2,1)S(1)} %get-tuple-element.38.features_ref.refs_5_.refs_6_, ...), custom_call_target="tpu_custom_call" | custom-call | flops 905969664 | bytes 4194304 | tf_op jit(solution)/shard_map/pallas_call | solution.py:520
  43.0 0.4 collective-permute-done.4.refs_1_
  43.4 0.0 copy-done.1
  43.4 2.4 %shard_map.100 = (f32[2,16,32,128]{3,2,1,0:T(8,128)S(1)}, f32[8,128]{1,0:T(8,128)S(1)}) custom-call(bf16[2,16,32,128]{3,2,1,0:T(8,128)(2,1)S(1)} %collective-permute-done.refs_0_.halo_ref, bf16[2,49,128]{2,1,0:T(8,128)(2,1)S(1)} %collective-permute-done.4.refs_1_, bf16[4,18,32,384]{3,2,1,0:T(8,128)(2,1)S(1)} %get-tuple-element.47.near_ref.refs_2_, ...), custom_call_target="tpu_custom_call" | custom-call | flops 905969664 | bytes 4194304 | tf_op jit(solution)/shard_map/pallas_call | solution.py:520
  45.7 0.2 collective-permute-start.5
  45.9 1.5 %collective-permute-start.6 = (f32[8,128]{1,0:T(8,128)S(1)}, f32[8,128]{1,0:T(8,128)S(1)}, u32[]{:S(2)}, u32[]{:S(2)}) collective-permute-start(f32[8,128]{1,0:T(8,128)S(1)} %get-tuple-element.49.refs_0_), channel_id=1, source_target_pairs={{0,2},{2,0},{1,3},{3,1},{4,6},{6,4},{5,7},{7,5},{8,10},{10,8},{9,1... | collective-permute-start | bytes 12296 | tf_op jit(solution)/shard_map/ppermute | solution.py:18
  47.4 0.2 collective-permute-start.7
  47.7 0.0 collective-permute-done.5.refs_1_
  47.7 1.8 %collective-permute-done.6.refs_2_ = f32[8,128]{1,0:T(8,128)S(1)} collective-permute-done((f32[8,128]{1,0:T(8,128)S(1)}, f32[8,128]{1,0:T(8,128)S(1)}, u32[]{:S(2)}, u32[]{:S(2)}) %collective-permute-start.6) | collective-permute-done | bytes 4128 | tf_op jit(solution)/shard_map/ppermute | solution.py:18
  49.5 1.0 %collective-permute-done.7.refs_3_ = f32[8,128]{1,0:T(8,128)S(1)} collective-permute-done((f32[8,128]{1,0:T(8,128)S(1)}, f32[8,128]{1,0:T(8,128)S(1)}, u32[]{:S(2)}, u32[]{:S(2)}) %collective-permute-start.7) | collective-permute-done | bytes 4128 | tf_op jit(solution)/shard_map/ppermute | solution.py:678
  50.5 1.4 %shard_map.101 = bf16[4,16,32,128]{3,2,1,0:T(8,128)(2,1)} custom-call(f32[8,128]{1,0:T(8,128)S(1)} %get-tuple-element.49.refs_0_, f32[8,128]{1,0:T(8,128)S(1)} %collective-permute-done.5.refs_1_, f32[8,128]{1,0:T(8,128)S(1)} %collective-permute-done.6.refs_2_, f32[8,128]{1,0:T(8,128)S(1)} %collective-permute-done.7.refs_3_, ...), custom_call_target="tpu_custom_call" | custom-call | flops 5242880 | bytes 2621440 | tf_op jit(solution)/shard_map/pallas_call | solution.py:520
  51.9 0.0 collective-permute-done.15.beside_ref
  51.9 0.7 %shard_map.108 = f32[432,128]{1,0:T(8,128)} custom-call(f32[1,216,128]{2,1,0:T(8,128)S(1)} %shard_map.106.own_ref, f32[1,216,128]{2,1,0:T(8,128)S(1)} %collective-permute-done.14.got_ref, f32[1,216,128]{2,1,0:T(8,128)S(1)} %collective-permute-done.15.beside_ref), custom_call_target="tpu_custom_call" | custom-call | tf_op jit(solution)/shard_map/pallas_call | solution.py:520
  (4 shorter events, 0.1 us)
Async XLA Ops:
  2.0 11.2 %collective-permute-start = (bf16[2,16,32,128]{3,2,1,0:T(8,128)(2,1)S(1)}, bf16[2,16,32,128]{3,2,1,0:T(8,128)(2,1)S(1)}, u32[]{:S(2)}, u32[]{:S(2)}) collective-permute-start(bf16[2,16,32,128]{3,2,1,0:T(8,128)(2,1)S(1)} %get-tuple-element.34), channel_id=1, source_target_pairs={{4,0},{8,4},{12,8},{16,12},{20,16},{24,20},{28,24},{5,1},{9,5},{13... | collective-permute-start | bytes 786440 | tf_op jit(solution)/shard_map/ppermute | solution.py:24
  3.3 6.1 %collective-permute-start.1 = (bf16[6,32,128]{2,1,0:T(8,128)(2,1)S(1)}, bf16[6,32,128]{2,1,0:T(8,128)(2,1)S(1)}, u32[]{:S(2)}, u32[]{:S(2)}) collective-permute-start(bf16[6,32,128]{2,1,0:T(8,128)(2,1)S(1)} %get-tuple-element.35), channel_id=1, source_target_pairs={{0,2},{2,0},{1,3},{3,1},{4,6},{6,4},{5,7},{7,5},{8,10},{10,8},{9,1... | collective-permute-start | bytes 147464 | tf_op jit(solution)/shard_map/ppermute | solution.py:18
  6.4 3.0 %collective-permute-start.2 = (bf16[6,16,128]{2,1,0:T(8,128)(2,1)S(1)}, bf16[6,16,128]{2,1,0:T(8,128)(2,1)S(1)}, u32[]{:S(2)}, u32[]{:S(2)}) collective-permute-start(bf16[6,16,128]{2,1,0:T(8,128)(2,1)S(1)} %get-tuple-element.36), channel_id=1, source_target_pairs={{0,1},{1,0},{2,3},{3,2},{4,5},{5,4},{6,7},{7,6},{8,9},{9,8},{10,11... | collective-permute-start | bytes 73736 | tf_op jit(solution)/shard_map/ppermute | solution.py:18
  6.4 3.0 %collective-permute-start.3 = (bf16[6,128]{1,0:T(8,128)(2,1)S(1)}, bf16[6,128]{1,0:T(8,128)(2,1)S(1)}, u32[]{:S(2)}, u32[]{:S(2)}) collective-permute-start(bf16[6,128]{1,0:T(8,128)(2,1)S(1)} %get-tuple-element.37), channel_id=1, source_target_pairs={{0,3},{1,2},{2,1},{3,0},{4,7},{5,6},{6,5},{7,4},{8,11},{9,10},{10,... | collective-permute-start | bytes 4616 | tf_op jit(solution)/shard_map/ppermute | solution.py:563
  14.2 26.6 %copy-start = (bf16[3,3,3,128,128]{4,3,2,1,0:T(8,128)(2,1)S(1)}, bf16[3,3,3,128,128]{4,3,2,1,0:T(8,128)(2,1)}, u32[]{:S(2)}) copy-start(bf16[3,3,3,128,128]{4,3,2,1,0:T(8,128)(2,1)} %refs_3_.3) | copy-start | bytes 2654212
  14.3 2.5 %collective-permute-start.8 = (f32[8,216,128]{2,1,0:T(8,128)S(1)}, f32[8,216,128]{2,1,0:T(8,128)S(1)}, u32[]{:S(2)}, u32[]{:S(2)}) collective-permute-start(f32[8,216,128]{2,1,0:T(8,128)S(1)} %get-tuple-element.55), channel_id=1, source_target_pairs={{0,1},{1,0},{2,3},{3,2},{4,5},{5,4},{6,7},{7,6},{8,9},{9,8},{10,11... | collective-permute-start | bytes 2654216 | tf_op jit(solution)/shard_map/ppermute | solution.py:18
  16.9 6.1 %collective-permute-start.9 = (bf16[2,216,128]{2,1,0:T(8,128)(2,1)S(1)}, bf16[2,216,128]{2,1,0:T(8,128)(2,1)S(1)}, u32[]{:S(2)}, u32[]{:S(2)}) collective-permute-start(bf16[2,216,128]{2,1,0:T(8,128)(2,1)S(1)} %get-tuple-element.57), channel_id=1, source_target_pairs={{0,4},{4,0},{8,12},{12,8},{16,20},{20,16},{24,28},{28,24},{1,5},{5... | collective-permute-start | bytes 331784 | tf_op jit(solution)/shard_map/ppermute | solution.py:18
  19.6 4.8 %collective-permute-start.10 = (bf16[2,216,128]{2,1,0:T(8,128)(2,1)S(1)}, bf16[2,216,128]{2,1,0:T(8,128)(2,1)S(1)}, u32[]{:S(2)}, u32[]{:S(2)}) collective-permute-start(bf16[2,216,128]{2,1,0:T(8,128)(2,1)S(1)} %get-tuple-element.59), channel_id=1, source_target_pairs={{0,8},{4,12},{8,0},{12,4},{16,24},{20,28},{24,16},{28,20},{1,9},{5... | collective-permute-start | bytes 331784 | tf_op jit(solution)/shard_map/ppermute | solution.py:18
  24.5 4.2 %collective-permute-start.11 = (bf16[1,216,128]{2,1,0:T(8,128)(2,1)S(1)}, bf16[1,216,128]{2,1,0:T(8,128)(2,1)S(1)}, u32[]{:S(2)}, u32[]{:S(2)}) collective-permute-start(bf16[1,216,128]{2,1,0:T(8,128)(2,1)S(1)} %get-tuple-element.61), channel_id=1, source_target_pairs={{0,8},{4,12},{8,0},{12,4},{16,24},{20,28},{24,16},{28,20},{1,9},{5... | collective-permute-start | bytes 165896 | tf_op jit(solution)/shard_map/ppermute | solution.py:18
  26.1 4.2 %collective-permute-start.12 = (bf16[1,216,128]{2,1,0:T(8,128)(2,1)S(1)}, bf16[1,216,128]{2,1,0:T(8,128)(2,1)S(1)}, u32[]{:S(2)}, u32[]{:S(2)}) collective-permute-start(bf16[1,216,128]{2,1,0:T(8,128)(2,1)S(1)} %get-tuple-element.63), channel_id=1, source_target_pairs={{0,4},{4,0},{8,12},{12,8},{16,20},{20,16},{24,28},{28,24},{1,5},{5... | collective-permute-start | bytes 165896 | tf_op jit(solution)/shard_map/ppermute | solution.py:18
  30.3 5.6 %collective-permute-start.13 = (bf16[1,216,128]{2,1,0:T(8,128)(2,1)S(1)}, bf16[1,216,128]{2,1,0:T(8,128)(2,1)S(1)}, u32[]{:S(2)}, u32[]{:S(2)}) collective-permute-start(bf16[1,216,128]{2,1,0:T(8,128)(2,1)S(1)} %get-tuple-element.65), channel_id=1, source_target_pairs={{0,16},{4,20},{8,24},{12,28},{16,0},{20,4},{24,8},{28,12},{1,17},{... | collective-permute-start | bytes 165896 | tf_op jit(solution)/shard_map/ppermute | solution.py:18
  35.9 4.8 %collective-permute-start.14 = (f32[1,216,128]{2,1,0:T(8,128)S(1)}, f32[1,216,128]{2,1,0:T(8,128)S(1)}, u32[]{:S(2)}, u32[]{:S(2)}) collective-permute-start(f32[1,216,128]{2,1,0:T(8,128)S(1)} %shard_map.106.own_ref), channel_id=1, source_target_pairs={{0,2},{2,0},{1,3},{3,1},{4,6},{6,4},{5,7},{7,5},{8,10},{10,8},{9,1... | collective-permute-start | bytes 331784 | tf_op jit(solution)/shard_map/ppermute | solution.py:18
  37.5 5.9 %copy-start.1 = (bf16[2,16,32,128]{3,2,1,0:T(8,128)(2,1)S(1)}, bf16[2,16,32,128]{3,2,1,0:T(8,128)(2,1)}, u32[]{:S(2)}) copy-start(bf16[2,16,32,128]{3,2,1,0:T(8,128)(2,1)} %refs_4_.1) | copy-start | bytes 786436
  37.5 5.9 %collective-permute-start.4 = (bf16[2,49,128]{2,1,0:T(8,128)(2,1)S(1)}, bf16[2,49,128]{2,1,0:T(8,128)(2,1)S(1)}, u32[]{:S(2)}, u32[]{:S(2)}) collective-permute-start(bf16[2,49,128]{2,1,0:T(8,128)(2,1)S(1)} %shard_map.96), channel_id=1, source_target_pairs={{4,0},{8,4},{12,8},{16,12},{20,16},{24,20},{28,24},{5,1},{9,5},{13... | collective-permute-start | bytes 75272 | tf_op jit(solution)/shard_map/ppermute | solution.py:24
  40.7 11.1 %collective-permute-start.15 = (f32[1,216,128]{2,1,0:T(8,128)S(1)}, f32[1,216,128]{2,1,0:T(8,128)S(1)}, u32[]{:S(2)}, u32[]{:S(2)}) collective-permute-start(f32[1,216,128]{2,1,0:T(8,128)S(1)} %shard_map.107), channel_id=1, source_target_pairs={{0,1},{1,0},{2,3},{3,2},{4,5},{5,4},{6,7},{7,6},{8,9},{9,8},{10,11... | collective-permute-start | bytes 331784 | tf_op jit(solution)/shard_map/ppermute | solution.py:18
  45.7 1.9 %collective-permute-start.5 = (f32[8,128]{1,0:T(8,128)S(1)}, f32[8,128]{1,0:T(8,128)S(1)}, u32[]{:S(2)}, u32[]{:S(2)}) collective-permute-start(f32[8,128]{1,0:T(8,128)S(1)} %get-tuple-element.49.refs_0_), channel_id=1, source_target_pairs={{0,1},{1,0},{2,3},{3,2},{4,5},{5,4},{6,7},{7,6},{8,9},{9,8},{10,11... | collective-permute-start | bytes 12296 | tf_op jit(solution)/shard_map/ppermute | solution.py:18
  45.9 3.6 %collective-permute-start.6 = (f32[8,128]{1,0:T(8,128)S(1)}, f32[8,128]{1,0:T(8,128)S(1)}, u32[]{:S(2)}, u32[]{:S(2)}) collective-permute-start(f32[8,128]{1,0:T(8,128)S(1)} %get-tuple-element.49.refs_0_), channel_id=1, source_target_pairs={{0,2},{2,0},{1,3},{3,1},{4,6},{6,4},{5,7},{7,5},{8,10},{10,8},{9,1... | collective-permute-start | bytes 12296 | tf_op jit(solution)/shard_map/ppermute | solution.py:18
  47.4 3.1 %collective-permute-start.7 = (f32[8,128]{1,0:T(8,128)S(1)}, f32[8,128]{1,0:T(8,128)S(1)}, u32[]{:S(2)}, u32[]{:S(2)}) collective-permute-start(f32[8,128]{1,0:T(8,128)S(1)} %get-tuple-element.49.refs_0_), channel_id=1, source_target_pairs={{0,3},{1,2},{2,1},{3,0},{4,7},{5,6},{6,5},{7,4},{8,11},{9,10},{10,... | collective-permute-start | bytes 12296 | tf_op jit(solution)/shard_map/ppermute | solution.py:678

commit v8 on v7

--- a/solution.py
+++ b/solution.py
@@ -45,7 +45,7 @@
     near_side, next_side = tm_side(1), tm_side(2)
 
     def block(at):
-        return mine_ref[at] + got_ref[at]
+        return mine_ref[at] + got_ref[at].astype(jnp.float32)
 
     for i in range(low_near.shape[0]):
         low_near[i] = block(2 * i + near_side)
@@ -92,17 +92,16 @@
                 far_ref[i] = block(2 * i + 1 - which).astype(far_ref.dtype)
 
 
-def add_kernel(own_ref, got_ref, out_ref):
-    out_ref[...] = own_ref[...] + got_ref[...].astype(jnp.float32)
-
-
-def whole_kernel(own_ref, got_ref, beside_ref, out_ref):
+def total_kernel(own_ref, got_ref, below_ref, below_got_ref, out_ref):
+    mine = own_ref[...] + got_ref[...].astype(jnp.float32)
+    out_ref[...] = mine + (below_ref[...] + below_got_ref[...].astype(jnp.float32))
+
+
+def whole_kernel(own_ref, beside_ref, out_ref):
     half = own_ref.shape[1]
     side = lax.axis_index("width")
-    mine = pl.multiple_of(side * half, 8)
-    other = pl.multiple_of((1 - side) * half, 8)
-    out_ref[pl.ds(mine, half), :] = own_ref[0] + got_ref[0]
-    out_ref[pl.ds(other, half), :] = beside_ref[0]
+    out_ref[pl.ds(pl.multiple_of(side * half, 8), half), :] = own_ref[0]
+    out_ref[pl.ds(pl.multiple_of((1 - side) * half, 8), half), :] = beside_ref[0]
 
 
 def reduced_share(mine, theirs, rows):
@@ -131,16 +130,16 @@
         )(*parts)
         parts = (near, exchanged(far, "tm", distance))
         distance *= 2
-    share = both(1)[0]
-    own = call(add_kernel, share)(*parts)
-    got = exchanged(own, "height", 1)
-    total = call(add_kernel, share)(own, got)
+    own, got = parts
+    below = exchanged(own, "height", 1)
+    below_got = exchanged(got, "height", 1)
+    total = call(total_kernel, both(1)[0])(own, got, below, below_got)
     beside = exchanged(total, "width", 1)
     return call(
         whole_kernel,
         jax.ShapeDtypeStruct((rows, channels), f32),
         out_specs=pl.BlockSpec((rows, channels), lambda: (0, 0)),
-    )(own, got, beside)
+    )(total, beside)
 
 
 def group_matrix(rows, cols, row_width, col_width):
@@ -390,8 +389,8 @@
     def place(low_ref, high_ref):
         for block in range(mine_ref.shape[0]):
             at = block * rows_out
-            low_ref[block] = sum_ref[at : at + half, :]
-            high_ref[block] = sum_ref[at + half : at + rows_out, :]
+            low_ref[block] = sum_ref[at : at + half, :].astype(low_ref.dtype)
+            high_ref[block] = sum_ref[at + half : at + rows_out, :].astype(high_ref.dtype)
 
     @pl.when(col_side == 0)
     def _():
@@ -631,7 +630,10 @@
     )(act, *near_sources)
 
     if halves:
-        sum_shapes = (shape(blocks, rows_out // 2), shape(blocks, rows_out // 2))
+        sum_shapes = (
+            shape(blocks, rows_out // 2),
+            shape(blocks, rows_out // 2, kind=bf16),
+        )
     else:
         sum_shapes = (shape(taps * channels),)
     sums = call(

time: 52.8 us -> 51.4 us (0.973)
  waiting for transfers between devices: 21 us -> 19 us
  starting transfers between devices: 18.4 us -> 19.1 us
    ppermute x12 -> x13, waiting for transfers between devices: 16.2 us -> 14.1 us  [exchanged(): return lax.ppermute(value, axis, [(i, i ^ distance) for i in range(count)])]
    ppermute x12 -> x13, starting transfers between devices: 15.3 us -> 15.7 us  [exchanged(): return lax.ppermute(value, axis, [(i, i ^ distance) for i in range(count)])]
    pallas_call x14 -> x13, Pallas kernels: 12.4 us -> 12.4 us  [run(): pl.pallas_call(kernel, out_shape=out_shape, in_specs=in_specs or [here] *...]
  transfers between devices with their start and end apart: 16 -> 17, of which waited for: 12 -> 12; matrix products, arithmetic and copies ran while one was open for 0% -> 0% of each run, Pallas kernels for 17% -> 18%
where the time goes in v8:
time: 51.4 us; the launch traced here: 51.2 us
  starting transfers between devices  19.1 us (37%)
  waiting for transfers between devices  19 us (37%)
  Pallas kernels  12.4 us (24%)
  between operations  0.76 us (1%)
    ppermute x13, starting transfers between devices, exchanged(): return lax.ppermute(value, axis, [(i, i ^ distance) for i in range(count)])  15.7 us
    ppermute x13, waiting for transfers between devices, exchanged(): return lax.ppermute(value, axis, [(i, i ^ distance) for i in range(count)])  14.1 us
    pallas_call x13, Pallas kernels, run(): pl.pallas_call(kernel, out_shape=out_shape, in_specs=in_specs or [here] *...  12.4 us
    ppermute x2, starting transfers between devices, shifted(): lax.ppermute(value, axis, [(source, source + steps) for source in range(i...  2.57 us
    ppermute x1, waiting for transfers between devices, rims(): lax.ppermute(corner, ('height', 'width'), [(i, 3 - i) for i in range(4)])  2.3 us
    ppermute x2, waiting for transfers between devices, shifted(): lax.ppermute(value, axis, [(source, source + steps) for source in range(i...  1.98 us
  transfers between devices with their start and end apart: 17, of which 12 were waited for; matrix products, arithmetic and copies ran while one was open for 0% of the time, Pallas kernels for 18%

profile of v8, /device:TPU:0, one launch (start us, length us, event | category | flops | bytes accessed | tf_op | source)
XLA Modules:
  0.0 51.2 jit_solution(6053496748330341165)
XLA Ops:
  0.6 1.4 %shard_map.95 = (bf16[2,16,32,128]{3,2,1,0:T(8,128)(2,1)S(1)}, bf16[6,32,128]{2,1,0:T(8,128)(2,1)S(1)}, bf16[6,16,128]{2,1,0:T(8,128)(2,1)S(1)}, bf16[6,128]{1,0...) custom-call(bf16[4,16,32,128]{3,2,1,0:T(8,128)(2,1)} %refs_0_.1, ...), custom_call_target="tpu_custom_call" | custom-call | tf_op jit(solution)/shard_map/pallas_call | solution.py:519
  2.0 1.3 %collective-permute-start = (bf16[2,16,32,128]{3,2,1,0:T(8,128)(2,1)S(1)}, bf16[2,16,32,128]{3,2,1,0:T(8,128)(2,1)S(1)}, u32[]{:S(2)}, u32[]{:S(2)}) collective-permute-start(bf16[2,16,32,128]{3,2,1,0:T(8,128)(2,1)S(1)} %get-tuple-element.34), channel_id=1, source_target_pairs={{4,0},{8,4},{12,8},{16,12},{20,16},{24,20},{28,24},{5,1},{9,5},{13... | collective-permute-start | bytes 786440 | tf_op jit(solution)/shard_map/ppermute | solution.py:24
  3.3 3.1 %collective-permute-start.1 = (bf16[6,32,128]{2,1,0:T(8,128)(2,1)S(1)}, bf16[6,32,128]{2,1,0:T(8,128)(2,1)S(1)}, u32[]{:S(2)}, u32[]{:S(2)}) collective-permute-start(bf16[6,32,128]{2,1,0:T(8,128)(2,1)S(1)} %get-tuple-element.35), channel_id=1, source_target_pairs={{0,2},{2,0},{1,3},{3,1},{4,6},{6,4},{5,7},{7,5},{8,10},{10,8},{9,1... | collective-permute-start | bytes 147464 | tf_op jit(solution)/shard_map/ppermute | solution.py:18
  6.4 0.0 collective-permute-start.2
  6.4 0.2 collective-permute-start.3
  6.6 0.5 shard_map.97
  7.1 2.3 %collective-permute-done.3.corner_ref.refs_3_ = bf16[6,128]{1,0:T(8,128)(2,1)S(1)} collective-permute-done((bf16[6,128]{1,0:T(8,128)(2,1)S(1)}, bf16[6,128]{1,0:T(8,128)(2,1)S(1)}, u32[]{:S(2)}, u32[]{:S(2)}) %collective-permute-start.3) | collective-permute-done | bytes 1568 | tf_op jit(solution)/shard_map/ppermute | solution.py:562
  9.4 0.0 collective-permute-done.2.col_ref.refs_2_
  9.4 0.0 collective-permute-done.1.row_ref.refs_1_
  9.4 2.7 %shard_map.98 = (bf16[4,18,32,384]{3,2,1,0:T(8,128)(2,1)S(1)}, f32[3456,128]{1,0:T(8,128)S(1)}, bf16[2,18,32,384]{3,2,1,0:T(8,128)(2,1)S(1)}) custom-call(bf16[128,2048]{1,0:T(8,128)(2,1)S(1)} %get-tuple-element.43.act_ref, bf16[4,16,32,128]{3,2,1,0:T(8,128)(2,1)S(1)} %get-tuple-element.44.refs_0_.refs_7_, ...), custom_call_target="tpu_custom_call" | custom-call | flops 1358954496 | bytes 4194304 | tf_op jit(solution)/shard_map/pallas_call | solution.py:519
  12.1 1.1 %collective-permute-done.refs_0_.halo_ref = bf16[2,16,32,128]{3,2,1,0:T(8,128)(2,1)S(1)} collective-permute-done((bf16[2,16,32,128]{3,2,1,0:T(8,128)(2,1)S(1)}, bf16[2,16,32,128]{3,2,1,0:T(8,128)(2,1)S(1)}, u32[]{:S(2)}, u32[]{:S(2)}) %collective-permute-start) | collective-permute-done | bytes 262176 | tf_op jit(solution)/shard_map/ppermute | solution.py:24
  13.2 1.0 %shard_map.102 = (f32[8,216,128]{2,1,0:T(8,128)S(1)}, bf16[8,216,128]{2,1,0:T(8,128)(2,1)S(1)}) custom-call(bf16[2,18,32,384]{3,2,1,0:T(8,128)(2,1)S(1)} %get-tuple-element.52.act_window_ref, f32[3456,128]{1,0:T(8,128)S(1)} %get-tuple-element.53.near_sum_ref, bf16[2,16,32,128]{3,2,1,0:T(8,128)(2,1)S(1)} %collective-permute-done.refs_0_.halo_ref), custom_call_target="tpu_custom_call" | custom-call | flops 452984832 | bytes 4194304 | tf_op jit(solution)/shard_map/pallas_call | solution.py:519
  14.2 0.0 copy-start
  14.2 0.1 collective-permute-start.8
  14.3 1.8 %collective-permute-done.8.got_ref = bf16[8,216,128]{2,1,0:T(8,128)(2,1)S(1)} collective-permute-done((bf16[8,216,128]{2,1,0:T(8,128)(2,1)S(1)}, bf16[8,216,128]{2,1,0:T(8,128)(2,1)S(1)}, u32[]{:S(2)}, u32[]{:S(2)}) %collective-permute-start.8) | collective-permute-done | bytes 442400 | tf_op jit(solution)/shard_map/ppermute | solution.py:18
  16.1 0.1 shard_map.103
  16.2 2.7 %collective-permute-start.9 = (bf16[2,216,128]{2,1,0:T(8,128)(2,1)S(1)}, bf16[2,216,128]{2,1,0:T(8,128)(2,1)S(1)}, u32[]{:S(2)}, u32[]{:S(2)}) collective-permute-start(bf16[2,216,128]{2,1,0:T(8,128)(2,1)S(1)} %get-tuple-element.57), channel_id=1, source_target_pairs={{0,4},{4,0},{8,12},{12,8},{16,20},{20,16},{24,28},{28,24},{1,5},{5... | collective-permute-start | bytes 331784 | tf_op jit(solution)/shard_map/ppermute | solution.py:18
  18.9 1.6 %collective-permute-start.10 = (bf16[2,216,128]{2,1,0:T(8,128)(2,1)S(1)}, bf16[2,216,128]{2,1,0:T(8,128)(2,1)S(1)}, u32[]{:S(2)}, u32[]{:S(2)}) collective-permute-start(bf16[2,216,128]{2,1,0:T(8,128)(2,1)S(1)} %get-tuple-element.59), channel_id=1, source_target_pairs={{0,8},{4,12},{8,0},{12,4},{16,24},{20,28},{24,16},{28,20},{1,9},{5... | collective-permute-start | bytes 331784 | tf_op jit(solution)/shard_map/ppermute | solution.py:18
  20.5 1.8 %collective-permute-done.9.low_got_ref = bf16[2,216,128]{2,1,0:T(8,128)(2,1)S(1)} collective-permute-done((bf16[2,216,128]{2,1,0:T(8,128)(2,1)S(1)}, bf16[2,216,128]{2,1,0:T(8,128)(2,1)S(1)}, u32[]{:S(2)}, u32[]{:S(2)}) %collective-permute-start.9) | collective-permute-done | bytes 110624 | tf_op jit(solution)/shard_map/ppermute | solution.py:18
  22.3 1.5 %collective-permute-done.10.high_got_ref = bf16[2,216,128]{2,1,0:T(8,128)(2,1)S(1)} collective-permute-done((bf16[2,216,128]{2,1,0:T(8,128)(2,1)S(1)}, bf16[2,216,128]{2,1,0:T(8,128)(2,1)S(1)}, u32[]{:S(2)}, u32[]{:S(2)}) %collective-permute-start.10) | collective-permute-done | bytes 110624 | tf_op jit(solution)/shard_map/ppermute | solution.py:18
  23.7 0.1 shard_map.104
  23.8 1.6 %collective-permute-start.11 = (bf16[1,216,128]{2,1,0:T(8,128)(2,1)S(1)}, bf16[1,216,128]{2,1,0:T(8,128)(2,1)S(1)}, u32[]{:S(2)}, u32[]{:S(2)}) collective-permute-start(bf16[1,216,128]{2,1,0:T(8,128)(2,1)S(1)} %get-tuple-element.61), channel_id=1, source_target_pairs={{0,8},{4,12},{8,0},{12,4},{16,24},{20,28},{24,16},{28,20},{1,9},{5... | collective-permute-start | bytes 165896 | tf_op jit(solution)/shard_map/ppermute | solution.py:18
  25.4 0.9 %collective-permute-start.12 = (bf16[1,216,128]{2,1,0:T(8,128)(2,1)S(1)}, bf16[1,216,128]{2,1,0:T(8,128)(2,1)S(1)}, u32[]{:S(2)}, u32[]{:S(2)}) collective-permute-start(bf16[1,216,128]{2,1,0:T(8,128)(2,1)S(1)} %get-tuple-element.63), channel_id=1, source_target_pairs={{0,4},{4,0},{8,12},{12,8},{16,20},{20,16},{24,28},{28,24},{1,5},{5... | collective-permute-start | bytes 165896 | tf_op jit(solution)/shard_map/ppermute | solution.py:18
  26.4 1.6 %collective-permute-done.11.refs_1_ = bf16[1,216,128]{2,1,0:T(8,128)(2,1)S(1)} collective-permute-done((bf16[1,216,128]{2,1,0:T(8,128)(2,1)S(1)}, bf16[1,216,128]{2,1,0:T(8,128)(2,1)S(1)}, u32[]{:S(2)}, u32[]{:S(2)}) %collective-permute-start.11) | collective-permute-done | bytes 55328 | tf_op jit(solution)/shard_map/ppermute | solution.py:18
  28.0 1.6 %collective-permute-done.12.refs_3_ = bf16[1,216,128]{2,1,0:T(8,128)(2,1)S(1)} collective-permute-done((bf16[1,216,128]{2,1,0:T(8,128)(2,1)S(1)}, bf16[1,216,128]{2,1,0:T(8,128)(2,1)S(1)}, u32[]{:S(2)}, u32[]{:S(2)}) %collective-permute-start.12) | collective-permute-done | bytes 55328 | tf_op jit(solution)/shard_map/ppermute | solution.py:18
  29.6 1.9 %collective-permute-start.13 = (bf16[1,216,128]{2,1,0:T(8,128)(2,1)S(1)}, bf16[1,216,128]{2,1,0:T(8,128)(2,1)S(1)}, u32[]{:S(2)}, u32[]{:S(2)}) collective-permute-start(bf16[1,216,128]{2,1,0:T(8,128)(2,1)S(1)} %get-tuple-element.65), channel_id=1, source_target_pairs={{0,16},{4,20},{8,24},{12,28},{16,0},{20,4},{24,8},{28,12},{1,17},{... | collective-permute-start | bytes 165896 | tf_op jit(solution)/shard_map/ppermute | solution.py:18
  31.5 0.9 %collective-permute-start.14 = (f32[1,216,128]{2,1,0:T(8,128)S(1)}, f32[1,216,128]{2,1,0:T(8,128)S(1)}, u32[]{:S(2)}, u32[]{:S(2)}) collective-permute-start(f32[1,216,128]{2,1,0:T(8,128)S(1)} %get-tuple-element.64.own_ref), channel_id=1, source_target_pairs={{0,2},{2,0},{1,3},{3,1},{4,6},{6,4},{5,7},{7,5},{8,10},{10,8},{9,1... | collective-permute-start | bytes 331784 | tf_op jit(solution)/shard_map/ppermute | solution.py:18
  32.5 2.7 %collective-permute-done.13.got_ref = bf16[1,216,128]{2,1,0:T(8,128)(2,1)S(1)} collective-permute-done((bf16[1,216,128]{2,1,0:T(8,128)(2,1)S(1)}, bf16[1,216,128]{2,1,0:T(8,128)(2,1)S(1)}, u32[]{:S(2)}, u32[]{:S(2)}) %collective-permute-start.13) | collective-permute-done | bytes 55328 | tf_op jit(solution)/shard_map/ppermute | solution.py:18
  35.2 1.5 %collective-permute-start.15 = (bf16[1,216,128]{2,1,0:T(8,128)(2,1)S(1)}, bf16[1,216,128]{2,1,0:T(8,128)(2,1)S(1)}, u32[]{:S(2)}, u32[]{:S(2)}) collective-permute-start(bf16[1,216,128]{2,1,0:T(8,128)(2,1)S(1)} %collective-permute-done.13.got_ref), channel_id=1, source_target_pairs={{0,2},{2,0},{1,3},{3,1},{4,6},{6,4},{5,7},{7,5},{8,10},{10,8},{9,1... | collective-permute-start | bytes 165896 | tf_op jit(solution)/shard_map/ppermute | solution.py:18
  36.7 1.3 %collective-permute-start.4 = (bf16[2,49,128]{2,1,0:T(8,128)(2,1)S(1)}, bf16[2,49,128]{2,1,0:T(8,128)(2,1)S(1)}, u32[]{:S(2)}, u32[]{:S(2)}) collective-permute-start(bf16[2,49,128]{2,1,0:T(8,128)(2,1)S(1)} %shard_map.96), channel_id=1, source_target_pairs={{4,0},{8,4},{12,8},{16,12},{20,16},{24,20},{28,24},{5,1},{9,5},{13... | collective-permute-start | bytes 75272 | tf_op jit(solution)/shard_map/ppermute | solution.py:24
  38.0 0.0 collective-permute-done.14.below_ref
  38.0 1.3 %collective-permute-done.15.below_got_ref = bf16[1,216,128]{2,1,0:T(8,128)(2,1)S(1)} collective-permute-done((bf16[1,216,128]{2,1,0:T(8,128)(2,1)S(1)}, bf16[1,216,128]{2,1,0:T(8,128)(2,1)S(1)}, u32[]{:S(2)}, u32[]{:S(2)}) %collective-permute-start.15) | collective-permute-done | bytes 55328 | tf_op jit(solution)/shard_map/ppermute | solution.py:18
  39.4 0.0 copy-start.1
  39.4 0.1 collective-permute-start.16
  39.5 0.0 copy-done
  39.5 2.1 %shard_map.99 = (f32[2,16,32,128]{3,2,1,0:T(8,128)S(1)}, f32[8,128]{1,0:T(8,128)S(1)}) custom-call(bf16[4,18,32,384]{3,2,1,0:T(8,128)(2,1)S(1)} %get-tuple-element.47.near_ref.refs_2_, bf16[3,3,3,128,128]{4,3,2,1,0:T(8,128)(2,1)S(1)} %copy-done, bf16[4,16,32,128]{3,2,1,0:T(8,128)(2,1)S(1)} %get-tuple-element.38.features_ref.refs_5_.refs_6_, ...), custom_call_target="tpu_custom_call" | custom-call | flops 905969664 | bytes 4194304 | tf_op jit(solution)/shard_map/pallas_call | solution.py:519
  41.6 0.8 %collective-permute-done.4.refs_1_ = bf16[2,49,128]{2,1,0:T(8,128)(2,1)S(1)} collective-permute-done((bf16[2,49,128]{2,1,0:T(8,128)(2,1)S(1)}, bf16[2,49,128]{2,1,0:T(8,128)(2,1)S(1)}, u32[]{:S(2)}, u32[]{:S(2)}) %collective-permute-start.4) | collective-permute-done | bytes 25120 | tf_op jit(solution)/shard_map/ppermute | solution.py:24
  42.5 0.0 copy-done.1
  42.5 2.4 %shard_map.100 = (f32[2,16,32,128]{3,2,1,0:T(8,128)S(1)}, f32[8,128]{1,0:T(8,128)S(1)}) custom-call(bf16[2,16,32,128]{3,2,1,0:T(8,128)(2,1)S(1)} %collective-permute-done.refs_0_.halo_ref, bf16[2,49,128]{2,1,0:T(8,128)(2,1)S(1)} %collective-permute-done.4.refs_1_, bf16[4,18,32,384]{3,2,1,0:T(8,128)(2,1)S(1)} %get-tuple-element.47.near_ref.refs_2_, ...), custom_call_target="tpu_custom_call" | custom-call | flops 905969664 | bytes 4194304 | tf_op jit(solution)/shard_map/pallas_call | solution.py:519
  44.8 0.1 collective-permute-start.5
  44.9 1.2 %collective-permute-start.6 = (f32[8,128]{1,0:T(8,128)S(1)}, f32[8,128]{1,0:T(8,128)S(1)}, u32[]{:S(2)}, u32[]{:S(2)}) collective-permute-start(f32[8,128]{1,0:T(8,128)S(1)} %get-tuple-element.49.refs_0_), channel_id=1, source_target_pairs={{0,2},{2,0},{1,3},{3,1},{4,6},{6,4},{5,7},{7,5},{8,10},{10,8},{9,1... | collective-permute-start | bytes 12296 | tf_op jit(solution)/shard_map/ppermute | solution.py:18
  46.1 0.7 %collective-permute-start.7 = (f32[8,128]{1,0:T(8,128)S(1)}, f32[8,128]{1,0:T(8,128)S(1)}, u32[]{:S(2)}, u32[]{:S(2)}) collective-permute-start(f32[8,128]{1,0:T(8,128)S(1)} %get-tuple-element.49.refs_0_), channel_id=1, source_target_pairs={{0,3},{1,2},{2,1},{3,0},{4,7},{5,6},{6,5},{7,4},{8,11},{9,10},{10,... | collective-permute-start | bytes 12296 | tf_op jit(solution)/shard_map/ppermute | solution.py:680
  46.8 0.0 collective-permute-done.5.refs_1_
  46.8 1.8 %collective-permute-done.6.refs_2_ = f32[8,128]{1,0:T(8,128)S(1)} collective-permute-done((f32[8,128]{1,0:T(8,128)S(1)}, f32[8,128]{1,0:T(8,128)S(1)}, u32[]{:S(2)}, u32[]{:S(2)}) %collective-permute-start.6) | collective-permute-done | bytes 4128 | tf_op jit(solution)/shard_map/ppermute | solution.py:18
  48.6 0.6 %collective-permute-done.7.refs_3_ = f32[8,128]{1,0:T(8,128)S(1)} collective-permute-done((f32[8,128]{1,0:T(8,128)S(1)}, f32[8,128]{1,0:T(8,128)S(1)}, u32[]{:S(2)}, u32[]{:S(2)}) %collective-permute-start.7) | collective-permute-done | bytes 4128 | tf_op jit(solution)/shard_map/ppermute | solution.py:680
  49.1 1.4 %shard_map.101 = bf16[4,16,32,128]{3,2,1,0:T(8,128)(2,1)} custom-call(f32[8,128]{1,0:T(8,128)S(1)} %get-tuple-element.49.refs_0_, f32[8,128]{1,0:T(8,128)S(1)} %collective-permute-done.5.refs_1_, f32[8,128]{1,0:T(8,128)S(1)} %collective-permute-done.6.refs_2_, f32[8,128]{1,0:T(8,128)S(1)} %collective-permute-done.7.refs_3_, ...), custom_call_target="tpu_custom_call" | custom-call | flops 5242880 | bytes 2621440 | tf_op jit(solution)/shard_map/pallas_call | solution.py:519
  50.5 0.0 collective-permute-done.16.beside_ref
  50.5 0.7 %shard_map.107 = f32[432,128]{1,0:T(8,128)} custom-call(f32[1,216,128]{2,1,0:T(8,128)S(1)} %shard_map.106.own_ref, f32[1,216,128]{2,1,0:T(8,128)S(1)} %collective-permute-done.16.beside_ref), custom_call_target="tpu_custom_call" | custom-call | tf_op jit(solution)/shard_map/pallas_call | solution.py:519
  (3 shorter events, 0.1 us)
Async XLA Ops:
  2.0 11.2 %collective-permute-start = (bf16[2,16,32,128]{3,2,1,0:T(8,128)(2,1)S(1)}, bf16[2,16,32,128]{3,2,1,0:T(8,128)(2,1)S(1)}, u32[]{:S(2)}, u32[]{:S(2)}) collective-permute-start(bf16[2,16,32,128]{3,2,1,0:T(8,128)(2,1)S(1)} %get-tuple-element.34), channel_id=1, source_target_pairs={{4,0},{8,4},{12,8},{16,12},{20,16},{24,20},{28,24},{5,1},{9,5},{13... | collective-permute-start | bytes 786440 | tf_op jit(solution)/shard_map/ppermute | solution.py:24
  3.3 6.1 %collective-permute-start.1 = (bf16[6,32,128]{2,1,0:T(8,128)(2,1)S(1)}, bf16[6,32,128]{2,1,0:T(8,128)(2,1)S(1)}, u32[]{:S(2)}, u32[]{:S(2)}) collective-permute-start(bf16[6,32,128]{2,1,0:T(8,128)(2,1)S(1)} %get-tuple-element.35), channel_id=1, source_target_pairs={{0,2},{2,0},{1,3},{3,1},{4,6},{6,4},{5,7},{7,5},{8,10},{10,8},{9,1... | collective-permute-start | bytes 147464 | tf_op jit(solution)/shard_map/ppermute | solution.py:18
  6.4 3.0 %collective-permute-start.2 = (bf16[6,16,128]{2,1,0:T(8,128)(2,1)S(1)}, bf16[6,16,128]{2,1,0:T(8,128)(2,1)S(1)}, u32[]{:S(2)}, u32[]{:S(2)}) collective-permute-start(bf16[6,16,128]{2,1,0:T(8,128)(2,1)S(1)} %get-tuple-element.36), channel_id=1, source_target_pairs={{0,1},{1,0},{2,3},{3,2},{4,5},{5,4},{6,7},{7,6},{8,9},{9,8},{10,11... | collective-permute-start | bytes 73736 | tf_op jit(solution)/shard_map/ppermute | solution.py:18
  6.4 3.0 %collective-permute-start.3 = (bf16[6,128]{1,0:T(8,128)(2,1)S(1)}, bf16[6,128]{1,0:T(8,128)(2,1)S(1)}, u32[]{:S(2)}, u32[]{:S(2)}) collective-permute-start(bf16[6,128]{1,0:T(8,128)(2,1)S(1)} %get-tuple-element.37), channel_id=1, source_target_pairs={{0,3},{1,2},{2,1},{3,0},{4,7},{5,6},{6,5},{7,4},{8,11},{9,10},{10,... | collective-permute-start | bytes 4616 | tf_op jit(solution)/shard_map/ppermute | solution.py:562
  14.2 25.3 %copy-start = (bf16[3,3,3,128,128]{4,3,2,1,0:T(8,128)(2,1)S(1)}, bf16[3,3,3,128,128]{4,3,2,1,0:T(8,128)(2,1)}, u32[]{:S(2)}) copy-start(bf16[3,3,3,128,128]{4,3,2,1,0:T(8,128)(2,1)} %refs_3_.3) | copy-start | bytes 2654212
  14.2 1.9 %collective-permute-start.8 = (bf16[8,216,128]{2,1,0:T(8,128)(2,1)S(1)}, bf16[8,216,128]{2,1,0:T(8,128)(2,1)S(1)}, u32[]{:S(2)}, u32[]{:S(2)}) collective-permute-start(bf16[8,216,128]{2,1,0:T(8,128)(2,1)S(1)} %get-tuple-element.55), channel_id=1, source_target_pairs={{0,1},{1,0},{2,3},{3,2},{4,5},{5,4},{6,7},{7,6},{8,9},{9,8},{10,11... | collective-permute-start | bytes 1327112 | tf_op jit(solution)/shard_map/ppermute | solution.py:18
  16.2 6.1 %collective-permute-start.9 = (bf16[2,216,128]{2,1,0:T(8,128)(2,1)S(1)}, bf16[2,216,128]{2,1,0:T(8,128)(2,1)S(1)}, u32[]{:S(2)}, u32[]{:S(2)}) collective-permute-start(bf16[2,216,128]{2,1,0:T(8,128)(2,1)S(1)} %get-tuple-element.57), channel_id=1, source_target_pairs={{0,4},{4,0},{8,12},{12,8},{16,20},{20,16},{24,28},{28,24},{1,5},{5... | collective-permute-start | bytes 331784 | tf_op jit(solution)/shard_map/ppermute | solution.py:18
  18.9 4.8 %collective-permute-start.10 = (bf16[2,216,128]{2,1,0:T(8,128)(2,1)S(1)}, bf16[2,216,128]{2,1,0:T(8,128)(2,1)S(1)}, u32[]{:S(2)}, u32[]{:S(2)}) collective-permute-start(bf16[2,216,128]{2,1,0:T(8,128)(2,1)S(1)} %get-tuple-element.59), channel_id=1, source_target_pairs={{0,8},{4,12},{8,0},{12,4},{16,24},{20,28},{24,16},{28,20},{1,9},{5... | collective-permute-start | bytes 331784 | tf_op jit(solution)/shard_map/ppermute | solution.py:18
  23.8 4.2 %collective-permute-start.11 = (bf16[1,216,128]{2,1,0:T(8,128)(2,1)S(1)}, bf16[1,216,128]{2,1,0:T(8,128)(2,1)S(1)}, u32[]{:S(2)}, u32[]{:S(2)}) collective-permute-start(bf16[1,216,128]{2,1,0:T(8,128)(2,1)S(1)} %get-tuple-element.61), channel_id=1, source_target_pairs={{0,8},{4,12},{8,0},{12,4},{16,24},{20,28},{24,16},{28,20},{1,9},{5... | collective-permute-start | bytes 165896 | tf_op jit(solution)/shard_map/ppermute | solution.py:18
  25.4 4.2 %collective-permute-start.12 = (bf16[1,216,128]{2,1,0:T(8,128)(2,1)S(1)}, bf16[1,216,128]{2,1,0:T(8,128)(2,1)S(1)}, u32[]{:S(2)}, u32[]{:S(2)}) collective-permute-start(bf16[1,216,128]{2,1,0:T(8,128)(2,1)S(1)} %get-tuple-element.63), channel_id=1, source_target_pairs={{0,4},{4,0},{8,12},{12,8},{16,20},{20,16},{24,28},{28,24},{1,5},{5... | collective-permute-start | bytes 165896 | tf_op jit(solution)/shard_map/ppermute | solution.py:18
  29.6 5.6 %collective-permute-start.13 = (bf16[1,216,128]{2,1,0:T(8,128)(2,1)S(1)}, bf16[1,216,128]{2,1,0:T(8,128)(2,1)S(1)}, u32[]{:S(2)}, u32[]{:S(2)}) collective-permute-start(bf16[1,216,128]{2,1,0:T(8,128)(2,1)S(1)} %get-tuple-element.65), channel_id=1, source_target_pairs={{0,16},{4,20},{8,24},{12,28},{16,0},{20,4},{24,8},{28,12},{1,17},{... | collective-permute-start | bytes 165896 | tf_op jit(solution)/shard_map/ppermute | solution.py:18
  31.5 6.5 %collective-permute-start.14 = (f32[1,216,128]{2,1,0:T(8,128)S(1)}, f32[1,216,128]{2,1,0:T(8,128)S(1)}, u32[]{:S(2)}, u32[]{:S(2)}) collective-permute-start(f32[1,216,128]{2,1,0:T(8,128)S(1)} %get-tuple-element.64.own_ref), channel_id=1, source_target_pairs={{0,2},{2,0},{1,3},{3,1},{4,6},{6,4},{5,7},{7,5},{8,10},{10,8},{9,1... | collective-permute-start | bytes 331784 | tf_op jit(solution)/shard_map/ppermute | solution.py:18
  35.2 4.2 %collective-permute-start.15 = (bf16[1,216,128]{2,1,0:T(8,128)(2,1)S(1)}, bf16[1,216,128]{2,1,0:T(8,128)(2,1)S(1)}, u32[]{:S(2)}, u32[]{:S(2)}) collective-permute-start(bf16[1,216,128]{2,1,0:T(8,128)(2,1)S(1)} %collective-permute-done.13.got_ref), channel_id=1, source_target_pairs={{0,2},{2,0},{1,3},{3,1},{4,6},{6,4},{5,7},{7,5},{8,10},{10,8},{9,1... | collective-permute-start | bytes 165896 | tf_op jit(solution)/shard_map/ppermute | solution.py:18
  36.7 5.8 %collective-permute-start.4 = (bf16[2,49,128]{2,1,0:T(8,128)(2,1)S(1)}, bf16[2,49,128]{2,1,0:T(8,128)(2,1)S(1)}, u32[]{:S(2)}, u32[]{:S(2)}) collective-permute-start(bf16[2,49,128]{2,1,0:T(8,128)(2,1)S(1)} %shard_map.96), channel_id=1, source_target_pairs={{4,0},{8,4},{12,8},{16,12},{20,16},{24,20},{28,24},{5,1},{9,5},{13... | collective-permute-start | bytes 75272 | tf_op jit(solution)/shard_map/ppermute | solution.py:24
  39.4 3.1 %copy-start.1 = (bf16[2,16,32,128]{3,2,1,0:T(8,128)(2,1)S(1)}, bf16[2,16,32,128]{3,2,1,0:T(8,128)(2,1)}, u32[]{:S(2)}) copy-start(bf16[2,16,32,128]{3,2,1,0:T(8,128)(2,1)} %refs_4_.1) | copy-start | bytes 786436
  39.4 11.1 %collective-permute-start.16 = (f32[1,216,128]{2,1,0:T(8,128)S(1)}, f32[1,216,128]{2,1,0:T(8,128)S(1)}, u32[]{:S(2)}, u32[]{:S(2)}) collective-permute-start(f32[1,216,128]{2,1,0:T(8,128)S(1)} %shard_map.106.own_ref), channel_id=1, source_target_pairs={{0,1},{1,0},{2,3},{3,2},{4,5},{5,4},{6,7},{7,6},{8,9},{9,8},{10,11... | collective-permute-start | bytes 331784 | tf_op jit(solution)/shard_map/ppermute | solution.py:18
  44.8 1.9 %collective-permute-start.5 = (f32[8,128]{1,0:T(8,128)S(1)}, f32[8,128]{1,0:T(8,128)S(1)}, u32[]{:S(2)}, u32[]{:S(2)}) collective-permute-start(f32[8,128]{1,0:T(8,128)S(1)} %get-tuple-element.49.refs_0_), channel_id=1, source_target_pairs={{0,1},{1,0},{2,3},{3,2},{4,5},{5,4},{6,7},{7,6},{8,9},{9,8},{10,11... | collective-permute-start | bytes 12296 | tf_op jit(solution)/shard_map/ppermute | solution.py:18
  44.9 3.7 %collective-permute-start.6 = (f32[8,128]{1,0:T(8,128)S(1)}, f32[8,128]{1,0:T(8,128)S(1)}, u32[]{:S(2)}, u32[]{:S(2)}) collective-permute-start(f32[8,128]{1,0:T(8,128)S(1)} %get-tuple-element.49.refs_0_), channel_id=1, source_target_pairs={{0,2},{2,0},{1,3},{3,1},{4,6},{6,4},{5,7},{7,5},{8,10},{10,8},{9,1... | collective-permute-start | bytes 12296 | tf_op jit(solution)/shard_map/ppermute | solution.py:18
  46.1 3.1 %collective-permute-start.7 = (f32[8,128]{1,0:T(8,128)S(1)}, f32[8,128]{1,0:T(8,128)S(1)}, u32[]{:S(2)}, u32[]{:S(2)}) collective-permute-start(f32[8,128]{1,0:T(8,128)S(1)} %get-tuple-element.49.refs_0_), channel_id=1, source_target_pairs={{0,3},{1,2},{2,1},{3,0},{4,7},{5,6},{6,5},{7,4},{8,11},{9,10},{10,... | collective-permute-start | bytes 12296 | tf_op jit(solution)/shard_map/ppermute | solution.py:680

commit v9 on v8

--- a/solution.py
+++ b/solution.py
@@ -97,11 +97,17 @@
     out_ref[...] = mine + (below_ref[...] + below_got_ref[...].astype(jnp.float32))
 
 
-def whole_kernel(own_ref, beside_ref, out_ref):
+def whole_kernel(own_ref, beside_ref, out_hbm, sems):
     half = own_ref.shape[1]
     side = lax.axis_index("width")
-    out_ref[pl.ds(pl.multiple_of(side * half, 8), half), :] = own_ref[0]
-    out_ref[pl.ds(pl.multiple_of((1 - side) * half, 8), half), :] = beside_ref[0]
+    copies = []
+    for i, (ref, place) in enumerate(((own_ref, side), (beside_ref, 1 - side))):
+        rows = pl.ds(pl.multiple_of(place * half, 8), half)
+        copies.append(pltpu.make_async_copy(ref.at[0], out_hbm.at[rows, :], sems.at[i]))
+    for copy in copies:
+        copy.start()
+    for copy in copies:
+        copy.wait()
 
 
 def reduced_share(mine, theirs, rows):
@@ -138,7 +144,8 @@
     return call(
         whole_kernel,
         jax.ShapeDtypeStruct((rows, channels), f32),
-        out_specs=pl.BlockSpec((rows, channels), lambda: (0, 0)),
+        scratch=(pltpu.SemaphoreType.DMA((2,)),),
+        out_specs=pl.BlockSpec(memory_space=pltpu.HBM),
     )(total, beside)
 
 

time: 51.4 us -> 51.4 us (level)
  no operation moved by 1% of the time
where the time goes in v9:
time: 51.4 us; the launch traced here: 51.2 us
  starting transfers between devices  19.1 us (37%)
  waiting for transfers between devices  19 us (37%)
  Pallas kernels  12.4 us (24%)
  between operations  0.76 us (1%)
    ppermute x13, starting transfers between devices, exchanged(): return lax.ppermute(value, axis, [(i, i ^ distance) for i in range(count)])  15.7 us
    ppermute x13, waiting for transfers between devices, exchanged(): return lax.ppermute(value, axis, [(i, i ^ distance) for i in range(count)])  14.1 us
    pallas_call x13, Pallas kernels, run(): pl.pallas_call(kernel, out_shape=out_shape, in_specs=in_specs or [here] *...  12.4 us
    ppermute x2, starting transfers between devices, shifted(): lax.ppermute(value, axis, [(source, source + steps) for source in range(i...  2.57 us
    ppermute x1, waiting for transfers between devices, rims(): lax.ppermute(corner, ('height', 'width'), [(i, 3 - i) for i in range(4)])  2.3 us
    ppermute x2, waiting for transfers between devices, shifted(): lax.ppermute(value, axis, [(source, source + steps) for source in range(i...  1.98 us
  transfers between devices with their start and end apart: 17, of which 12 were waited for; matrix products, arithmetic and copies ran while one was open for 0% of the time, Pallas kernels for 18%

profile of v9, /device:TPU:0, one launch (start us, length us, event | category | flops | bytes accessed | tf_op | source)
XLA Modules:
  0.0 51.2 jit_solution(8698276109775386745)
XLA Ops:
  0.6 1.4 %shard_map.95 = (bf16[2,16,32,128]{3,2,1,0:T(8,128)(2,1)S(1)}, bf16[6,32,128]{2,1,0:T(8,128)(2,1)S(1)}, bf16[6,16,128]{2,1,0:T(8,128)(2,1)S(1)}, bf16[6,128]{1,0...) custom-call(bf16[4,16,32,128]{3,2,1,0:T(8,128)(2,1)} %refs_0_.1, ...), custom_call_target="tpu_custom_call" | custom-call | tf_op jit(solution)/shard_map/pallas_call | solution.py:526
  2.0 1.3 %collective-permute-start = (bf16[2,16,32,128]{3,2,1,0:T(8,128)(2,1)S(1)}, bf16[2,16,32,128]{3,2,1,0:T(8,128)(2,1)S(1)}, u32[]{:S(2)}, u32[]{:S(2)}) collective-permute-start(bf16[2,16,32,128]{3,2,1,0:T(8,128)(2,1)S(1)} %get-tuple-element.34), channel_id=1, source_target_pairs={{4,0},{8,4},{12,8},{16,12},{20,16},{24,20},{28,24},{5,1},{9,5},{13... | collective-permute-start | bytes 786440 | tf_op jit(solution)/shard_map/ppermute | solution.py:24
  3.3 3.1 %collective-permute-start.1 = (bf16[6,32,128]{2,1,0:T(8,128)(2,1)S(1)}, bf16[6,32,128]{2,1,0:T(8,128)(2,1)S(1)}, u32[]{:S(2)}, u32[]{:S(2)}) collective-permute-start(bf16[6,32,128]{2,1,0:T(8,128)(2,1)S(1)} %get-tuple-element.35), channel_id=1, source_target_pairs={{0,2},{2,0},{1,3},{3,1},{4,6},{6,4},{5,7},{7,5},{8,10},{10,8},{9,1... | collective-permute-start | bytes 147464 | tf_op jit(solution)/shard_map/ppermute | solution.py:18
  6.4 0.0 collective-permute-start.2
  6.4 0.2 collective-permute-start.3
  6.6 0.5 shard_map.97
  7.1 2.3 %collective-permute-done.3.corner_ref.refs_3_ = bf16[6,128]{1,0:T(8,128)(2,1)S(1)} collective-permute-done((bf16[6,128]{1,0:T(8,128)(2,1)S(1)}, bf16[6,128]{1,0:T(8,128)(2,1)S(1)}, u32[]{:S(2)}, u32[]{:S(2)}) %collective-permute-start.3) | collective-permute-done | bytes 1568 | tf_op jit(solution)/shard_map/ppermute | solution.py:569
  9.4 0.0 collective-permute-done.2.col_ref.refs_2_
  9.4 0.0 collective-permute-done.1.row_ref.refs_1_
  9.4 2.7 %shard_map.98 = (bf16[4,18,32,384]{3,2,1,0:T(8,128)(2,1)S(1)}, f32[3456,128]{1,0:T(8,128)S(1)}, bf16[2,18,32,384]{3,2,1,0:T(8,128)(2,1)S(1)}) custom-call(bf16[128,2048]{1,0:T(8,128)(2,1)S(1)} %get-tuple-element.43.act_ref, bf16[4,16,32,128]{3,2,1,0:T(8,128)(2,1)S(1)} %get-tuple-element.44.refs_0_.refs_7_, ...), custom_call_target="tpu_custom_call" | custom-call | flops 1358954496 | bytes 4194304 | tf_op jit(solution)/shard_map/pallas_call | solution.py:526
  12.1 1.1 %collective-permute-done.refs_0_.halo_ref = bf16[2,16,32,128]{3,2,1,0:T(8,128)(2,1)S(1)} collective-permute-done((bf16[2,16,32,128]{3,2,1,0:T(8,128)(2,1)S(1)}, bf16[2,16,32,128]{3,2,1,0:T(8,128)(2,1)S(1)}, u32[]{:S(2)}, u32[]{:S(2)}) %collective-permute-start) | collective-permute-done | bytes 262176 | tf_op jit(solution)/shard_map/ppermute | solution.py:24
  13.2 1.0 %shard_map.102 = (f32[8,216,128]{2,1,0:T(8,128)S(1)}, bf16[8,216,128]{2,1,0:T(8,128)(2,1)S(1)}) custom-call(bf16[2,18,32,384]{3,2,1,0:T(8,128)(2,1)S(1)} %get-tuple-element.52.act_window_ref, f32[3456,128]{1,0:T(8,128)S(1)} %get-tuple-element.53.near_sum_ref, bf16[2,16,32,128]{3,2,1,0:T(8,128)(2,1)S(1)} %collective-permute-done.refs_0_.halo_ref), custom_call_target="tpu_custom_call" | custom-call | flops 452984832 | bytes 4194304 | tf_op jit(solution)/shard_map/pallas_call | solution.py:526
  14.2 0.0 copy-start
  14.2 0.1 collective-permute-start.8
  14.3 1.8 %collective-permute-done.8.got_ref = bf16[8,216,128]{2,1,0:T(8,128)(2,1)S(1)} collective-permute-done((bf16[8,216,128]{2,1,0:T(8,128)(2,1)S(1)}, bf16[8,216,128]{2,1,0:T(8,128)(2,1)S(1)}, u32[]{:S(2)}, u32[]{:S(2)}) %collective-permute-start.8) | collective-permute-done | bytes 442400 | tf_op jit(solution)/shard_map/ppermute | solution.py:18
  16.1 0.1 shard_map.103
  16.2 2.7 %collective-permute-start.9 = (bf16[2,216,128]{2,1,0:T(8,128)(2,1)S(1)}, bf16[2,216,128]{2,1,0:T(8,128)(2,1)S(1)}, u32[]{:S(2)}, u32[]{:S(2)}) collective-permute-start(bf16[2,216,128]{2,1,0:T(8,128)(2,1)S(1)} %get-tuple-element.57), channel_id=1, source_target_pairs={{0,4},{4,0},{8,12},{12,8},{16,20},{20,16},{24,28},{28,24},{1,5},{5... | collective-permute-start | bytes 331784 | tf_op jit(solution)/shard_map/ppermute | solution.py:18
  18.9 1.6 %collective-permute-start.10 = (bf16[2,216,128]{2,1,0:T(8,128)(2,1)S(1)}, bf16[2,216,128]{2,1,0:T(8,128)(2,1)S(1)}, u32[]{:S(2)}, u32[]{:S(2)}) collective-permute-start(bf16[2,216,128]{2,1,0:T(8,128)(2,1)S(1)} %get-tuple-element.59), channel_id=1, source_target_pairs={{0,8},{4,12},{8,0},{12,4},{16,24},{20,28},{24,16},{28,20},{1,9},{5... | collective-permute-start | bytes 331784 | tf_op jit(solution)/shard_map/ppermute | solution.py:18
  20.5 1.8 %collective-permute-done.9.low_got_ref = bf16[2,216,128]{2,1,0:T(8,128)(2,1)S(1)} collective-permute-done((bf16[2,216,128]{2,1,0:T(8,128)(2,1)S(1)}, bf16[2,216,128]{2,1,0:T(8,128)(2,1)S(1)}, u32[]{:S(2)}, u32[]{:S(2)}) %collective-permute-start.9) | collective-permute-done | bytes 110624 | tf_op jit(solution)/shard_map/ppermute | solution.py:18
  22.3 1.5 %collective-permute-done.10.high_got_ref = bf16[2,216,128]{2,1,0:T(8,128)(2,1)S(1)} collective-permute-done((bf16[2,216,128]{2,1,0:T(8,128)(2,1)S(1)}, bf16[2,216,128]{2,1,0:T(8,128)(2,1)S(1)}, u32[]{:S(2)}, u32[]{:S(2)}) %collective-permute-start.10) | collective-permute-done | bytes 110624 | tf_op jit(solution)/shard_map/ppermute | solution.py:18
  23.7 0.1 shard_map.104
  23.8 1.6 %collective-permute-start.11 = (bf16[1,216,128]{2,1,0:T(8,128)(2,1)S(1)}, bf16[1,216,128]{2,1,0:T(8,128)(2,1)S(1)}, u32[]{:S(2)}, u32[]{:S(2)}) collective-permute-start(bf16[1,216,128]{2,1,0:T(8,128)(2,1)S(1)} %get-tuple-element.61), channel_id=1, source_target_pairs={{0,8},{4,12},{8,0},{12,4},{16,24},{20,28},{24,16},{28,20},{1,9},{5... | collective-permute-start | bytes 165896 | tf_op jit(solution)/shard_map/ppermute | solution.py:18
  25.4 0.9 %collective-permute-start.12 = (bf16[1,216,128]{2,1,0:T(8,128)(2,1)S(1)}, bf16[1,216,128]{2,1,0:T(8,128)(2,1)S(1)}, u32[]{:S(2)}, u32[]{:S(2)}) collective-permute-start(bf16[1,216,128]{2,1,0:T(8,128)(2,1)S(1)} %get-tuple-element.63), channel_id=1, source_target_pairs={{0,4},{4,0},{8,12},{12,8},{16,20},{20,16},{24,28},{28,24},{1,5},{5... | collective-permute-start | bytes 165896 | tf_op jit(solution)/shard_map/ppermute | solution.py:18
  26.4 1.6 %collective-permute-done.11.refs_1_ = bf16[1,216,128]{2,1,0:T(8,128)(2,1)S(1)} collective-permute-done((bf16[1,216,128]{2,1,0:T(8,128)(2,1)S(1)}, bf16[1,216,128]{2,1,0:T(8,128)(2,1)S(1)}, u32[]{:S(2)}, u32[]{:S(2)}) %collective-permute-start.11) | collective-permute-done | bytes 55328 | tf_op jit(solution)/shard_map/ppermute | solution.py:18
  28.0 1.6 %collective-permute-done.12.refs_3_ = bf16[1,216,128]{2,1,0:T(8,128)(2,1)S(1)} collective-permute-done((bf16[1,216,128]{2,1,0:T(8,128)(2,1)S(1)}, bf16[1,216,128]{2,1,0:T(8,128)(2,1)S(1)}, u32[]{:S(2)}, u32[]{:S(2)}) %collective-permute-start.12) | collective-permute-done | bytes 55328 | tf_op jit(solution)/shard_map/ppermute | solution.py:18
  29.6 1.9 %collective-permute-start.13 = (bf16[1,216,128]{2,1,0:T(8,128)(2,1)S(1)}, bf16[1,216,128]{2,1,0:T(8,128)(2,1)S(1)}, u32[]{:S(2)}, u32[]{:S(2)}) collective-permute-start(bf16[1,216,128]{2,1,0:T(8,128)(2,1)S(1)} %get-tuple-element.65), channel_id=1, source_target_pairs={{0,16},{4,20},{8,24},{12,28},{16,0},{20,4},{24,8},{28,12},{1,17},{... | collective-permute-start | bytes 165896 | tf_op jit(solution)/shard_map/ppermute | solution.py:18
  31.5 0.9 %collective-permute-start.14 = (f32[1,216,128]{2,1,0:T(8,128)S(1)}, f32[1,216,128]{2,1,0:T(8,128)S(1)}, u32[]{:S(2)}, u32[]{:S(2)}) collective-permute-start(f32[1,216,128]{2,1,0:T(8,128)S(1)} %get-tuple-element.64.own_ref), channel_id=1, source_target_pairs={{0,2},{2,0},{1,3},{3,1},{4,6},{6,4},{5,7},{7,5},{8,10},{10,8},{9,1... | collective-permute-start | bytes 331784 | tf_op jit(solution)/shard_map/ppermute | solution.py:18
  32.5 2.7 %collective-permute-done.13.got_ref = bf16[1,216,128]{2,1,0:T(8,128)(2,1)S(1)} collective-permute-done((bf16[1,216,128]{2,1,0:T(8,128)(2,1)S(1)}, bf16[1,216,128]{2,1,0:T(8,128)(2,1)S(1)}, u32[]{:S(2)}, u32[]{:S(2)}) %collective-permute-start.13) | collective-permute-done | bytes 55328 | tf_op jit(solution)/shard_map/ppermute | solution.py:18
  35.2 1.5 %collective-permute-start.15 = (bf16[1,216,128]{2,1,0:T(8,128)(2,1)S(1)}, bf16[1,216,128]{2,1,0:T(8,128)(2,1)S(1)}, u32[]{:S(2)}, u32[]{:S(2)}) collective-permute-start(bf16[1,216,128]{2,1,0:T(8,128)(2,1)S(1)} %collective-permute-done.13.got_ref), channel_id=1, source_target_pairs={{0,2},{2,0},{1,3},{3,1},{4,6},{6,4},{5,7},{7,5},{8,10},{10,8},{9,1... | collective-permute-start | bytes 165896 | tf_op jit(solution)/shard_map/ppermute | solution.py:18
  36.7 1.3 %collective-permute-start.4 = (bf16[2,49,128]{2,1,0:T(8,128)(2,1)S(1)}, bf16[2,49,128]{2,1,0:T(8,128)(2,1)S(1)}, u32[]{:S(2)}, u32[]{:S(2)}) collective-permute-start(bf16[2,49,128]{2,1,0:T(8,128)(2,1)S(1)} %shard_map.96), channel_id=1, source_target_pairs={{4,0},{8,4},{12,8},{16,12},{20,16},{24,20},{28,24},{5,1},{9,5},{13... | collective-permute-start | bytes 75272 | tf_op jit(solution)/shard_map/ppermute | solution.py:24
  38.0 0.0 collective-permute-done.14.below_ref
  38.0 1.3 %collective-permute-done.15.below_got_ref = bf16[1,216,128]{2,1,0:T(8,128)(2,1)S(1)} collective-permute-done((bf16[1,216,128]{2,1,0:T(8,128)(2,1)S(1)}, bf16[1,216,128]{2,1,0:T(8,128)(2,1)S(1)}, u32[]{:S(2)}, u32[]{:S(2)}) %collective-permute-start.15) | collective-permute-done | bytes 55328 | tf_op jit(solution)/shard_map/ppermute | solution.py:18
  39.4 0.0 copy-start.1
  39.4 0.1 collective-permute-start.16
  39.5 0.0 copy-done
  39.5 2.1 %shard_map.99 = (f32[2,16,32,128]{3,2,1,0:T(8,128)S(1)}, f32[8,128]{1,0:T(8,128)S(1)}) custom-call(bf16[4,18,32,384]{3,2,1,0:T(8,128)(2,1)S(1)} %get-tuple-element.47.near_ref.refs_2_, bf16[3,3,3,128,128]{4,3,2,1,0:T(8,128)(2,1)S(1)} %copy-done, bf16[4,16,32,128]{3,2,1,0:T(8,128)(2,1)S(1)} %get-tuple-element.38.features_ref.refs_5_.refs_6_, ...), custom_call_target="tpu_custom_call" | custom-call | flops 905969664 | bytes 4194304 | tf_op jit(solution)/shard_map/pallas_call | solution.py:526
  41.6 0.8 %collective-permute-done.4.refs_1_ = bf16[2,49,128]{2,1,0:T(8,128)(2,1)S(1)} collective-permute-done((bf16[2,49,128]{2,1,0:T(8,128)(2,1)S(1)}, bf16[2,49,128]{2,1,0:T(8,128)(2,1)S(1)}, u32[]{:S(2)}, u32[]{:S(2)}) %collective-permute-start.4) | collective-permute-done | bytes 25120 | tf_op jit(solution)/shard_map/ppermute | solution.py:24
  42.5 0.0 copy-done.1
  42.5 2.4 %shard_map.100 = (f32[2,16,32,128]{3,2,1,0:T(8,128)S(1)}, f32[8,128]{1,0:T(8,128)S(1)}) custom-call(bf16[2,16,32,128]{3,2,1,0:T(8,128)(2,1)S(1)} %collective-permute-done.refs_0_.halo_ref, bf16[2,49,128]{2,1,0:T(8,128)(2,1)S(1)} %collective-permute-done.4.refs_1_, bf16[4,18,32,384]{3,2,1,0:T(8,128)(2,1)S(1)} %get-tuple-element.47.near_ref.refs_2_, ...), custom_call_target="tpu_custom_call" | custom-call | flops 905969664 | bytes 4194304 | tf_op jit(solution)/shard_map/pallas_call | solution.py:526
  44.8 0.1 collective-permute-start.5
  44.9 1.2 %collective-permute-start.6 = (f32[8,128]{1,0:T(8,128)S(1)}, f32[8,128]{1,0:T(8,128)S(1)}, u32[]{:S(2)}, u32[]{:S(2)}) collective-permute-start(f32[8,128]{1,0:T(8,128)S(1)} %get-tuple-element.49.refs_0_), channel_id=1, source_target_pairs={{0,2},{2,0},{1,3},{3,1},{4,6},{6,4},{5,7},{7,5},{8,10},{10,8},{9,1... | collective-permute-start | bytes 12296 | tf_op jit(solution)/shard_map/ppermute | solution.py:18
  46.1 0.7 %collective-permute-start.7 = (f32[8,128]{1,0:T(8,128)S(1)}, f32[8,128]{1,0:T(8,128)S(1)}, u32[]{:S(2)}, u32[]{:S(2)}) collective-permute-start(f32[8,128]{1,0:T(8,128)S(1)} %get-tuple-element.49.refs_0_), channel_id=1, source_target_pairs={{0,3},{1,2},{2,1},{3,0},{4,7},{5,6},{6,5},{7,4},{8,11},{9,10},{10,... | collective-permute-start | bytes 12296 | tf_op jit(solution)/shard_map/ppermute | solution.py:687
  46.8 0.0 collective-permute-done.5.refs_1_
  46.8 1.8 %collective-permute-done.6.refs_2_ = f32[8,128]{1,0:T(8,128)S(1)} collective-permute-done((f32[8,128]{1,0:T(8,128)S(1)}, f32[8,128]{1,0:T(8,128)S(1)}, u32[]{:S(2)}, u32[]{:S(2)}) %collective-permute-start.6) | collective-permute-done | bytes 4128 | tf_op jit(solution)/shard_map/ppermute | solution.py:18
  48.6 0.6 %collective-permute-done.7.refs_3_ = f32[8,128]{1,0:T(8,128)S(1)} collective-permute-done((f32[8,128]{1,0:T(8,128)S(1)}, f32[8,128]{1,0:T(8,128)S(1)}, u32[]{:S(2)}, u32[]{:S(2)}) %collective-permute-start.7) | collective-permute-done | bytes 4128 | tf_op jit(solution)/shard_map/ppermute | solution.py:687
  49.1 1.4 %shard_map.101 = bf16[4,16,32,128]{3,2,1,0:T(8,128)(2,1)} custom-call(f32[8,128]{1,0:T(8,128)S(1)} %get-tuple-element.49.refs_0_, f32[8,128]{1,0:T(8,128)S(1)} %collective-permute-done.5.refs_1_, f32[8,128]{1,0:T(8,128)S(1)} %collective-permute-done.6.refs_2_, f32[8,128]{1,0:T(8,128)S(1)} %collective-permute-done.7.refs_3_, ...), custom_call_target="tpu_custom_call" | custom-call | flops 5242880 | bytes 2621440 | tf_op jit(solution)/shard_map/pallas_call | solution.py:526
  50.5 0.0 collective-permute-done.16.beside_ref
  50.5 0.7 %shard_map.107 = f32[432,128]{1,0:T(8,128)} custom-call(f32[1,216,128]{2,1,0:T(8,128)S(1)} %shard_map.106.own_ref, f32[1,216,128]{2,1,0:T(8,128)S(1)} %collective-permute-done.16.beside_ref), custom_call_target="tpu_custom_call" | custom-call | tf_op jit(solution)/shard_map/pallas_call | solution.py:526
  (3 shorter events, 0.1 us)
Async XLA Ops:
  2.0 11.2 %collective-permute-start = (bf16[2,16,32,128]{3,2,1,0:T(8,128)(2,1)S(1)}, bf16[2,16,32,128]{3,2,1,0:T(8,128)(2,1)S(1)}, u32[]{:S(2)}, u32[]{:S(2)}) collective-permute-start(bf16[2,16,32,128]{3,2,1,0:T(8,128)(2,1)S(1)} %get-tuple-element.34), channel_id=1, source_target_pairs={{4,0},{8,4},{12,8},{16,12},{20,16},{24,20},{28,24},{5,1},{9,5},{13... | collective-permute-start | bytes 786440 | tf_op jit(solution)/shard_map/ppermute | solution.py:24
  3.3 6.1 %collective-permute-start.1 = (bf16[6,32,128]{2,1,0:T(8,128)(2,1)S(1)}, bf16[6,32,128]{2,1,0:T(8,128)(2,1)S(1)}, u32[]{:S(2)}, u32[]{:S(2)}) collective-permute-start(bf16[6,32,128]{2,1,0:T(8,128)(2,1)S(1)} %get-tuple-element.35), channel_id=1, source_target_pairs={{0,2},{2,0},{1,3},{3,1},{4,6},{6,4},{5,7},{7,5},{8,10},{10,8},{9,1... | collective-permute-start | bytes 147464 | tf_op jit(solution)/shard_map/ppermute | solution.py:18
  6.4 3.0 %collective-permute-start.2 = (bf16[6,16,128]{2,1,0:T(8,128)(2,1)S(1)}, bf16[6,16,128]{2,1,0:T(8,128)(2,1)S(1)}, u32[]{:S(2)}, u32[]{:S(2)}) collective-permute-start(bf16[6,16,128]{2,1,0:T(8,128)(2,1)S(1)} %get-tuple-element.36), channel_id=1, source_target_pairs={{0,1},{1,0},{2,3},{3,2},{4,5},{5,4},{6,7},{7,6},{8,9},{9,8},{10,11... | collective-permute-start | bytes 73736 | tf_op jit(solution)/shard_map/ppermute | solution.py:18
  6.4 3.0 %collective-permute-start.3 = (bf16[6,128]{1,0:T(8,128)(2,1)S(1)}, bf16[6,128]{1,0:T(8,128)(2,1)S(1)}, u32[]{:S(2)}, u32[]{:S(2)}) collective-permute-start(bf16[6,128]{1,0:T(8,128)(2,1)S(1)} %get-tuple-element.37), channel_id=1, source_target_pairs={{0,3},{1,2},{2,1},{3,0},{4,7},{5,6},{6,5},{7,4},{8,11},{9,10},{10,... | collective-permute-start | bytes 4616 | tf_op jit(solution)/shard_map/ppermute | solution.py:569
  14.2 25.3 %copy-start = (bf16[3,3,3,128,128]{4,3,2,1,0:T(8,128)(2,1)S(1)}, bf16[3,3,3,128,128]{4,3,2,1,0:T(8,128)(2,1)}, u32[]{:S(2)}) copy-start(bf16[3,3,3,128,128]{4,3,2,1,0:T(8,128)(2,1)} %refs_3_.3) | copy-start | bytes 2654212
  14.2 1.9 %collective-permute-start.8 = (bf16[8,216,128]{2,1,0:T(8,128)(2,1)S(1)}, bf16[8,216,128]{2,1,0:T(8,128)(2,1)S(1)}, u32[]{:S(2)}, u32[]{:S(2)}) collective-permute-start(bf16[8,216,128]{2,1,0:T(8,128)(2,1)S(1)} %get-tuple-element.55), channel_id=1, source_target_pairs={{0,1},{1,0},{2,3},{3,2},{4,5},{5,4},{6,7},{7,6},{8,9},{9,8},{10,11... | collective-permute-start | bytes 1327112 | tf_op jit(solution)/shard_map/ppermute | solution.py:18
  16.2 6.1 %collective-permute-start.9 = (bf16[2,216,128]{2,1,0:T(8,128)(2,1)S(1)}, bf16[2,216,128]{2,1,0:T(8,128)(2,1)S(1)}, u32[]{:S(2)}, u32[]{:S(2)}) collective-permute-start(bf16[2,216,128]{2,1,0:T(8,128)(2,1)S(1)} %get-tuple-element.57), channel_id=1, source_target_pairs={{0,4},{4,0},{8,12},{12,8},{16,20},{20,16},{24,28},{28,24},{1,5},{5... | collective-permute-start | bytes 331784 | tf_op jit(solution)/shard_map/ppermute | solution.py:18
  18.9 4.8 %collective-permute-start.10 = (bf16[2,216,128]{2,1,0:T(8,128)(2,1)S(1)}, bf16[2,216,128]{2,1,0:T(8,128)(2,1)S(1)}, u32[]{:S(2)}, u32[]{:S(2)}) collective-permute-start(bf16[2,216,128]{2,1,0:T(8,128)(2,1)S(1)} %get-tuple-element.59), channel_id=1, source_target_pairs={{0,8},{4,12},{8,0},{12,4},{16,24},{20,28},{24,16},{28,20},{1,9},{5... | collective-permute-start | bytes 331784 | tf_op jit(solution)/shard_map/ppermute | solution.py:18
  23.8 4.2 %collective-permute-start.11 = (bf16[1,216,128]{2,1,0:T(8,128)(2,1)S(1)}, bf16[1,216,128]{2,1,0:T(8,128)(2,1)S(1)}, u32[]{:S(2)}, u32[]{:S(2)}) collective-permute-start(bf16[1,216,128]{2,1,0:T(8,128)(2,1)S(1)} %get-tuple-element.61), channel_id=1, source_target_pairs={{0,8},{4,12},{8,0},{12,4},{16,24},{20,28},{24,16},{28,20},{1,9},{5... | collective-permute-start | bytes 165896 | tf_op jit(solution)/shard_map/ppermute | solution.py:18
  25.4 4.2 %collective-permute-start.12 = (bf16[1,216,128]{2,1,0:T(8,128)(2,1)S(1)}, bf16[1,216,128]{2,1,0:T(8,128)(2,1)S(1)}, u32[]{:S(2)}, u32[]{:S(2)}) collective-permute-start(bf16[1,216,128]{2,1,0:T(8,128)(2,1)S(1)} %get-tuple-element.63), channel_id=1, source_target_pairs={{0,4},{4,0},{8,12},{12,8},{16,20},{20,16},{24,28},{28,24},{1,5},{5... | collective-permute-start | bytes 165896 | tf_op jit(solution)/shard_map/ppermute | solution.py:18
  29.6 5.6 %collective-permute-start.13 = (bf16[1,216,128]{2,1,0:T(8,128)(2,1)S(1)}, bf16[1,216,128]{2,1,0:T(8,128)(2,1)S(1)}, u32[]{:S(2)}, u32[]{:S(2)}) collective-permute-start(bf16[1,216,128]{2,1,0:T(8,128)(2,1)S(1)} %get-tuple-element.65), channel_id=1, source_target_pairs={{0,16},{4,20},{8,24},{12,28},{16,0},{20,4},{24,8},{28,12},{1,17},{... | collective-permute-start | bytes 165896 | tf_op jit(solution)/shard_map/ppermute | solution.py:18
  31.5 6.5 %collective-permute-start.14 = (f32[1,216,128]{2,1,0:T(8,128)S(1)}, f32[1,216,128]{2,1,0:T(8,128)S(1)}, u32[]{:S(2)}, u32[]{:S(2)}) collective-permute-start(f32[1,216,128]{2,1,0:T(8,128)S(1)} %get-tuple-element.64.own_ref), channel_id=1, source_target_pairs={{0,2},{2,0},{1,3},{3,1},{4,6},{6,4},{5,7},{7,5},{8,10},{10,8},{9,1... | collective-permute-start | bytes 331784 | tf_op jit(solution)/shard_map/ppermute | solution.py:18
  35.2 4.2 %collective-permute-start.15 = (bf16[1,216,128]{2,1,0:T(8,128)(2,1)S(1)}, bf16[1,216,128]{2,1,0:T(8,128)(2,1)S(1)}, u32[]{:S(2)}, u32[]{:S(2)}) collective-permute-start(bf16[1,216,128]{2,1,0:T(8,128)(2,1)S(1)} %collective-permute-done.13.got_ref), channel_id=1, source_target_pairs={{0,2},{2,0},{1,3},{3,1},{4,6},{6,4},{5,7},{7,5},{8,10},{10,8},{9,1... | collective-permute-start | bytes 165896 | tf_op jit(solution)/shard_map/ppermute | solution.py:18
  36.7 5.8 %collective-permute-start.4 = (bf16[2,49,128]{2,1,0:T(8,128)(2,1)S(1)}, bf16[2,49,128]{2,1,0:T(8,128)(2,1)S(1)}, u32[]{:S(2)}, u32[]{:S(2)}) collective-permute-start(bf16[2,49,128]{2,1,0:T(8,128)(2,1)S(1)} %shard_map.96), channel_id=1, source_target_pairs={{4,0},{8,4},{12,8},{16,12},{20,16},{24,20},{28,24},{5,1},{9,5},{13... | collective-permute-start | bytes 75272 | tf_op jit(solution)/shard_map/ppermute | solution.py:24
  39.4 3.1 %copy-start.1 = (bf16[2,16,32,128]{3,2,1,0:T(8,128)(2,1)S(1)}, bf16[2,16,32,128]{3,2,1,0:T(8,128)(2,1)}, u32[]{:S(2)}) copy-start(bf16[2,16,32,128]{3,2,1,0:T(8,128)(2,1)} %refs_4_.1) | copy-start | bytes 786436
  39.4 11.1 %collective-permute-start.16 = (f32[1,216,128]{2,1,0:T(8,128)S(1)}, f32[1,216,128]{2,1,0:T(8,128)S(1)}, u32[]{:S(2)}, u32[]{:S(2)}) collective-permute-start(f32[1,216,128]{2,1,0:T(8,128)S(1)} %shard_map.106.own_ref), channel_id=1, source_target_pairs={{0,1},{1,0},{2,3},{3,2},{4,5},{5,4},{6,7},{7,6},{8,9},{9,8},{10,11... | collective-permute-start | bytes 331784 | tf_op jit(solution)/shard_map/ppermute | solution.py:18
  44.8 1.9 %collective-permute-start.5 = (f32[8,128]{1,0:T(8,128)S(1)}, f32[8,128]{1,0:T(8,128)S(1)}, u32[]{:S(2)}, u32[]{:S(2)}) collective-permute-start(f32[8,128]{1,0:T(8,128)S(1)} %get-tuple-element.49.refs_0_), channel_id=1, source_target_pairs={{0,1},{1,0},{2,3},{3,2},{4,5},{5,4},{6,7},{7,6},{8,9},{9,8},{10,11... | collective-permute-start | bytes 12296 | tf_op jit(solution)/shard_map/ppermute | solution.py:18
  44.9 3.7 %collective-permute-start.6 = (f32[8,128]{1,0:T(8,128)S(1)}, f32[8,128]{1,0:T(8,128)S(1)}, u32[]{:S(2)}, u32[]{:S(2)}) collective-permute-start(f32[8,128]{1,0:T(8,128)S(1)} %get-tuple-element.49.refs_0_), channel_id=1, source_target_pairs={{0,2},{2,0},{1,3},{3,1},{4,6},{6,4},{5,7},{7,5},{8,10},{10,8},{9,1... | collective-permute-start | bytes 12296 | tf_op jit(solution)/shard_map/ppermute | solution.py:18
  46.1 3.1 %collective-permute-start.7 = (f32[8,128]{1,0:T(8,128)S(1)}, f32[8,128]{1,0:T(8,128)S(1)}, u32[]{:S(2)}, u32[]{:S(2)}) collective-permute-start(f32[8,128]{1,0:T(8,128)S(1)} %get-tuple-element.49.refs_0_), channel_id=1, source_target_pairs={{0,3},{1,2},{2,1},{3,0},{4,7},{5,6},{6,5},{7,4},{8,11},{9,10},{10,... | collective-permute-start | bytes 12296 | tf_op jit(solution)/shard_map/ppermute | solution.py:687
